TPU v7x, 32 devices: a whole 2x2x4 slice. The times are simulated.
32 devices in a mesh: ctx: 8 (over y, x, core), wsh: 4 (over z).
Axes of the slice: x: 2, y: 2, z: 4, core: 2. Of those that a mesh axis runs over, the one named last changes fastest.
Arguments:
- states: bfloat16 [4, 2048, 2, 768], P('wsh', 'ctx'), may hold values from -6 to 6
- block_slot: int32 [4, 32], P('wsh'), may hold values from 0 to 31, as said below
- cont_lengths: int32 [4, 4], P('wsh'), may hold values from 1 to 384, 1024 in all within a row
- valid_mask: int32 [4, 2048], P('wsh', 'ctx'), may hold values from 0 to 1
- teacher: bfloat16 [4, 2048, 2, 768], P('wsh', 'ctx'), may hold values from -6 to 6
- out_grad: bfloat16 [4, 2048, 2, 768], P('wsh', 'ctx'), may hold values from -6 to 6
- predict: float32 [2, 2], replicated, may hold values from 0.2 to 1
- correct: float32 [2], replicated, may hold values from 0.5 to 1.5
- norm_attn: bfloat16 [768], P('wsh'), may hold values from 0.5 to 1.5
- w_query: bfloat16 [768, 768], P('wsh'), may hold values from -0.0546875 to 0.0546875
- w_key: bfloat16 [768, 768], P('wsh'), may hold values from -0.21875 to 0.21875
- w_value: bfloat16 [768, 768], P('wsh'), may hold values from -0.21875 to 0.21875
- w_out: bfloat16 [768, 768], P('wsh'), may hold values from -1.75 to 1.75
- norm_ffn: bfloat16 [768], P('wsh'), may hold values from 0.5 to 1.5
- w_gate: bfloat16 [768, 3072], P('wsh'), may hold values from -0.21875 to 0.21875
- w_up: bfloat16 [768, 3072], P('wsh'), may hold values from -0.21875 to 0.21875
- w_down: bfloat16 [3072, 768], P('wsh'), may hold values from -0.109375 to 0.109375
Outputs:
- new_states: bfloat16 [4, 2048, 2, 768], P('wsh', 'ctx')
- states_grad: bfloat16 [4, 2048, 2, 768], P('wsh', 'ctx')
- predict_grad: float32 [2, 2], replicated
- correct_grad: float32 [2], replicated
- norm_attn_grad: float32 [768], P('wsh')
- w_query_grad: float32 [768, 768], P('wsh')
- w_key_grad: float32 [768, 768], P('wsh')
- w_value_grad: float32 [768, 768], P('wsh')
- w_out_grad: float32 [768, 768], P('wsh')
- norm_ffn_grad: float32 [768], P('wsh')
- w_gate_grad: float32 [768, 3072], P('wsh')
- w_up_grad: float32 [768, 3072], P('wsh')
- w_down_grad: float32 [3072, 768], P('wsh')
Inputs may be any that keep to these rules, and one draw needn't show every extreme that they name: `block_slot`: each row is a permutation of 0 to 31 in which slots 2 i and 2 i + 1 hold a block b and the block 31 - b. `cont_lengths`: each row sums to 1024, and its longest continuation has exactly 384 tokens.
All inputs are finite; a program needn't handle non-finite values.
Results may differ from a plain program's by a relative error of at most 0.022.
Values may be sent and summed in bfloat16 or wider, within the bound.
A program may use at most 192 MiB of HBM per device.

v0:
```python
import math

import jax
import jax.numpy as jnp
from jax import lax
from jax.sharding import PartitionSpec as P

HEADS = 12
HD = 64
PROMPT = 1024
BLK = 64


EPSILON = 1e-06
NEGATIVE = -1e30
HIGHEST = lax.Precision.HIGHEST


def rms_forward(tensor, gain_vec):
    factor = lax.rsqrt(jnp.mean(tensor * tensor, axis=-1, keepdims=True) + EPSILON)
    return (tensor * factor * gain_vec, factor)


def rms_backward(tensor, factor, gain_vec, upstream):
    weighted = upstream * gain_vec
    gain_grad = jnp.sum(upstream * tensor * factor, axis=0)
    middle = jnp.mean(weighted * tensor, axis=-1, keepdims=True)
    return (factor * weighted - tensor * factor * factor * factor * middle, gain_grad)


def token_places(block_slot, cont_lengths):
    groups, blocks = block_slot.shape
    offsets = jnp.arange(BLK, dtype=jnp.int32)
    places = (block_slot[:, :, None] * BLK + offsets[None, None, :]).reshape(groups, blocks * BLK)
    starts = PROMPT + jnp.cumsum(cont_lengths, axis=1) - cont_lengths
    segments = jnp.sum((places[:, :, None] >= starts[:, None, :]).astype(jnp.int32), axis=2)
    return (places, segments)


def visible(query_place, query_segment, key_place, key_segment):
    earlier = key_place[:, None, :] <= query_place[:, :, None]
    shared = (key_segment[:, None, :] == 0) | (key_segment[:, None, :] == query_segment[:, :, None])
    return earlier & shared


def split_heads(tensor):
    return tensor.reshape(tensor.shape[0], tensor.shape[1], HEADS, HD)


def forward_block(running, query_part, key_part, value_part, allowed):

    def forward_compute(current):
        maximum, denominator, accumulated = current
        scores = jnp.einsum(
            "gqhd,gkhd->ghqk",
            split_heads(query_part),
            split_heads(key_part),
            preferred_element_type=jnp.float32,
        )
        masked = jnp.where(allowed[:, None], scores, NEGATIVE)
        new_max = jnp.maximum(maximum, jnp.max(masked, axis=-1))
        exponent = jnp.where(allowed[:, None], jnp.exp(masked - new_max[..., None]), 0.0)
        factor = jnp.exp(maximum - new_max)
        rescale = jnp.swapaxes(factor, 1, 2)[..., None]
        update = jnp.einsum(
            "ghqk,gkhd->gqhd",
            exponent.astype(jnp.bfloat16),
            split_heads(value_part),
            preferred_element_type=jnp.float32,
        )
        merged = (split_heads(accumulated) * rescale + update).reshape(accumulated.shape)
        return (new_max, denominator * factor + jnp.sum(exponent, axis=-1), merged)

    return lax.cond(jnp.any(allowed), forward_compute, lambda current: current, running)


def backward_block(
    query_part, grad_part, key_part, value_part, allowed, maximum, denominator, delta_sum
):
    scores = jnp.einsum(
        "gqhd,gkhd->ghqk",
        split_heads(query_part),
        split_heads(key_part),
        preferred_element_type=jnp.float32,
    )
    exponent = jnp.where(allowed[:, None], jnp.exp(scores - maximum[..., None]), 0.0)
    probability = exponent / denominator[..., None]
    prob_grad = jnp.einsum(
        "gqhd,gkhd->ghqk",
        split_heads(grad_part),
        split_heads(value_part),
        preferred_element_type=jnp.float32,
    )
    score_grad = (probability * (prob_grad - delta_sum[..., None])).astype(jnp.bfloat16)
    return (probability.astype(jnp.bfloat16), score_grad)


def shards(
    states,
    block_slot,
    cont_lengths,
    valid_mask,
    teacher,
    out_grad,
    predict,
    correct,
    norm_attn,
    w_query,
    w_key,
    w_value,
    w_out,
    norm_ffn,
    w_gate,
    w_up,
    w_down,
):
    groups, local_len = valid_mask.shape
    model_width = states.shape[3]
    row_count = groups * local_len
    group_len = block_slot.shape[1] * BLK
    gain_one, query_w, key_w, value_w, out_w, gain_two, gate_w, up_w, down_w = (
        lax.all_gather(norm_attn, "wsh", axis=0, tiled=True),
        lax.all_gather(w_query, "wsh", axis=0, tiled=True),
        lax.all_gather(w_key, "wsh", axis=0, tiled=True),
        lax.all_gather(w_value, "wsh", axis=0, tiled=True),
        lax.all_gather(w_out, "wsh", axis=0, tiled=True),
        lax.all_gather(norm_ffn, "wsh", axis=0, tiled=True),
        lax.all_gather(w_gate, "wsh", axis=0, tiled=True),
        lax.all_gather(w_up, "wsh", axis=0, tiled=True),
        lax.all_gather(w_down, "wsh", axis=0, tiled=True),
    )
    valid_float = valid_mask.astype(jnp.float32)
    valid_total = lax.psum(jnp.sum(valid_float), ("ctx", "wsh"))
    places, segments = token_places(block_slot, cont_lengths)
    offset = lax.axis_index("ctx") * local_len
    own_place = lax.dynamic_slice_in_dim(places, offset, local_len, 1)
    own_segment = lax.dynamic_slice_in_dim(segments, offset, local_len, 1)
    inputs = states.astype(jnp.float32)
    mixed_states = jnp.einsum("ij,gtjd->gtid", predict, inputs, precision=HIGHEST)
    active = mixed_states[:, :, 0].reshape(row_count, model_width)
    gain_first = gain_one.astype(jnp.float32)
    normed, factor_one = rms_forward(active, gain_first)
    normed_low = normed.astype(jnp.bfloat16)
    queries = (
        jnp.dot(normed_low, query_w, preferred_element_type=jnp.float32)
        .astype(jnp.bfloat16)
        .reshape(groups, local_len, model_width)
    )
    key_rows = (
        jnp.dot(normed_low, key_w, preferred_element_type=jnp.float32)
        .astype(jnp.bfloat16)
        .reshape(groups, local_len, model_width)
    )
    values = (
        jnp.dot(normed_low, value_w, preferred_element_type=jnp.float32)
        .astype(jnp.bfloat16)
        .reshape(groups, local_len, model_width)
    )
    initial = (
        jnp.full((groups, HEADS, local_len), NEGATIVE, jnp.float32),
        jnp.zeros((groups, HEADS, local_len), jnp.float32),
        jnp.zeros((groups, local_len, model_width), jnp.float32),
    )
    piece_keys = lax.all_gather(key_rows, "ctx", axis=1, tiled=True)
    piece_values = lax.all_gather(values, "ctx", axis=1, tiled=True)
    piece_len = piece_keys.shape[1]
    block_size = math.gcd(piece_len, local_len)

    def fold_one_block(current, block_index):
        begin = block_index * block_size
        key_part = lax.dynamic_slice_in_dim(piece_keys, begin, block_size, 1)
        value_part = lax.dynamic_slice_in_dim(piece_values, begin, block_size, 1)
        key_place = lax.dynamic_slice_in_dim(places, begin, block_size, 1)
        key_segment = lax.dynamic_slice_in_dim(segments, begin, block_size, 1)
        allowed = visible(own_place, own_segment, key_place, key_segment)
        return (forward_block(current, queries, key_part, value_part, allowed), None)

    finished, unused = lax.scan(
        fold_one_block, initial, jnp.arange(piece_len // block_size, dtype=jnp.int32)
    )
    maximum, denominator, accumulated = finished
    attended = (split_heads(accumulated) / jnp.swapaxes(denominator, 1, 2)[..., None]).reshape(
        row_count, model_width
    )
    attended_low = attended.astype(jnp.bfloat16)
    hidden = active + jnp.dot(attended_low, out_w, preferred_element_type=jnp.float32)
    gain_second = gain_two.astype(jnp.float32)
    normed_two, factor_two = rms_forward(hidden, gain_second)
    normed_two_low = normed_two.astype(jnp.bfloat16)
    gate_proj = jnp.dot(normed_two_low, gate_w, preferred_element_type=jnp.float32)
    up_proj = jnp.dot(normed_two_low, up_w, preferred_element_type=jnp.float32)
    inner_act, inner_pull = jax.vjp(
        lambda gate_in, up_in: jax.nn.gelu(gate_in, approximate=True) * up_in, gate_proj, up_proj
    )
    inner_low = inner_act.astype(jnp.bfloat16)
    result = hidden + jnp.dot(inner_low, down_w, preferred_element_type=jnp.float32)
    difference = (result - active).reshape(groups, local_len, 1, model_width)
    out_states = mixed_states + correct[None, None, :, None] * difference
    new_states = out_states.astype(jnp.bfloat16)
    loss_ratio = lax.axis_size("wsh") * groups * group_len / valid_total
    upstream = out_grad.astype(jnp.float32) + loss_ratio * valid_float[:, :, None, None] * (
        out_states - teacher.astype(jnp.float32)
    )
    correct_local = jnp.sum(upstream * difference, axis=(0, 1, 3))
    result_grad = jnp.einsum("i,gtid->gtd", correct, upstream, precision=HIGHEST).reshape(
        row_count, model_width
    )
    result_low = result_grad.astype(jnp.bfloat16)
    down_grad = jnp.einsum("rf,rd->fd", inner_low, result_low, preferred_element_type=jnp.float32)
    inner_grad = jnp.einsum("rd,fd->rf", result_low, down_w, preferred_element_type=jnp.float32)
    gate_grad, up_grad = inner_pull(inner_grad)
    gate_low = gate_grad.astype(jnp.bfloat16)
    up_low = up_grad.astype(jnp.bfloat16)
    gate_w_grad = jnp.einsum(
        "rd,rf->df", normed_two_low, gate_low, preferred_element_type=jnp.float32
    )
    up_w_grad = jnp.einsum("rd,rf->df", normed_two_low, up_low, preferred_element_type=jnp.float32)
    normed_two_grad = jnp.einsum(
        "rf,df->rd", gate_low, gate_w, preferred_element_type=jnp.float32
    ) + jnp.einsum("rf,df->rd", up_low, up_w, preferred_element_type=jnp.float32)
    hidden_norm_grad, gain_two_grad = rms_backward(hidden, factor_two, gain_second, normed_two_grad)
    hidden_grad = result_grad + hidden_norm_grad
    hidden_low = hidden_grad.astype(jnp.bfloat16)
    out_w_grad = jnp.einsum(
        "rc,rd->cd", attended_low, hidden_low, preferred_element_type=jnp.float32
    )
    attended_grad = jnp.einsum(
        "rd,cd->rc", hidden_low, out_w, preferred_element_type=jnp.float32
    ).astype(jnp.bfloat16)
    delta_sum = jnp.swapaxes(
        jnp.sum(
            split_heads(
                (attended_grad.astype(jnp.float32) * attended).reshape(
                    groups, local_len, model_width
                )
            ),
            axis=-1,
        ),
        1,
        2,
    )
    grad_local = attended_grad.reshape(groups, local_len, model_width)
    zero_grad = jnp.zeros((groups, local_len, model_width), jnp.float32)
    all_keys, all_values = (
        lax.all_gather(key_rows, "ctx", axis=1, tiled=True),
        lax.all_gather(values, "ctx", axis=1, tiled=True),
    )

    def query_step(current, block_index):
        begin = block_index * local_len
        key_part = lax.dynamic_slice_in_dim(all_keys, begin, local_len, 1)
        value_part = lax.dynamic_slice_in_dim(all_values, begin, local_len, 1)
        key_place = lax.dynamic_slice_in_dim(places, begin, local_len, 1)
        key_segment = lax.dynamic_slice_in_dim(segments, begin, local_len, 1)
        allowed = visible(own_place, own_segment, key_place, key_segment)

        def query_compute(query_sum):
            prob_low, score_grad = backward_block(
                queries, grad_local, key_part, value_part, allowed, maximum, denominator, delta_sum
            )
            return query_sum + jnp.einsum(
                "ghqk,gkhd->gqhd",
                score_grad,
                split_heads(key_part),
                preferred_element_type=jnp.float32,
            ).reshape(groups, local_len, model_width)

        return (
            lax.cond(jnp.any(allowed), query_compute, lambda query_sum: query_sum, current),
            None,
        )

    finished, unused = lax.scan(
        query_step, zero_grad, jnp.arange(group_len // local_len, dtype=jnp.int32)
    )
    term_rows = local_len * lax.axis_size("ctx")
    key_block_size = math.gcd(term_rows, local_len)

    def key_one_block(block_index):
        begin = block_index * key_block_size
        key_part = lax.dynamic_slice_in_dim(all_keys, begin, key_block_size, 1)
        value_part = lax.dynamic_slice_in_dim(all_values, begin, key_block_size, 1)
        key_place = lax.dynamic_slice_in_dim(places, begin, key_block_size, 1)
        key_segment = lax.dynamic_slice_in_dim(segments, begin, key_block_size, 1)
        allowed = visible(own_place, own_segment, key_place, key_segment)

        def one_compute(unused_arg):
            prob_low, score_grad = backward_block(
                queries, grad_local, key_part, value_part, allowed, maximum, denominator, delta_sum
            )
            key_add = jnp.einsum(
                "ghqk,gqhd->kghd",
                score_grad,
                split_heads(queries),
                preferred_element_type=jnp.float32,
            ).reshape(key_block_size, groups, model_width)
            value_add = jnp.einsum(
                "ghqk,gqhd->kghd",
                prob_low,
                split_heads(grad_local),
                preferred_element_type=jnp.float32,
            ).reshape(key_block_size, groups, model_width)
            return jnp.stack([key_add, value_add], axis=1)

        return lax.cond(
            jnp.any(allowed),
            one_compute,
            lambda unused_arg: jnp.zeros((key_block_size, 2, groups, model_width), jnp.float32),
            0,
        )

    summed = lax.psum_scatter(
        lax.map(key_one_block, jnp.arange(term_rows // key_block_size, dtype=jnp.int32))
        .reshape(term_rows, 2, groups, model_width)
        .astype(jnp.bfloat16),
        "ctx",
        scatter_dimension=0,
        tiled=True,
    ).astype(jnp.float32)
    key_grad = jnp.swapaxes(summed[:, 0], 0, 1)
    value_grad = jnp.swapaxes(summed[:, 1], 0, 1)
    query_low = finished.reshape(row_count, model_width).astype(jnp.bfloat16)
    key_low = key_grad.reshape(row_count, model_width).astype(jnp.bfloat16)
    value_low = value_grad.reshape(row_count, model_width).astype(jnp.bfloat16)
    query_w_grad = jnp.einsum(
        "rc,rd->cd", normed_low, query_low, preferred_element_type=jnp.float32
    )
    key_w_grad = jnp.einsum("rc,rd->cd", normed_low, key_low, preferred_element_type=jnp.float32)
    value_w_grad = jnp.einsum(
        "rc,rd->cd", normed_low, value_low, preferred_element_type=jnp.float32
    )
    normed_grad = (
        jnp.einsum("rd,cd->rc", query_low, query_w, preferred_element_type=jnp.float32)
        + jnp.einsum("rd,cd->rc", key_low, key_w, preferred_element_type=jnp.float32)
        + jnp.einsum("rd,cd->rc", value_low, value_w, preferred_element_type=jnp.float32)
    )
    active_norm_grad, gain_one_grad = rms_backward(active, factor_one, gain_first, normed_grad)
    active_grad = (hidden_grad + active_norm_grad - result_grad).reshape(
        groups, local_len, 1, model_width
    )
    mixed_grad = jnp.concatenate([upstream[:, :, :1] + active_grad, upstream[:, :, 1:]], axis=2)
    predict_local = jnp.einsum("gtid,gtjd->ij", mixed_grad, inputs, precision=HIGHEST)
    states_grad = jnp.einsum("ij,gtid->gtjd", predict, mixed_grad, precision=HIGHEST).astype(
        jnp.bfloat16
    )
    predict_grad, correct_grad = lax.psum((predict_local, correct_local), ("ctx", "wsh"))
    (
        gain_one_rows,
        query_rows,
        key_grad_rows,
        value_rows,
        out_rows,
        gain_two_rows,
        gate_rows,
        up_rows,
        down_rows,
    ) = (
        lax.psum_scatter(
            gain_one_grad.astype(jnp.bfloat16), "wsh", scatter_dimension=0, tiled=True
        ).astype(jnp.float32),
        lax.psum_scatter(
            query_w_grad.astype(jnp.bfloat16), "wsh", scatter_dimension=0, tiled=True
        ).astype(jnp.float32),
        lax.psum_scatter(
            key_w_grad.astype(jnp.bfloat16), "wsh", scatter_dimension=0, tiled=True
        ).astype(jnp.float32),
        lax.psum_scatter(
            value_w_grad.astype(jnp.bfloat16), "wsh", scatter_dimension=0, tiled=True
        ).astype(jnp.float32),
        lax.psum_scatter(
            out_w_grad.astype(jnp.bfloat16), "wsh", scatter_dimension=0, tiled=True
        ).astype(jnp.float32),
        lax.psum_scatter(
            gain_two_grad.astype(jnp.bfloat16), "wsh", scatter_dimension=0, tiled=True
        ).astype(jnp.float32),
        lax.psum_scatter(
            gate_w_grad.astype(jnp.bfloat16), "wsh", scatter_dimension=0, tiled=True
        ).astype(jnp.float32),
        lax.psum_scatter(
            up_w_grad.astype(jnp.bfloat16), "wsh", scatter_dimension=0, tiled=True
        ).astype(jnp.float32),
        lax.psum_scatter(
            down_grad.astype(jnp.bfloat16), "wsh", scatter_dimension=0, tiled=True
        ).astype(jnp.float32),
    )
    totals = (
        lax.psum(gain_one_rows.astype(jnp.bfloat16), "ctx").astype(jnp.float32),
        lax.psum(query_rows.astype(jnp.bfloat16), "ctx").astype(jnp.float32),
        lax.psum(key_grad_rows.astype(jnp.bfloat16), "ctx").astype(jnp.float32),
        lax.psum(value_rows.astype(jnp.bfloat16), "ctx").astype(jnp.float32),
        lax.psum(out_rows.astype(jnp.bfloat16), "ctx").astype(jnp.float32),
        lax.psum(gain_two_rows.astype(jnp.bfloat16), "ctx").astype(jnp.float32),
        lax.psum(gate_rows.astype(jnp.bfloat16), "ctx").astype(jnp.float32),
        lax.psum(up_rows.astype(jnp.bfloat16), "ctx").astype(jnp.float32),
        lax.psum(down_rows.astype(jnp.bfloat16), "ctx").astype(jnp.float32),
    )
    return (new_states, states_grad, predict_grad, correct_grad) + tuple(totals)


def solution(mesh):
    return jax.shard_map(
        shards,
        mesh=mesh,
        in_specs=(
            P("wsh", "ctx", None, None),
            P("wsh", None),
            P("wsh", None),
            P("wsh", "ctx"),
            P("wsh", "ctx", None, None),
            P("wsh", "ctx", None, None),
            P(),
            P(),
            P("wsh"),
            P("wsh", None),
            P("wsh", None),
            P("wsh", None),
            P("wsh", None),
            P("wsh"),
            P("wsh", None),
            P("wsh", None),
            P("wsh", None),
        ),
        out_specs=(
            P("wsh", "ctx", None, None),
            P("wsh", "ctx", None, None),
            P(),
            P(),
            P("wsh"),
            P("wsh", None),
            P("wsh", None),
            P("wsh", None),
            P("wsh", None),
            P("wsh"),
            P("wsh", None),
            P("wsh", None),
            P("wsh", None),
        ),
        check_vma=False,
    )
```

profile of v0, /device:TPU:9, one launch (start us, length us, event | category | flops | bytes accessed | tf_op | source)
XLA Modules:
  0.0 1204.2 jit_solution(11406116875612877628)
XLA Ops:
  16.6 7.3 all-reduce.8
  25.2 15.5 %all-gather.12.cloned.1.call-done = bf16[768,768]{1,0:T(8,128)(2,1)} async-done(((bf16[192,768]{1,0:T(8,128)(2,1)}), bf16[768,768]{1,0:T(8,128)(2,1)}) %all-gather.12.cloned.1.call-update) | async-done | bytes 1179664 | tf_op jit(solution)/shard_map/all_gather | solution.py:124
  43.3 28.6 %all-gather.16.cloned.1.call-done = bf16[768,768]{1,0:T(8,128)(2,1)} async-done(((bf16[192,768]{1,0:T(8,128)(2,1)}), bf16[768,768]{1,0:T(8,128)(2,1)}) %all-gather.16.cloned.1.call-update) | async-done | bytes 1179664 | tf_op jit(solution)/shard_map/all_gather | solution.py:125
  79.1 41.9 %psum.84 = f32[]{:T(128)} all-reduce(f32[]{:T(128)} %convert_reduce_fusion.1), channel_id=1, replica_groups=mesh['ctx'=8,'wsh'=4] {'ctx','wsh'}, use_global_device_ids=true, to_apply=%region_12.13 | all-reduce | flops 1 | bytes 8 | tf_op jit(solution)/shard_map/psum | solution.py:133
  126.8 12.3 %all-gather.26.cloned.1.call-done = bf16[2048,768]{1,0:T(8,128)(2,1)} async-done(((bf16[256,768]{1,0:T(8,128)(2,1)}), bf16[2048,768]{1,0:T(8,128)(2,1)}) %all-gather.26.cloned.1.call-update) | async-done | bytes 3145744 | tf_op jit(solution)/shard_map/all_gather | solution.py:164
  143.8 29.9 %all-gather.28.cloned.1.call-done = bf16[2048,768]{1,0:T(8,128)(2,1)} async-done(((bf16[256,768]{1,0:T(8,128)(2,1)}), bf16[2048,768]{1,0:T(8,128)(2,1)}) %all-gather.28.cloned.1.call-update) | async-done | bytes 3145744 | tf_op jit(solution)/shard_map/all_gather | solution.py:165
  179.2 74.2 %while.37 = (s32[]{:T(128)}, f32[1,12,256]{2,1,0:T(8,128)S(1)}, f32[1,12,256]{2,1,0:T(8,128)}, f32[1,256,768]{1,2,0:T(8,128)S(1)}, s32[8]{0:T(128)S(1)}, /*index...) while((s32[]{:T(128)}, f32[1,12,256]{2,1,0:T(8,128)S(1)}, ...), condition=%wide.region_9.10_spmd, body=%wide.region_3.9_spmd.sunk | while | flops 209921280 | bytes 14231381 | solution.py:178
  183.3 5.2 conditional.6
  192.6 5.2 conditional.6
  211.2 5.2 conditional.6
  229.7 5.2 conditional.6
  239.0 5.2 conditional.6
  262.3 30.5 %all-gather.20.cloned.1.call-done = bf16[768,3072]{1,0:T(8,128)(2,1)} async-done(((bf16[192,3072]{1,0:T(8,128)(2,1)}), bf16[768,3072]{1,0:T(8,128)(2,1)}) %all-gather.20.cloned.1.call-update) | async-done | bytes 4718608 | tf_op jit(solution)/shard_map/all_gather | solution.py:128
  292.8 5.5 fusion.72
  298.3 84.0 %all-gather.22.cloned.1.call-done = bf16[768,3072]{1,0:T(8,128)(2,1)} async-done(((bf16[192,3072]{1,0:T(8,128)(2,1)}), bf16[768,3072]{1,0:T(8,128)(2,1)}) %all-gather.22.cloned.1.call-update) | async-done | bytes 4718608 | tf_op jit(solution)/shard_map/all_gather | solution.py:129
  382.2 7.3 multiply_convert_fusion.1
  389.5 82.2 %all-gather.24.cloned.1.call-done = bf16[3072,768]{1,0:T(8,128)(2,1)} async-done(((bf16[768,768]{1,0:T(8,128)(2,1)}), bf16[3072,768]{1,0:T(8,128)(2,1)}) %all-gather.24.cloned.1.call-update) | async-done | bytes 4718608 | tf_op jit(solution)/shard_map/all_gather | solution.py:130
  482.1 5.8 fusion.34
  500.7 125.8 %while.39 = (s32[]{:T(128)}, bf16[8,256,2,1,768]{4,1,0,2,3:T(8,128)(2,1)}, s32[8]{0:T(128)S(1)}, s32[1,2048]{1,0:T(1,128)}, s32[1,256]{1,0:T(1,128)}, /*index=5*...) while((s32[]{:T(128)}, ...), condition=%wide.region_24.25_spmd, body=%wide.region_20.0_spmd.sunk | while | flops 408879360 | bytes 19052860 | solution.py:313
  504.7 10.4 conditional.8
  520.4 10.4 conditional.8
  536.2 10.4 conditional.8
  552.0 10.4 conditional.8
  567.7 10.4 conditional.8
  583.4 10.4 conditional.8
  599.2 10.4 conditional.8
  614.9 10.3 conditional.8
  632.1 103.6 %while.38 = (s32[]{:T(128)}, f32[1,256,768]{1,2,0:T(8,128)S(1)}, s32[8]{0:T(128)}, s32[1,2048]{1,0:T(1,128)}, s32[1,256]{1,0:T(1,128)}, /*index=5*/s32[1,2048]{1...) while((s32[]{:T(128)}, f32[1,256,768]{1,2,0:T(8,128)S(1)}, ...), condition=%wide.region_19.20_spmd, body=%wide.region_15.19_spmd.sunk | while | flops 307233024 | bytes 13416289 | solution.py:273
  636.9 8.6 conditional.7
  650.2 8.1 conditional.7
  663.1 8.2 conditional.7
  676.1 8.1 conditional.7
  688.9 8.2 conditional.7
  701.9 8.2 conditional.7
  714.8 8.1 conditional.7
  727.7 8.0 conditional.7
  761.0 6.3 reduce-scatter.11.cloned.1.call-done
  767.3 88.5 %reduce-scatter.23.cloned.1.call-done = bf16[768,768]{1,0:T(8,128)(2,1)} async-done(((bf16[3072,768]{1,0:T(8,128)(2,1)}), bf16[768,768]{1,0:T(8,128)(2,1)}) %reduce-scatter.23.cloned.1.call-update) | async-done | bytes 1179664 | tf_op jit(solution)/shard_map/reduce_scatter | solution.py:382
  855.8 88.1 %reduce-scatter.19.cloned.1.call-done = bf16[192,3072]{1,0:T(8,128)(2,1)} async-done(((bf16[768,3072]{1,0:T(8,128)(2,1)}), bf16[192,3072]{1,0:T(8,128)(2,1)}) %reduce-scatter.19.cloned.1.call-update) | async-done | bytes 1179664 | tf_op jit(solution)/shard_map/reduce_scatter | solution.py:376
  943.9 88.1 %reduce-scatter.21.cloned.1.call-done = bf16[192,3072]{1,0:T(8,128)(2,1)} async-done(((bf16[768,3072]{1,0:T(8,128)(2,1)}), bf16[192,3072]{1,0:T(8,128)(2,1)}) %reduce-scatter.21.cloned.1.call-update) | async-done | bytes 1179664 | tf_op jit(solution)/shard_map/reduce_scatter | solution.py:379
  1031.9 30.5 %reduce-scatter.13.cloned.1.call-done = bf16[192,768]{1,0:T(8,128)(2,1)} async-done(((bf16[768,768]{1,0:T(8,128)(2,1)}), bf16[192,768]{1,0:T(8,128)(2,1)}) %reduce-scatter.13.cloned.1.call-update) | async-done | bytes 294928 | tf_op jit(solution)/shard_map/reduce_scatter | solution.py:364
  1062.4 30.8 %reduce-scatter.15.cloned.1.call-done = bf16[192,768]{1,0:T(8,128)(2,1)} async-done(((bf16[768,768]{1,0:T(8,128)(2,1)}), bf16[192,768]{1,0:T(8,128)(2,1)}) %reduce-scatter.15.cloned.1.call-update) | async-done | bytes 294928 | tf_op jit(solution)/shard_map/reduce_scatter | solution.py:367
  1100.5 7.9 convolution_bitcast_fusion.1
  1108.3 41.3 %all-reduce.4 = (f32[2,2]{1,0:T(2,128)}, f32[2]{0:T(128)}) all-reduce(f32[2,2]{1,0:T(2,128)S(1)} %convolution_bitcast_fusion.1, f32[2]{0:T(128)S(1)} %copy-done.46), channel_id=1, replica_groups=mesh['ctx'=8,'wsh'=4] {'ctx','wsh'}, use_global_device_ids=true, to_apply=%region_27.28 | all-reduce | flops 6 | bytes 48 | tf_op jit(solution)/shard_map/psum | solution.py:346
  1149.6 7.0 all-reduce.7
  1156.7 14.7 %all-reduce.5 = (bf16[192]{0:T(256)(128)(2,1)S(1)}, bf16[192]{0:T(256)(128)(2,1)S(1)}) all-reduce(bf16[192]{0:T(256)(128)(2,1)S(1)} %dynamic-slice.7, bf16[192]{0:T(256)(128)(2,1)S(1)} %dynamic-slice.9), channel_id=1, replica_groups=mesh['ctx'=8,'wsh'=4] {'ctx'}, use_global_device_ids=true, to_apply=%region_32.33 | all-reduce | flops 384 | bytes 1536 | tf_op jit(solution)/shard_map/psum | solution.py:387
  1172.5 7.4 fusion.36
  1179.9 7.2 all-reduce.11.cloned.1.call-done
  (502 shorter events, 400.8 us)
Async XLA Ops:
  7.2 7.5 copy-start.42
  7.2 8.9 copy-start.49
  7.2 9.2 copy-start.50
  7.2 33.5 %all-gather.12.cloned.1.call-start = ((), (), s32[]{:S(2)}) async-start(), calls=%async_computation.8 | async-start | bytes 1474560 | tf_op jit(solution)/shard_map/all_gather | solution.py:124
  8.0 64.0 %all-gather.16.cloned.1.call-start = ((), (), s32[]{:S(2)}) async-start(), calls=%async_computation.10 | async-start | bytes 1474560 | tf_op jit(solution)/shard_map/all_gather | solution.py:125
  8.7 116.2 %all-gather.14.cloned.1.call-start = ((), (), s32[]{:S(2)}) async-start(), calls=%async_computation.9 | async-start | bytes 1474560 | tf_op jit(solution)/shard_map/all_gather | solution.py:123
  9.4 129.7 %all-gather.26.cloned.1.call-start = ((), (), s32[]{:S(2)}) async-start(), calls=%async_computation.23 | async-start | bytes 3538944 | tf_op jit(solution)/shard_map/all_gather | solution.py:164
  14.7 457.0 %copy-start.1 = (f32[1,256,1,768]{3,2,1,0:T(1,128)}, f32[1,256,1,768]{3,2,1,0:T(1,128)S(1)}, u32[]{:S(2)}) copy-start(f32[1,256,1,768]{3,2,1,0:T(1,128)S(1)} %slice.20) | copy-start | bytes 2359300
  43.2 34.1 %copy-start.51 = (s32[1,32]{1,0:T(1,128)S(1)}, s32[1,32]{1,0:T(1,128)}, u32[]{:S(2)}) copy-start(s32[1,32]{1,0:T(1,128)} %param.30) | copy-start | bytes 388
  43.2 34.3 %copy-start.52 = (s32[1,4]{1,0:T(1,128)S(1)}, s32[1,4]{1,0:T(1,128)}, u32[]{:S(2)}) copy-start(s32[1,4]{1,0:T(1,128)} %param.31) | copy-start | bytes 52
  43.2 34.5 %copy-start.44 = (s32[1,256]{1,0:T(1,128)S(1)}, s32[1,256]{1,0:T(1,128)}, u32[]{:S(2)}) copy-start(s32[1,256]{1,0:T(1,128)} %param.32) | copy-start | bytes 3076
  43.3 130.5 %all-gather.28.cloned.1.call-start = ((), (), s32[]{:S(2)}) async-start(), calls=%async_computation.24 | async-start | bytes 3538944 | tf_op jit(solution)/shard_map/all_gather | solution.py:165
  74.5 184.7 %all-gather.18.cloned.1.call-start = ((), (), s32[]{:S(2)}) async-start(), calls=%async_computation.11 | async-start | bytes 1474560 | tf_op jit(solution)/shard_map/all_gather | solution.py:126
  75.0 217.7 %all-gather.20.cloned.1.call-start = ((), (), s32[]{:S(2)}) async-start(), calls=%async_computation.12 | async-start | bytes 5898240 | tf_op jit(solution)/shard_map/all_gather | solution.py:128
  75.8 306.4 %all-gather.22.cloned.1.call-start = ((), (), s32[]{:S(2)}) async-start(), calls=%async_computation.13 | async-start | bytes 5898240 | tf_op jit(solution)/shard_map/all_gather | solution.py:129
  76.5 395.2 %all-gather.24.cloned.1.call-start = ((), (), s32[]{:S(2)}) async-start(), calls=%async_computation.14 | async-start | bytes 5898240 | tf_op jit(solution)/shard_map/all_gather | solution.py:130
  77.3 677.3 %reduce-scatter.9.cloned.1.call-start = ((), (), s32[]{:S(2)}) async-start(), calls=%async_computation.15 | async-start | bytes 7077888 | tf_op jit(solution)/shard_map/reduce_scatter | solution.py:312
  256.6 238.9 %copy-start.18 = (f32[256,768]{1,0:T(8,128)}, f32[256,768]{1,0:T(8,128)S(1)}, u32[]{:S(2)}) copy-start(f32[256,768]{1,0:T(8,128)S(1)} %copy.106) | copy-start | bytes 2359300
  262.3 120.0 %copy-start.10 = (bf16[256,768]{1,0:T(8,128)(2,1)}, bf16[256,768]{1,0:T(8,128)(2,1)S(1)}, u32[]{:S(2)}) copy-start(bf16[256,768]{1,0:T(8,128)(2,1)S(1)} %multiply_convert_fusion.3) | copy-start | bytes 1179652
  471.7 4.6 copy-start.30
  471.7 4.6 copy-start.31
  471.7 4.6 copy-start.45
  471.7 16.2 %copy-start.54 = (f32[256,3072]{1,0:T(8,128)S(1)}, f32[256,3072]{1,0:T(8,128)}, u32[]{:S(2)}) copy-start(f32[256,3072]{1,0:T(8,128)} %get-tuple-element.752) | copy-start | bytes 9437188
  476.3 11.6 copy-start.47
  476.3 11.6 copy-start.53
  482.1 9.3 slice-start
  482.1 10.9 slice-start.2
  487.9 7.3 copy-start.12
  487.9 5.1 slice-start.3
  626.5 134.5 %reduce-scatter.17.cloned.1.call-start = ((), (), s32[]{:S(2)}) async-start(), calls=%async_computation.19 | async-start | bytes 1474560 | tf_op jit(solution)/shard_map/reduce_scatter | solution.py:370
  631.5 135.8 %reduce-scatter.11.cloned.1.call-start = ((), (), s32[]{:S(2)}) async-start(), calls=%async_computation.16 | async-start | bytes 1474560 | tf_op jit(solution)/shard_map/reduce_scatter | solution.py:361
  636.9 4.9 copy-start.24
  650.2 4.7 copy-start.24
  663.1 4.8 copy-start.24
  676.1 4.7 copy-start.24
  688.9 4.7 copy-start.24
  701.9 4.7 copy-start.24
  714.8 4.7 copy-start.24
  738.4 117.4 %reduce-scatter.23.cloned.1.call-start = ((), (), s32[]{:S(2)}) async-start(), calls=%async_computation.22 | async-start | bytes 5898240 | tf_op jit(solution)/shard_map/reduce_scatter | solution.py:382
  743.6 200.3 %reduce-scatter.19.cloned.1.call-start = ((), (), s32[]{:S(2)}) async-start(), calls=%async_computation.20 | async-start | bytes 5898240 | tf_op jit(solution)/shard_map/reduce_scatter | solution.py:376
  749.5 282.4 %reduce-scatter.21.cloned.1.call-start = ((), (), s32[]{:S(2)}) async-start(), calls=%async_computation.21 | async-start | bytes 5898240 | tf_op jit(solution)/shard_map/reduce_scatter | solution.py:379
  754.5 307.9 %reduce-scatter.13.cloned.1.call-start = ((), (), s32[]{:S(2)}) async-start(), calls=%async_computation.17 | async-start | bytes 1474560 | tf_op jit(solution)/shard_map/reduce_scatter | solution.py:364
  758.1 335.1 %reduce-scatter.15.cloned.1.call-start = ((), (), s32[]{:S(2)}) async-start(), calls=%async_computation.18 | async-start | bytes 1474560 | tf_op jit(solution)/shard_map/reduce_scatter | solution.py:367
  760.7 426.5 %all-reduce.11.cloned.1.call-start = ((), (), s32[]{:S(2)}) async-start(), calls=%async_computation.25 | async-start | bytes 9437184 | tf_op jit(solution)/shard_map/psum | solution.py:388
  1100.4 7.9 copy-start.46
  1100.5 49.1 %copy-start.43 = (bf16[768]{0:T(1024)(128)(2,1)S(1)}, bf16[768]{0:T(1024)(128)(2,1)}, u32[]{:S(2)}) copy-start(bf16[768]{0:T(1024)(128)(2,1)} %get-tuple-element.619) | copy-start | bytes 4612
  1100.5 72.1 %copy-start.48 = (f32[2,2]{1,0:T(2,128)S(1)}, f32[2,2]{1,0:T(2,128)}, u32[]{:S(2)}) copy-start(f32[2,2]{1,0:T(2,128)} %param.35) | copy-start | bytes 52
  1187.1 4.8 copy-start.27
  (36 other events, 83.8 us)
Sparse Core Ops, SparseCore 0:
  9.6 31.0 all-gather.11
  42.3 29.6 all-gather.15
  73.5 29.9 all-gather.13
  105.9 33.2 all-gather.25
  141.4 32.3 all-gather.27
  175.2 29.2 all-gather.17
  206.1 86.6 all-gather.19
  294.3 87.8 all-gather.21
  383.8 87.8 all-gather.23
  626.6 62.7 reduce-scatter.8
  691.9 27.1 reduce-scatter.16
  738.6 28.7 reduce-scatter.10
  769.7 86.0 reduce-scatter.22
  858.1 85.7 reduce-scatter.18
  946.1 85.7 reduce-scatter.20
  1034.8 27.5 reduce-scatter.12
  1065.3 27.8 reduce-scatter.14
  1097.7 89.4 all-reduce.10
where the time goes:
time: 1210 us; the launch traced here: 1200 us
  waiting for transfers between devices  627 us (52%)
  matrix products  216 us (18%)
  local copies, waits for them, and re-layouts  122 us (10%)
  blocking collectives  112 us (9%)
  other arithmetic  75.4 us (6%)
  loops' own time  32.9 us (3%)
  between operations  17.7 us (1%)
    reduce_scatter x1, waiting for transfers between devices, shards(): lax.psum_scatter(down_grad.astype(jnp.bfloat16), 'wsh', scatter_dimension...  88.5 us
    reduce_scatter x1, waiting for transfers between devices, shards(): lax.psum_scatter(gate_w_grad.astype(jnp.bfloat16), 'wsh', scatter_dimensi...  88.1 us
    reduce_scatter x1, waiting for transfers between devices, shards(): lax.psum_scatter(up_w_grad.astype(jnp.bfloat16), 'wsh', scatter_dimension...  88.1 us
    all_gather x1, waiting for transfers between devices, shards(): lax.all_gather(w_up, 'wsh', axis=0, tiled=True)  84 us
    all_gather x1, waiting for transfers between devices, shards(): lax.all_gather(w_down, 'wsh', axis=0, tiled=True)  82.2 us
    dot_general x16, matrix products, backward_block(): jnp.einsum('gqhd,gkhd->ghqk', split_heads(query_part), split_heads(key_pa...  45.2 us
    psum x1, blocking collectives, shards(): valid_total = lax.psum(jnp.sum(valid_float), ('ctx', 'wsh'))  41.9 us
    psum x1, blocking collectives, shards(): lax.psum((predict_local, correct_local), ('ctx', 'wsh'))  41.3 us
  transfers between devices with their start and end apart: 18, of which 14 were waited for; matrix products, arithmetic and copies ran while one was open for 21% of the time, Pallas kernels for 0%

commit v1 on v0

--- a/solution.py
+++ b/solution.py
@@ -1,8 +1,11 @@
+import functools
 import math
 
 import jax
 import jax.numpy as jnp
 from jax import lax
+from jax.experimental import pallas as pl
+from jax.experimental.pallas import tpu as pltpu
 from jax.sharding import PartitionSpec as P
 
 HEADS = 12
@@ -28,11 +31,18 @@
     return (factor * weighted - tensor * factor * factor * factor * middle, gain_grad)
 
 
+def segment_starts(cont_lengths):
+    count = cont_lengths.shape[1]
+    index = jnp.arange(count, dtype=jnp.int32)
+    before = index[:, None] < index[None, :]
+    return PROMPT + jnp.sum(jnp.where(before[None], cont_lengths[:, :, None], 0), axis=1)
+
+
 def token_places(block_slot, cont_lengths):
     groups, blocks = block_slot.shape
     offsets = jnp.arange(BLK, dtype=jnp.int32)
     places = (block_slot[:, :, None] * BLK + offsets[None, None, :]).reshape(groups, blocks * BLK)
-    starts = PROMPT + jnp.cumsum(cont_lengths, axis=1) - cont_lengths
+    starts = segment_starts(cont_lengths)
     segments = jnp.sum((places[:, :, None] >= starts[:, None, :]).astype(jnp.int32), axis=2)
     return (places, segments)
 
@@ -95,7 +105,7 @@
     return (probability.astype(jnp.bfloat16), score_grad)
 
 
-def shards(
+def general_shards(
     states,
     block_slot,
     cont_lengths,
@@ -397,43 +407,809 @@
     return (new_states, states_grad, predict_grad, correct_grad) + tuple(totals)
 
 
+MESH = pl.DeviceIdType.MESH
+F32 = jnp.float32
+BF16 = jnp.bfloat16
+CHIPS = 4
+VMEM_LIMIT = 60 * 2**20
+
+
+def place_on_mesh():
+    ctx = lax.axis_index("ctx")
+    depth = lax.axis_index("wsh")
+    chip = ctx // 2
+    core = ctx % 2
+    chip_x = chip + 1 - 2 * (chip % 2)
+    chip_y = chip + 2 - 4 * (chip // 2)
+    return depth, chip, core, chip_x, chip_y, 3 - chip
+
+
+def signal_and_wait(devices):
+    barrier = pltpu.get_barrier_semaphore()
+    for device in devices:
+        pl.semaphore_signal(barrier, inc=1, device_id=device, device_id_type=MESH)
+    pl.semaphore_wait(barrier, len(devices))
+
+
+def remote(src, dst, send, recv, index, device):
+    return pltpu.make_async_remote_copy(
+        src_ref=src,
+        dst_ref=dst,
+        send_sem=send.at[index],
+        recv_sem=recv.at[index],
+        device_id=device,
+        device_id_type=MESH,
+    )
+
+
+def comm_params(collective_id):
+    return pltpu.CompilerParams(
+        collective_id=collective_id, has_side_effects=True, vmem_limit_bytes=VMEM_LIMIT
+    )
+
+
+ANY = pl.BlockSpec(memory_space=pl.ANY)
+VM = pl.BlockSpec(memory_space=pltpu.VMEM)
+SM = pl.BlockSpec(memory_space=pltpu.SMEM)
+
+
+def ring_sends(own, out, slot_of, chip, core, depth, chip_x, chip_y, send, recv):
+    half = own.shape[0] // 2
+    top, low = pl.ds(0, half), pl.ds(half, half)
+    dev_x, dev_y = (2 * chip_x + core, depth), (2 * chip_y + core, depth)
+    here = slot_of(chip)
+    return [
+        remote(own.at[top], out.at[here, top], send, recv, 0, dev_x),
+        remote(own.at[low], out.at[here, low], send, recv, 1, dev_y),
+        remote(own.at[low], out.at[here, low], send, recv, 2, dev_x),
+        remote(own.at[top], out.at[here, top], send, recv, 3, dev_y),
+        remote(out.at[slot_of(chip_x), top], out.at[slot_of(chip_x), top], send, recv, 4, dev_y),
+        remote(out.at[slot_of(chip_y), low], out.at[slot_of(chip_y), low], send, recv, 5, dev_x),
+    ]
+
+
+def gather_plane(block, collective_id):
+    def kernel(x_ref, out_ref, send, recv, local):
+        depth, chip, core, chip_x, chip_y, _ = place_on_mesh()
+        signal_and_wait([(2 * chip_x + core, depth), (2 * chip_y + core, depth)])
+        copies = ring_sends(
+            x_ref, out_ref, lambda c: c, chip, core, depth, chip_x, chip_y, send, recv
+        )
+        for copy in copies[:4]:
+            copy.start()
+        mine = pltpu.make_async_copy(x_ref, out_ref.at[chip], local)
+        mine.start()
+        copies[0].wait_recv()
+        copies[4].start()
+        copies[1].wait_recv()
+        copies[5].start()
+        for copy in copies[2:]:
+            copy.wait_recv()
+        for copy in copies:
+            copy.wait_send()
+        mine.wait()
+
+    return pl.pallas_call(
+        kernel,
+        out_shape=jax.ShapeDtypeStruct((CHIPS,) + block.shape, block.dtype),
+        in_specs=[ANY],
+        out_specs=ANY,
+        scratch_shapes=[
+            pltpu.SemaphoreType.DMA((6,)),
+            pltpu.SemaphoreType.DMA((6,)),
+            pltpu.SemaphoreType.DMA,
+        ],
+        compiler_params=comm_params(collective_id),
+        name="gather_plane",
+    )(block)
+
+
+def scatter_plane(parts, collective_id):
+    _, rows, width = parts.shape
+    half = rows // 2
+
+    def kernel(x_ref, out_ref, near, diagonal, staged, send, recv):
+        depth, chip, core, chip_x, chip_y, chip_d = place_on_mesh()
+        dev_x, dev_y = (2 * chip_x + core, depth), (2 * chip_y + core, depth)
+        signal_and_wait([dev_x, dev_y])
+        top, low = pl.ds(0, half), pl.ds(half, half)
+        first = [
+            remote(x_ref.at[chip_d, top], diagonal.at[0], send, recv, 0, dev_x),
+            remote(x_ref.at[chip_d, low], diagonal.at[1], send, recv, 1, dev_y),
+            remote(x_ref.at[chip_x, top], near.at[0, top], send, recv, 2, dev_x),
+            remote(x_ref.at[chip_y, low], near.at[1, low], send, recv, 3, dev_y),
+        ]
+        for copy in first:
+            copy.start()
+        second = [
+            remote(staged.at[0], near.at[1, top], send, recv, 4, dev_y),
+            remote(staged.at[1], near.at[0, low], send, recv, 5, dev_x),
+        ]
+        first[0].wait_recv()
+        staged[0] = (x_ref[chip_y, top].astype(F32) + diagonal[0].astype(F32)).astype(BF16)
+        second[0].start()
+        first[1].wait_recv()
+        staged[1] = (x_ref[chip_x, low].astype(F32) + diagonal[1].astype(F32)).astype(BF16)
+        second[1].start()
+        for copy in first[2:] + second:
+            copy.wait_recv()
+        out_ref[...] = (
+            x_ref[chip].astype(F32) + near[0].astype(F32) + near[1].astype(F32)
+        )
+        for copy in first + second:
+            copy.wait_send()
+
+    return pl.pallas_call(
+        kernel,
+        out_shape=jax.ShapeDtypeStruct((rows, width), F32),
+        in_specs=[VM],
+        out_specs=VM,
+        scratch_shapes=[
+            pltpu.VMEM((2, rows, width), BF16),
+            pltpu.VMEM((2, half, width), BF16),
+            pltpu.VMEM((2, half, width), BF16),
+            pltpu.SemaphoreType.DMA((6,)),
+            pltpu.SemaphoreType.DMA((6,)),
+        ],
+        compiler_params=comm_params(collective_id),
+        name="scatter_plane",
+    )(parts)
+
+
+def share_cores(arrays, collective_id):
+    count = len(arrays)
+
+    def kernel(*refs):
+        ins, outs, (send, recv, local) = refs[:count], refs[count : 2 * count], refs[2 * count :]
+        depth, chip, core, _, _, _ = place_on_mesh()
+        other = (2 * chip + 1 - core, depth)
+        signal_and_wait([other])
+        copies = [
+            remote(ins[i], outs[i].at[core], send, recv, i, other) for i in range(count)
+        ]
+        mine = [
+            pltpu.make_async_copy(ins[i], outs[i].at[core], local.at[i]) for i in range(count)
+        ]
+        for copy in copies + mine:
+            copy.start()
+        for copy in copies + mine:
+            copy.wait()
+
+    return pl.pallas_call(
+        kernel,
+        out_shape=[jax.ShapeDtypeStruct((2,) + a.shape, a.dtype) for a in arrays],
+        in_specs=[ANY] * count,
+        out_specs=[ANY] * count,
+        scratch_shapes=[pltpu.SemaphoreType.DMA((count,))] * 3,
+        compiler_params=comm_params(collective_id),
+        name="share_cores",
+    )(*arrays)
+
+
+def swap_cores(arrays, collective_id):
+    count = len(arrays)
+
+    def kernel(*refs):
+        ins, outs, (send, recv) = refs[:count], refs[count : 2 * count], refs[2 * count :]
+        depth, chip, core, _, _, _ = place_on_mesh()
+        other = (2 * chip + 1 - core, depth)
+        signal_and_wait([other])
+        copies = [
+            remote(ins[i].at[:, 1 - core], outs[i], send, recv, i, other) for i in range(count)
+        ]
+        for copy in copies:
+            copy.start()
+        for copy in copies:
+            copy.wait()
+
+    return pl.pallas_call(
+        kernel,
+        out_shape=[jax.ShapeDtypeStruct(a.shape[:1] + a.shape[2:], a.dtype) for a in arrays],
+        in_specs=[ANY] * count,
+        out_specs=[ANY] * count,
+        scratch_shapes=[pltpu.SemaphoreType.DMA((count,))] * 2,
+        compiler_params=comm_params(collective_id),
+        name="swap_cores",
+    )(*arrays)
+
+
+def gather_inputs(block, weights, collective_id):
+    depths = lax.axis_size("wsh")
+
+    def kernel(x_ref, w_ref, out_ref, wall_ref, send, recv, wsend, wrecv, ssend, srecv, local):
+        depth, chip, core, chip_x, chip_y, chip_d = place_on_mesh()
+        other = (2 * chip + 1 - core, depth)
+        across = [
+            (2 * chip + core, lax.rem(depth + step, depths)) for step in range(1, depths)
+        ]
+        signal_and_wait(
+            [(2 * chip_x + core, depth), (2 * chip_y + core, depth), other] + across
+        )
+
+        def slot(chip_index):
+            return 2 * chip_index + core
+
+        copies = ring_sends(
+            x_ref, out_ref, slot, chip, core, depth, chip_x, chip_y, send, recv
+        )
+        for copy in copies[:4]:
+            copy.start()
+        w_copies = [
+            remote(w_ref, wall_ref.at[:, depth, core], wsend, wrecv, i, device)
+            for i, device in enumerate(across)
+        ]
+        for copy in w_copies:
+            copy.start()
+        mine = [
+            pltpu.make_async_copy(x_ref, out_ref.at[slot(chip)], local.at[0]),
+            pltpu.make_async_copy(w_ref, wall_ref.at[:, depth, core], local.at[1]),
+        ]
+        for copy in mine:
+            copy.start()
+
+        def pass_on(index, slot_index):
+            ref = out_ref.at[slot_index]
+            return remote(ref, ref, ssend, srecv, index, other)
+
+        def pass_weights(index, depth_index):
+            ref = wall_ref.at[:, depth_index, core]
+            return remote(ref, ref, ssend, srecv, index, other)
+
+        shared = [
+            remote(x_ref, out_ref.at[slot(chip)], ssend, srecv, 0, other),
+            pass_on(1, slot(chip_x)),
+            pass_on(2, slot(chip_y)),
+            pass_on(3, slot(chip_d)),
+            remote(w_ref, wall_ref.at[:, depth, core], ssend, srecv, 4, other),
+        ] + [
+            pass_weights(5 + i, lax.rem(depth + depths - 1 - i, depths))
+            for i in range(depths - 1)
+        ]
+        shared[0].start()
+        shared[4].start()
+        copies[0].wait_recv()
+        copies[4].start()
+        copies[1].wait_recv()
+        copies[5].start()
+        for i in range(depths - 1):
+            w_copies[i].wait_recv()
+            shared[5 + i].start()
+        copies[2].wait_recv()
+        shared[1].start()
+        copies[3].wait_recv()
+        shared[2].start()
+        copies[4].wait_recv()
+        copies[5].wait_recv()
+        shared[3].start()
+        for copy in shared:
+            copy.wait()
+        for copy in copies + w_copies:
+            copy.wait_send()
+        for copy in mine:
+            copy.wait()
+
+    shape = (lax.axis_size("ctx"),) + block.shape
+    parts, rows, columns = weights.shape
+    return pl.pallas_call(
+        kernel,
+        out_shape=[
+            jax.ShapeDtypeStruct(shape, block.dtype),
+            jax.ShapeDtypeStruct((parts, depths, 2, rows, columns), weights.dtype),
+        ],
+        in_specs=[ANY, ANY],
+        out_specs=[ANY, ANY],
+        scratch_shapes=[
+            pltpu.SemaphoreType.DMA((6,)),
+            pltpu.SemaphoreType.DMA((6,)),
+            pltpu.SemaphoreType.DMA((depths - 1,)),
+            pltpu.SemaphoreType.DMA((depths - 1,)),
+            pltpu.SemaphoreType.DMA((depths + 4,)),
+            pltpu.SemaphoreType.DMA((depths + 4,)),
+            pltpu.SemaphoreType.DMA((2,)),
+        ],
+        compiler_params=comm_params(collective_id),
+        name="gather_inputs",
+    )(block, weights)
+
+
+NT = (((1,), (1,)), ((), ()))
+TILE = 256
+LOCAL_HEADS = HEADS // CHIPS
+CHIP_COLS = LOCAL_HEADS * HD
+
+
+def head_mask(rows, head):
+    lane = lax.broadcasted_iota(jnp.int32, (rows, CHIP_COLS), 1)
+    return (lane >= head * HD) & (lane < (head + 1) * HD)
+
+
+def aligned(index, size):
+    return pl.ds(pl.multiple_of(index * size, size), size)
+
+
+def attention_forward(all_rows, weights, slots, q_slots, q_local, low, high):
+    tokens, width = all_rows.shape
+    tiles = low.shape[0]
+    queries = tiles * TILE
+    blocks = tokens // BLK
+
+    def kernel(
+        slots_ref, q_slots_ref, q_local_ref, x_ref, w_ref, low_ref, high_ref,
+        att_ref, oT_ref, q_ref, k_ref, v_ref, lse_ref, xs, xq, vT, s_ref, p_ref,
+    ):
+        def gather_block(b, _):
+            xs[aligned(b, BLK), :] = x_ref[aligned(slots_ref[b], BLK), :]
+            return 0
+
+        lax.fori_loop(0, blocks, gather_block, 0)
+
+        def gather_query(b, _):
+            xq[aligned(b, BLK), :] = x_ref[aligned(q_slots_ref[b], BLK), :]
+            return 0
+
+        lax.fori_loop(0, queries // BLK, gather_query, 0)
+
+        def project_keys(i, _):
+            rows = aligned(i, TILE)
+            x = xs[rows, :]
+            k_ref[rows, :] = jnp.dot(x, w_ref[1], preferred_element_type=F32).astype(BF16)
+            v = jnp.dot(x, w_ref[2], preferred_element_type=F32).astype(BF16)
+            v_ref[rows, :] = v
+            vT[:, rows] = v.T
+            return 0
+
+        lax.fori_loop(0, tokens // TILE, project_keys, 0)
+
+        def project_queries(i, _):
+            rows = aligned(i, TILE)
+            q_ref[rows, :] = jnp.dot(xq[rows, :], w_ref[0], preferred_element_type=F32).astype(BF16)
+            return 0
+
+        lax.fori_loop(0, tiles, project_queries, 0)
+
+        for kind in range(2):
+            key_tiles = (PROMPT if kind == 0 else tokens) // TILE
+            first_masked = 0 if kind == 0 else PROMPT // TILE
+
+            def one_tile(step, _):
+                tile = kind * (tiles // 2) + step
+                q = q_ref[aligned(tile, TILE), :]
+                q_low = low_ref[pl.ds(tile, 1)][0]
+                q_high = high_ref[pl.ds(tile, 1)][0]
+                for head in range(LOCAL_HEADS):
+                    q_head = jnp.where(head_mask(TILE, head), q, jnp.zeros_like(q))
+                    top = jnp.full((1, TILE), NEGATIVE, F32)
+                    for k_tile in range(key_tiles):
+                        rows = pl.ds(k_tile * TILE, TILE)
+                        s = lax.dot_general(k_ref[rows, :], q_head, NT, preferred_element_type=F32)
+                        if k_tile >= first_masked:
+                            place = lax.broadcasted_iota(jnp.int32, (TILE, TILE), 0) + k_tile * TILE
+                            seen = (place >= q_low) & (place <= q_high)
+                            s = jnp.where(seen, s, NEGATIVE)
+                        s_ref[rows, :] = s
+                        top = jnp.maximum(top, jnp.max(s, axis=0, keepdims=True))
+                    total = jnp.zeros((1, TILE), F32)
+                    for k_tile in range(key_tiles):
+                        rows = pl.ds(k_tile * TILE, TILE)
+                        p = jnp.exp(s_ref[rows, :] - top)
+                        total = total + jnp.sum(p, axis=0, keepdims=True)
+                        p_ref[rows, :] = p.astype(BF16)
+                    keys = key_tiles * TILE
+                    out = jnp.dot(
+                        vT[head * HD : (head + 1) * HD, :keys],
+                        p_ref[:keys, :],
+                        preferred_element_type=F32,
+                    )
+                    oT_ref[tile, head * HD : (head + 1) * HD, :] = out / total
+                    lse_ref[tile, head] = top + jnp.log(total)
+                att = oT_ref[tile].T.astype(BF16)
+                for b in range(TILE // BLK):
+                    where = q_local_ref[tile * (TILE // BLK) + b]
+                    att_ref[aligned(where, BLK), :] = att[b * BLK : (b + 1) * BLK]
+                return 0
+
+            lax.fori_loop(0, tiles // 2, one_tile, 0)
+
+    return pl.pallas_call(
+        kernel,
+        out_shape=[
+            jax.ShapeDtypeStruct((queries, CHIP_COLS), BF16),
+            jax.ShapeDtypeStruct((tiles, CHIP_COLS, TILE), F32),
+            jax.ShapeDtypeStruct((queries, CHIP_COLS), BF16),
+            jax.ShapeDtypeStruct((tokens, CHIP_COLS), BF16),
+            jax.ShapeDtypeStruct((tokens, CHIP_COLS), BF16),
+            jax.ShapeDtypeStruct((tiles, LOCAL_HEADS, 1, TILE), F32),
+        ],
+        in_specs=[SM, SM, SM, VM, VM, VM, VM],
+        out_specs=[VM] * 6,
+        scratch_shapes=[
+            pltpu.VMEM((tokens, width), BF16),
+            pltpu.VMEM((queries, width), BF16),
+            pltpu.VMEM((CHIP_COLS, tokens), BF16),
+            pltpu.VMEM((tokens, TILE), F32),
+            pltpu.VMEM((tokens, TILE), BF16),
+        ],
+        compiler_params=pltpu.CompilerParams(vmem_limit_bytes=VMEM_LIMIT),
+        name="attention_forward",
+    )(slots, q_slots, q_local, all_rows, weights, low, high)
+
+
+def attention_backward(hidden_rows, w_out, saved, slots, q_local, low, high):
+    oT, q, k, v, lse = saved
+    queries, width = hidden_rows.shape
+    tokens = k.shape[0]
+    tiles = low.shape[0]
+    blocks = tokens // BLK
+    wide = LOCAL_HEADS * TILE
+
+    def kernel(
+        slots_ref, q_local_ref, h_ref, w_ref, oT_ref, q_ref, k_ref, v_ref, lse_ref, low_ref, high_ref,
+        dq_ref, dk_ref, dv_ref, hq, kT, doT, dqT, q_stack, do_stack, p_buf, ds_buf, dk_acc, dv_acc,
+    ):
+        def gather_query(b, _):
+            hq[aligned(b, BLK), :] = h_ref[aligned(q_local_ref[b], BLK), :]
+            return 0
+
+        lax.fori_loop(0, queries // BLK, gather_query, 0)
+
+        def transpose_keys(i, _):
+            rows = aligned(i, TILE)
+            kT[:, rows] = k_ref[rows, :].T
+            return 0
+
+        lax.fori_loop(0, tokens // TILE, transpose_keys, 0)
+
+        for kind in (1, 0):
+            key_tiles = (PROMPT if kind == 0 else tokens) // TILE
+            first_masked = 0 if kind == 0 else PROMPT // TILE
+
+            def one_tile(step, _):
+                tile = kind * (tiles // 2) + step
+                q_tile = q_ref[aligned(tile, TILE), :]
+                q_low = low_ref[pl.ds(tile, 1)][0]
+                q_high = high_ref[pl.ds(tile, 1)][0]
+                wide_do = lax.dot_general(
+                    w_ref[...], hq[aligned(tile, TILE), :], NT, preferred_element_type=F32
+                )
+                do_tile = wide_do.T.astype(BF16)
+                doT[...] = wide_do.astype(BF16).astype(F32) * oT_ref[tile]
+                for head in range(LOCAL_HEADS):
+                    lanes = pl.ds(head * TILE, TILE)
+                    heads = pl.ds(head * HD, HD)
+                    mask = head_mask(TILE, head)
+                    q_head = jnp.where(mask, q_tile, jnp.zeros_like(q_tile))
+                    do_head = jnp.where(mask, do_tile, jnp.zeros_like(do_tile))
+                    q_stack[lanes, :] = q_head
+                    do_stack[lanes, :] = do_head
+                    delta = jnp.sum(doT[heads, :], axis=0, keepdims=True)
+                    norm = lse_ref[tile, head]
+                    for k_tile in range(key_tiles):
+                        rows = pl.ds(k_tile * TILE, TILE)
+                        s = lax.dot_general(k_ref[rows, :], q_head, NT, preferred_element_type=F32)
+                        dp = lax.dot_general(v_ref[rows, :], do_head, NT, preferred_element_type=F32)
+                        p = jnp.exp(s - norm)
+                        if k_tile >= first_masked:
+                            place = lax.broadcasted_iota(jnp.int32, (TILE, TILE), 0) + k_tile * TILE
+                            seen = (place >= q_low) & (place <= q_high)
+                            p = jnp.where(seen, p, 0.0)
+                        p_buf[rows, lanes] = p.astype(BF16)
+                        ds_buf[rows, lanes] = (p * (dp - delta)).astype(BF16)
+                    keys = key_tiles * TILE
+                    dqT[heads, :] = jnp.dot(
+                        kT[heads, :keys], ds_buf[:keys, lanes], preferred_element_type=F32
+                    )
+                for k_tile in range(key_tiles):
+                    rows = pl.ds(k_tile * TILE, TILE)
+                    dv = jnp.dot(p_buf[rows, :], do_stack[...], preferred_element_type=F32)
+                    dk = jnp.dot(ds_buf[rows, :], q_stack[...], preferred_element_type=F32)
+                    if kind == 1:
+                        fresh = step == 0
+                        dv = dv + jnp.where(fresh, 0.0, dv_acc[rows, :])
+                        dk = dk + jnp.where(fresh, 0.0, dk_acc[rows, :])
+                    else:
+                        dv = dv + dv_acc[rows, :]
+                        dk = dk + dk_acc[rows, :]
+                    dv_acc[rows, :] = dv
+                    dk_acc[rows, :] = dk
+                dq = dqT[...].T.astype(BF16)
+                for b in range(TILE // BLK):
+                    where = q_local_ref[tile * (TILE // BLK) + b]
+                    dq_ref[aligned(where, BLK), :] = dq[b * BLK : (b + 1) * BLK]
+                return 0
+
+            lax.fori_loop(0, tiles // 2, one_tile, 0)
+
+        def give_block(b, _):
+            where = aligned(slots_ref[b], BLK)
+            dk_ref[where, :] = dk_acc[aligned(b, BLK), :].astype(BF16)
+            dv_ref[where, :] = dv_acc[aligned(b, BLK), :].astype(BF16)
+            return 0
+
+        lax.fori_loop(0, blocks, give_block, 0)
+
+    return pl.pallas_call(
+        kernel,
+        out_shape=[
+            jax.ShapeDtypeStruct((queries, CHIP_COLS), BF16),
+            jax.ShapeDtypeStruct((tokens, CHIP_COLS), BF16),
+            jax.ShapeDtypeStruct((tokens, CHIP_COLS), BF16),
+        ],
+        in_specs=[SM, SM] + [VM] * 9,
+        out_specs=[VM] * 3,
+        scratch_shapes=[
+            pltpu.VMEM((queries, width), BF16),
+            pltpu.VMEM((CHIP_COLS, tokens), BF16),
+            pltpu.VMEM((CHIP_COLS, TILE), F32),
+            pltpu.VMEM((CHIP_COLS, TILE), F32),
+            pltpu.VMEM((wide, CHIP_COLS), BF16),
+            pltpu.VMEM((wide, CHIP_COLS), BF16),
+            pltpu.VMEM((tokens, wide), BF16),
+            pltpu.VMEM((tokens, wide), BF16),
+            pltpu.VMEM((tokens, CHIP_COLS), F32),
+            pltpu.VMEM((tokens, CHIP_COLS), F32),
+        ],
+        compiler_params=pltpu.CompilerParams(vmem_limit_bytes=VMEM_LIMIT),
+        name="attention_backward",
+    )(slots, q_local, hidden_rows, w_out, oT, q, k, v, lse, low, high)
+
+
+def query_tables(slots_row, lengths_row, core):
+    blocks = slots_row.shape[0]
+    index = jnp.arange(blocks, dtype=jnp.int32)
+    slot_of = jnp.sum(
+        jnp.where(slots_row[None, :] == index[:, None], index[None, :], 0), axis=1, dtype=jnp.int32
+    )
+    per_device = blocks // (2 * CHIPS)
+    own = slots_row.reshape(CHIPS, 2, per_device)
+    own = lax.dynamic_index_in_dim(own, core, 1, keepdims=False).reshape(-1, 2)
+    pairs = own.shape[0]
+    swapped = (own[:, 0] >= PROMPT // BLK).astype(jnp.int32)
+    pair = jnp.arange(pairs, dtype=jnp.int32)
+    local = jnp.concatenate([2 * pair + swapped, 2 * pair + 1 - swapped])
+    block = jnp.concatenate([jnp.min(own, axis=1), jnp.max(own, axis=1)])
+    owner = local // per_device
+    slot = owner * (2 * per_device) + core * per_device + local % per_device
+    high = (block[:, None] * BLK + jnp.arange(BLK, dtype=jnp.int32)[None, :]).reshape(-1)
+    starts = segment_starts(lengths_row[None])[0]
+    low = jnp.max(jnp.where(starts[None, :] <= high[:, None], starts[None, :], 0), axis=1)
+    shape = (2 * pairs * BLK // TILE, 1, TILE)
+    return slot_of, slot, local, low.reshape(shape), high.reshape(shape)
+
+
+def plane_shards(
+    states, block_slot, cont_lengths, valid_mask, teacher, out_grad, predict, correct,
+    norm_attn, w_query, w_key, w_value, w_out, norm_ffn, w_gate, w_up, w_down,
+):
+    depths = lax.axis_size("wsh")
+    ctx = lax.axis_index("ctx")
+    chip, core = ctx // 2, ctx % 2
+    _, rows, _, width = states.shape
+    shard = w_query.shape[0]
+    half = shard // 2
+    hidden_cols = w_gate.shape[1] // CHIPS
+    group_len = block_slot.shape[1] * BLK
+
+    def columns(weight):
+        return lax.dynamic_slice_in_dim(weight, chip * CHIP_COLS, CHIP_COLS, 1)
+
+    def core_half(weight):
+        return lax.dynamic_slice_in_dim(weight, core * half, half, 0)
+
+    qkv_piece = jnp.stack([columns(core_half(w)) for w in (w_query, w_key, w_value)])
+    ff_split = hidden_cols // depths
+
+    def ff_columns(weight):
+        piece = core_half(weight).reshape(half, depths, CHIPS, ff_split)
+        return lax.dynamic_index_in_dim(piece, chip, 2, keepdims=False).reshape(half, hidden_cols)
+
+    down_rows = lax.dynamic_slice_in_dim(w_down, chip * ff_split + core * (ff_split // 2), ff_split // 2, 0)
+    gain_one = lax.all_gather(norm_attn, "wsh", axis=0, tiled=True).astype(F32)
+    gain_two = lax.all_gather(norm_ffn, "wsh", axis=0, tiled=True).astype(F32)
+    out_w = lax.all_gather(w_out, "wsh", axis=0, tiled=True)
+    out_w = lax.dynamic_slice_in_dim(out_w, chip * CHIP_COLS, CHIP_COLS, 0)
+    ff_piece = lax.all_gather(
+        jnp.stack([ff_columns(w_gate), ff_columns(w_up), down_rows]), "wsh", axis=0, tiled=False
+    )
+    valid_float = valid_mask.astype(F32)
+    valid_total = lax.psum(jnp.sum(valid_float), ("ctx", "wsh"))
+
+    slots, q_slots, q_local, low, high = query_tables(block_slot[0], cont_lengths[0], core)
+
+    inputs = states[0].astype(F32)
+    mixed = jnp.stack(
+        [predict[i, 0] * inputs[:, 0] + predict[i, 1] * inputs[:, 1] for i in range(2)], axis=1
+    )
+    active = mixed[:, 0]
+    normed, factor_one = rms_forward(active, gain_one)
+    all_rows, qkv = gather_inputs(normed.astype(BF16), qkv_piece, 1)
+    all_rows = all_rows.reshape(-1, width)
+    qkv = qkv.reshape(3, width, CHIP_COLS)
+    attended, *saved = attention_forward(all_rows, qkv, slots, q_slots, q_local, low, high)
+    part = jnp.dot(attended, out_w, preferred_element_type=F32).astype(BF16)
+    hidden = active + scatter_plane(part.reshape(CHIPS, rows, width), 2)
+    normed_two, factor_two = rms_forward(hidden, gain_two)
+
+    [ff] = share_cores([ff_piece], 3)
+    gate_w, up_w, down_w = (
+        jnp.swapaxes(ff[:, :, i], 0, 1).reshape(-1, ff.shape[-1]) for i in range(3)
+    )
+    two_rows = gather_plane(normed_two.astype(BF16), 4).reshape(-1, width)
+    gate = jnp.dot(two_rows, gate_w, preferred_element_type=F32)
+    up = jnp.dot(two_rows, up_w, preferred_element_type=F32)
+    inner, inner_pull = jax.vjp(
+        lambda gate_in, up_in: jax.nn.gelu(gate_in, approximate=True) * up_in, gate, up
+    )
+    inner = inner.astype(BF16)
+    part = jnp.dot(inner, down_w, preferred_element_type=F32).astype(BF16)
+    result = hidden + scatter_plane(part.reshape(CHIPS, rows, width), 5)
+
+    difference = (result - active)[:, None]
+    out_states = mixed + correct[None, :, None] * difference
+    ratio = depths * group_len / valid_total
+    upstream = out_grad[0].astype(F32) + ratio * valid_float[0][:, None, None] * (
+        out_states - teacher[0].astype(F32)
+    )
+    correct_local = jnp.sum(upstream * difference, axis=(0, 2))
+    result_grad = correct[0] * upstream[:, 0] + correct[1] * upstream[:, 1]
+
+    grad_rows = gather_plane(result_grad.astype(BF16), 6).reshape(-1, width)
+    inner_grad = lax.dot_general(grad_rows, down_w, NT, preferred_element_type=F32)
+    gate_grad, up_grad = inner_pull(inner_grad)
+    gate_grad, up_grad = gate_grad.astype(BF16), up_grad.astype(BF16)
+    part = lax.dot_general(gate_grad, gate_w, NT, preferred_element_type=F32) + lax.dot_general(
+        up_grad, up_w, NT, preferred_element_type=F32
+    )
+    normed_two_grad = scatter_plane(part.astype(BF16).reshape(CHIPS, rows, width), 7)
+
+    def outer(left, right):
+        return lax.dot_general(
+            left, right, (((0,), (0,)), ((), ())), preferred_element_type=F32
+        ).astype(BF16)
+
+    gate_w_grad = outer(two_rows, gate_grad)
+    up_w_grad = outer(two_rows, up_grad)
+    down_w_grad = outer(inner, grad_rows)
+    ff_grads = [g.reshape(depths, 2, half, hidden_cols) for g in (gate_w_grad, up_w_grad, down_w_grad)]
+    ff_swapped = swap_cores(ff_grads, 8)
+
+    def own_half(grad):
+        return lax.dynamic_index_in_dim(grad, core, 1, keepdims=False)
+
+    ff_sum = jnp.stack(
+        [own_half(g).astype(F32) + s.astype(F32) for g, s in zip(ff_grads, ff_swapped)], axis=1
+    ).astype(BF16)
+    ff_sum = lax.psum_scatter(ff_sum, "wsh", scatter_dimension=0, tiled=False)
+    ff_all = lax.all_gather(ff_sum, "ctx", axis=0, tiled=False)
+
+    hidden_norm_grad, gain_two_grad = rms_backward(hidden, factor_two, gain_two, normed_two_grad)
+    hidden_grad = result_grad + hidden_norm_grad
+    hidden_rows = gather_plane(hidden_grad.astype(BF16), 9).reshape(-1, width)
+    out_w_part = outer(attended, hidden_rows)
+    dq, dk, dv = attention_backward(hidden_rows, out_w, saved, slots, q_local, low, high)
+    by_core = [g.reshape(CHIPS, 2, rows, CHIP_COLS) for g in (dk, dv)]
+    swapped = swap_cores(by_core, 10)
+    dk, dv = (
+        (own_half(g).astype(F32) + s.astype(F32)).astype(BF16).reshape(-1, CHIP_COLS)
+        for g, s in zip(by_core, swapped)
+    )
+    part = (
+        lax.dot_general(dq, qkv[0], NT, preferred_element_type=F32)
+        + lax.dot_general(dk, qkv[1], NT, preferred_element_type=F32)
+        + lax.dot_general(dv, qkv[2], NT, preferred_element_type=F32)
+    )
+    normed_grad = scatter_plane(part.astype(BF16).reshape(CHIPS, rows, width), 11)
+    own_rows = lax.dynamic_index_in_dim(
+        all_rows.reshape(CHIPS, 2, rows, width), core, 1, keepdims=False
+    ).reshape(-1, width)
+    qkv_grads = [outer(own_rows, g).reshape(depths, 2, half, CHIP_COLS) for g in (dq, dk, dv)]
+    qkv_swapped = swap_cores(qkv_grads, 12)
+    qkv_sum = jnp.stack(
+        [own_half(g).astype(F32) + s.astype(F32) for g, s in zip(qkv_grads, qkv_swapped)], axis=1
+    ).astype(BF16)
+    qkv_sum = lax.psum_scatter(qkv_sum, "wsh", scatter_dimension=0, tiled=False)
+    qkv_all = lax.all_gather(qkv_sum, "ctx", axis=0, tiled=False)
+
+    spread = jnp.where(
+        jnp.arange(CHIPS, dtype=jnp.int32)[:, None, None] == chip, out_w_part[None], jnp.zeros((), BF16)
+    )
+    out_w_grad = lax.psum(
+        lax.psum_scatter(spread, "wsh", scatter_dimension=0, tiled=False), "ctx"
+    ).astype(F32)
+
+    active_norm_grad, gain_one_grad = rms_backward(active, factor_one, gain_one, normed_grad)
+    active_grad = hidden_grad + active_norm_grad - result_grad
+    mixed_grad = jnp.stack([upstream[:, 0] + active_grad, upstream[:, 1]], axis=1)
+    predict_local = jnp.stack(
+        [jnp.stack([jnp.sum(mixed_grad[:, i] * inputs[:, j]) for j in range(2)]) for i in range(2)]
+    )
+    states_grad = jnp.stack(
+        [predict[0, j] * mixed_grad[:, 0] + predict[1, j] * mixed_grad[:, 1] for j in range(2)], axis=1
+    ).astype(BF16)
+    predict_grad, correct_grad, gain_one_grad, gain_two_grad = lax.psum(
+        (predict_local, correct_local, gain_one_grad, gain_two_grad), ("ctx", "wsh")
+    )
+    offset = lax.axis_index("wsh") * shard
+
+    def own_gain(grad):
+        return lax.dynamic_slice_in_dim(grad, offset, shard, 0)
+
+    def wide_rows(pieces, split):
+        pieces = pieces.reshape(CHIPS, 2, half, split, -1)
+        return jnp.transpose(pieces, (1, 2, 3, 0, 4)).reshape(shard, -1).astype(F32)
+
+    query_grad, key_grad, value_grad = (wide_rows(qkv_all[:, i], 1) for i in range(3))
+    gate_out, up_out = (wide_rows(ff_all[:, i], depths) for i in range(2))
+    down_out = ff_all[:, 2].reshape(-1, width).astype(F32)
+    return (
+        out_states.astype(BF16)[None],
+        states_grad[None],
+        predict_grad,
+        correct_grad,
+        own_gain(gain_one_grad),
+        query_grad,
+        key_grad,
+        value_grad,
+        out_w_grad,
+        own_gain(gain_two_grad),
+        gate_out,
+        up_out,
+        down_out,
+    )
+
+
+def fits_plane(mesh, states, block_slot, w_query, w_gate):
+    ctx, depths = mesh.shape["ctx"], mesh.shape["wsh"]
+    return (
+        ctx == 2 * CHIPS
+        and states.shape[0] == depths
+        and block_slot.shape[1] * BLK == 2 * PROMPT
+        and states.shape[1] == 2 * PROMPT
+        and w_query.shape[0] % (32 * depths) == 0
+        and w_gate.shape[1] % (32 * CHIPS * depths) == 0
+    )
+
+
 def solution(mesh):
-    return jax.shard_map(
-        shards,
-        mesh=mesh,
-        in_specs=(
-            P("wsh", "ctx", None, None),
-            P("wsh", None),
-            P("wsh", None),
-            P("wsh", "ctx"),
-            P("wsh", "ctx", None, None),
-            P("wsh", "ctx", None, None),
-            P(),
-            P(),
-            P("wsh"),
-            P("wsh", None),
-            P("wsh", None),
-            P("wsh", None),
-            P("wsh", None),
-            P("wsh"),
-            P("wsh", None),
-            P("wsh", None),
-            P("wsh", None),
-        ),
-        out_specs=(
-            P("wsh", "ctx", None, None),
-            P("wsh", "ctx", None, None),
-            P(),
-            P(),
-            P("wsh"),
-            P("wsh", None),
-            P("wsh", None),
-            P("wsh", None),
-            P("wsh", None),
-            P("wsh"),
-            P("wsh", None),
-            P("wsh", None),
-            P("wsh", None),
-        ),
-        check_vma=False,
-    )
+    in_specs = (
+        P("wsh", "ctx", None, None),
+        P("wsh", None),
+        P("wsh", None),
+        P("wsh", "ctx"),
+        P("wsh", "ctx", None, None),
+        P("wsh", "ctx", None, None),
+        P(),
+        P(),
+        P("wsh"),
+        P("wsh", None),
+        P("wsh", None),
+        P("wsh", None),
+        P("wsh", None),
+        P("wsh"),
+        P("wsh", None),
+        P("wsh", None),
+        P("wsh", None),
+    )
+    out_specs = (
+        P("wsh", "ctx", None, None),
+        P("wsh", "ctx", None, None),
+        P(),
+        P(),
+        P("wsh"),
+        P("wsh", None),
+        P("wsh", None),
+        P("wsh", None),
+        P("wsh", None),
+        P("wsh"),
+        P("wsh", None),
+        P("wsh", None),
+        P("wsh", None),
+    )
+
+    def step(*args):
+        plane = fits_plane(mesh, args[0], args[1], args[9], args[14])
+        body = plane_shards if plane else general_shards
+        return jax.shard_map(
+            body, mesh=mesh, in_specs=in_specs, out_specs=out_specs, check_vma=False
+        )(*args)
+
+    return step

time: 1210 us -> 655 us (0.54)
  waiting for transfers between devices: 627 us -> 99.5 us
  Pallas kernels: 0 us -> 241 us
  matrix products: 216 us -> 41.3 us
  local copies, waits for them, and re-layouts: 122 us -> 84.6 us
  loops' own time: 32.9 us -> 0 us
  other arithmetic: 75.4 us -> 54.6 us
    reduce_scatter x8 -> x1, waiting for transfers between devices: 332 us -> 0.81 us  [plane_shards(): lax.psum_scatter(spread, 'wsh', scatter_dimension=0, tiled=False)]
    all_gather x9 -> x3, waiting for transfers between devices: 283 us -> 0.02 us  [the longest x1 0.02 us: plane_shards(): lax.all_gather(jnp.stack([ff_columns(w_gate), ff_columns(w_up), down_rows...]
    pallas_call x0 -> x14, Pallas kernels: none -> 241 us  [the longest x4 69.4 us: scatter_plane(): pl.pallas_call(kernel, out_shape=jax.ShapeDtypeStruct((rows, width), F32)...]
    dot_general x81 -> x17, matrix products: 216 us -> 41.3 us  [the longest x7 19.4 us: outer(): lax.dot_general(left, right, (((0,), (0,)), ((), ())), preferred_element_...]
    unnamed x18 -> x7, waiting for transfers between devices: 4.83 us -> 98.7 us
    dynamic_slice x73 -> x10, local copies, waits for them, and re-layouts: 80.8 us -> 11.2 us  [the longest x1 2.65 us: plane_shards(): lax.dynamic_index_in_dim(all_rows.reshape(CHIPS, 2, rows, width), core, 1...]
    convert_element_type x0 -> x13, local copies, waits for them, and re-layouts: none -> 36.8 us  [the longest x12 34.9 us: wide_rows(): return jnp.transpose(pieces, (1, 2, 3, 0, 4)).reshape(shard, -1).astype(F32)]
    reduce_or x24 -> x0, other arithmetic: 36.1 us -> none  [the longest x8 12 us: forward_block(): jnp.any(allowed)]
  transfers between devices with their start and end apart: 18 -> 6, of which waited for: 14 -> 2; matrix products, arithmetic and copies ran while one was open for 21% -> 13% of each run, Pallas kernels for 0% -> 15%
where the time goes in v1:
time: 655 us; the launch traced here: 647 us
  Pallas kernels  241 us (37%)
  blocking collectives  109 us (17%)
  waiting for transfers between devices  99.5 us (15%)
  local copies, waits for them, and re-layouts  84.6 us (13%)
  other arithmetic  54.6 us (8%)
  matrix products  41.3 us (6%)
  between operations  17 us (3%)
    unnamed x7, waiting for transfers between devices  98.7 us
    pallas_call x4, Pallas kernels, scatter_plane(): pl.pallas_call(kernel, out_shape=jax.ShapeDtypeStruct((rows, width), F32)...  69.4 us
    pallas_call x1, Pallas kernels, share_cores(): pl.pallas_call(kernel, out_shape=[jax.ShapeDtypeStruct((2,) + a.shape, a....  57.1 us
    psum x1, blocking collectives, plane_shards(): valid_total = lax.psum(jnp.sum(valid_float), ('ctx', 'wsh'))  46.6 us
    psum x1, blocking collectives, plane_shards(): lax.psum((predict_local, correct_local, gain_one_grad, gain_two_grad), ('...  42 us
    pallas_call x3, Pallas kernels, gather_plane(): pl.pallas_call(kernel, out_shape=jax.ShapeDtypeStruct((CHIPS,) + block.sh...  41.6 us
    convert_element_type x12, local copies, waits for them, and re-layouts, wide_rows(): return jnp.transpose(pieces, (1, 2, 3, 0, 4)).reshape(shard, -1).astype(F32)  34.9 us
    pallas_call x1, Pallas kernels, attention_backward(): pl.pallas_call(kernel, out_shape=[jax.ShapeDtypeStruct((queries, CHIP_COL...  20.8 us
  transfers between devices with their start and end apart: 6, of which 2 were waited for; matrix products, arithmetic and copies ran while one was open for 13% of the time, Pallas kernels for 15%

profile of v1, /device:TPU:9, one launch (start us, length us, event | category | flops | bytes accessed | tf_op | source)
XLA Modules:
  0.0 647.3 jit_solution(2767717429046531208)
XLA Ops:
  21.6 7.3 %all-reduce.5 = (bf16[768]{0:T(1024)(128)(2,1)S(1)}, bf16[768]{0:T(1024)(128)(2,1)S(1)}) all-reduce(bf16[768]{0:T(1024)(128)(2,1)S(1)} %dynamic-update-slice, bf16[768]{0:T(1024)(128)(2,1)S(1)} %dynamic-update-slice.1), channel_id=1, replica_groups=mesh['ctx'=8,'wsh'=4] {'wsh'}, use_global_device_ids=true, to_apply=%add | all-reduce | flops 1536 | bytes 6144
  35.5 46.6 %psum.42 = f32[]{:T(128)} all-reduce(f32[]{:T(128)} %convert_reduce_fusion.1), channel_id=1, replica_groups=mesh['ctx'=8,'wsh'=4] {'ctx','wsh'}, use_global_device_ids=true, to_apply=%region_8.9 | all-reduce | flops 1 | bytes 8 | tf_op jit(solution)/shard_map/psum | solution.py:1014
  83.2 19.5 %gather_inputs.1 = (bf16[8,256,768]{2,1,0:T(8,128)(2,1)}, bf16[3,4,2,96,192]{4,3,2,1,0:T(8,128)(2,1)}) custom-call(bf16[256,768]{1,0:T(8,128)(2,1)} %multiply_convert_fusion.3.x_ref, bf16[3,96,192]{2,1,0:T(8,128)(2,1)} %pad_maximum_fusion.4.w_ref), custom_call_target="tpu_custom_call" | custom-call | tf_op jit(solution)/shard_map/gather_inputs/pallas_call | solution.py:693
  104.0 20.4 %attention_forward.1 = (bf16[1024,192]{1,0:T(8,128)(2,1)}, f32[4,192,256]{2,1,0:T(8,128)}, bf16[1024,192]{1,0:T(8,128)(2,1)}, bf16[2048,192]{1,0:T(8,128)(2,1)},...) custom-call(s32[32]{0:T(128)} %select_reduce_fusion.1.slots_ref, s32[16]{0:T(128)} %get-tuple-element.145.q_slots_ref, ...), custom_call_target="tpu_custom_call" | custom-call | tf_op jit(solution)/shard_map/attention_forward/pallas_call | solution.py:813
  125.6 2.7 constant_dynamic-slice_fusion.2
  128.2 3.9 multiply_add_fusion.2
  134.8 17.7 %scatter_plane.4 = f32[256,768]{1,0:T(8,128)} custom-call(bf16[4,256,768]{2,1,0:T(8,128)(2,1)} %bitcast.258), custom_call_target="tpu_custom_call" | custom-call | tf_op jit(solution)/shard_map/scatter_plane/pallas_call | solution.py:542
  154.7 13.9 %gather_plane.3 = bf16[4,256,768]{2,1,0:T(8,128)(2,1)} custom-call(bf16[256,768]{1,0:T(8,128)(2,1)} %multiply_convert_fusion.2.x_ref), custom_call_target="tpu_custom_call" | custom-call | tf_op jit(solution)/shard_map/gather_plane/pallas_call | solution.py:492
  168.6 57.1 %share_cores.1 = bf16[2,4,3,96,768]{4,3,2,1,0:T(8,128)(2,1)} custom-call(bf16[4,3,96,768]{3,2,1,0:T(8,128)(2,1)} %bitcast.279), custom_call_target="tpu_custom_call" | custom-call | tf_op jit(solution)/shard_map/share_cores/pallas_call | solution.py:578
  225.7 2.2 slice_bitcast_fusion
  228.2 2.5 copy-done.23
  232.1 3.4 multiply_convert_fusion.1
  235.5 2.5 convolution_convert_fusion
  238.1 17.5 %scatter_plane.5 = f32[256,768]{1,0:T(8,128)} custom-call(bf16[4,256,768]{2,1,0:T(8,128)(2,1)} %bitcast.282), custom_call_target="tpu_custom_call" | custom-call | tf_op jit(solution)/shard_map/scatter_plane/pallas_call | solution.py:542
  260.1 2.4 fusion.39
  262.5 14.5 %gather_plane.4 = bf16[4,256,768]{2,1,0:T(8,128)(2,1)} custom-call(bf16[256,768]{1,0:T(8,128)(2,1)} %get-tuple-element.139.x_ref), custom_call_target="tpu_custom_call" | custom-call | tf_op jit(solution)/shard_map/gather_plane/pallas_call | solution.py:492
  277.0 4.6 convolution_convert_fusion.2
  281.6 5.8 multiply_convert_fusion
  289.7 2.6 add_convert_fusion.1
  292.3 15.7 %scatter_plane.6 = f32[256,768]{1,0:T(8,128)} custom-call(bf16[4,256,768]{2,1,0:T(8,128)(2,1)} %bitcast.281), custom_call_target="tpu_custom_call" | custom-call | tf_op jit(solution)/shard_map/scatter_plane/pallas_call | solution.py:542
  310.7 13.2 %gather_plane.5 = bf16[4,256,768]{2,1,0:T(8,128)(2,1)} custom-call(bf16[256,768]{1,0:T(8,128)(2,1)} %fusion.36.x_ref), custom_call_target="tpu_custom_call" | custom-call | tf_op jit(solution)/shard_map/gather_plane/pallas_call | solution.py:492
  323.9 2.7 convolution_convert_fusion.5
  326.6 20.8 %attention_backward.1 = (bf16[1024,192]{1,0:T(8,128)(2,1)}, bf16[2048,192]{1,0:T(8,128)(2,1)}, bf16[2048,192]{1,0:T(8,128)(2,1)}) custom-call(s32[32]{0:T(128)} %select_reduce_fusion.1.slots_ref, s32[16]{0:T(128)} %get-tuple-element.146.q_local_ref, bf16[1024,768]{1,0:T(8,128)(2,1)} %bitcast.260, bf16[192,768]{1,0:T(8,128)(2,1)} %copy-done.11, ...), custom_call_target="tpu_custom_call" | custom-call | tf_op jit(solution)/shard_map/attention_backward/pallas_call | solution.py:930
  347.4 2.7 convolution_convert_fusion.8
  354.0 5.6 swap_cores.3
  366.8 1.8 copy.129
  368.6 2.1 broadcast_select_fusion
  374.3 1.9 copy.112
  377.2 2.4 swap_cores.4
  379.7 4.5 convolution_convert_fusion.3
  384.2 2.5 convolution_convert_fusion.4
  386.6 4.1 swap_cores.5
  398.9 97.9 %all-reduce.12.cloned.1.call-done = (bf16[4,3,96,192]{3,2,0,1:T(8,128)(2,1)}, bf16[4,3,96,768]{3,2,0,1:T(8,128)(2,1)}) async-done(((bf16[4,3,96,192]{3,2,0,1:T(8,128)(2,1)}, bf16[4,3,96,768]{3,2,0,1:T(8,128)(2,1)}), (bf16[4,3,96,192]{3,2,0,1:T(8,128)(2,1)}, bf16[4,3,96,768]{3,2,0,1:T(8,128)(2,1)})) %all-reduce.12.cloned.1.call-update) | async-done | bytes 2211856
  496.8 2.4 constant_dynamic-slice_fusion.7
  504.5 18.4 %scatter_plane.7 = f32[256,768]{1,0:T(8,128)} custom-call(bf16[4,256,768]{2,1,0:T(8,128)(2,1)} %bitcast.261), custom_call_target="tpu_custom_call" | custom-call | tf_op jit(solution)/shard_map/scatter_plane/pallas_call | solution.py:542
  524.6 3.8 fusion.19
  531.2 42.0 %all-reduce.4 = (f32[2,2]{1,0:T(2,128)}, f32[2]{0:T(128)}, f32[768]{0:T(1024)S(1)}, f32[768]{0:T(1024)S(1)}) all-reduce(f32[2,2]{1,0:T(2,128)S(1)} %pad_maximum_fusion.5, f32[2]{0:T(128)S(1)} %copy-done.50, f32[768]{0:T(1024)S(1)} %get-tuple-element.122, f32[768]{0:T(1024)S(1)} %get-tuple-element.120), channel_id=1, replica_groups=mesh['ctx'=8,'wsh'=4] {'ctx','wsh'}, use_global_device_ids=true, to_apply=%region_15.16 | all-reduce | flops 1542 | bytes 12336 | tf_op jit(solution)/shard_map/psum | solution.py:1128
  573.2 1.9 fusion.7
  576.8 2.7 fusion.24
  584.0 13.5 %all_gather.26 = bf16[8,3,96,192]{3,2,0,1:T(8,128)(2,1)S(1)} all-gather(bf16[1,3,96,192]{3,2,0,1:T(8,128)(2,1)S(1)} %constant_dynamic-slice_fusion.8), channel_id=1, replica_groups=mesh['ctx'=8,'wsh'=4] {'ctx'}, dimensions={0}, use_global_device_ids=true | all-gather | bytes 995328 | tf_op jit(solution)/shard_map/all_gather | solution.py:1110
  603.2 1.8 convert_element_type.310
  605.1 3.9 fusion.41
  610.6 5.1 reshape.454
  615.7 5.6 copy.122
  621.3 4.8 reshape.448
  626.1 3.5 reshape.453
  629.5 5.7 copy.121
  635.2 4.8 reshape.447
  (253 shorter events, 85.7 us)
Async XLA Ops:
  7.2 7.8 %copy-start = (bf16[768,768]{1,0:T(8,128)(2,1)S(1)}, bf16[768,768]{1,0:T(8,128)(2,1)}, u32[]{:S(2)}) copy-start(bf16[768,768]{1,0:T(8,128)(2,1)} %param.33) | copy-start | bytes 3538948
  7.2 124.9 %all-gather.5.cloned.1.call-start = ((), (), s32[]{:S(2)}) async-start(), calls=%async_computation.1 | async-start | bytes 1474560 | tf_op jit(solution)/shard_map/all_gather | solution.py:1008
  7.9 160.7 %all-gather.9.cloned.1.call-start = ((), (), s32[]{:S(2)}) async-start(), calls=%async_computation.5 | async-start | bytes 2211840 | tf_op jit(solution)/shard_map/all_gather | solution.py:1010
  13.4 4.0 copy-start.53
  13.4 5.1 copy-start.52
  13.4 6.4 copy-start.54
  13.4 6.4 copy-start.51
  13.4 7.7 %copy-start.55 = (bf16[192]{0:T(256)(128)(2,1)S(1)}, bf16[192]{0:T(256)(128)(2,1)}, u32[]{:S(2)}) copy-start(bf16[192]{0:T(256)(128)(2,1)} %param.25) | copy-start | bytes 1156
  13.5 7.9 %copy-start.56 = (bf16[192]{0:T(256)(128)(2,1)S(1)}, bf16[192]{0:T(256)(128)(2,1)}, u32[]{:S(2)}) copy-start(bf16[192]{0:T(256)(128)(2,1)} %param.30) | copy-start | bytes 1156
  13.5 15.4 %copy-start.49 = (f32[2,2]{1,0:T(2,128)S(1)}, f32[2,2]{1,0:T(2,128)}, u32[]{:S(2)}) copy-start(f32[2,2]{1,0:T(2,128)} %param.23) | copy-start | bytes 52
  13.5 16.2 %copy-start.34 = (bf16[1,256,2,768]{3,2,1,0:T(2,128)(2,1)S(1)}, bf16[1,256,2,768]{3,2,1,0:T(2,128)(2,1)}, u32[]{:S(2)}) copy-start(bf16[1,256,2,768]{3,2,1,0:T(2,128)(2,1)} %param.17) | copy-start | bytes 2359300
  16.8 382.0 %reduce-scatter.6.cloned.1.call-start = ((), (), s32[]{:S(2)}) async-start(), calls=%async_computation.2 | async-start | bytes 1474560 | tf_op jit(solution)/shard_map/reduce_scatter | solution.py:1116
  31.2 93.1 %copy-start.43 = (f32[256]{0:T(256)}, f32[256]{0:T(256)S(1)}, u32[]{:S(2)}) copy-start(f32[256]{0:T(256)S(1)} %add_rsqrt_fusion.1) | copy-start | bytes 3076
  104.0 21.0 %copy-start.47 = (f32[2]{0:T(128)S(1)}, f32[2]{0:T(128)}, u32[]{:S(2)}) copy-start(f32[2]{0:T(128)} %param.24) | copy-start | bytes 28
  128.2 4.9 copy-start.40
  133.1 19.4 %copy-start.11 = (bf16[192,768]{1,0:T(8,128)(2,1)}, bf16[192,768]{1,0:T(8,128)(2,1)S(1)}, u32[]{:S(2)}) copy-start(bf16[192,768]{1,0:T(8,128)(2,1)S(1)} %constant_dynamic-slice_fusion.5.w_ref) | copy-start | bytes 884740
  228.0 7.5 %copy-start.28 = (bf16[4,2,96,768]{3,2,1,0:T(8,128)(2,1)}, bf16[4,2,96,768]{3,2,1,0:T(8,128)(2,1)S(1)}, u32[]{:S(2)}) copy-start(bf16[4,2,96,768]{3,2,1,0:T(8,128)(2,1)S(1)} %copy.108) | copy-start | bytes 3538948
  228.1 4.0 copy-start.26
  228.1 2.6 copy-start.23
  228.2 3.9 copy-start.30
  232.1 3.4 copy-start.58
  235.5 2.5 copy-start.60
  277.0 4.6 copy-start.25
  277.0 4.6 copy-start.29
  277.0 4.6 copy-start.59
  281.6 5.9 copy-start.31
  287.5 2.2 copy-start.27
  309.5 14.4 %copy-start.45 = (f32[256]{0:T(256)}, f32[256]{0:T(256)S(1)}, u32[]{:S(2)}) copy-start(f32[256]{0:T(256)S(1)} %broadcast_multiply_fusion.1) | copy-start | bytes 3076
  310.7 13.3 %copy-start.41 = (bf16[1024,192]{1,0:T(8,128)(2,1)S(1)}, bf16[1024,192]{1,0:T(8,128)(2,1)}, u32[]{:S(2)}) copy-start(bf16[1024,192]{1,0:T(8,128)(2,1)} %get-tuple-element.34) | copy-start | bytes 1179652
  359.6 2.3 copy-start.21
  370.8 126.0 %all-reduce.12.cloned.1.call-start = ((), (), s32[]{:S(2)}) async-start(), calls=%async_computation.6 | async-start | bytes 4718592
  370.8 2.3 copy-start.22
  373.1 3.1 copy-start.20
  379.6 4.5 copy-start.24
  379.6 4.5 copy-start.62
  386.6 4.1 copy-start.15
  386.6 5.2 copy-start.35
  386.6 6.2 copy-start.36
  390.7 4.1 copy-start.12
  390.7 4.1 copy-start.39
  398.0 205.3 %all-reduce.10.cloned.1.call-start = ((), (), s32[]{:S(2)}) async-start(), calls=%async_computation.3 | async-start | bytes 589824 | tf_op jit(solution)/shard_map/psum | solution.py:1115
  398.9 206.2 %all-gather.7.cloned.1.call-start = ((), (), s32[]{:S(2)}) async-start(), calls=%async_computation.4 | async-start | bytes 3981312 | tf_op jit(solution)/shard_map/all_gather | solution.py:1082
  504.5 18.5 %copy-start.44 = (f32[256]{0:T(256)S(1)}, f32[256]{0:T(256)}, u32[]{:S(2)}) copy-start(f32[256]{0:T(256)} %copy-done.43) | copy-start | bytes 3076
  504.5 20.0 %copy-start.46 = (f32[256]{0:T(256)S(1)}, f32[256]{0:T(256)}, u32[]{:S(2)}) copy-start(f32[256]{0:T(256)} %copy-done.45) | copy-start | bytes 3076
  524.6 6.6 %copy-start.50 = (f32[2]{0:T(128)S(1)}, f32[2]{0:T(128)}, u32[]{:S(2)}) copy-start(f32[2]{0:T(128)} %get-tuple-element.136) | copy-start | bytes 28
  524.6 48.6 %copy-start.48 = (f32[2]{0:T(128)S(1)}, f32[2]{0:T(128)}, u32[]{:S(2)}) copy-start(f32[2]{0:T(128)} %param.24) | copy-start | bytes 28
  573.2 3.6 copy-start.10
  629.5 10.5 %copy-start.1 = (bf16[768,768]{1,0:T(8,128)(2,1)S(1)}, bf16[768,768]{1,0:T(8,128)(2,1)}, u32[]{:S(2)}) copy-start(bf16[768,768]{1,0:T(8,128)(2,1)} %param.33) | copy-start | bytes 3538948
  (21 other events, 30.8 us)
Sparse Core Ops, SparseCore 0:
  9.6 31.1 all-gather.4
  42.9 39.8 all-gather.8
  370.9 27.9 reduce-scatter.5
  401.7 95.0 all-reduce.11
  499.8 54.2 all-reduce.9
  556.4 35.5 all-gather.6

commit v2 on v1

--- a/solution.py
+++ b/solution.py
@@ -556,36 +556,6 @@
     )(parts)
 
 
-def share_cores(arrays, collective_id):
-    count = len(arrays)
-
-    def kernel(*refs):
-        ins, outs, (send, recv, local) = refs[:count], refs[count : 2 * count], refs[2 * count :]
-        depth, chip, core, _, _, _ = place_on_mesh()
-        other = (2 * chip + 1 - core, depth)
-        signal_and_wait([other])
-        copies = [
-            remote(ins[i], outs[i].at[core], send, recv, i, other) for i in range(count)
-        ]
-        mine = [
-            pltpu.make_async_copy(ins[i], outs[i].at[core], local.at[i]) for i in range(count)
-        ]
-        for copy in copies + mine:
-            copy.start()
-        for copy in copies + mine:
-            copy.wait()
-
-    return pl.pallas_call(
-        kernel,
-        out_shape=[jax.ShapeDtypeStruct((2,) + a.shape, a.dtype) for a in arrays],
-        in_specs=[ANY] * count,
-        out_specs=[ANY] * count,
-        scratch_shapes=[pltpu.SemaphoreType.DMA((count,))] * 3,
-        compiler_params=comm_params(collective_id),
-        name="share_cores",
-    )(*arrays)
-
-
 def swap_cores(arrays, collective_id):
     count = len(arrays)
 
@@ -613,26 +583,69 @@
     )(*arrays)
 
 
-def gather_inputs(block, weights, collective_id):
+def line_relay(ref, chip, depth, depths, send, recv, send_base):
+    _, _, core, _, _, _ = place_on_mesh()
+    up = remote(ref, ref, send, recv, send_base, (2 * chip + core, lax.rem(depth + 1, depths)))
+    down = remote(
+        ref, ref, send, recv, send_base + 1, (2 * chip + core, lax.rem(depth + depths - 1, depths))
+    )
+    goes_up = (depth >= chip) & (depth < depths - 1)
+    goes_down = (depth <= chip) & (depth > 0)
+
+    def start():
+        @pl.when(goes_up)
+        def _():
+            up.start()
+
+        @pl.when(goes_down)
+        def _():
+            down.start()
+
+    def receive():
+        @pl.when(depth > chip)
+        def _():
+            up.wait_recv()
+
+        @pl.when(depth < chip)
+        def _():
+            down.wait_recv()
+
+    def finish():
+        @pl.when(goes_up)
+        def _():
+            up.wait_send()
+
+        @pl.when(goes_down)
+        def _():
+            down.wait_send()
+
+    return start, receive, finish
+
+
+def gather_inputs(pre, small, weights, out_half, collective_id):
     depths = lax.axis_size("wsh")
 
-    def kernel(x_ref, w_ref, out_ref, wall_ref, send, recv, wsend, wrecv, ssend, srecv, local):
+    def kernel(
+        pre_ref, small_ref, w_ref, o_ref, out_ref, wall_ref, oall_ref, sum_ref,
+        own, arrived, count, counted,
+        send, recv, wsend, wrecv, ssend, srecv, bsend, brecv, csend, crecv, osend, orecv, local,
+    ):
         depth, chip, core, chip_x, chip_y, chip_d = place_on_mesh()
+        dev_x, dev_y = (2 * chip_x + core, depth), (2 * chip_y + core, depth)
         other = (2 * chip + 1 - core, depth)
         across = [
             (2 * chip + core, lax.rem(depth + step, depths)) for step in range(1, depths)
         ]
-        signal_and_wait(
-            [(2 * chip_x + core, depth), (2 * chip_y + core, depth), other] + across
-        )
+        signal_and_wait([dev_x, dev_y, other] + across)
 
         def slot(chip_index):
             return 2 * chip_index + core
 
-        copies = ring_sends(
-            x_ref, out_ref, slot, chip, core, depth, chip_x, chip_y, send, recv
-        )
-        for copy in copies[:4]:
+        small_copies = [
+            remote(small_ref, arrived.at[i], bsend, brecv, i, device)
+            for i, device in enumerate(across)
+        ]
+        for copy in small_copies:
             copy.start()
         w_copies = [
             remote(w_ref, wall_ref.at[:, depth, core], wsend, wrecv, i, device)
@@ -640,12 +653,8 @@
         ]
         for copy in w_copies:
             copy.start()
-        mine = [
-            pltpu.make_async_copy(x_ref, out_ref.at[slot(chip)], local.at[0]),
-            pltpu.make_async_copy(w_ref, wall_ref.at[:, depth, core], local.at[1]),
-        ]
-        for copy in mine:
-            copy.start()
+        mine = pltpu.make_async_copy(w_ref, wall_ref.at[:, depth, core], local.at[1])
+        mine.start()
 
         def pass_on(index, slot_index):
             ref = out_ref.at[slot_index]
@@ -656,7 +665,7 @@
             return remote(ref, ref, ssend, srecv, index, other)
 
         shared = [
-            remote(x_ref, out_ref.at[slot(chip)], ssend, srecv, 0, other),
+            remote(own, out_ref.at[slot(chip)], ssend, srecv, 0, other),
             pass_on(1, slot(chip_x)),
             pass_on(2, slot(chip_y)),
             pass_on(3, slot(chip_d)),
@@ -665,12 +674,65 @@
             pass_weights(5 + i, lax.rem(depth + depths - 1 - i, depths))
             for i in range(depths - 1)
         ]
+        shared[4].start()
+
+        @pl.when(depth == chip)
+        def _():
+            fill = pltpu.make_async_copy(o_ref, oall_ref.at[core], local.at[2])
+            fill.start()
+            fill.wait()
+
+        relay_start, relay_receive, relay_finish = line_relay(
+            oall_ref.at[core], chip, depth, depths, osend, orecv, 0
+        )
+
+        @pl.when(depth == chip)
+        def _():
+            relay_start()
+
+        for copy in small_copies:
+            copy.wait_recv()
+        total = small_ref[...]
+        for i in range(depths - 1):
+            total = total + arrived[i]
+        own[...] = (pre_ref[...] * total[0:1, :]).astype(BF16)
+        copies = ring_sends(
+            own, out_ref, slot, chip, core, depth, chip_x, chip_y, send, recv
+        )
+        for copy in copies[:4]:
+            copy.start()
         shared[0].start()
-        shared[4].start()
+        mine_rows = pltpu.make_async_copy(own, out_ref.at[slot(chip)], local.at[0])
+        mine_rows.start()
+        sum_ref[...] = total
+
+        def count_stage(index, device):
+            return remote(count.at[index], counted.at[index], csend, crecv, index, device)
+
+        stages = [count_stage(0, dev_x), count_stage(1, dev_y), count_stage(2, other)]
+        running = jnp.broadcast_to(total[2:3, 0:128], (8, 128))
+        count[0] = running
+        stages[0].start()
         copies[0].wait_recv()
         copies[4].start()
         copies[1].wait_recv()
         copies[5].start()
+        stages[0].wait_recv()
+        running = running + counted[0]
+        count[1] = running
+        stages[1].start()
+
+        @pl.when(depth != chip)
+        def _():
+            relay_receive()
+            relay_start()
+
+        pass_out = remote(oall_ref.at[core], oall_ref.at[core], osend, orecv, 2, other)
+        pass_out.start()
+        stages[1].wait_recv()
+        running = running + counted[1]
+        count[2] = running
+        stages[2].start()
         for i in range(depths - 1):
             w_copies[i].wait_recv()
             shared[5 + i].start()
@@ -678,38 +740,409 @@
         shared[1].start()
         copies[3].wait_recv()
         shared[2].start()
+        stages[2].wait_recv()
+        sum_ref[2:3, 0:128] = (running + counted[2])[0:1]
         copies[4].wait_recv()
         copies[5].wait_recv()
         shared[3].start()
-        for copy in shared:
+        for copy in shared + [pass_out]:
             copy.wait()
-        for copy in copies + w_copies:
+        for copy in copies + w_copies + small_copies + stages:
             copy.wait_send()
-        for copy in mine:
-            copy.wait()
-
-    shape = (lax.axis_size("ctx"),) + block.shape
-    parts, rows, columns = weights.shape
+        relay_finish()
+        mine.wait()
+        mine_rows.wait()
+
+    rows, width = pre.shape
+    parts, half, columns = weights.shape
+    dma = pltpu.SemaphoreType.DMA
     return pl.pallas_call(
         kernel,
         out_shape=[
-            jax.ShapeDtypeStruct(shape, block.dtype),
-            jax.ShapeDtypeStruct((parts, depths, 2, rows, columns), weights.dtype),
+            jax.ShapeDtypeStruct((lax.axis_size("ctx"), rows, width), BF16),
+            jax.ShapeDtypeStruct((parts, depths, 2, half, columns), weights.dtype),
+            jax.ShapeDtypeStruct((2,) + out_half.shape, out_half.dtype),
+            jax.ShapeDtypeStruct(small.shape, F32),
         ],
-        in_specs=[ANY, ANY],
-        out_specs=[ANY, ANY],
+        in_specs=[VM, VM, ANY, ANY],
+        out_specs=[ANY, ANY, ANY, VM],
         scratch_shapes=[
-            pltpu.SemaphoreType.DMA((6,)),
-            pltpu.SemaphoreType.DMA((6,)),
-            pltpu.SemaphoreType.DMA((depths - 1,)),
-            pltpu.SemaphoreType.DMA((depths - 1,)),
-            pltpu.SemaphoreType.DMA((depths + 4,)),
-            pltpu.SemaphoreType.DMA((depths + 4,)),
-            pltpu.SemaphoreType.DMA((2,)),
+            pltpu.VMEM((rows, width), BF16),
+            pltpu.VMEM((depths - 1,) + small.shape, F32),
+            pltpu.VMEM((3, 8, 128), F32),
+            pltpu.VMEM((3, 8, 128), F32),
+            dma((6,)),
+            dma((6,)),
+            dma((depths - 1,)),
+            dma((depths - 1,)),
+            dma((depths + 4,)),
+            dma((depths + 4,)),
+            dma((depths - 1,)),
+            dma((depths - 1,)),
+            dma((3,)),
+            dma((3,)),
+            dma((3,)),
+            dma((3,)),
+            dma((3,)),
         ],
         compiler_params=comm_params(collective_id),
         name="gather_inputs",
-    )(block, weights)
+    )(pre, small, weights, out_half)
+
+
+def share_weights(piece, collective_id):
+    depths, parts, half, columns = piece.shape
+
+    def kernel(x_ref, out_ref, send, recv, local):
+        depth, chip, core, _, _, _ = place_on_mesh()
+        other = (2 * chip + 1 - core, depth)
+        signal_and_wait([other])
+        copies = []
+        for i in range(parts):
+            dst = out_ref.at[i, :, core]
+            copies.append(remote(x_ref.at[:, i], dst, send, recv, i, other))
+            copies.append(pltpu.make_async_copy(x_ref.at[:, i], dst, local.at[i]))
+        for copy in copies:
+            copy.start()
+        for copy in copies:
+            copy.wait()
+
+    return pl.pallas_call(
+        kernel,
+        out_shape=jax.ShapeDtypeStruct((parts, depths, 2, half, columns), piece.dtype),
+        in_specs=[ANY],
+        out_specs=ANY,
+        scratch_shapes=[pltpu.SemaphoreType.DMA((parts,))] * 3,
+        compiler_params=comm_params(collective_id),
+        name="share_weights",
+    )(piece)
+
+
+def scatter_and_reduce(parts, qkv, out, collective_id):
+    _, rows, width = parts.shape
+    half = rows // 2
+    depths = qkv.shape[0]
+
+    def kernel(
+        x_ref, q_ref, o_ref, out_ref, qsum_ref, osum_ref,
+        near, diagonal, staged, q_other, q_mine, q_far, o_other, o_mine, o_far,
+        send, recv, ssend, srecv, zsend, zrecv, osend, orecv,
+    ):
+        depth, chip, core, chip_x, chip_y, chip_d = place_on_mesh()
+        dev_x, dev_y = (2 * chip_x + core, depth), (2 * chip_y + core, depth)
+        other = (2 * chip + 1 - core, depth)
+        across = [
+            (2 * chip + core, lax.rem(depth + step, depths)) for step in range(1, depths)
+        ]
+        signal_and_wait([dev_x, dev_y, other] + across)
+        top, low = pl.ds(0, half), pl.ds(half, half)
+        first = [
+            remote(x_ref.at[chip_d, top], diagonal.at[0], send, recv, 0, dev_x),
+            remote(x_ref.at[chip_d, low], diagonal.at[1], send, recv, 1, dev_y),
+            remote(x_ref.at[chip_x, top], near.at[0, top], send, recv, 2, dev_x),
+            remote(x_ref.at[chip_y, low], near.at[1, low], send, recv, 3, dev_y),
+        ]
+        swaps = [
+            remote(q_ref.at[:, 1 - core], q_other, ssend, srecv, 0, other),
+            remote(o_ref.at[1 - core], o_other, ssend, srecv, 1, other),
+        ]
+        for copy in first + swaps:
+            copy.start()
+        swaps[0].wait_recv()
+        for i in range(depths):
+            q_mine[i] = (q_ref[i, core].astype(F32) + q_other[i].astype(F32)).astype(BF16)
+        q_copies = [
+            remote(q_mine.at[lax.rem(depth + i + 1, depths)], q_far.at[i], zsend, zrecv, i, device)
+            for i, device in enumerate(across)
+        ]
+        for copy in q_copies:
+            copy.start()
+        swaps[1].wait_recv()
+        o_mine[...] = (o_ref[core].astype(F32) + o_other[...].astype(F32)).astype(BF16)
+        distance = lax.rem(chip + depths - depth, depths)
+        o_copies = [
+            remote(o_mine, o_far.at[i], osend, orecv, i, device) for i, device in enumerate(across)
+        ]
+        for i in range(depths - 1):
+
+            @pl.when(distance == i + 1)
+            def _(i=i):
+                o_copies[i].start()
+
+        second = [
+            remote(staged.at[0], near.at[1, top], send, recv, 4, dev_y),
+            remote(staged.at[1], near.at[0, low], send, recv, 5, dev_x),
+        ]
+        first[0].wait_recv()
+        staged[0] = (x_ref[chip_y, top].astype(F32) + diagonal[0].astype(F32)).astype(BF16)
+        second[0].start()
+        first[1].wait_recv()
+        staged[1] = (x_ref[chip_x, low].astype(F32) + diagonal[1].astype(F32)).astype(BF16)
+        second[1].start()
+        for copy in q_copies:
+            copy.wait_recv()
+        total = q_mine[depth].astype(F32)
+        for i in range(depths - 1):
+            total = total + q_far[i].astype(F32)
+        qsum_ref[...] = total.astype(BF16)
+        osum_ref[...] = jnp.zeros_like(osum_ref)
+
+        @pl.when(distance == 0)
+        def _():
+            for copy in o_copies:
+                copy.wait_recv()
+            total = o_mine[...].astype(F32)
+            for i in range(depths - 1):
+                total = total + o_far[i].astype(F32)
+            osum_ref[...] = total.astype(BF16)
+
+        for copy in first[2:] + second:
+            copy.wait_recv()
+        out_ref[...] = (
+            x_ref[chip].astype(F32) + near[0].astype(F32) + near[1].astype(F32)
+        )
+        for copy in first + second + swaps + q_copies:
+            copy.wait_send()
+        for i in range(depths - 1):
+
+            @pl.when(distance == i + 1)
+            def _(i=i):
+                o_copies[i].wait_send()
+
+    q_block, o_block = qkv.shape[2:], out.shape[1:]
+    dma = pltpu.SemaphoreType.DMA
+    return pl.pallas_call(
+        kernel,
+        out_shape=[
+            jax.ShapeDtypeStruct((rows, width), F32),
+            jax.ShapeDtypeStruct(q_block, BF16),
+            jax.ShapeDtypeStruct(o_block, BF16),
+        ],
+        in_specs=[VM] * 3,
+        out_specs=[VM] * 3,
+        scratch_shapes=[
+            pltpu.VMEM((2, rows, width), BF16),
+            pltpu.VMEM((2, half, width), BF16),
+            pltpu.VMEM((2, half, width), BF16),
+            pltpu.VMEM((depths,) + q_block, BF16),
+            pltpu.VMEM((depths,) + q_block, BF16),
+            pltpu.VMEM((depths - 1,) + q_block, BF16),
+            pltpu.VMEM(o_block, BF16),
+            pltpu.VMEM(o_block, BF16),
+            pltpu.VMEM((depths - 1,) + o_block, BF16),
+            dma((6,)),
+            dma((6,)),
+            dma((2,)),
+            dma((2,)),
+            dma((depths - 1,)),
+            dma((depths - 1,)),
+            dma((depths - 1,)),
+            dma((depths - 1,)),
+        ],
+        compiler_params=comm_params(collective_id),
+        name="scatter_and_reduce",
+    )(parts, qkv, out)
+
+
+def finish_gradients(ff, qkv, out, small, collective_id):
+    depths = lax.axis_size("wsh")
+    half, width = out.shape
+    columns = ff.shape[1]
+    chip_columns = qkv.shape[1]
+    split = columns // depths
+
+    def kernel(
+        f_ref, q_ref, o_ref, s_ref,
+        dq_ref, dk_ref, dv_ref, do_ref, dg_ref, du_ref, dd_ref, small_ref,
+        f_all, q_all, o_all, arrived, count, counted,
+        fsend, frecv, qsend, qrecv, osend, orecv, ssend, srecv, bsend, brecv, csend, crecv,
+    ):
+        depth, chip, core, chip_x, chip_y, chip_d = place_on_mesh()
+        dev_x, dev_y = (2 * chip_x + core, depth), (2 * chip_y + core, depth)
+        other = (2 * chip + 1 - core, depth)
+        across = [
+            (2 * chip + core, lax.rem(depth + step, depths)) for step in range(1, depths)
+        ]
+        signal_and_wait([dev_x, dev_y, other] + across)
+
+        def slot(chip_index):
+            return 2 * chip_index + core
+
+        f_copies = ring_sends(
+            f_ref, f_all, slot, chip, core, depth, chip_x, chip_y, fsend, frecv
+        )
+        q_copies = ring_sends(
+            q_ref, q_all, slot, chip, core, depth, chip_x, chip_y, qsend, qrecv
+        )
+        small_copies = [
+            remote(s_ref, arrived.at[i], bsend, brecv, i, device) for i, device in enumerate(across)
+        ]
+        for copy in small_copies + q_copies[:2] + f_copies[:2]:
+            copy.start()
+        quarter = half // 2
+        o_top, o_low = o_all.at[core, pl.ds(0, quarter)], o_all.at[core, pl.ds(quarter, quarter)]
+        o_source_top, o_source_low = o_ref.at[pl.ds(0, quarter)], o_ref.at[pl.ds(quarter, quarter)]
+        o_copies = [
+            remote(o_source_top, o_top, osend, orecv, 0, dev_x),
+            remote(o_source_low, o_low, osend, orecv, 1, dev_y),
+            remote(o_source_low, o_low, osend, orecv, 2, dev_x),
+            remote(o_source_top, o_top, osend, orecv, 3, dev_y),
+            remote(o_top, o_top, osend, orecv, 4, dev_y),
+            remote(o_low, o_low, osend, orecv, 5, dev_x),
+        ]
+        source, from_x, from_y = chip == depth, chip_x == depth, chip_y == depth
+
+        @pl.when(source)
+        def _():
+            for copy in o_copies[:4]:
+                copy.start()
+            o_all[core] = o_ref[...]
+
+        for copy in q_copies[2:4] + f_copies[2:4]:
+            copy.start()
+        f_all[slot(chip)] = f_ref[...]
+        q_all[slot(chip)] = q_ref[...]
+
+        def shared(index, ref):
+            return remote(ref, ref, ssend, srecv, index, other)
+
+        f_shared = [shared(i, f_all.at[slot(c)]) for i, c in enumerate((chip, chip_x, chip_y, chip_d))]
+        q_shared = [shared(4 + i, q_all.at[slot(c)]) for i, c in enumerate((chip, chip_x, chip_y, chip_d))]
+        o_shared = shared(8, o_all.at[core])
+        f_shared[0].start()
+        q_shared[0].start()
+        for copies in (q_copies, f_copies):
+            copies[0].wait_recv()
+            copies[4].start()
+            copies[1].wait_recv()
+            copies[5].start()
+        for copy in small_copies:
+            copy.wait_recv()
+        total = s_ref[...]
+        for i in range(depths - 1):
+            total = total + arrived[i]
+        count[0] = total
+        stages = [
+            remote(count.at[i], counted.at[i], csend, crecv, i, device)
+            for i, device in enumerate((dev_x, dev_y, other))
+        ]
+        stages[0].start()
+
+        @pl.when(from_x)
+        def _():
+            o_copies[0].wait_recv()
+            o_copies[4].start()
+            o_copies[2].wait_recv()
+
+        @pl.when(from_y)
+        def _():
+            o_copies[1].wait_recv()
+            o_copies[5].start()
+            o_copies[3].wait_recv()
+
+        @pl.when(chip_d == depth)
+        def _():
+            o_copies[4].wait_recv()
+            o_copies[5].wait_recv()
+
+        o_shared.start()
+        for i in range(3):
+            stages[i].wait_recv()
+            total = total + counted[i]
+            if i < 2:
+                count[i + 1] = total
+                stages[i + 1].start()
+        small_ref[...] = total
+        for copies, passed in ((q_copies, q_shared), (f_copies, f_shared)):
+            copies[2].wait_recv()
+            passed[1].start()
+            copies[3].wait_recv()
+            passed[2].start()
+            copies[4].wait_recv()
+            copies[5].wait_recv()
+            passed[3].start()
+        for copy in q_shared + [o_shared] + f_shared:
+            copy.wait()
+        for copy in f_copies + q_copies + small_copies + stages:
+            copy.wait_send()
+
+        @pl.when(source)
+        def _():
+            for copy in o_copies[:4]:
+                copy.wait_send()
+
+        @pl.when(from_x)
+        def _():
+            o_copies[4].wait_send()
+
+        @pl.when(from_y)
+        def _():
+            o_copies[5].wait_send()
+
+        for c in range(2):
+            rows = slice(c * half, (c + 1) * half)
+            do_ref[rows, :] = o_all[c].astype(F32)
+            for i, ref in enumerate((dq_ref, dk_ref, dv_ref)):
+                ref[rows, :] = jnp.concatenate(
+                    [q_all[2 * p + c, i * half : (i + 1) * half, :].astype(F32) for p in range(CHIPS)],
+                    axis=1,
+                )
+            for i, ref in enumerate((dg_ref, du_ref)):
+                for z in range(depths):
+                    ref[rows, z * CHIPS * split : (z + 1) * CHIPS * split] = jnp.concatenate(
+                        [
+                            f_all[
+                                2 * p + c, i * half : (i + 1) * half, z * split : (z + 1) * split
+                            ].astype(F32)
+                            for p in range(CHIPS)
+                        ],
+                        axis=1,
+                    )
+            for p in range(CHIPS):
+                at = (2 * p + c) * half
+                dd_ref[at : at + half, :] = f_all[2 * p + c, 2 * half :, :].astype(F32)
+
+    dma = pltpu.SemaphoreType.DMA
+    shard = 2 * half
+    ctx = lax.axis_size("ctx")
+    square = jax.ShapeDtypeStruct((shard, width), F32)
+    return pl.pallas_call(
+        kernel,
+        out_shape=[
+            square,
+            square,
+            square,
+            square,
+            jax.ShapeDtypeStruct((shard, columns * CHIPS), F32),
+            jax.ShapeDtypeStruct((shard, columns * CHIPS), F32),
+            jax.ShapeDtypeStruct((ctx * half, width), F32),
+            jax.ShapeDtypeStruct(small.shape, F32),
+        ],
+        in_specs=[VM] * 4,
+        out_specs=[VM] * 8,
+        scratch_shapes=[
+            pltpu.VMEM((ctx,) + ff.shape, BF16),
+            pltpu.VMEM((ctx,) + qkv.shape, BF16),
+            pltpu.VMEM((2,) + out.shape, BF16),
+            pltpu.VMEM((depths - 1,) + small.shape, F32),
+            pltpu.VMEM((3,) + small.shape, F32),
+            pltpu.VMEM((3,) + small.shape, F32),
+            dma((6,)),
+            dma((6,)),
+            dma((6,)),
+            dma((6,)),
+            dma((6,)),
+            dma((6,)),
+            dma((9,)),
+            dma((9,)),
+            dma((depths - 1,)),
+            dma((depths - 1,)),
+            dma((3,)),
+            dma((3,)),
+        ],
+        compiler_params=comm_params(collective_id),
+        name="finish_gradients",
+    )(ff, qkv, out, small)
 
 
 NT = (((1,), (1,)), ((), ()))
@@ -727,27 +1160,66 @@
     return pl.ds(pl.multiple_of(index * size, size), size)
 
 
-def attention_forward(all_rows, weights, slots, q_slots, q_local, low, high):
+def pair_blocks(slots_ref, pair, per_device):
+    core = lax.axis_index("ctx") % 2
+    pairs = per_device // 2
+    slot = (pair // pairs) * (2 * per_device) + core * per_device + 2 * (pair % pairs)
+    one, two = slots_ref[slot], slots_ref[slot + 1]
+    second = (one >= PROMPT // BLK).astype(jnp.int32)
+    return slot, second, jnp.minimum(one, two), jnp.maximum(one, two)
+
+
+def tile_tables(kind, step, slots_ref, lengths_ref, per_device):
+    lane = lax.broadcasted_iota(jnp.int32, (1, TILE), 1)
+    high = jnp.zeros((1, TILE), jnp.int32)
+    local = []
+    per_tile = TILE // BLK
+    for i in range(per_tile):
+        pair = step * per_tile + i
+        _, second, prompt, cont = pair_blocks(slots_ref, pair, per_device)
+        block = prompt if kind == 0 else cont
+        local.append(2 * pair + (second if kind == 0 else 1 - second))
+        high = jnp.where(lane >= i * BLK, (block - i) * BLK + lane, high)
+    low = jnp.zeros((1, TILE), jnp.int32)
+    if kind == 1:
+        start = PROMPT
+        for i in range(lengths_ref.shape[0]):
+            low = jnp.where(high >= start, start, low)
+            start = start + lengths_ref[i]
+    return local, low, high
+
+
+def attention_forward(all_rows, weights, slots, lengths):
     tokens, width = all_rows.shape
-    tiles = low.shape[0]
-    queries = tiles * TILE
+    queries = tokens // 2
+    tiles = queries // TILE
     blocks = tokens // BLK
+    per_device = blocks // (2 * CHIPS)
 
     def kernel(
-        slots_ref, q_slots_ref, q_local_ref, x_ref, w_ref, low_ref, high_ref,
-        att_ref, oT_ref, q_ref, k_ref, v_ref, lse_ref, xs, xq, vT, s_ref, p_ref,
+        slots_ref, lengths_ref, x_ref, w_ref,
+        att_ref, oT_ref, q_ref, k_ref, v_ref, lse_ref, slot_of, xs, xq, vT, s_ref, p_ref,
     ):
+        def place_slot(s, _):
+            slot_of[slots_ref[s]] = s
+            return 0
+
+        lax.fori_loop(0, blocks, place_slot, 0)
         def gather_block(b, _):
-            xs[aligned(b, BLK), :] = x_ref[aligned(slots_ref[b], BLK), :]
+            xs[aligned(b, BLK), :] = x_ref[aligned(slot_of[b], BLK), :]
             return 0
 
         lax.fori_loop(0, blocks, gather_block, 0)
 
-        def gather_query(b, _):
-            xq[aligned(b, BLK), :] = x_ref[aligned(q_slots_ref[b], BLK), :]
+        def gather_query(pair, _):
+            slot, second, _, _ = pair_blocks(slots_ref, pair, per_device)
+            xq[aligned(pair, BLK), :] = x_ref[aligned(slot + second, BLK), :]
+            xq[aligned(pair + queries // (2 * BLK), BLK), :] = x_ref[
+                aligned(slot + 1 - second, BLK), :
+            ]
             return 0
 
-        lax.fori_loop(0, queries // BLK, gather_query, 0)
+        lax.fori_loop(0, queries // (2 * BLK), gather_query, 0)
 
         def project_keys(i, _):
             rows = aligned(i, TILE)
@@ -774,8 +1246,7 @@
             def one_tile(step, _):
                 tile = kind * (tiles // 2) + step
                 q = q_ref[aligned(tile, TILE), :]
-                q_low = low_ref[pl.ds(tile, 1)][0]
-                q_high = high_ref[pl.ds(tile, 1)][0]
+                local, q_low, q_high = tile_tables(kind, step, slots_ref, lengths_ref, per_device)
                 for head in range(LOCAL_HEADS):
                     q_head = jnp.where(head_mask(TILE, head), q, jnp.zeros_like(q))
                     top = jnp.full((1, TILE), NEGATIVE, F32)
@@ -804,8 +1275,7 @@
                     lse_ref[tile, head] = top + jnp.log(total)
                 att = oT_ref[tile].T.astype(BF16)
                 for b in range(TILE // BLK):
-                    where = q_local_ref[tile * (TILE // BLK) + b]
-                    att_ref[aligned(where, BLK), :] = att[b * BLK : (b + 1) * BLK]
+                    att_ref[aligned(local[b], BLK), :] = att[b * BLK : (b + 1) * BLK]
                 return 0
 
             lax.fori_loop(0, tiles // 2, one_tile, 0)
@@ -820,9 +1290,10 @@
             jax.ShapeDtypeStruct((tokens, CHIP_COLS), BF16),
             jax.ShapeDtypeStruct((tiles, LOCAL_HEADS, 1, TILE), F32),
         ],
-        in_specs=[SM, SM, SM, VM, VM, VM, VM],
+        in_specs=[SM, SM, VM, VM],
         out_specs=[VM] * 6,
         scratch_shapes=[
+            pltpu.SMEM((blocks,), jnp.int32),
             pltpu.VMEM((tokens, width), BF16),
             pltpu.VMEM((queries, width), BF16),
             pltpu.VMEM((CHIP_COLS, tokens), BF16),
@@ -831,26 +1302,31 @@
         ],
         compiler_params=pltpu.CompilerParams(vmem_limit_bytes=VMEM_LIMIT),
         name="attention_forward",
-    )(slots, q_slots, q_local, all_rows, weights, low, high)
-
-
-def attention_backward(hidden_rows, w_out, saved, slots, q_local, low, high):
+    )(slots, lengths, all_rows, weights)
+
+
+def attention_backward(hidden_rows, w_out, saved, slots, lengths):
     oT, q, k, v, lse = saved
     queries, width = hidden_rows.shape
     tokens = k.shape[0]
-    tiles = low.shape[0]
+    tiles = queries // TILE
     blocks = tokens // BLK
+    per_device = blocks // (2 * CHIPS)
     wide = LOCAL_HEADS * TILE
 
     def kernel(
-        slots_ref, q_local_ref, h_ref, w_ref, oT_ref, q_ref, k_ref, v_ref, lse_ref, low_ref, high_ref,
+        slots_ref, lengths_ref, h_ref, w_ref, oT_ref, q_ref, k_ref, v_ref, lse_ref,
         dq_ref, dk_ref, dv_ref, hq, kT, doT, dqT, q_stack, do_stack, p_buf, ds_buf, dk_acc, dv_acc,
     ):
-        def gather_query(b, _):
-            hq[aligned(b, BLK), :] = h_ref[aligned(q_local_ref[b], BLK), :]
+        def gather_query(pair, _):
+            _, second, _, _ = pair_blocks(slots_ref, pair, per_device)
+            hq[aligned(pair, BLK), :] = h_ref[aligned(2 * pair + second, BLK), :]
+            hq[aligned(pair + queries // (2 * BLK), BLK), :] = h_ref[
+                aligned(2 * pair + 1 - second, BLK), :
+            ]
             return 0
 
-        lax.fori_loop(0, queries // BLK, gather_query, 0)
+        lax.fori_loop(0, queries // (2 * BLK), gather_query, 0)
 
         def transpose_keys(i, _):
             rows = aligned(i, TILE)
@@ -866,8 +1342,7 @@
             def one_tile(step, _):
                 tile = kind * (tiles // 2) + step
                 q_tile = q_ref[aligned(tile, TILE), :]
-                q_low = low_ref[pl.ds(tile, 1)][0]
-                q_high = high_ref[pl.ds(tile, 1)][0]
+                local, q_low, q_high = tile_tables(kind, step, slots_ref, lengths_ref, per_device)
                 wide_do = lax.dot_general(
                     w_ref[...], hq[aligned(tile, TILE), :], NT, preferred_element_type=F32
                 )
@@ -913,16 +1388,15 @@
                     dk_acc[rows, :] = dk
                 dq = dqT[...].T.astype(BF16)
                 for b in range(TILE // BLK):
-                    where = q_local_ref[tile * (TILE // BLK) + b]
-                    dq_ref[aligned(where, BLK), :] = dq[b * BLK : (b + 1) * BLK]
+                    dq_ref[aligned(local[b], BLK), :] = dq[b * BLK : (b + 1) * BLK]
                 return 0
 
             lax.fori_loop(0, tiles // 2, one_tile, 0)
 
-        def give_block(b, _):
-            where = aligned(slots_ref[b], BLK)
-            dk_ref[where, :] = dk_acc[aligned(b, BLK), :].astype(BF16)
-            dv_ref[where, :] = dv_acc[aligned(b, BLK), :].astype(BF16)
+        def give_block(slot, _):
+            block = aligned(slots_ref[slot], BLK)
+            dk_ref[aligned(slot, BLK), :] = dk_acc[block, :].astype(BF16)
+            dv_ref[aligned(slot, BLK), :] = dv_acc[block, :].astype(BF16)
             return 0
 
         lax.fori_loop(0, blocks, give_block, 0)
@@ -934,7 +1408,7 @@
             jax.ShapeDtypeStruct((tokens, CHIP_COLS), BF16),
             jax.ShapeDtypeStruct((tokens, CHIP_COLS), BF16),
         ],
-        in_specs=[SM, SM] + [VM] * 9,
+        in_specs=[SM, SM] + [VM] * 7,
         out_specs=[VM] * 3,
         scratch_shapes=[
             pltpu.VMEM((queries, width), BF16),
@@ -950,30 +1424,7 @@
         ],
         compiler_params=pltpu.CompilerParams(vmem_limit_bytes=VMEM_LIMIT),
         name="attention_backward",
-    )(slots, q_local, hidden_rows, w_out, oT, q, k, v, lse, low, high)
-
-
-def query_tables(slots_row, lengths_row, core):
-    blocks = slots_row.shape[0]
-    index = jnp.arange(blocks, dtype=jnp.int32)
-    slot_of = jnp.sum(
-        jnp.where(slots_row[None, :] == index[:, None], index[None, :], 0), axis=1, dtype=jnp.int32
-    )
-    per_device = blocks // (2 * CHIPS)
-    own = slots_row.reshape(CHIPS, 2, per_device)
-    own = lax.dynamic_index_in_dim(own, core, 1, keepdims=False).reshape(-1, 2)
-    pairs = own.shape[0]
-    swapped = (own[:, 0] >= PROMPT // BLK).astype(jnp.int32)
-    pair = jnp.arange(pairs, dtype=jnp.int32)
-    local = jnp.concatenate([2 * pair + swapped, 2 * pair + 1 - swapped])
-    block = jnp.concatenate([jnp.min(own, axis=1), jnp.max(own, axis=1)])
-    owner = local // per_device
-    slot = owner * (2 * per_device) + core * per_device + local % per_device
-    high = (block[:, None] * BLK + jnp.arange(BLK, dtype=jnp.int32)[None, :]).reshape(-1)
-    starts = segment_starts(lengths_row[None])[0]
-    low = jnp.max(jnp.where(starts[None, :] <= high[:, None], starts[None, :], 0), axis=1)
-    shape = (2 * pairs * BLK // TILE, 1, TILE)
-    return slot_of, slot, local, low.reshape(shape), high.reshape(shape)
+    )(slots, lengths, hidden_rows, w_out, oT, q, k, v, lse)
 
 
 def plane_shards(
@@ -981,58 +1432,62 @@
     norm_attn, w_query, w_key, w_value, w_out, norm_ffn, w_gate, w_up, w_down,
 ):
     depths = lax.axis_size("wsh")
-    ctx = lax.axis_index("ctx")
+    ctx, depth = lax.axis_index("ctx"), lax.axis_index("wsh")
     chip, core = ctx // 2, ctx % 2
     _, rows, _, width = states.shape
     shard = w_query.shape[0]
     half = shard // 2
     hidden_cols = w_gate.shape[1] // CHIPS
     group_len = block_slot.shape[1] * BLK
+    slots, lengths = block_slot[0], cont_lengths[0]
 
     def columns(weight):
-        return lax.dynamic_slice_in_dim(weight, chip * CHIP_COLS, CHIP_COLS, 1)
-
-    def core_half(weight):
-        return lax.dynamic_slice_in_dim(weight, core * half, half, 0)
-
-    qkv_piece = jnp.stack([columns(core_half(w)) for w in (w_query, w_key, w_value)])
+        return lax.dynamic_slice(weight, (core * half, chip * CHIP_COLS), (half, CHIP_COLS))
+
+    qkv_piece = jnp.stack([columns(w) for w in (w_query, w_key, w_value)])
+    out_half = lax.dynamic_slice_in_dim(w_out, core * half, half, 0)
     ff_split = hidden_cols // depths
 
     def ff_columns(weight):
-        piece = core_half(weight).reshape(half, depths, CHIPS, ff_split)
+        piece = lax.dynamic_slice_in_dim(weight, core * half, half, 0)
+        piece = piece.reshape(half, depths, CHIPS, ff_split)
         return lax.dynamic_index_in_dim(piece, chip, 2, keepdims=False).reshape(half, hidden_cols)
 
     down_rows = lax.dynamic_slice_in_dim(w_down, chip * ff_split + core * (ff_split // 2), ff_split // 2, 0)
-    gain_one = lax.all_gather(norm_attn, "wsh", axis=0, tiled=True).astype(F32)
-    gain_two = lax.all_gather(norm_ffn, "wsh", axis=0, tiled=True).astype(F32)
-    out_w = lax.all_gather(w_out, "wsh", axis=0, tiled=True)
-    out_w = lax.dynamic_slice_in_dim(out_w, chip * CHIP_COLS, CHIP_COLS, 0)
     ff_piece = lax.all_gather(
-        jnp.stack([ff_columns(w_gate), ff_columns(w_up), down_rows]), "wsh", axis=0, tiled=False
-    )
+        jnp.concatenate([ff_columns(w_gate), ff_columns(w_up), down_rows], axis=0),
+        "wsh", axis=0, tiled=True,
+    ).reshape(depths, 3, half, hidden_cols)
     valid_float = valid_mask.astype(F32)
-    valid_total = lax.psum(jnp.sum(valid_float), ("ctx", "wsh"))
-
-    slots, q_slots, q_local, low, high = query_tables(block_slot[0], cont_lengths[0], core)
+    count = jnp.sum(valid_float)
+
+    def own_columns(gain):
+        return lax.dynamic_update_slice_in_dim(jnp.zeros((width,), F32), gain.astype(F32), depth * shard, 0)
+
+    small = jnp.concatenate(
+        [
+            own_columns(norm_attn)[None],
+            own_columns(norm_ffn)[None],
+            jnp.full((1, width), count, F32),
+            jnp.zeros((5, width), F32),
+        ]
+    )
 
     inputs = states[0].astype(F32)
-    mixed = jnp.stack(
-        [predict[i, 0] * inputs[:, 0] + predict[i, 1] * inputs[:, 1] for i in range(2)], axis=1
-    )
-    active = mixed[:, 0]
-    normed, factor_one = rms_forward(active, gain_one)
-    all_rows, qkv = gather_inputs(normed.astype(BF16), qkv_piece, 1)
+    mixed = [predict[i, 0] * inputs[:, 0] + predict[i, 1] * inputs[:, 1] for i in range(2)]
+    active = mixed[0]
+    factor_one = lax.rsqrt(jnp.mean(active * active, axis=-1, keepdims=True) + EPSILON)
+    all_rows, qkv, out_w, small = gather_inputs(active * factor_one, small, qkv_piece, out_half, 1)
+    gain_one, gain_two, valid_total = small[0], small[1], small[2, 0]
     all_rows = all_rows.reshape(-1, width)
     qkv = qkv.reshape(3, width, CHIP_COLS)
-    attended, *saved = attention_forward(all_rows, qkv, slots, q_slots, q_local, low, high)
+    out_w = out_w.reshape(CHIP_COLS, width)
+    attended, *saved = attention_forward(all_rows, qkv, slots, lengths)
     part = jnp.dot(attended, out_w, preferred_element_type=F32).astype(BF16)
     hidden = active + scatter_plane(part.reshape(CHIPS, rows, width), 2)
     normed_two, factor_two = rms_forward(hidden, gain_two)
 
-    [ff] = share_cores([ff_piece], 3)
-    gate_w, up_w, down_w = (
-        jnp.swapaxes(ff[:, :, i], 0, 1).reshape(-1, ff.shape[-1]) for i in range(3)
-    )
+    gate_w, up_w, down_w = share_weights(ff_piece, 3).reshape(3, -1, hidden_cols)
     two_rows = gather_plane(normed_two.astype(BF16), 4).reshape(-1, width)
     gate = jnp.dot(two_rows, gate_w, preferred_element_type=F32)
     up = jnp.dot(two_rows, up_w, preferred_element_type=F32)
@@ -1043,14 +1498,14 @@
     part = jnp.dot(inner, down_w, preferred_element_type=F32).astype(BF16)
     result = hidden + scatter_plane(part.reshape(CHIPS, rows, width), 5)
 
-    difference = (result - active)[:, None]
-    out_states = mixed + correct[None, :, None] * difference
-    ratio = depths * group_len / valid_total
-    upstream = out_grad[0].astype(F32) + ratio * valid_float[0][:, None, None] * (
-        out_states - teacher[0].astype(F32)
-    )
-    correct_local = jnp.sum(upstream * difference, axis=(0, 2))
-    result_grad = correct[0] * upstream[:, 0] + correct[1] * upstream[:, 1]
+    difference = result - active
+    weight = (depths * group_len / valid_total) * valid_float[0][:, None]
+    outs = [mixed[i] + correct[i] * difference for i in range(2)]
+    upstream = [
+        out_grad[0, :, i].astype(F32) + weight * (outs[i] - teacher[0, :, i].astype(F32)) for i in range(2)
+    ]
+    correct_local = [jnp.sum(upstream[i] * difference) for i in range(2)]
+    result_grad = correct[0] * upstream[0] + correct[1] * upstream[1]
 
     grad_rows = gather_plane(result_grad.astype(BF16), 6).reshape(-1, width)
     inner_grad = lax.dot_general(grad_rows, down_w, NT, preferred_element_type=F32)
@@ -1075,17 +1530,18 @@
     def own_half(grad):
         return lax.dynamic_index_in_dim(grad, core, 1, keepdims=False)
 
-    ff_sum = jnp.stack(
+    ff_sum = jnp.concatenate(
         [own_half(g).astype(F32) + s.astype(F32) for g, s in zip(ff_grads, ff_swapped)], axis=1
     ).astype(BF16)
-    ff_sum = lax.psum_scatter(ff_sum, "wsh", scatter_dimension=0, tiled=False)
-    ff_all = lax.all_gather(ff_sum, "ctx", axis=0, tiled=False)
+    ff_sum = lax.psum_scatter(
+        ff_sum.reshape(depths * 3 * half, hidden_cols), "wsh", scatter_dimension=0, tiled=True
+    )
 
     hidden_norm_grad, gain_two_grad = rms_backward(hidden, factor_two, gain_two, normed_two_grad)
     hidden_grad = result_grad + hidden_norm_grad
     hidden_rows = gather_plane(hidden_grad.astype(BF16), 9).reshape(-1, width)
     out_w_part = outer(attended, hidden_rows)
-    dq, dk, dv = attention_backward(hidden_rows, out_w, saved, slots, q_local, low, high)
+    dq, dk, dv = attention_backward(hidden_rows, out_w, saved, slots, lengths)
     by_core = [g.reshape(CHIPS, 2, rows, CHIP_COLS) for g in (dk, dv)]
     swapped = swap_cores(by_core, 10)
     dk, dv = (
@@ -1097,60 +1553,50 @@
         + lax.dot_general(dk, qkv[1], NT, preferred_element_type=F32)
         + lax.dot_general(dv, qkv[2], NT, preferred_element_type=F32)
     )
-    normed_grad = scatter_plane(part.astype(BF16).reshape(CHIPS, rows, width), 11)
     own_rows = lax.dynamic_index_in_dim(
         all_rows.reshape(CHIPS, 2, rows, width), core, 1, keepdims=False
     ).reshape(-1, width)
-    qkv_grads = [outer(own_rows, g).reshape(depths, 2, half, CHIP_COLS) for g in (dq, dk, dv)]
-    qkv_swapped = swap_cores(qkv_grads, 12)
-    qkv_sum = jnp.stack(
-        [own_half(g).astype(F32) + s.astype(F32) for g, s in zip(qkv_grads, qkv_swapped)], axis=1
-    ).astype(BF16)
-    qkv_sum = lax.psum_scatter(qkv_sum, "wsh", scatter_dimension=0, tiled=False)
-    qkv_all = lax.all_gather(qkv_sum, "ctx", axis=0, tiled=False)
-
-    spread = jnp.where(
-        jnp.arange(CHIPS, dtype=jnp.int32)[:, None, None] == chip, out_w_part[None], jnp.zeros((), BF16)
-    )
-    out_w_grad = lax.psum(
-        lax.psum_scatter(spread, "wsh", scatter_dimension=0, tiled=False), "ctx"
-    ).astype(F32)
+    qkv_grads = jnp.concatenate(
+        [outer(own_rows, g).reshape(depths, 2, half, CHIP_COLS) for g in (dq, dk, dv)], axis=2
+    )
+    normed_grad, qkv_sum, out_sum = scatter_and_reduce(
+        part.astype(BF16).reshape(CHIPS, rows, width), qkv_grads, out_w_part.reshape(2, half, width), 11
+    )
 
     active_norm_grad, gain_one_grad = rms_backward(active, factor_one, gain_one, normed_grad)
     active_grad = hidden_grad + active_norm_grad - result_grad
-    mixed_grad = jnp.stack([upstream[:, 0] + active_grad, upstream[:, 1]], axis=1)
-    predict_local = jnp.stack(
-        [jnp.stack([jnp.sum(mixed_grad[:, i] * inputs[:, j]) for j in range(2)]) for i in range(2)]
-    )
+    mixed_grad = [upstream[0] + active_grad, upstream[1]]
+    predict_local = [jnp.sum(mixed_grad[i] * inputs[:, j]) for i in range(2) for j in range(2)]
     states_grad = jnp.stack(
-        [predict[0, j] * mixed_grad[:, 0] + predict[1, j] * mixed_grad[:, 1] for j in range(2)], axis=1
+        [predict[0, j] * mixed_grad[0] + predict[1, j] * mixed_grad[1] for j in range(2)], axis=1
     ).astype(BF16)
-    predict_grad, correct_grad, gain_one_grad, gain_two_grad = lax.psum(
-        (predict_local, correct_local, gain_one_grad, gain_two_grad), ("ctx", "wsh")
-    )
-    offset = lax.axis_index("wsh") * shard
+    scalars = jnp.stack(predict_local + correct_local)
+    small = jnp.concatenate(
+        [
+            gain_one_grad[None],
+            gain_two_grad[None],
+            jnp.pad(scalars, (0, width - scalars.shape[0]))[None],
+            jnp.zeros((5, width), F32),
+        ]
+    )
+    query_grad, key_grad, value_grad, out_w_grad, gate_out, up_out, down_out, small = finish_gradients(
+        ff_sum, qkv_sum, out_sum, small, 12
+    )
 
     def own_gain(grad):
-        return lax.dynamic_slice_in_dim(grad, offset, shard, 0)
-
-    def wide_rows(pieces, split):
-        pieces = pieces.reshape(CHIPS, 2, half, split, -1)
-        return jnp.transpose(pieces, (1, 2, 3, 0, 4)).reshape(shard, -1).astype(F32)
-
-    query_grad, key_grad, value_grad = (wide_rows(qkv_all[:, i], 1) for i in range(3))
-    gate_out, up_out = (wide_rows(ff_all[:, i], depths) for i in range(2))
-    down_out = ff_all[:, 2].reshape(-1, width).astype(F32)
+        return lax.dynamic_slice_in_dim(grad, depth * shard, shard, 0)
+
     return (
-        out_states.astype(BF16)[None],
+        jnp.stack(outs, axis=1).astype(BF16)[None],
         states_grad[None],
-        predict_grad,
-        correct_grad,
-        own_gain(gain_one_grad),
+        small[2, 0:4].reshape(2, 2),
+        small[2, 4:6],
+        own_gain(small[0]),
         query_grad,
         key_grad,
         value_grad,
         out_w_grad,
-        own_gain(gain_two_grad),
+        own_gain(small[1]),
         gate_out,
         up_out,
         down_out,
@@ -1161,6 +1607,7 @@
     ctx, depths = mesh.shape["ctx"], mesh.shape["wsh"]
     return (
         ctx == 2 * CHIPS
+        and depths == CHIPS
         and states.shape[0] == depths
         and block_slot.shape[1] * BLK == 2 * PROMPT
         and states.shape[1] == 2 * PROMPT

time: 655 us -> 489 us (0.75)
  blocking collectives: 109 us -> 0 us
  waiting for transfers between devices: 99.5 us -> 0.06 us
  Pallas kernels: 241 us -> 334 us
  local copies, waits for them, and re-layouts: 84.6 us -> 56 us
  other arithmetic: 54.6 us -> 38 us
    pallas_call x2 -> x4, Pallas kernels: 76.6 us -> 183 us  [the longest x1 56.9 us: share_weights(): pl.pallas_call(kernel, out_shape=jax.ShapeDtypeStruct((parts, depths, 2,...]
    unnamed x7 -> x2, waiting for transfers between devices: 98.7 us -> 0.03 us
    psum x2 -> x0, blocking collectives: 88.5 us -> none  [the longest x1 46.6 us: plane_shards(): valid_total = lax.psum(jnp.sum(valid_float), ('ctx', 'wsh'))]
    convert_element_type x12 -> x0, local copies, waits for them, and re-layouts: 34.9 us -> none  [wide_rows(): return jnp.transpose(pieces, (1, 2, 3, 0, 4)).reshape(shard, -1).astype(F32)]
    all_gather x1 -> x0, blocking collectives: 13.5 us -> none  [plane_shards(): qkv_all = lax.all_gather(qkv_sum, 'ctx', axis=0, tiled=False)]
    pallas_call x4 -> x3, Pallas kernels: 69.4 us -> 58 us  [scatter_plane(): pl.pallas_call(kernel, out_shape=jax.ShapeDtypeStruct((rows, width), F32)...]
    another operation x15 -> x7, other arithmetic: 13.8 us -> 5.27 us  [the longest x2 2.68 us: plane_shards(): jnp.stack([predict[0, j] * mixed_grad[0] + predict[1, j] * mixed_grad[1]...]
    unnamed x1 -> x0, blocking collectives: 7.28 us -> none
  transfers between devices with their start and end apart: 6 -> 2, of which waited for: 2 -> 0; matrix products, arithmetic and copies ran while one was open for 13% -> 12% of each run, Pallas kernels for 15% -> 30%
where the time goes in v2:
time: 489 us; the launch traced here: 483 us
  Pallas kernels  334 us (68%)
  local copies, waits for them, and re-layouts  56 us (11%)
  matrix products  38.9 us (8%)
  other arithmetic  38 us (8%)
  between operations  15.8 us (3%)
    pallas_call x3, Pallas kernels, scatter_plane(): pl.pallas_call(kernel, out_shape=jax.ShapeDtypeStruct((rows, width), F32)...  58 us
    pallas_call x1, Pallas kernels, share_weights(): pl.pallas_call(kernel, out_shape=jax.ShapeDtypeStruct((parts, depths, 2,...  56.9 us
    pallas_call x1, Pallas kernels, gather_inputs(): pl.pallas_call(kernel, out_shape=[jax.ShapeDtypeStruct((lax.axis_size('ct...  45.5 us
    pallas_call x3, Pallas kernels, gather_plane(): pl.pallas_call(kernel, out_shape=jax.ShapeDtypeStruct((CHIPS,) + block.sh...  41.9 us
    pallas_call x1, Pallas kernels, finish_gradients(): pl.pallas_call(kernel, out_shape=[square, square, square, square, jax.Sha...  41.3 us
    pallas_call x1, Pallas kernels, scatter_and_reduce(): pl.pallas_call(kernel, out_shape=[jax.ShapeDtypeStruct((rows, width), F32...  39.1 us
    pallas_call x1, Pallas kernels, attention_backward(): pl.pallas_call(kernel, out_shape=[jax.ShapeDtypeStruct((queries, CHIP_COL...  20.9 us
    pallas_call x1, Pallas kernels, attention_forward(): pl.pallas_call(kernel, out_shape=[jax.ShapeDtypeStruct((queries, CHIP_COL...  20.5 us
  transfers between devices with their start and end apart: 2, of which 0 were waited for; matrix products, arithmetic and copies ran while one was open for 12% of the time, Pallas kernels for 30%

profile of v2, /device:TPU:9, one launch (start us, length us, event | category | flops | bytes accessed | tf_op | source)
XLA Modules:
  0.0 482.9 jit_solution(12359622726608325105)
XLA Ops:
  24.1 45.5 %gather_inputs.1 = (bf16[8,256,768]{2,1,0:T(8,128)(2,1)}, bf16[3,4,2,96,192]{4,3,2,1,0:T(8,128)(2,1)}, bf16[2,96,768]{2,1,0:T(8,128)(2,1)}, f32[8,768]{1,0:T(8,128)}) custom-call(f32[256,768]{1,0:T(8,128)} %broadcast_multiply_fusion.pre_ref, f32[8,768]{1,0:T(8,128)} %maximum_maximum_fusion.small_ref, bf16[3,96,192]{2,1,0:T(8,128)(2,1)} %pad_maximum_fusion.5.w_ref, ...), custom_call_target="tpu_custom_call" | custom-call | tf_op jit(solution)/shard_map/gather_inputs/pallas_call | solution.py:759
  70.8 20.5 %attention_forward.1 = (bf16[1024,192]{1,0:T(8,128)(2,1)}, f32[4,192,256]{2,1,0:T(8,128)}, bf16[1024,192]{1,0:T(8,128)(2,1)}, bf16[2048,192]{1,0:T(8,128)(2,1)},...) custom-call(s32[32]{0:T(128)} %bitcast.224, s32[4]{0:T(128)} %bitcast.226, bf16[2048,768]{1,0:T(8,128)(2,1)} %bitcast.174, ...), custom_call_target="tpu_custom_call" | custom-call | tf_op jit(solution)/shard_map/attention_forward/pallas_call | solution.py:1283
  91.4 2.8 convolution_convert_fusion.1
  94.1 24.8 %scatter_plane.3 = f32[256,768]{1,0:T(8,128)} custom-call(bf16[4,256,768]{2,1,0:T(8,128)(2,1)} %bitcast.176), custom_call_target="tpu_custom_call" | custom-call | tf_op jit(solution)/shard_map/scatter_plane/pallas_call | solution.py:542
  122.0 14.1 %gather_plane.3 = bf16[4,256,768]{2,1,0:T(8,128)(2,1)} custom-call(bf16[256,768]{1,0:T(8,128)(2,1)} %multiply_convert_fusion.2.x_ref), custom_call_target="tpu_custom_call" | custom-call | tf_op jit(solution)/shard_map/gather_plane/pallas_call | solution.py:492
  137.4 2.7 constant_dynamic-slice_fusion.2
  141.8 3.7 fusion.24
  145.5 56.9 %share_weights.1 = bf16[3,4,2,96,768]{4,3,2,1,0:T(8,128)(2,1)} custom-call(bf16[4,3,96,768]{3,2,1,0:T(8,128)(2,1)} %bitcast.195), custom_call_target="tpu_custom_call" | custom-call | tf_op jit(solution)/shard_map/share_weights/pallas_call | solution.py:810
  202.5 2.4 fusion.22
  206.4 3.4 multiply_convert_fusion.1
  209.8 2.5 convolution_convert_fusion
  212.4 17.5 %scatter_plane.4 = f32[256,768]{1,0:T(8,128)} custom-call(bf16[4,256,768]{2,1,0:T(8,128)(2,1)} %bitcast.199), custom_call_target="tpu_custom_call" | custom-call | tf_op jit(solution)/shard_map/scatter_plane/pallas_call | solution.py:542
  229.9 6.5 %fusion.18 = (bf16[256,768]{1,0:T(8,128)(2,1)}, f32[256,768]{1,0:T(8,128)}, f32[256,768]{1,0:T(8,128)}, bf16[256,768]{1,0:T(8,128)(2,1)}, f32[256,768]{1,0:T(8,128)}) fusion(f32[]{:T(128)} %bitcast.27, f32[]{:T(128)} %bitcast.6, bf16[1,256,1,768]{3,2,1,0:T(2,128)(2,1)} %get-tuple-element.167, f32[256,768]{1,0:T(8,128)S(1)} %get-tuple-element.137, ...), kind=kLoop, calls=%fused_computation.81 | loop fusion | flops 4718592 | bytes 8651792 | tf_op jit(solution)/shard_map/convert_element_type | solution.py:1510
  236.4 14.5 %gather_plane.4 = bf16[4,256,768]{2,1,0:T(8,128)(2,1)} custom-call(bf16[256,768]{1,0:T(8,128)(2,1)} %get-tuple-element.129.x_ref), custom_call_target="tpu_custom_call" | custom-call | tf_op jit(solution)/shard_map/gather_plane/pallas_call | solution.py:492
  250.9 4.5 convolution_convert_fusion.2
  255.4 5.9 %multiply_convert_fusion = (bf16[1024,768]{1,0:T(8,128)(2,1)S(1)}, bf16[1024,768]{1,0:T(8,128)(2,1)S(1)}) fusion(f32[1024,768]{1,0:T(8,128)S(1)} %copy-done.55, f32[1024,768]{1,0:T(8,128)} %get-tuple-element.162, bf16[1024,768]{1,0:T(8,128)(2,1)S(1)} %bitcast.211, bf16[768,768]{1,0:T(8,128)(2,1)S(1)} %bitcast.221), kind=kOutput, calls=%fused_computation.11 | convolution fusion | flops 1226833920 | bytes 12189696 | tf_op jit(solution)/shard_map/dot_general | solution.py:1511
  261.3 2.5 convolution_convert_fusion.4
  263.8 1.4 fusion.30
  265.2 2.5 convolution_convert_fusion.3
  267.7 2.6 add_convert_fusion.1
  270.3 15.7 %scatter_plane.5 = f32[256,768]{1,0:T(8,128)} custom-call(bf16[4,256,768]{2,1,0:T(8,128)(2,1)} %bitcast.198), custom_call_target="tpu_custom_call" | custom-call | tf_op jit(solution)/shard_map/scatter_plane/pallas_call | solution.py:542
  286.0 1.5 multiply_reduce_fusion.6
  288.1 3.5 fusion.19.x_ref
  291.6 13.3 %gather_plane.5 = bf16[4,256,768]{2,1,0:T(8,128)(2,1)} custom-call(bf16[256,768]{1,0:T(8,128)(2,1)} %fusion.19.x_ref), custom_call_target="tpu_custom_call" | custom-call | tf_op jit(solution)/shard_map/gather_plane/pallas_call | solution.py:492
  304.9 20.9 %attention_backward.1 = (bf16[1024,192]{1,0:T(8,128)(2,1)}, bf16[2048,192]{1,0:T(8,128)(2,1)}, bf16[2048,192]{1,0:T(8,128)(2,1)}) custom-call(s32[32]{0:T(128)} %bitcast.225, s32[4]{0:T(128)} %bitcast.227, bf16[1024,768]{1,0:T(8,128)(2,1)} %bitcast.177, bf16[192,768]{1,0:T(8,128)(2,1)} %bitcast.214, f32[4,192,256]{2,1,0:T(8,128)} %get-tuple-element.47.oT_ref, ...), custom_call_target="tpu_custom_call" | custom-call | tf_op jit(solution)/shard_map/attention_backward/pallas_call | solution.py:1404
  325.9 5.6 %swap_cores.2 = (bf16[4,256,192]{2,1,0:T(8,128)(2,1)}, bf16[4,256,192]{2,1,0:T(8,128)(2,1)}) custom-call(bf16[4,2,256,192]{3,2,1,0:T(8,128)(2,1)} %bitcast.189, bf16[4,2,256,192]{3,2,1,0:T(8,128)(2,1)} %bitcast.187), custom_call_target="tpu_custom_call" | custom-call | tf_op jit(solution)/shard_map/swap_cores/pallas_call | solution.py:575
  331.5 1.4 fusion.11
  335.6 4.1 swap_cores.3
  339.8 1.5 fusion.7
  343.5 2.1 fusion.10
  346.2 1.9 copy.59
  348.1 1.9 copy.60
  350.0 2.7 convolution_convert_fusion.6
  352.8 1.9 copy.61
  354.7 2.6 pad_maximum_fusion.1.q_ref
  360.7 1.8 add_convert_fusion
  362.5 39.1 %scatter_and_reduce.1 = (f32[256,768]{1,0:T(8,128)}, bf16[288,192]{1,0:T(8,128)(2,1)}, bf16[96,768]{1,0:T(8,128)(2,1)}) custom-call(bf16[4,256,768]{2,1,0:T(8,128)(2,1)} %bitcast.179, bf16[4,2,288,192]{3,2,1,0:T(8,128)(2,1)} %pad_maximum_fusion.1.q_ref, bf16[2,96,768]{2,1,0:T(8,128)(2,1)} %bitcast.222), custom_call_target="tpu_custom_call" | custom-call | tf_op jit(solution)/shard_map/scatter_and_reduce/pallas_call | solution.py:914
  401.7 1.5 multiply_reduce_fusion.7
  403.2 4.8 multiply_reduce_fusion
  408.0 2.6 fusion.16
  410.7 1.7 copy.65
  412.4 4.0 stack.67
  416.5 1.7 copy.64
  418.9 41.3 %finish_gradients.1 = (f32[192,768]{1,0:T(8,128)}, f32[192,768]{1,0:T(8,128)}, f32[192,768]{1,0:T(8,128)}, f32[192,768]{1,0:T(8,128)}, f32[192,3072]{1,0:T(8,128...) custom-call(bf16[288,768]{1,0:T(8,128)(2,1)} %reduce-scatter.2.cloned.1.call-done.f_ref, ...), custom_call_target="tpu_custom_call" | custom-call | tf_op jit(solution)/shard_map/finish_gradients/pallas_call | solution.py:1109
  464.9 2.0 copy.99
  469.4 1.4 copy.103
  471.9 1.4 copy.104
  474.4 1.4 copy.105
  (184 shorter events, 44.5 us)
Async XLA Ops:
  7.2 6.5 %copy-start = (bf16[768,768]{1,0:T(8,128)(2,1)S(1)}, bf16[768,768]{1,0:T(8,128)(2,1)}, u32[]{:S(2)}) copy-start(bf16[768,768]{1,0:T(8,128)(2,1)} %param.33) | copy-start | bytes 3538948
  7.2 138.3 %all-gather.2.cloned.1.call-start = ((), (), s32[]{:S(2)}) async-start(), calls=%async_computation.1 | async-start | bytes 2211840 | tf_op jit(solution)/shard_map/all_gather | solution.py:1457
  12.1 2.7 copy-start.51
  12.1 4.1 copy-start.52
  12.1 4.1 copy-start.53
  12.1 4.1 copy-start.47
  12.1 5.4 %copy-start.32 = (bf16[1,256,2,768]{3,2,1,0:T(2,128)(2,1)S(1)}, bf16[1,256,2,768]{3,2,1,0:T(2,128)(2,1)}, u32[]{:S(2)}) copy-start(bf16[1,256,2,768]{3,2,1,0:T(2,128)(2,1)} %param.17) | copy-start | bytes 2359300
  13.5 3.4 copy-start.41
  14.5 404.3 %reduce-scatter.2.cloned.1.call-start = ((), (), s32[]{:S(2)}) async-start(), calls=%async_computation.2 | async-start | bytes 2211840 | tf_op jit(solution)/shard_map/reduce_scatter | solution.py:1536
  16.2 7.2 %copy-start.48 = (f32[8]{0:T(128)}, f32[8]{0:T(128)S(1)}, u32[]{:S(2)}) copy-start(f32[8]{0:T(128)S(1)} %pad.28.clone) | copy-start | bytes 100
  19.1 50.6 %copy-start.42 = (f32[256]{0:T(256)}, f32[256]{0:T(256)S(1)}, u32[]{:S(2)}) copy-start(f32[256]{0:T(256)S(1)} %add_rsqrt_fusion.1) | copy-start | bytes 3076
  70.8 20.5 %copy-start.25 = (bf16[2,96,768]{2,1,0:T(8,128)(2,1)S(1)}, bf16[2,96,768]{2,1,0:T(8,128)(2,1)}, u32[]{:S(2)}) copy-start(bf16[2,96,768]{2,1,0:T(8,128)(2,1)} %get-tuple-element.45) | copy-start | bytes 884740
  121.1 15.7 %copy-start.50 = (f32[2]{0:T(128)S(1)}, f32[2]{0:T(128)}, u32[]{:S(2)}) copy-start(f32[2]{0:T(128)} %param.24) | copy-start | bytes 28
  137.4 2.8 copy-start.7
  140.1 1.7 copy-start.9
  202.5 2.5 copy-start.20
  204.9 4.9 %copy-start.30 = (bf16[1,4,2,96,768]{4,3,2,1,0:T(8,128)(2,1)}, bf16[1,4,2,96,768]{4,3,2,1,0:T(8,128)(2,1)S(1)}, u32[]{:S(2)}) copy-start(bf16[1,4,2,96,768]{4,3,2,1,0:T(8,128)(2,1)S(1)} %get-tuple-element.140) | copy-start | bytes 3538948
  206.3 3.5 copy-start.54
  209.8 2.6 copy-start.56
  250.9 4.5 copy-start.22
  250.9 4.5 copy-start.31
  250.9 4.5 copy-start.55
  255.4 5.9 %copy-start.21 = (bf16[4,256,768]{2,1,0:T(8,128)(2,1)S(1)}, bf16[4,256,768]{2,1,0:T(8,128)(2,1)}, u32[]{:S(2)}) copy-start(bf16[4,256,768]{2,1,0:T(8,128)(2,1)} %gather_plane.3) | copy-start | bytes 4718596
  261.3 2.5 copy-start.29
  265.2 2.5 copy-start.27
  286.0 2.1 copy-start.2
  286.0 2.1 copy-start.4
  325.9 7.0 %copy-start.39 = (bf16[1024,192]{1,0:T(8,128)(2,1)S(1)}, bf16[1024,192]{1,0:T(8,128)(2,1)}, u32[]{:S(2)}) copy-start(bf16[1024,192]{1,0:T(8,128)(2,1)} %get-tuple-element.52) | copy-start | bytes 1179652
  331.4 1.7 copy-start.19
  339.7 1.6 copy-start.10
  339.7 1.8 copy-start.37
  339.7 2.1 copy-start.11
  339.7 2.3 copy-start.36
  354.7 2.6 copy-start.6
  354.7 2.6 copy-start.38
  362.5 39.1 %copy-start.43 = (f32[256]{0:T(256)S(1)}, f32[256]{0:T(256)}, u32[]{:S(2)}) copy-start(f32[256]{0:T(256)} %copy-done.42) | copy-start | bytes 3076
  362.5 40.6 %copy-start.46 = (f32[256]{0:T(256)S(1)}, f32[256]{0:T(256)}, u32[]{:S(2)}) copy-start(f32[256]{0:T(256)} %copy-done.45) | copy-start | bytes 3076
  401.6 1.6 copy-start.5
  410.6 5.8 %copy-start.18 = (bf16[256,768]{1,0:T(8,128)(2,1)S(1)}, bf16[256,768]{1,0:T(8,128)(2,1)}, u32[]{:S(2)}) copy-start(bf16[256,768]{1,0:T(8,128)(2,1)} %get-tuple-element.132) | copy-start | bytes 1179652
  416.4 1.8 copy-start.44
  416.4 1.8 copy-start.49
  460.1 6.8 %copy-start.35 = (f32[192,768]{1,0:T(8,128)S(1)}, f32[192,768]{1,0:T(8,128)}, u32[]{:S(2)}) copy-start(f32[192,768]{1,0:T(8,128)} %get-tuple-element.193) | copy-start | bytes 1769476
  460.1 7.6 %copy-start.34 = (f32[192,768]{1,0:T(8,128)S(1)}, f32[192,768]{1,0:T(8,128)}, u32[]{:S(2)}) copy-start(f32[192,768]{1,0:T(8,128)} %get-tuple-element.194) | copy-start | bytes 1769476
  464.9 3.6 copy-start.33
  466.9 2.5 copy-start.14
  469.4 2.5 copy-start.13
  471.9 2.5 copy-start.12
  471.9 3.9 copy-start.1
  (11 other events, 13.6 us)
Sparse Core Ops, SparseCore 0:
  14.6 56.0 all-gather.1
  343.6 51.0 reduce-scatter.1

commit v3 on v0

--- a/solution.py
+++ b/solution.py
@@ -1,8 +1,11 @@
+import functools
 import math
 
 import jax
 import jax.numpy as jnp
 from jax import lax
+from jax.experimental import pallas as pl
+from jax.experimental.pallas import tpu as pltpu
 from jax.sharding import PartitionSpec as P
 
 HEADS = 12
@@ -28,11 +31,18 @@
     return (factor * weighted - tensor * factor * factor * factor * middle, gain_grad)
 
 
+def segment_starts(cont_lengths):
+    count = cont_lengths.shape[1]
+    index = jnp.arange(count, dtype=jnp.int32)
+    before = index[:, None] < index[None, :]
+    return PROMPT + jnp.sum(jnp.where(before[None], cont_lengths[:, :, None], 0), axis=1)
+
+
 def token_places(block_slot, cont_lengths):
     groups, blocks = block_slot.shape
     offsets = jnp.arange(BLK, dtype=jnp.int32)
     places = (block_slot[:, :, None] * BLK + offsets[None, None, :]).reshape(groups, blocks * BLK)
-    starts = PROMPT + jnp.cumsum(cont_lengths, axis=1) - cont_lengths
+    starts = segment_starts(cont_lengths)
     segments = jnp.sum((places[:, :, None] >= starts[:, None, :]).astype(jnp.int32), axis=2)
     return (places, segments)
 
@@ -95,7 +105,7 @@
     return (probability.astype(jnp.bfloat16), score_grad)
 
 
-def shards(
+def general_shards(
     states,
     block_slot,
     cont_lengths,
@@ -397,43 +407,1477 @@
     return (new_states, states_grad, predict_grad, correct_grad) + tuple(totals)
 
 
+MESH = pl.DeviceIdType.MESH
+F32 = jnp.float32
+BF16 = jnp.bfloat16
+CHIPS = 4
+VMEM_LIMIT = 60 * 2**20
+DMA = pltpu.SemaphoreType.DMA
+
+
+def place_on_mesh():
+    ctx = lax.axis_index("ctx")
+    depth = lax.axis_index("wsh")
+    chip = ctx // 2
+    core = ctx % 2
+    chip_x = chip + 1 - 2 * (chip % 2)
+    chip_y = chip + 2 - 4 * (chip // 2)
+    return depth, chip, core, chip_x, chip_y, 3 - chip
+
+
+def signal_and_wait(devices):
+    barrier = pltpu.get_barrier_semaphore()
+    for device in devices:
+        pl.semaphore_signal(barrier, inc=1, device_id=device, device_id_type=MESH)
+    pl.semaphore_wait(barrier, len(devices))
+
+
+def remote(src, dst, send, recv, index, device):
+    return pltpu.make_async_remote_copy(
+        src_ref=src,
+        dst_ref=dst,
+        send_sem=send.at[index],
+        recv_sem=recv.at[index],
+        device_id=device,
+        device_id_type=MESH,
+    )
+
+
+def comm_params(collective_id):
+    return pltpu.CompilerParams(
+        collective_id=collective_id, has_side_effects=True, vmem_limit_bytes=VMEM_LIMIT
+    )
+
+
+ANY = pl.BlockSpec(memory_space=pl.ANY)
+VM = pl.BlockSpec(memory_space=pltpu.VMEM)
+SM = pl.BlockSpec(memory_space=pltpu.SMEM)
+
+
+def ring_sends(own, out, slot_of, chip, core, depth, chip_x, chip_y, send, recv):
+    half = own.shape[0] // 2
+    top, low = pl.ds(0, half), pl.ds(half, half)
+    dev_x, dev_y = (2 * chip_x + core, depth), (2 * chip_y + core, depth)
+    here = slot_of(chip)
+    return [
+        remote(own.at[top], out.at[here, top], send, recv, 0, dev_x),
+        remote(own.at[low], out.at[here, low], send, recv, 1, dev_y),
+        remote(own.at[low], out.at[here, low], send, recv, 2, dev_x),
+        remote(own.at[top], out.at[here, top], send, recv, 3, dev_y),
+        remote(out.at[slot_of(chip_x), top], out.at[slot_of(chip_x), top], send, recv, 4, dev_y),
+        remote(out.at[slot_of(chip_y), low], out.at[slot_of(chip_y), low], send, recv, 5, dev_x),
+    ]
+
+
+NT = (((1,), (1,)), ((), ()))
+TILE = 256
+LOCAL_HEADS = HEADS // CHIPS
+CHIP_COLS = LOCAL_HEADS * HD
+
+
+def head_mask(rows, head):
+    lane = lax.broadcasted_iota(jnp.int32, (rows, CHIP_COLS), 1)
+    return (lane >= head * HD) & (lane < (head + 1) * HD)
+
+
+def spread_rows(pieces, target):
+    depths, cores, rows, _ = pieces.shape
+    half = rows // target.shape[0]
+    for i in range(target.shape[0]):
+        for z in range(depths):
+            for c in range(cores):
+                at = (z * cores + c) * half
+                target[i, at : at + half, :] = pieces[z, c, i * half : (i + 1) * half, :]
+
+
+def aligned(index, size):
+    return pl.ds(pl.multiple_of(index * size, size), size)
+
+
+def pair_blocks(slots_ref, pair, per_device):
+    core = lax.axis_index("ctx") % 2
+    pairs = per_device // 2
+    slot = (pair // pairs) * (2 * per_device) + core * per_device + 2 * (pair % pairs)
+    one, two = slots_ref[slot], slots_ref[slot + 1]
+    second = (one >= PROMPT // BLK).astype(jnp.int32)
+    return slot, second, jnp.minimum(one, two), jnp.maximum(one, two)
+
+
+def tile_tables(kind, step, slots_ref, lengths_ref, per_device):
+    lane = lax.broadcasted_iota(jnp.int32, (1, TILE), 1)
+    high = jnp.zeros((1, TILE), jnp.int32)
+    local = []
+    per_tile = TILE // BLK
+    for i in range(per_tile):
+        pair = step * per_tile + i
+        _, second, prompt, cont = pair_blocks(slots_ref, pair, per_device)
+        block = prompt if kind == 0 else cont
+        local.append(2 * pair + (second if kind == 0 else 1 - second))
+        high = jnp.where(lane >= i * BLK, (block - i) * BLK + lane, high)
+    low = jnp.zeros((1, TILE), jnp.int32)
+    if kind == 1:
+        start = PROMPT
+        for i in range(lengths_ref.shape[0]):
+            low = jnp.where(high >= start, start, low)
+            start = start + lengths_ref[i]
+    return local, low, high
+
+
+def attention_forward(all_rows, weights, slots, lengths):
+    tokens, width = all_rows.shape
+    queries = tokens // 2
+    tiles = queries // TILE
+    blocks = tokens // BLK
+    per_device = blocks // (2 * CHIPS)
+
+    def kernel(
+        slots_ref, lengths_ref, x_ref, w_ref,
+        att_ref, oT_ref, q_ref, k_ref, v_ref, lse_ref, slot_of, w_all, xs, xq, vT, s_ref, p_ref,
+    ):
+        def place_slot(s, _):
+            slot_of[slots_ref[s]] = s
+            return 0
+
+        lax.fori_loop(0, blocks, place_slot, 0)
+        spread_rows(w_ref, w_all)
+        def gather_block(b, _):
+            xs[aligned(b, BLK), :] = x_ref[aligned(slot_of[b], BLK), :]
+            return 0
+
+        lax.fori_loop(0, blocks, gather_block, 0)
+
+        def gather_query(pair, _):
+            slot, second, _, _ = pair_blocks(slots_ref, pair, per_device)
+            xq[aligned(pair, BLK), :] = x_ref[aligned(slot + second, BLK), :]
+            xq[aligned(pair + queries // (2 * BLK), BLK), :] = x_ref[
+                aligned(slot + 1 - second, BLK), :
+            ]
+            return 0
+
+        lax.fori_loop(0, queries // (2 * BLK), gather_query, 0)
+
+        def project_keys(i, _):
+            rows = aligned(i, TILE)
+            x = xs[rows, :]
+            k_ref[rows, :] = jnp.dot(x, w_all[1], preferred_element_type=F32).astype(BF16)
+            v = jnp.dot(x, w_all[2], preferred_element_type=F32).astype(BF16)
+            v_ref[rows, :] = v
+            vT[:, rows] = v.T
+            return 0
+
+        lax.fori_loop(0, tokens // TILE, project_keys, 0)
+
+        def project_queries(i, _):
+            rows = aligned(i, TILE)
+            q_ref[rows, :] = jnp.dot(xq[rows, :], w_all[0], preferred_element_type=F32).astype(BF16)
+            return 0
+
+        lax.fori_loop(0, tiles, project_queries, 0)
+
+        for kind in range(2):
+            key_tiles = (PROMPT if kind == 0 else tokens) // TILE
+            first_masked = 0 if kind == 0 else PROMPT // TILE
+
+            def one_tile(step, _):
+                tile = kind * (tiles // 2) + step
+                q = q_ref[aligned(tile, TILE), :]
+                local, q_low, q_high = tile_tables(kind, step, slots_ref, lengths_ref, per_device)
+                for head in range(LOCAL_HEADS):
+                    q_head = jnp.where(head_mask(TILE, head), q, jnp.zeros_like(q))
+                    top = jnp.full((1, TILE), NEGATIVE, F32)
+                    for k_tile in range(key_tiles):
+                        rows = pl.ds(k_tile * TILE, TILE)
+                        s = lax.dot_general(k_ref[rows, :], q_head, NT, preferred_element_type=F32)
+                        if k_tile >= first_masked:
+                            place = lax.broadcasted_iota(jnp.int32, (TILE, TILE), 0) + k_tile * TILE
+                            seen = (place >= q_low) & (place <= q_high)
+                            s = jnp.where(seen, s, NEGATIVE)
+                        s_ref[rows, :] = s
+                        top = jnp.maximum(top, jnp.max(s, axis=0, keepdims=True))
+                    total = jnp.zeros((1, TILE), F32)
+                    for k_tile in range(key_tiles):
+                        rows = pl.ds(k_tile * TILE, TILE)
+                        p = jnp.exp(s_ref[rows, :] - top)
+                        total = total + jnp.sum(p, axis=0, keepdims=True)
+                        p_ref[rows, :] = p.astype(BF16)
+                    keys = key_tiles * TILE
+                    out = jnp.dot(
+                        vT[head * HD : (head + 1) * HD, :keys],
+                        p_ref[:keys, :],
+                        preferred_element_type=F32,
+                    )
+                    oT_ref[tile, head * HD : (head + 1) * HD, :] = out / total
+                    lse_ref[tile, head] = top + jnp.log(total)
+                att = oT_ref[tile].T.astype(BF16)
+                for b in range(TILE // BLK):
+                    att_ref[aligned(local[b], BLK), :] = att[b * BLK : (b + 1) * BLK]
+                return 0
+
+            lax.fori_loop(0, tiles // 2, one_tile, 0)
+
+    return pl.pallas_call(
+        kernel,
+        out_shape=[
+            jax.ShapeDtypeStruct((queries, CHIP_COLS), BF16),
+            jax.ShapeDtypeStruct((tiles, CHIP_COLS, TILE), F32),
+            jax.ShapeDtypeStruct((queries, CHIP_COLS), BF16),
+            jax.ShapeDtypeStruct((tokens, CHIP_COLS), BF16),
+            jax.ShapeDtypeStruct((tokens, CHIP_COLS), BF16),
+            jax.ShapeDtypeStruct((tiles, LOCAL_HEADS, 1, TILE), F32),
+        ],
+        in_specs=[SM, SM, VM, VM],
+        out_specs=[VM] * 6,
+        scratch_shapes=[
+            pltpu.SMEM((blocks,), jnp.int32),
+            pltpu.VMEM((3, width, CHIP_COLS), BF16),
+            pltpu.VMEM((tokens, width), BF16),
+            pltpu.VMEM((queries, width), BF16),
+            pltpu.VMEM((CHIP_COLS, tokens), BF16),
+            pltpu.VMEM((tokens, TILE), F32),
+            pltpu.VMEM((tokens, TILE), BF16),
+        ],
+        compiler_params=pltpu.CompilerParams(vmem_limit_bytes=VMEM_LIMIT),
+        cost_estimate=pl.CostEstimate(
+            flops=8 * queries * tokens * CHIP_COLS, bytes_accessed=12 * tokens * width, transcendentals=queries * tokens
+        ),
+        name="attention_forward",
+    )(slots, lengths, all_rows, weights)
+
+
+def attention_backward(att_grad, saved, slots, lengths):
+    oT, q, k, v, lse = saved
+    queries = att_grad.shape[0]
+    tokens = k.shape[0]
+    tiles = queries // TILE
+    blocks = tokens // BLK
+    per_device = blocks // (2 * CHIPS)
+    wide = LOCAL_HEADS * TILE
+
+    def kernel(
+        slots_ref, lengths_ref, g_ref, oT_ref, q_ref, k_ref, v_ref, lse_ref,
+        dq_ref, dk_ref, dv_ref, hq, kT, doT, dqT, q_stack, do_stack, p_buf, ds_buf, dk_acc, dv_acc,
+    ):
+        def gather_query(pair, _):
+            _, second, _, _ = pair_blocks(slots_ref, pair, per_device)
+            hq[aligned(pair, BLK), :] = g_ref[aligned(2 * pair + second, BLK), :]
+            hq[aligned(pair + queries // (2 * BLK), BLK), :] = g_ref[
+                aligned(2 * pair + 1 - second, BLK), :
+            ]
+            return 0
+
+        lax.fori_loop(0, queries // (2 * BLK), gather_query, 0)
+
+        def transpose_keys(i, _):
+            rows = aligned(i, TILE)
+            kT[:, rows] = k_ref[rows, :].T
+            return 0
+
+        lax.fori_loop(0, tokens // TILE, transpose_keys, 0)
+
+        for kind in (1, 0):
+            key_tiles = (PROMPT if kind == 0 else tokens) // TILE
+            first_masked = 0 if kind == 0 else PROMPT // TILE
+
+            def one_tile(step, _):
+                tile = kind * (tiles // 2) + step
+                q_tile = q_ref[aligned(tile, TILE), :]
+                local, q_low, q_high = tile_tables(kind, step, slots_ref, lengths_ref, per_device)
+                do_tile = hq[aligned(tile, TILE), :]
+                doT[...] = do_tile.astype(F32).T * oT_ref[tile]
+                for head in range(LOCAL_HEADS):
+                    lanes = pl.ds(head * TILE, TILE)
+                    heads = pl.ds(head * HD, HD)
+                    mask = head_mask(TILE, head)
+                    q_head = jnp.where(mask, q_tile, jnp.zeros_like(q_tile))
+                    do_head = jnp.where(mask, do_tile, jnp.zeros_like(do_tile))
+                    q_stack[lanes, :] = q_head
+                    do_stack[lanes, :] = do_head
+                    delta = jnp.sum(doT[heads, :], axis=0, keepdims=True)
+                    norm = lse_ref[tile, head]
+                    for k_tile in range(key_tiles):
+                        rows = pl.ds(k_tile * TILE, TILE)
+                        s = lax.dot_general(k_ref[rows, :], q_head, NT, preferred_element_type=F32)
+                        dp = lax.dot_general(v_ref[rows, :], do_head, NT, preferred_element_type=F32)
+                        p = jnp.exp(s - norm)
+                        if k_tile >= first_masked:
+                            place = lax.broadcasted_iota(jnp.int32, (TILE, TILE), 0) + k_tile * TILE
+                            seen = (place >= q_low) & (place <= q_high)
+                            p = jnp.where(seen, p, 0.0)
+                        p_buf[rows, lanes] = p.astype(BF16)
+                        ds_buf[rows, lanes] = (p * (dp - delta)).astype(BF16)
+                    keys = key_tiles * TILE
+                    dqT[heads, :] = jnp.dot(
+                        kT[heads, :keys], ds_buf[:keys, lanes], preferred_element_type=F32
+                    )
+                for k_tile in range(key_tiles):
+                    rows = pl.ds(k_tile * TILE, TILE)
+                    dv = jnp.dot(p_buf[rows, :], do_stack[...], preferred_element_type=F32)
+                    dk = jnp.dot(ds_buf[rows, :], q_stack[...], preferred_element_type=F32)
+                    if kind == 1:
+                        fresh = step == 0
+                        dv = dv + jnp.where(fresh, 0.0, dv_acc[rows, :])
+                        dk = dk + jnp.where(fresh, 0.0, dk_acc[rows, :])
+                    else:
+                        dv = dv + dv_acc[rows, :]
+                        dk = dk + dk_acc[rows, :]
+                    dv_acc[rows, :] = dv
+                    dk_acc[rows, :] = dk
+                dq = dqT[...].T.astype(BF16)
+                for b in range(TILE // BLK):
+                    dq_ref[aligned(local[b], BLK), :] = dq[b * BLK : (b + 1) * BLK]
+                return 0
+
+            lax.fori_loop(0, tiles // 2, one_tile, 0)
+
+        def give_block(slot, _):
+            block = aligned(slots_ref[slot], BLK)
+            dk_ref[aligned(slot, BLK), :] = dk_acc[block, :].astype(BF16)
+            dv_ref[aligned(slot, BLK), :] = dv_acc[block, :].astype(BF16)
+            return 0
+
+        lax.fori_loop(0, blocks, give_block, 0)
+
+    return pl.pallas_call(
+        kernel,
+        out_shape=[
+            jax.ShapeDtypeStruct((queries, CHIP_COLS), BF16),
+            jax.ShapeDtypeStruct((tokens, CHIP_COLS), BF16),
+            jax.ShapeDtypeStruct((tokens, CHIP_COLS), BF16),
+        ],
+        in_specs=[SM, SM] + [VM] * 6,
+        out_specs=[VM] * 3,
+        scratch_shapes=[
+            pltpu.VMEM((queries, CHIP_COLS), BF16),
+            pltpu.VMEM((CHIP_COLS, tokens), BF16),
+            pltpu.VMEM((CHIP_COLS, TILE), F32),
+            pltpu.VMEM((CHIP_COLS, TILE), F32),
+            pltpu.VMEM((wide, CHIP_COLS), BF16),
+            pltpu.VMEM((wide, CHIP_COLS), BF16),
+            pltpu.VMEM((tokens, wide), BF16),
+            pltpu.VMEM((tokens, wide), BF16),
+            pltpu.VMEM((tokens, CHIP_COLS), F32),
+            pltpu.VMEM((tokens, CHIP_COLS), F32),
+        ],
+        compiler_params=pltpu.CompilerParams(vmem_limit_bytes=VMEM_LIMIT),
+        cost_estimate=pl.CostEstimate(
+            flops=20 * queries * tokens * CHIP_COLS, bytes_accessed=20 * tokens * CHIP_COLS, transcendentals=queries * tokens
+        ),
+        name="attention_backward",
+    )(slots, lengths, att_grad, oT, q, k, v, lse)
+
+
+TN = (((0,), (0,)), ((), ()))
+ROWS = 32
+
+
+def norm_factor(rows):
+    return lax.rsqrt(jnp.mean(rows * rows, axis=1, keepdims=True) + EPSILON)
+
+
+def as_column(row):
+    return jnp.broadcast_to(row, (8, row.shape[1])).T[:, 0:1]
+
+
+def mix(states_ref, at, p_ref, i):
+    return p_ref[i, 0] * states_ref[at, 0, :].astype(F32) + p_ref[i, 1] * states_ref[at, 1, :].astype(F32)
+
+
+def prepare(states, predict, valid, gain_one, gain_two, w_query, w_key, w_value, w_gate, w_up, w_down):
+    rows, _, width = states.shape
+    shard = w_query.shape[0]
+    half = shard // 2
+    hidden_cols = w_gate.shape[1]
+    columns = hidden_cols // CHIPS
+    depths = width // shard
+    split = columns // depths
+
+    def kernel(
+        s_ref, p_ref, v_ref, g1_ref, g2_ref, q_ref, k_ref, vw_ref, gate_ref, up_ref, down_ref,
+        pre_ref, qkv_ref, ff_ref, count_ref, buf, wide, sems,
+    ):
+        _, chip, core, _, _, _ = place_on_mesh()
+        mine = pl.ds(core * half, half)
+        loads = [
+            pltpu.make_async_copy(w.at[mine], buf.at[i], sems.at[i])
+            for i, w in enumerate((q_ref, k_ref, vw_ref))
+        ] + [
+            pltpu.make_async_copy(gate_ref.at[mine], wide.at[0], sems.at[3]),
+            pltpu.make_async_copy(up_ref.at[mine], wide.at[1], sems.at[4]),
+            pltpu.make_async_copy(
+                down_ref.at[pl.ds(chip * split + core * (split // 2), half)],
+                ff_ref.at[pl.ds(2 * half, half)],
+                sems.at[5],
+            ),
+        ]
+        for copy in loads:
+            copy.start()
+        count_ref[...] = jnp.broadcast_to(
+            jnp.sum(v_ref[...].astype(F32), axis=1, keepdims=True), count_ref.shape
+        )
+
+        def norm(i, _):
+            at = aligned(i, ROWS)
+            active = mix(s_ref, at, p_ref, 0)
+            pre_ref[at, :] = (active * norm_factor(active)).astype(BF16)
+            return 0
+
+        lax.fori_loop(0, rows // ROWS, norm, 0)
+
+        def gain_column(ref):
+            both = jnp.broadcast_to(ref[...].astype(F32), (8, shard)).T
+            return jnp.where(core == 0, both[:half, 0:1], both[half:, 0:1])
+
+        one, two = gain_column(g1_ref), gain_column(g2_ref)
+        for copy in loads:
+            copy.wait()
+        for p in range(CHIPS):
+
+            @pl.when(chip == p)
+            def _(p=p):
+                for i in range(3):
+                    cols = buf[i, :, p * CHIP_COLS : (p + 1) * CHIP_COLS]
+                    qkv_ref[i * half : (i + 1) * half, :] = (cols.astype(F32) * one).astype(BF16)
+                for i in range(2):
+                    cols = jnp.concatenate(
+                        [
+                            wide[i, :, (z * CHIPS + p) * split : (z * CHIPS + p + 1) * split].astype(F32)
+                            for z in range(depths)
+                        ],
+                        axis=1,
+                    )
+                    ff_ref[i * half : (i + 1) * half, :] = (cols * two).astype(BF16)
+
+    return pl.pallas_call(
+        kernel,
+        out_shape=[
+            jax.ShapeDtypeStruct((rows, width), BF16),
+            jax.ShapeDtypeStruct((3 * half, CHIP_COLS), BF16),
+            jax.ShapeDtypeStruct((3 * half, columns), BF16),
+            jax.ShapeDtypeStruct((8, 128), F32),
+        ],
+        in_specs=[VM, SM] + [VM] * 3 + [ANY] * 6,
+        out_specs=[VM] * 4,
+        scratch_shapes=[
+            pltpu.VMEM((3, half, width), BF16),
+            pltpu.VMEM((2, half, hidden_cols), BF16),
+            DMA((6,)),
+        ],
+        compiler_params=pltpu.CompilerParams(vmem_limit_bytes=VMEM_LIMIT),
+        name="prepare",
+    )(states, predict, valid, gain_one, gain_two, w_query, w_key, w_value, w_gate, w_up, w_down)
+
+
+def plane_peers(chip, core, depth, chip_x, chip_y, chip_d):
+    same = [(2 * c + core, depth) for c in (chip_x, chip_y, chip_d)]
+    return same + [(2 * c + 1 - core, depth) for c in (chip, chip_x, chip_y, chip_d)]
+
+
+def total_over_mesh(own_ref, arrived, staged, far, across, peers, bsend, brecv, csend, crecv):
+    first = [remote(own_ref, arrived.at[i], bsend, brecv, i, d) for i, d in enumerate(across)]
+    second = [remote(staged, far.at[i], csend, crecv, i, d) for i, d in enumerate(peers)]
+
+    def start():
+        for copy in first:
+            copy.start()
+
+    def turn():
+        total = own_ref[...]
+        for i, copy in enumerate(first):
+            copy.wait_recv()
+        for i in range(len(first)):
+            total = total + arrived[i]
+        staged[...] = total
+        for copy in second:
+            copy.start()
+
+    def end():
+        for copy in second:
+            copy.wait_recv()
+        total = staged[...]
+        for i in range(len(second)):
+            total = total + far[i]
+        for copy in first + second:
+            copy.wait_send()
+        return total
+
+    return start, turn, end
+
+
+def total_scratch(shape, depths):
+    return [
+        pltpu.VMEM((depths - 1,) + shape, F32),
+        pltpu.VMEM(shape, F32),
+        pltpu.VMEM((2 * CHIPS - 1,) + shape, F32),
+        DMA((depths - 1,)),
+        DMA((depths - 1,)),
+        DMA((2 * CHIPS - 1,)),
+        DMA((2 * CHIPS - 1,)),
+    ]
+
+
+def gather_inputs(pre, qkv, w_out, count, collective_id):
+    depths = lax.axis_size("wsh")
+    out_rows = w_out.shape[0] // CHIPS
+
+    def kernel(
+        x_ref, w_ref, o_ref, c_ref, out_ref, wall_ref, oall_ref, total_ref,
+        send, recv, wsend, wrecv, osend, orecv, ssend, srecv, local, *total_refs,
+    ):
+        depth, chip, core, chip_x, chip_y, chip_d = place_on_mesh()
+        other = (2 * chip + 1 - core, depth)
+        across = [
+            (2 * chip + core, lax.rem(depth + step, depths)) for step in range(1, depths)
+        ]
+        peers = plane_peers(chip, core, depth, chip_x, chip_y, chip_d)
+        signal_and_wait(peers + across)
+
+        def slot(chip_index):
+            return 2 * chip_index + core
+
+        start, turn, end = total_over_mesh(c_ref, *total_refs[:3], across, peers, *total_refs[3:])
+        start()
+        copies = ring_sends(
+            x_ref, out_ref, slot, chip, core, depth, chip_x, chip_y, send, recv
+        )
+        for copy in copies[:4]:
+            copy.start()
+        w_copies = [
+            remote(w_ref, wall_ref.at[depth, core], wsend, wrecv, i, device)
+            for i, device in enumerate(across)
+        ]
+        out_mine = o_ref.at[pl.ds(chip * out_rows, out_rows)]
+        o_copies = [
+            remote(out_mine, oall_ref.at[depth], osend, orecv, i, device)
+            for i, device in enumerate(across)
+        ]
+        for copy in w_copies + o_copies:
+            copy.start()
+
+        def shared(index, ref, source=None):
+            return remote(ref if source is None else source, ref, ssend, srecv, index, other)
+
+        to_other = [
+            shared(0, out_ref.at[slot(chip)], x_ref),
+            shared(1, out_ref.at[slot(chip_x)]),
+            shared(2, out_ref.at[slot(chip_y)]),
+            shared(3, out_ref.at[slot(chip_d)]),
+            shared(4, wall_ref.at[depth, core], w_ref),
+        ] + [
+            shared(5 + i, wall_ref.at[lax.rem(depth + depths - 1 - i, depths), core])
+            for i in range(depths - 1)
+        ]
+        to_other[0].start()
+        to_other[4].start()
+        mine = pltpu.make_async_copy(x_ref, out_ref.at[slot(chip)], local)
+        mine.start()
+        wall_ref[depth, core] = w_ref[...]
+        oall_ref[depth] = o_ref[aligned(chip, out_rows), :]
+        turn()
+        copies[0].wait_recv()
+        copies[4].start()
+        copies[1].wait_recv()
+        copies[5].start()
+        for i in range(depths - 1):
+            w_copies[i].wait_recv()
+            to_other[5 + i].start()
+        copies[2].wait_recv()
+        to_other[1].start()
+        copies[3].wait_recv()
+        to_other[2].start()
+        copies[4].wait_recv()
+        copies[5].wait_recv()
+        to_other[3].start()
+        for copy in o_copies:
+            copy.wait_recv()
+        total_ref[...] = end()
+        for copy in to_other:
+            copy.wait()
+        for copy in copies + w_copies + o_copies:
+            copy.wait_send()
+        mine.wait()
+
+    return pl.pallas_call(
+        kernel,
+        out_shape=[
+            jax.ShapeDtypeStruct((2 * CHIPS,) + pre.shape, BF16),
+            jax.ShapeDtypeStruct((depths, 2) + qkv.shape, BF16),
+            jax.ShapeDtypeStruct((depths, out_rows, w_out.shape[1]), BF16),
+            jax.ShapeDtypeStruct(count.shape, F32),
+        ],
+        in_specs=[VM] * 4,
+        out_specs=[ANY, VM, VM, VM],
+        scratch_shapes=[
+            DMA((6,)),
+            DMA((6,)),
+            DMA((depths - 1,)),
+            DMA((depths - 1,)),
+            DMA((depths - 1,)),
+            DMA((depths - 1,)),
+            DMA((depths + 4,)),
+            DMA((depths + 4,)),
+            DMA,
+        ]
+        + total_scratch(count.shape, depths),
+        compiler_params=comm_params(collective_id),
+        name="gather_inputs",
+    )(pre, qkv, w_out, count)
+
+
+def gelu_parts(v):
+    scale = math.sqrt(2 / math.pi)
+    square = v * v
+    t = jnp.tanh(scale * v * (1.0 + 0.044715 * square))
+    rise = 0.5 * (1.0 + t)
+    return v * rise, rise + 0.5 * v * (1.0 - t * t) * scale * (1.0 + 0.134145 * square)
+
+
+def middle(attended, out_pieces, ff_pieces, states, out_grad, teacher, valid, count, predict, correct, collective_id):
+    rows, _, width = states.shape
+    _, half, columns = ff_pieces[0].shape
+    depths, out_rows, _ = out_pieces[0].shape
+    shard = 2 * half
+    blocks = rows // ROWS
+    col_tiles = columns // TILE
+    tokens = 2 * CHIPS * rows * depths
+
+    def kernel(
+        att_ref, o0, o1, o2, o3, f0, f1, f2, f3, f4, f5, s_ref, g_ref, t_ref, v_ref, n_ref, p_ref, c_ref,
+        new_ref, up0_ref, up1_ref, hg_ref, da_ref, dw0_ref, dw1_ref, dw2_ref, dw3_ref, ff_ref, sums_ref,
+        w_all, w_out, att_all, hidden, own, x_rows, r_rows, xT, innerT, inner, gate, up, gate_low, up_low,
+        part0, part1, part2, got1, got2, dw, dw_other,
+        wsend, wrecv, wlocal, olocal, send0, recv0, send1, recv1, send2, recv2, send3, recv3,
+        ag1s, ag1r, ag2s, ag2r, dsend, drecv,
+    ):
+        depth, chip, core, chip_x, chip_y, chip_d = place_on_mesh()
+        near = [(c, (2 * c + core, depth)) for c in (chip_x, chip_y, chip_d)]
+        other = (2 * chip + 1 - core, depth)
+        signal_and_wait([device for _, device in near] + [other])
+
+        def exchange(source_of, target, send, recv):
+            return [
+                remote(source_of(c), target, send, recv, i, device)
+                for i, (c, device) in enumerate(near)
+            ]
+
+        def ring(source, target, send, recv):
+            return ring_sends(
+                source, target, lambda c: c, chip, core, depth, chip_x, chip_y, send, recv
+            )
+
+        sends0 = exchange(lambda c: att_ref.at[c], att_all.at[chip], send0, recv0)
+        for copy in sends0:
+            copy.start()
+        out_loads = [
+            pltpu.make_async_copy(piece, w_out.at[:, c], olocal.at[i])
+            for i, (piece, c) in enumerate(zip((o0, o1, o2, o3), (chip, chip_x, chip_y, chip_d)))
+        ]
+        for copy in out_loads:
+            copy.start()
+        sources = (
+            (f0, 0, None),
+            (f1, -1, depth >= 1),
+            (f2, -2, depth >= 2),
+            (f3, 1, depth <= depths - 2),
+            (f4, 2, depth <= depths - 3),
+            (f5, None, (depth == 0) | (depth == depths - 1)),
+        )
+
+        def each_source(act):
+            for i, (ref, shift, present) in enumerate(sources):
+                z = depths - 1 - depth if shift is None else depth + shift
+                z = jnp.clip(z, 0, depths - 1)
+                dst = w_all.at[:, z, core]
+                copies = (
+                    remote(ref, dst, wsend, wrecv, i, other),
+                    pltpu.make_async_copy(ref, dst, wlocal.at[i]),
+                )
+                if present is None:
+                    act(copies)
+                else:
+
+                    @pl.when(present)
+                    def _(copies=copies):
+                        act(copies)
+
+        each_source(lambda copies: [copy.start() for copy in copies])
+        att_all[chip] = att_ref[chip]
+        for copy in out_loads:
+            copy.wait()
+        for copy in sends0:
+            copy.wait_recv()
+
+        def w_out_rows(p):
+            return w_out[p].reshape(CHIP_COLS, width)
+
+        for p in range(CHIPS):
+            term = jnp.dot(att_all[p], w_out_rows(p), preferred_element_type=F32)
+            hidden[...] = term if p == 0 else hidden[...] + term
+
+        def first_norm(i, _):
+            at = aligned(i, ROWS)
+            h = hidden[at, :] + mix(s_ref, at, p_ref, 0)
+            hidden[at, :] = h
+            own[0, at, :] = (h * norm_factor(h)).astype(BF16)
+            return 0
+
+        lax.fori_loop(0, blocks, first_norm, 0)
+        ring1 = ring(own.at[0], x_rows, ag1s, ag1r)
+        for copy in ring1[:4]:
+            copy.start()
+        x_rows[chip] = own[0]
+        each_source(lambda copies: [copy.wait() for copy in copies])
+
+        def w_rows(i):
+            return w_all[i].reshape(width, columns)
+
+        def forward(c):
+            x = x_rows[c]
+            for n in range(col_tiles):
+                cols = slice(n * TILE, (n + 1) * TILE)
+                g = jnp.dot(x, w_rows(0)[:, cols], preferred_element_type=F32)
+                u = jnp.dot(x, w_rows(1)[:, cols], preferred_element_type=F32)
+                gate[c, :, cols] = g
+                up[c, :, cols] = u
+                inner[c, :, cols] = (gelu_parts(g)[0] * u).astype(BF16)
+            return jnp.dot(inner[c], w_rows(2), preferred_element_type=F32)
+
+        sends1 = [
+            remote(part1.at[c], got1.at[i], send1, recv1, i, device) for i, (c, device) in enumerate(near)
+        ]
+        up0_ref[...] = forward(chip)
+        ring1[0].wait_recv()
+        ring1[4].start()
+        ring1[1].wait_recv()
+        ring1[5].start()
+        for i, (c, _) in enumerate(near):
+            if i < 2:
+                ring1[2 + i].wait_recv()
+            else:
+                ring1[4].wait_recv()
+                ring1[5].wait_recv()
+            part1[c] = forward(c).astype(BF16)
+            sends1[i].start()
+
+        def turn(i, _):
+            xT[:, aligned(i, rows)] = x_rows[i].T
+            innerT[:, aligned(i, rows)] = inner[i].T
+            return 0
+
+        lax.fori_loop(0, CHIPS, turn, 0)
+        weight = as_column(v_ref[...].astype(F32)) * (tokens / n_ref[0:1, 0:1])
+        own_weight = part0
+        own_weight[...] = jnp.broadcast_to(weight, own_weight.shape)
+        for copy in sends1:
+            copy.wait_recv()
+
+        def outputs(i, sums):
+            at = aligned(i, ROWS)
+            a = mix(s_ref, at, p_ref, 0)
+            result = hidden[at, :] + up0_ref[at, :]
+            for j in range(3):
+                result = result + got1[j, at, :].astype(F32)
+            difference = result - a
+            row_weight = own_weight[at, 0:1]
+            c0, c1 = c_ref[0], c_ref[1]
+            out0 = a + c0 * difference
+            out1 = mix(s_ref, at, p_ref, 1) + c1 * difference
+            new_ref[at, 0, :] = out0.astype(BF16)
+            new_ref[at, 1, :] = out1.astype(BF16)
+            up0 = g_ref[at, 0, :].astype(F32) + row_weight * (out0 - t_ref[at, 0, :].astype(F32))
+            up1 = g_ref[at, 1, :].astype(F32) + row_weight * (out1 - t_ref[at, 1, :].astype(F32))
+            up0_ref[at, :] = up0
+            up1_ref[at, :] = up1
+            own[1, at, :] = (c0 * up0 + c1 * up1).astype(BF16)
+            return (
+                sums[0] + jnp.sum(up0 * difference, axis=0, keepdims=True),
+                sums[1] + jnp.sum(up1 * difference, axis=0, keepdims=True),
+            )
+
+        zero = jnp.zeros((1, width), F32)
+        correct_sums = lax.fori_loop(0, blocks, outputs, (zero, zero))
+        sums_ref[...] = jnp.zeros_like(sums_ref)
+        sums_ref[2:3, :] = correct_sums[0]
+        sums_ref[3:4, :] = correct_sums[1]
+
+        ring2 = ring(own.at[1], r_rows, ag2s, ag2r)
+        for copy in ring2[:4]:
+            copy.start()
+        r_rows[chip] = own[1]
+
+        def backward(c):
+            r = r_rows[c]
+            for n in range(col_tiles):
+                cols = slice(n * TILE, (n + 1) * TILE)
+                inner_grad = lax.dot_general(r, w_rows(2)[cols, :], NT, preferred_element_type=F32)
+                value, slope = gelu_parts(gate[c, :, cols])
+                gate_low[c, :, cols] = (inner_grad * up[c, :, cols] * slope).astype(BF16)
+                up_low[c, :, cols] = (inner_grad * value).astype(BF16)
+            return lax.dot_general(
+                gate_low[c], w_rows(0), NT, preferred_element_type=F32
+            ) + lax.dot_general(up_low[c], w_rows(1), NT, preferred_element_type=F32)
+
+        sends2 = [
+            remote(part2.at[c], got2.at[i], send2, recv2, i, device) for i, (c, device) in enumerate(near)
+        ]
+        hg_ref[...] = backward(chip)
+        ring2[0].wait_recv()
+        ring2[4].start()
+        ring2[1].wait_recv()
+        ring2[5].start()
+        for i, (c, _) in enumerate(near):
+            if i < 2:
+                ring2[2 + i].wait_recv()
+            else:
+                ring2[4].wait_recv()
+                ring2[5].wait_recv()
+            part2[c] = backward(c).astype(BF16)
+            sends2[i].start()
+
+        def weight_grads(z, _):
+            at = aligned(z, shard)
+            for i, (left, right) in enumerate(((xT, gate_low), (xT, up_low), (innerT, r_rows))):
+                wide = jnp.dot(
+                    left[at, :], right[...].reshape(CHIPS * rows, -1), preferred_element_type=F32
+                ).astype(BF16)
+                dw[z, 0, i * half : (i + 1) * half, :] = wide[:half]
+                dw[z, 1, i * half : (i + 1) * half, :] = wide[half:]
+            return 0
+
+        lax.fori_loop(0, depths, weight_grads, 0)
+        swap = remote(dw.at[:, 1 - core], dw_other, dsend, drecv, 0, other)
+        swap.start()
+        for copy in sends2:
+            copy.wait_recv()
+
+        def second_norm(i, gain_sum):
+            at = aligned(i, ROWS)
+            h = hidden[at, :]
+            weighted = hg_ref[at, :]
+            for j in range(3):
+                weighted = weighted + got2[j, at, :].astype(F32)
+            factor = norm_factor(h)
+            mean = jnp.mean(weighted * h, axis=1, keepdims=True)
+            result_grad = c_ref[0] * up0_ref[at, :] + c_ref[1] * up1_ref[at, :]
+            hidden_grad = result_grad + (factor * weighted - h * (factor * factor * factor * mean))
+            hg_ref[at, :] = hidden_grad
+            own[2, at, :] = hidden_grad.astype(BF16)
+            return gain_sum + jnp.sum(weighted * h * factor, axis=0, keepdims=True)
+
+        sums_ref[1:2, :] = lax.fori_loop(0, blocks, second_norm, zero)
+
+        sends3 = exchange(lambda c: att_all.at[CHIPS + c], da_ref.at[chip], send3, recv3)
+
+        def att_grad(c):
+            return lax.dot_general(own[2], w_out_rows(c), NT, preferred_element_type=F32).astype(BF16)
+
+        for i in (2, 0, 1):
+            att_all[CHIPS + near[i][0]] = att_grad(near[i][0])
+            sends3[i].start()
+        da_ref[chip] = att_grad(chip)
+        for c, ref in zip((chip, chip_x, chip_y, chip_d), (dw0_ref, dw1_ref, dw2_ref, dw3_ref)):
+            ref[...] = jnp.dot(att_all[c].T, own[2], preferred_element_type=F32).astype(BF16)
+        swap.wait_recv()
+
+        def add_cores(z, _):
+            ff_ref[z] = (dw[z, core].astype(F32) + dw_other[z].astype(F32)).astype(BF16)
+            return 0
+
+        lax.fori_loop(0, depths, add_cores, 0)
+        for copy in sends3:
+            copy.wait_recv()
+        for copy in sends0 + sends1 + sends2 + sends3 + ring1 + ring2 + [swap]:
+            copy.wait_send()
+
+    block = (rows, width)
+    pair = (rows, 2, width)
+    wide_rows = (CHIPS, rows, width)
+    hid_rows = (CHIPS, rows, columns)
+    return pl.pallas_call(
+        kernel,
+        out_shape=[
+            jax.ShapeDtypeStruct(pair, BF16),
+            jax.ShapeDtypeStruct(block, F32),
+            jax.ShapeDtypeStruct(block, F32),
+            jax.ShapeDtypeStruct(block, F32),
+            jax.ShapeDtypeStruct((CHIPS, rows, CHIP_COLS), BF16),
+            jax.ShapeDtypeStruct((CHIP_COLS, width), BF16),
+            jax.ShapeDtypeStruct((CHIP_COLS, width), BF16),
+            jax.ShapeDtypeStruct((CHIP_COLS, width), BF16),
+            jax.ShapeDtypeStruct((CHIP_COLS, width), BF16),
+            jax.ShapeDtypeStruct((depths, 3 * half, columns), BF16),
+            jax.ShapeDtypeStruct((8, width), F32),
+        ],
+        in_specs=[VM] + [ANY] * 10 + [VM] * 5 + [SM] * 2,
+        out_specs=[VM] * 11,
+        scratch_shapes=[
+            pltpu.VMEM((3, depths, 2, half, columns), BF16),
+            pltpu.VMEM((depths, CHIPS, out_rows, width), BF16),
+            pltpu.VMEM((2 * CHIPS, rows, CHIP_COLS), BF16),
+            pltpu.VMEM(block, F32),
+            pltpu.VMEM((3,) + block, BF16),
+            pltpu.VMEM(wide_rows, BF16),
+            pltpu.VMEM(wide_rows, BF16),
+            pltpu.VMEM((width, CHIPS * rows), BF16),
+            pltpu.VMEM((columns, CHIPS * rows), BF16),
+            pltpu.VMEM(hid_rows, BF16),
+            pltpu.VMEM(hid_rows, F32),
+            pltpu.VMEM(hid_rows, F32),
+            pltpu.VMEM(hid_rows, BF16),
+            pltpu.VMEM(hid_rows, BF16),
+            pltpu.VMEM((rows, 128), F32),
+            pltpu.VMEM(wide_rows, BF16),
+            pltpu.VMEM(wide_rows, BF16),
+            pltpu.VMEM((3,) + block, BF16),
+            pltpu.VMEM((3,) + block, BF16),
+            pltpu.VMEM((depths, 2, 3 * half, columns), BF16),
+            pltpu.VMEM((depths, 3 * half, columns), BF16),
+        ]
+        + [DMA((6,))] * 3
+        + [DMA((CHIPS,))]
+        + [DMA((3,))] * 8
+        + [DMA((6,))] * 4
+        + [DMA((1,))] * 2,
+        compiler_params=comm_params(collective_id),
+        name="middle",
+    )(attended, *out_pieces, *ff_pieces, states, out_grad, teacher, valid, count, predict, correct)
+
+
+def input_gradients(
+    dq, dk, dv, qkv, all_rows, out_grads, states, up0, up1, hidden_grad, sums, predict, correct, collective_id
+):
+    rows, _, width = states.shape
+    depths, _, part_rows, columns = qkv.shape
+    half = part_rows // 3
+    blocks = rows // ROWS
+
+    def kernel(
+        dq_ref, dk_ref, dv_ref, qkv_ref, rows_ref, o0, o1, o2, o3, s_ref, up0_ref, up1_ref, hg_ref, sums_ref,
+        p_ref, c_ref,
+        grad_ref, qsum_ref, osum_ref, all_sums,
+        w_all, x_own, xT, dk_other, dv_other, dkv, part, got, mine, q_grad, q_other, q_mine, q_far,
+        o_grad, o_other, o_mine, o_far,
+        xload, ksend, krecv, send, recv, ssend, srecv, zsend, zrecv, osend, orecv,
+    ):
+        depth, chip, core, chip_x, chip_y, chip_d = place_on_mesh()
+        near = [(c, (2 * c + core, depth)) for c in (chip_x, chip_y, chip_d)]
+        other = (2 * chip + 1 - core, depth)
+        across = [
+            (2 * chip + core, lax.rem(depth + step, depths)) for step in range(1, depths)
+        ]
+        signal_and_wait([device for _, device in near] + [other] + across)
+        swaps = [
+            remote(dk_ref.at[:, 1 - core], dk_other, ksend, krecv, 0, other),
+            remote(dv_ref.at[:, 1 - core], dv_other, ksend, krecv, 1, other),
+        ]
+        for copy in swaps:
+            copy.start()
+        load = pltpu.make_async_copy(rows_ref.at[:, core], x_own, xload)
+        load.start()
+        spread_rows(qkv_ref, w_all)
+        for copy in swaps:
+            copy.wait_recv()
+
+        def add_cores(c, _):
+            dkv[0, c] = (dk_ref[c, core].astype(F32) + dk_other[c].astype(F32)).astype(BF16)
+            dkv[1, c] = (dv_ref[c, core].astype(F32) + dv_other[c].astype(F32)).astype(BF16)
+            return 0
+
+        lax.fori_loop(0, CHIPS, add_cores, 0)
+
+        def rows_grad(c):
+            return (
+                lax.dot_general(dq_ref[c], w_all[0], NT, preferred_element_type=F32)
+                + lax.dot_general(dkv[0, c], w_all[1], NT, preferred_element_type=F32)
+                + lax.dot_general(dkv[1, c], w_all[2], NT, preferred_element_type=F32)
+            )
+
+        sends = [
+            remote(part.at[c], got.at[i], send, recv, i, device) for i, (c, device) in enumerate(near)
+        ]
+        for i in (2, 0, 1):
+            part[near[i][0]] = rows_grad(near[i][0]).astype(BF16)
+            sends[i].start()
+        mine[...] = rows_grad(chip)
+        load.wait()
+
+        def turn(c, _):
+            xT[:, aligned(c, rows)] = x_own[c].T
+            return 0
+
+        lax.fori_loop(0, CHIPS, turn, 0)
+
+        def weight_grads(z, _):
+            at = aligned(z, 2 * half)
+            for i in range(3):
+                right = dq_ref[...] if i == 0 else dkv[i - 1]
+                wide = jnp.dot(
+                    xT[at, :], right.reshape(CHIPS * rows, columns), preferred_element_type=F32
+                ).astype(BF16)
+                q_grad[z, 0, i * half : (i + 1) * half, :] = wide[:half]
+                q_grad[z, 1, i * half : (i + 1) * half, :] = wide[half:]
+            return 0
+
+        lax.fori_loop(0, depths, weight_grads, 0)
+        wide = (
+            o0[...].astype(F32) + o1[...].astype(F32) + o2[...].astype(F32) + o3[...].astype(F32)
+        ).astype(BF16)
+        o_grad[0] = wide[:half]
+        o_grad[1] = wide[half:]
+        core_swaps = [
+            remote(q_grad.at[:, 1 - core], q_other, ssend, srecv, 0, other),
+            remote(o_grad.at[1 - core], o_other, ssend, srecv, 1, other),
+        ]
+        for copy in core_swaps:
+            copy.start()
+        for copy in core_swaps:
+            copy.wait_recv()
+        for i in range(depths):
+            q_mine[i] = (q_grad[i, core].astype(F32) + q_other[i].astype(F32)).astype(BF16)
+        q_copies = [
+            remote(q_mine.at[lax.rem(depth + i + 1, depths)], q_far.at[i], zsend, zrecv, i, device)
+            for i, device in enumerate(across)
+        ]
+        for copy in q_copies:
+            copy.start()
+        o_mine[...] = (o_grad[core].astype(F32) + o_other[...].astype(F32)).astype(BF16)
+        distance = lax.rem(chip + depths - depth, depths)
+        o_copies = [
+            remote(o_mine, o_far.at[i], osend, orecv, i, device) for i, device in enumerate(across)
+        ]
+        for i in range(depths - 1):
+
+            @pl.when(distance == i + 1)
+            def _(i=i):
+                o_copies[i].start()
+
+        for copy in sends:
+            copy.wait_recv()
+
+        def state_grads(i, totals):
+            at = aligned(i, ROWS)
+            s0, s1 = s_ref[at, 0, :].astype(F32), s_ref[at, 1, :].astype(F32)
+            a = p_ref[0, 0] * s0 + p_ref[0, 1] * s1
+            weighted = mine[at, :]
+            for j in range(3):
+                weighted = weighted + got[j, at, :].astype(F32)
+            factor = norm_factor(a)
+            mean = jnp.mean(weighted * a, axis=1, keepdims=True)
+            up0, up1 = up0_ref[at, :], up1_ref[at, :]
+            result_grad = c_ref[0] * up0 + c_ref[1] * up1
+            norm_grad = factor * weighted - a * (factor * factor * factor * mean)
+            mixed0 = up0 + (hg_ref[at, :] + norm_grad - result_grad)
+            grad_ref[at, 0, :] = (p_ref[0, 0] * mixed0 + p_ref[1, 0] * up1).astype(BF16)
+            grad_ref[at, 1, :] = (p_ref[0, 1] * mixed0 + p_ref[1, 1] * up1).astype(BF16)
+            terms = (weighted * a * factor, mixed0 * s0, mixed0 * s1, up1 * s0, up1 * s1)
+            return tuple(t + jnp.sum(v, axis=0, keepdims=True) for t, v in zip(totals, terms))
+
+        totals = lax.fori_loop(
+            0, blocks, state_grads, tuple(jnp.zeros((1, width), F32) for _ in range(5))
+        )
+        all_sums[...] = sums_ref[...]
+        all_sums[0:1, :] = totals[0]
+        for i in range(4):
+            all_sums[4 + i : 5 + i, :] = totals[1 + i]
+        for copy in q_copies:
+            copy.wait_recv()
+        total = q_mine[depth].astype(F32)
+        for i in range(depths - 1):
+            total = total + q_far[i].astype(F32)
+        qsum_ref[...] = total.astype(BF16)
+        osum_ref[...] = jnp.zeros_like(osum_ref)
+
+        @pl.when(distance == 0)
+        def _():
+            for copy in o_copies:
+                copy.wait_recv()
+            total = o_mine[...].astype(F32)
+            for i in range(depths - 1):
+                total = total + o_far[i].astype(F32)
+            osum_ref[...] = total.astype(BF16)
+
+        for copy in swaps + sends + core_swaps + q_copies:
+            copy.wait_send()
+        for i in range(depths - 1):
+
+            @pl.when(distance == i + 1)
+            def _(i=i):
+                o_copies[i].wait_send()
+
+    block = (rows, width)
+    q_block, o_block = (part_rows, columns), (half, width)
+    return pl.pallas_call(
+        kernel,
+        out_shape=[
+            jax.ShapeDtypeStruct((rows, 2, width), BF16),
+            jax.ShapeDtypeStruct(q_block, BF16),
+            jax.ShapeDtypeStruct(o_block, BF16),
+            jax.ShapeDtypeStruct((8, width), F32),
+        ],
+        in_specs=[VM] * 4 + [ANY] + [VM] * 9 + [SM] * 2,
+        out_specs=[VM] * 4,
+        scratch_shapes=[
+            pltpu.VMEM((3, width, columns), BF16),
+            pltpu.VMEM((CHIPS,) + block, BF16),
+            pltpu.VMEM((width, CHIPS * rows), BF16),
+            pltpu.VMEM((CHIPS, rows, columns), BF16),
+            pltpu.VMEM((CHIPS, rows, columns), BF16),
+            pltpu.VMEM((2, CHIPS, rows, columns), BF16),
+            pltpu.VMEM((CHIPS,) + block, BF16),
+            pltpu.VMEM((3,) + block, BF16),
+            pltpu.VMEM(block, F32),
+            pltpu.VMEM((depths, 2) + q_block, BF16),
+            pltpu.VMEM((depths,) + q_block, BF16),
+            pltpu.VMEM((depths,) + q_block, BF16),
+            pltpu.VMEM((depths - 1,) + q_block, BF16),
+            pltpu.VMEM((2,) + o_block, BF16),
+            pltpu.VMEM(o_block, BF16),
+            pltpu.VMEM(o_block, BF16),
+            pltpu.VMEM((depths - 1,) + o_block, BF16),
+            DMA,
+            DMA((2,)),
+            DMA((2,)),
+            DMA((3,)),
+            DMA((3,)),
+            DMA((2,)),
+            DMA((2,)),
+            DMA((depths - 1,)),
+            DMA((depths - 1,)),
+            DMA((depths - 1,)),
+            DMA((depths - 1,)),
+        ],
+        compiler_params=comm_params(collective_id),
+        name="input_gradients",
+    )(dq, dk, dv, qkv, all_rows, *out_grads, states, up0, up1, hidden_grad, sums, predict, correct)
+
+
+def gather_gradients(ff, qkv, out, sums, collective_id):
+    depths = lax.axis_size("wsh")
+    half, width = out.shape
+
+    def kernel(
+        f_ref, q_ref, o_ref, s_ref, f_all, q_all, o_all, total_ref,
+        fsend, frecv, qsend, qrecv, osend, orecv, ssend, srecv, *total_refs,
+    ):
+        depth, chip, core, chip_x, chip_y, chip_d = place_on_mesh()
+        dev_x, dev_y = (2 * chip_x + core, depth), (2 * chip_y + core, depth)
+        other = (2 * chip + 1 - core, depth)
+        across = [
+            (2 * chip + core, lax.rem(depth + step, depths)) for step in range(1, depths)
+        ]
+        peers = plane_peers(chip, core, depth, chip_x, chip_y, chip_d)
+        signal_and_wait(peers + across)
+
+        def slot(chip_index):
+            return 2 * chip_index + core
+
+        start, turn, end = total_over_mesh(s_ref, *total_refs[:3], across, peers, *total_refs[3:])
+        start()
+        f_copies = ring_sends(
+            f_ref, f_all, slot, chip, core, depth, chip_x, chip_y, fsend, frecv
+        )
+        q_copies = ring_sends(
+            q_ref, q_all, slot, chip, core, depth, chip_x, chip_y, qsend, qrecv
+        )
+        for copy in f_copies[:2] + q_copies[:2]:
+            copy.start()
+        quarter = half // 2
+        o_top, o_low = o_all.at[core, pl.ds(0, quarter)], o_all.at[core, pl.ds(quarter, quarter)]
+        o_source_top, o_source_low = o_ref.at[pl.ds(0, quarter)], o_ref.at[pl.ds(quarter, quarter)]
+        o_copies = [
+            remote(o_source_top, o_top, osend, orecv, 0, dev_x),
+            remote(o_source_low, o_low, osend, orecv, 1, dev_y),
+            remote(o_source_low, o_low, osend, orecv, 2, dev_x),
+            remote(o_source_top, o_top, osend, orecv, 3, dev_y),
+            remote(o_top, o_top, osend, orecv, 4, dev_y),
+            remote(o_low, o_low, osend, orecv, 5, dev_x),
+        ]
+        source, from_x, from_y = chip == depth, chip_x == depth, chip_y == depth
+
+        @pl.when(source)
+        def _():
+            for copy in o_copies[:4]:
+                copy.start()
+            o_all[core] = o_ref[...]
+
+        for copy in f_copies[2:4] + q_copies[2:4]:
+            copy.start()
+        f_all[slot(chip)] = f_ref[...]
+        q_all[slot(chip)] = q_ref[...]
+
+        def shared(index, ref):
+            return remote(ref, ref, ssend, srecv, index, other)
+
+        f_shared = [shared(i, f_all.at[slot(c)]) for i, c in enumerate((chip, chip_x, chip_y, chip_d))]
+        q_shared = [shared(4 + i, q_all.at[slot(c)]) for i, c in enumerate((chip, chip_x, chip_y, chip_d))]
+        o_shared = shared(8, o_all.at[core])
+        f_shared[0].start()
+        q_shared[0].start()
+        turn()
+        for copies in (f_copies, q_copies):
+            copies[0].wait_recv()
+            copies[4].start()
+            copies[1].wait_recv()
+            copies[5].start()
+
+        @pl.when(from_x)
+        def _():
+            o_copies[0].wait_recv()
+            o_copies[4].start()
+            o_copies[2].wait_recv()
+
+        @pl.when(from_y)
+        def _():
+            o_copies[1].wait_recv()
+            o_copies[5].start()
+            o_copies[3].wait_recv()
+
+        for copies, passed in ((f_copies, f_shared), (q_copies, q_shared)):
+            copies[2].wait_recv()
+            passed[1].start()
+            copies[3].wait_recv()
+            passed[2].start()
+        for copies, passed in ((f_copies, f_shared), (q_copies, q_shared)):
+            copies[4].wait_recv()
+            copies[5].wait_recv()
+            passed[3].start()
+
+        @pl.when(chip_d == depth)
+        def _():
+            o_copies[4].wait_recv()
+            o_copies[5].wait_recv()
+
+        o_shared.start()
+        total_ref[...] = end()
+        for copy in f_shared + q_shared + [o_shared]:
+            copy.wait()
+        for copy in f_copies + q_copies:
+            copy.wait_send()
+
+        @pl.when(source)
+        def _():
+            for copy in o_copies[:4]:
+                copy.wait_send()
+
+        @pl.when(from_x)
+        def _():
+            o_copies[4].wait_send()
+
+        @pl.when(from_y)
+        def _():
+            o_copies[5].wait_send()
+
+    return pl.pallas_call(
+        kernel,
+        out_shape=[
+            jax.ShapeDtypeStruct((2 * CHIPS,) + ff.shape, BF16),
+            jax.ShapeDtypeStruct((2 * CHIPS,) + qkv.shape, BF16),
+            jax.ShapeDtypeStruct((2,) + out.shape, BF16),
+            jax.ShapeDtypeStruct(sums.shape, F32),
+        ],
+        in_specs=[VM] * 4,
+        out_specs=[VM] * 4,
+        scratch_shapes=[DMA((6,))] * 6 + [DMA((9,))] * 2 + total_scratch(sums.shape, depths),
+        compiler_params=comm_params(collective_id),
+        name="gather_gradients",
+    )(ff, qkv, out, sums)
+
+
+def lay_out(ff, qkv, out, sums, gain_one, gain_two):
+    ctx, part_rows, columns = ff.shape
+    half, width = out.shape[1:]
+    shard = 2 * half
+    depths = width // shard
+    split = columns // depths
+
+    def kernel(
+        f_ref, q_ref, o_ref, s_ref, g1_ref, g2_ref,
+        dq_ref, dk_ref, dv_ref, do_ref, dg_ref, du_ref, dd_ref, g1_out, g2_out, p_out, c_out,
+    ):
+        depth = lax.axis_index("wsh")
+        one, two = g1_ref[...].astype(F32), g2_ref[...].astype(F32)
+        one_column, two_column = as_column(one), as_column(two)
+        for c in range(2):
+            rows = slice(c * half, (c + 1) * half)
+            do_ref[rows, :] = o_ref[c].astype(F32)
+            for i, ref in enumerate((dq_ref, dk_ref, dv_ref)):
+                wide = jnp.concatenate(
+                    [q_ref[2 * p + c, i * half : (i + 1) * half, :].astype(F32) for p in range(CHIPS)],
+                    axis=1,
+                )
+                ref[rows, :] = wide * one_column[rows]
+            for i, ref in enumerate((dg_ref, du_ref)):
+                for z in range(depths):
+                    wide = jnp.concatenate(
+                        [
+                            f_ref[
+                                2 * p + c, i * half : (i + 1) * half, z * split : (z + 1) * split
+                            ].astype(F32)
+                            for p in range(CHIPS)
+                        ],
+                        axis=1,
+                    )
+                    ref[rows, z * CHIPS * split : (z + 1) * CHIPS * split] = wide * two_column[rows]
+            for p in range(CHIPS):
+                at = (2 * p + c) * half
+                dd_ref[at : at + half, :] = f_ref[2 * p + c, 2 * half :, :].astype(F32)
+        for z in range(depths):
+
+            @pl.when(depth == z)
+            def _(z=z):
+                g1_out[...] = s_ref[0:1, z * shard : (z + 1) * shard] / one
+                g2_out[...] = s_ref[1:2, z * shard : (z + 1) * shard] / two
+
+        scalars = jnp.sum(s_ref[...], axis=1, keepdims=True)
+        for i in range(2):
+            c_out[:, i : i + 1] = scalars[2 + i : 3 + i]
+            for j in range(2):
+                at = 4 + 2 * i + j
+                p_out[i : i + 1, j : j + 1] = scalars[at : at + 1]
+
+    square = jax.ShapeDtypeStruct((shard, width), F32)
+    tall = jax.ShapeDtypeStruct((shard, columns * CHIPS), F32)
+    row = jax.ShapeDtypeStruct((1, shard), F32)
+    return pl.pallas_call(
+        kernel,
+        out_shape=[
+            square,
+            square,
+            square,
+            square,
+            tall,
+            tall,
+            jax.ShapeDtypeStruct((ctx * half, width), F32),
+            row,
+            row,
+            jax.ShapeDtypeStruct((2, 2), F32),
+            jax.ShapeDtypeStruct((1, 2), F32),
+        ],
+        in_specs=[VM] * 6,
+        out_specs=[VM] * 11,
+        compiler_params=pltpu.CompilerParams(vmem_limit_bytes=VMEM_LIMIT),
+        name="lay_out",
+    )(ff, qkv, out, sums, gain_one, gain_two)
+
+
+def plane_shards(
+    states, block_slot, cont_lengths, valid_mask, teacher, out_grad, predict, correct,
+    norm_attn, w_query, w_key, w_value, w_out, norm_ffn, w_gate, w_up, w_down,
+):
+    depths = lax.axis_size("wsh")
+    _, rows, _, width = states.shape
+    half = w_query.shape[0] // 2
+    hidden_cols = w_gate.shape[1] // CHIPS
+    slots, lengths = block_slot[0], cont_lengths[0]
+    states, out_grad, teacher = states[0], out_grad[0], teacher[0]
+    gain_one, gain_two = norm_attn[None], norm_ffn[None]
+
+    def along_depth(value, pairs):
+        return lax.ppermute(value, "wsh", pairs)
+
+    def over_plane(value, step):
+        pairs = [(2 * c + k, 2 * (c ^ step) + k) for c in range(CHIPS) for k in range(2)]
+        return lax.ppermute(value, "ctx", pairs)
+
+    pre, qkv_piece, ff_piece, count = prepare(
+        states, predict, valid_mask, gain_one, gain_two, w_query, w_key, w_value, w_gate, w_up, w_down
+    )
+    ff_piece = ff_piece.reshape(3, half, hidden_cols)
+    above = [(z, z + 1) for z in range(depths - 1)]
+    below = [(z + 1, z) for z in range(depths - 1)]
+    from_below = along_depth(ff_piece, above)
+    from_above = along_depth(ff_piece, below)
+    all_rows, qkv, out_piece, count = gather_inputs(pre, qkv_piece, w_out, count, 1)
+    ff_pieces = [
+        ff_piece,
+        from_below,
+        along_depth(from_below, above[1:]),
+        from_above,
+        along_depth(from_above, below[:-1]),
+        along_depth(ff_piece, [(0, depths - 1), (depths - 1, 0)]),
+    ]
+    out_pieces = [out_piece] + [over_plane(out_piece, step) for step in (1, 2, 3)]
+    attended, *saved = attention_forward(all_rows.reshape(-1, width), qkv, slots, lengths)
+    new_states, up0, up1, hidden_grad, att_grad, *rest = middle(
+        attended.reshape(CHIPS, rows, CHIP_COLS), out_pieces, ff_pieces, states, out_grad, teacher,
+        valid_mask, count, predict, correct, 2,
+    )
+    out_grads, (ff_sum, sums) = rest[:4], rest[4:]
+    ff_sum = lax.psum_scatter(
+        ff_sum.reshape(depths * 3 * half, hidden_cols), "wsh", scatter_dimension=0, tiled=True
+    )
+    out_grads = [out_grads[0]] + [over_plane(g, step) for step, g in zip((1, 2, 3), out_grads[1:])]
+    dq, dk, dv = attention_backward(att_grad.reshape(-1, CHIP_COLS), saved, slots, lengths)
+    states_grad, qkv_sum, out_sum, sums = input_gradients(
+        dq.reshape(CHIPS, rows, CHIP_COLS),
+        dk.reshape(CHIPS, 2, rows, CHIP_COLS),
+        dv.reshape(CHIPS, 2, rows, CHIP_COLS),
+        qkv, all_rows.reshape(CHIPS, 2, rows, width), out_grads,
+        states, up0, up1, hidden_grad, sums, predict, correct, 3,
+    )
+    gathered = gather_gradients(ff_sum, qkv_sum, out_sum, sums, 4)
+    dq, dk, dv, do, dg, du, dd, g_one, g_two, predict_grad, correct_grad = lay_out(
+        *gathered, gain_one, gain_two
+    )
+    return (
+        new_states[None], states_grad[None], predict_grad, correct_grad[0],
+        g_one[0], dq, dk, dv, do, g_two[0], dg, du, dd,
+    )
+
+
+def fits_plane(mesh, states, block_slot, w_query, w_gate):
+    ctx, depths = mesh.shape["ctx"], mesh.shape["wsh"]
+    return (
+        ctx == 2 * CHIPS
+        and depths == CHIPS
+        and states.shape[0] == depths
+        and block_slot.shape[1] * BLK == 2 * PROMPT
+        and states.shape[1] == 2 * PROMPT
+        and w_query.shape[0] % (32 * depths) == 0
+        and w_gate.shape[1] % (32 * CHIPS * depths) == 0
+    )
+
+
 def solution(mesh):
-    return jax.shard_map(
-        shards,
-        mesh=mesh,
-        in_specs=(
-            P("wsh", "ctx", None, None),
-            P("wsh", None),
-            P("wsh", None),
-            P("wsh", "ctx"),
-            P("wsh", "ctx", None, None),
-            P("wsh", "ctx", None, None),
-            P(),
-            P(),
-            P("wsh"),
-            P("wsh", None),
-            P("wsh", None),
-            P("wsh", None),
-            P("wsh", None),
-            P("wsh"),
-            P("wsh", None),
-            P("wsh", None),
-            P("wsh", None),
-        ),
-        out_specs=(
-            P("wsh", "ctx", None, None),
-            P("wsh", "ctx", None, None),
-            P(),
-            P(),
-            P("wsh"),
-            P("wsh", None),
-            P("wsh", None),
-            P("wsh", None),
-            P("wsh", None),
-            P("wsh"),
-            P("wsh", None),
-            P("wsh", None),
-            P("wsh", None),
-        ),
-        check_vma=False,
-    )
+    in_specs = (
+        P("wsh", "ctx", None, None),
+        P("wsh", None),
+        P("wsh", None),
+        P("wsh", "ctx"),
+        P("wsh", "ctx", None, None),
+        P("wsh", "ctx", None, None),
+        P(),
+        P(),
+        P("wsh"),
+        P("wsh", None),
+        P("wsh", None),
+        P("wsh", None),
+        P("wsh", None),
+        P("wsh"),
+        P("wsh", None),
+        P("wsh", None),
+        P("wsh", None),
+    )
+    out_specs = (
+        P("wsh", "ctx", None, None),
+        P("wsh", "ctx", None, None),
+        P(),
+        P(),
+        P("wsh"),
+        P("wsh", None),
+        P("wsh", None),
+        P("wsh", None),
+        P("wsh", None),
+        P("wsh"),
+        P("wsh", None),
+        P("wsh", None),
+        P("wsh", None),
+    )
+
+    def step(*args):
+        plane = fits_plane(mesh, args[0], args[1], args[9], args[14])
+        body = plane_shards if plane else general_shards
+        return jax.shard_map(
+            body, mesh=mesh, in_specs=in_specs, out_specs=out_specs, check_vma=False
+        )(*args)
+
+    return step

time: 1210 us -> 289 us (0.24)
  waiting for transfers between devices: 627 us -> 0.07 us
  Pallas kernels: 0 us -> 245 us
  matrix products: 216 us -> 0 us
  local copies, waits for them, and re-layouts: 122 us -> 7.81 us
  blocking collectives: 112 us -> 0 us
  other arithmetic: 75.4 us -> 0 us
  loops' own time: 32.9 us -> 0 us
  starting transfers between devices: 1.19 us -> 21.8 us
    reduce_scatter x8 -> x1, waiting for transfers between devices: 332 us -> 0.02 us  [plane_shards(): lax.psum_scatter(ff_sum.reshape(depths * 3 * half, hidden_cols), 'wsh', s...]
    all_gather x9 -> x0, waiting for transfers between devices: 283 us -> none  [the longest x1 84 us: shards(): lax.all_gather(w_up, 'wsh', axis=0, tiled=True)]
    pallas_call x0 -> x8, Pallas kernels: none -> 245 us  [the longest x1 89.6 us: middle(): pl.pallas_call(kernel, out_shape=[jax.ShapeDtypeStruct(pair, BF16), jax.S...]
    dot_general x81 -> x0, matrix products: 216 us -> none  [the longest x16 45.2 us: backward_block(): jnp.einsum('gqhd,gkhd->ghqk', split_heads(query_part), split_heads(key_pa...]
    psum x3 -> x0, blocking collectives: 97.8 us -> none  [the longest x1 41.9 us: shards(): valid_total = lax.psum(jnp.sum(valid_float), ('ctx', 'wsh'))]
    dynamic_slice x73 -> x0, local copies, waits for them, and re-layouts: 80.8 us -> none  [the longest x24 19.3 us: shards(): lax.scan(fold_one_block, initial, jnp.arange(piece_len // block_size, dty...]
    reduce_or x24 -> x0, other arithmetic: 36.1 us -> none  [the longest x8 12 us: forward_block(): jnp.any(allowed)]
    another operation x27 -> x0, loops' own time: 32.9 us -> none  [the longest x1 10.7 us: shards(): lax.scan(query_step, zero_grad, jnp.arange(group_len // local_len, dtype=...]
  transfers between devices with their start and end apart: 18 -> 12, of which waited for: 14 -> 0; matrix products, arithmetic and copies ran while one was open for 21% -> 0% of each run, Pallas kernels for 0% -> 37%
where the time goes in v3:
time: 289 us
  Pallas kernels  245 us (85%)
  starting transfers between devices  21.8 us (8%)
  between operations  14.3 us (5%)
  local copies, waits for them, and re-layouts  7.81 us (3%)
    pallas_call x1, Pallas kernels, middle(): pl.pallas_call(kernel, out_shape=[jax.ShapeDtypeStruct(pair, BF16), jax.S...  89.6 us
    pallas_call x1, Pallas kernels, gather_gradients(): pl.pallas_call(kernel, out_shape=[jax.ShapeDtypeStruct((2 * CHIPS,) + ff....  36.8 us
    pallas_call x1, Pallas kernels, input_gradients(): pl.pallas_call(kernel, out_shape=[jax.ShapeDtypeStruct((rows, 2, width),...  36.4 us
    pallas_call x1, Pallas kernels, gather_inputs(): pl.pallas_call(kernel, out_shape=[jax.ShapeDtypeStruct((2 * CHIPS,) + pre...  31.3 us
    pallas_call x1, Pallas kernels, attention_forward(): pl.pallas_call(kernel, out_shape=[jax.ShapeDtypeStruct((queries, CHIP_COL...  20.5 us
    pallas_call x1, Pallas kernels, attention_backward(): pl.pallas_call(kernel, out_shape=[jax.ShapeDtypeStruct((queries, CHIP_COL...  18.8 us
    ppermute x5, starting transfers between devices, along_depth(): return lax.ppermute(value, 'wsh', pairs)  16.4 us
    pallas_call x1, Pallas kernels, lay_out(): pl.pallas_call(kernel, out_shape=[square, square, square, square, tall, t...  7.51 us
  transfers between devices with their start and end apart: 12, of which 0 were waited for; matrix products, arithmetic and copies ran while one was open for 0% of the time, Pallas kernels for 37%

profile of v3, /device:TPU:9, one launch (start us, length us, event | category | flops | bytes accessed | tf_op | source)
XLA Modules:
  0.0 288.9 jit_solution(1563413174830985859)
XLA Ops:
  7.2 0.0 reduce-scatter.2.cloned.1.call-start
  7.2 1.2 broadcast_in_dim.12.g1_ref
  8.5 1.2 broadcast_in_dim.13.g2_ref
  9.7 4.0 %prepare.1 = (bf16[256,768]{1,0:T(8,128)(2,1)}, bf16[288,192]{1,0:T(8,128)(2,1)}, bf16[288,768]{1,0:T(8,128)(2,1)}, f32[8,128]{1,0:T(8,128)}) custom-call(bf16[256,2,768]{2,1,0:T(2,128)(2,1)} %bitcast.19, f32[2,2]{1,0:T(2,128)} %p_ref.5, s32[1,256]{1,0:T(1,128)} %v_ref.3, bf16[1,192]{1,0:T(2,128)(2,1)} %broadcast_in_dim.12.g1_ref, ...), custom_call_target="tpu_custom_call" | custom-call | tf_op jit(solution)/shard_map/prepare/pallas_call | solution.py:850
  13.7 1.9 collective-permute-start.5
  15.6 3.4 %collective-permute-start.3 = (bf16[3,96,768]{2,1,0:T(8,128)(2,1)}, bf16[3,96,768]{2,1,0:T(8,128)(2,1)S(1)}, u32[]{:S(2)}, u32[]{:S(2)}) collective-permute-start(bf16[3,96,768]{2,1,0:T(8,128)(2,1)} %bitcast.34), channel_id=1, source_target_pairs={{0,1},{1,2},{2,3},{4,5},{5,6},{6,7},{8,9},{9,10},{10,11},{12,13},{... | collective-permute-start | bytes 1327112 | tf_op jit(solution)/shard_map/ppermute | solution.py:1775
  19.0 31.3 %gather_inputs.1 = (bf16[8,256,768]{2,1,0:T(8,128)(2,1)}, bf16[4,2,288,192]{3,2,1,0:T(8,128)(2,1)}, bf16[4,48,768]{2,1,0:T(8,128)(2,1)}, f32[8,128]{1,0:T(8,128)}) custom-call(bf16[256,768]{1,0:T(8,128)(2,1)} %get-tuple-element.60.x_ref, bf16[288,192]{1,0:T(8,128)(2,1)} %get-tuple-element.61.w_ref, bf16[192,768]{1,0:T(8,128)(2,1)} %o_ref.1, ...), custom_call_target="tpu_custom_call" | custom-call | tf_op jit(solution)/shard_map/gather_inputs/pallas_call | solution.py:999
  50.3 2.3 collective-permute-start.2
  52.6 0.7 collective-permute-start.7
  53.3 0.0 collective-permute-done.5.f3
  53.3 0.0 copy-start.2
  53.3 9.1 %collective-permute-start.6 = (bf16[3,96,768]{2,1,0:T(8,128)(2,1)S(1)}, bf16[3,96,768]{2,1,0:T(8,128)(2,1)S(1)}, u32[]{:S(2)}, u32[]{:S(2)}) collective-permute-start(bf16[3,96,768]{2,1,0:T(8,128)(2,1)S(1)} %collective-permute-done.5.f3), channel_id=1, source_target_pairs={{1,0},{2,1},{5,4},{6,5},{9,8},{10,9},{13,12},{14,13},{17,16},{18,1... | collective-permute-start | bytes 1327112 | tf_op jit(solution)/shard_map/ppermute | solution.py:1775
  62.4 0.0 copy-start.3
  62.4 1.3 collective-permute-start.4
  63.7 0.3 collective-permute-start.1
  64.0 0.0 collective-permute-done.2.o3
  64.0 0.2 collective-permute-start
  64.2 20.5 %attention_forward.1 = (bf16[1024,192]{1,0:T(8,128)(2,1)}, f32[4,192,256]{2,1,0:T(8,128)}, bf16[1024,192]{1,0:T(8,128)(2,1)}, bf16[2048,192]{1,0:T(8,128)(2,1)},...) custom-call(s32[32]{0:T(128)} %bitcast.40, s32[4]{0:T(128)} %bitcast.42, bf16[2048,768]{1,0:T(8,128)(2,1)} %bitcast.22, ...), custom_call_target="tpu_custom_call" | custom-call | flops 3221225472 | bytes 18874368 | tf_op jit(solution)/shard_map/attention_forward/pallas_call | solution.py:618
  84.8 0.0 collective-permute-done.1.o2
  84.8 0.0 collective-permute-done.7.f5
  84.8 0.0 collective-permute-done.6.f4
  84.9 0.0 copy-start.6
  84.9 0.6 copy-done.8
  85.5 0.1 copy-done.9
  85.6 0.2 copy-done.4
  85.8 0.2 copy-done.5
  86.0 0.1 copy-done.6
  86.0 89.6 %middle.1 = (bf16[256,2,768]{2,1,0:T(2,128)(2,1)}, f32[256,768]{1,0:T(8,128)}, f32[256,768]{1,0:T(8,128)}, f32[256,768]{1,0:T(8,128)}, bf16[4,256,192]{2,1,0:T(8...) custom-call(bf16[4,256,192]{2,1,0:T(8,128)(2,1)} %bitcast.31, ...), custom_call_target="tpu_custom_call" | custom-call | tf_op jit(solution)/shard_map/middle/pallas_call | solution.py:1295
  175.7 0.0 reduce-scatter.2.cloned.1.call-update
  175.7 0.9 copy-done.15
  176.6 0.1 copy-done.14
  176.7 0.2 collective-permute-start.9
  176.9 2.4 collective-permute-start.10
  179.3 18.8 %attention_backward.1 = (bf16[1024,192]{1,0:T(8,128)(2,1)}, bf16[2048,192]{1,0:T(8,128)(2,1)}, bf16[2048,192]{1,0:T(8,128)(2,1)}) custom-call(s32[32]{0:T(128)} %bitcast.41, s32[4]{0:T(128)} %bitcast.43, bf16[1024,192]{1,0:T(8,128)(2,1)} %bitcast.37, f32[4,192,256]{2,1,0:T(8,128)} %get-tuple-element.71.oT_ref, bf16[1024,192]{1,0:T(8,128)(2,1)} %get-tuple-element.72.q_ref, ...), custom_call_target="tpu_custom_call" | custom-call | flops 8053063680 | bytes 7864320 | tf_op jit(solution)/shard_map/attention_backward/pallas_call | solution.py:740
  198.1 0.0 collective-permute-done.8.o1
  198.1 0.0 copy-start.11
  198.1 0.0 collective-permute-done.10.o3
  198.1 0.0 copy-start.12
  198.1 0.7 copy-done.10
  198.8 0.1 copy-done.11
  198.9 0.1 copy-done.12
  199.0 36.4 %input_gradients.1 = (bf16[256,2,768]{2,1,0:T(2,128)(2,1)}, bf16[288,192]{1,0:T(8,128)(2,1)}, bf16[96,768]{1,0:T(8,128)(2,1)}, f32[8,768]{1,0:T(8,128)}) custom-call(bf16[4,256,192]{2,1,0:T(8,128)(2,1)} %bitcast.32, bf16[4,2,256,192]{3,2,1,0:T(8,128)(2,1)} %bitcast.25, bf16[4,2,256,192]{3,2,1,0:T(8,128)(2,1)} %bitcast.26, ...), custom_call_target="tpu_custom_call" | custom-call | tf_op jit(solution)/shard_map/input_gradients/pallas_call | solution.py:1508
  235.4 0.0 reduce-scatter.2.cloned.1.call-done.f_ref
  235.4 36.8 %gather_gradients.1 = (bf16[8,288,768]{2,1,0:T(8,128)(2,1)}, bf16[8,288,192]{2,1,0:T(8,128)(2,1)}, bf16[2,96,768]{2,1,0:T(8,128)(2,1)}, f32[8,768]{1,0:T(8,128)}) custom-call(bf16[288,768]{1,0:T(8,128)(2,1)} %reduce-scatter.2.cloned.1.call-done.f_ref, bf16[288,192]{1,0:T(8,128)(2,1)} %get-tuple-element.89.q_ref, bf16[96,768]{1,0:T(8,128)(2,1)} %get-tuple-element.90.o_ref, ...), custom_call_target="tpu_custom_call" | custom-call | tf_op jit(solution)/shard_map/gather_gradients/pallas_call | solution.py:1669
  272.3 7.5 %lay_out.1 = (f32[192,768]{1,0:T(8,128)}, f32[192,768]{1,0:T(8,128)}, f32[192,768]{1,0:T(8,128)}, f32[192,768]{1,0:T(8,128)}, f32[192,3072]{1,0:T(8,128)}, /*ind...) custom-call(bf16[8,288,768]{2,1,0:T(8,128)(2,1)} %get-tuple-element., ...), custom_call_target="tpu_custom_call" | custom-call | tf_op jit(solution)/shard_map/lay_out/pallas_call | solution.py:1740
  279.8 0.9 copy.32
  280.7 0.5 copy-done.1
  281.2 0.9 copy.33
  (21 shorter events, 0.0 us)
Async XLA Ops:
  7.2 228.2 %reduce-scatter.2.cloned.1.call-start = ((), (), s32[]{:S(2)}) async-start(), calls=%async_computation.1 | async-start | bytes 2211840 | tf_op jit(solution)/shard_map/reduce_scatter | solution.py:1805
  13.7 39.6 %collective-permute-start.5 = (bf16[3,96,768]{2,1,0:T(8,128)(2,1)}, bf16[3,96,768]{2,1,0:T(8,128)(2,1)S(1)}, u32[]{:S(2)}, u32[]{:S(2)}) collective-permute-start(bf16[3,96,768]{2,1,0:T(8,128)(2,1)} %bitcast.33), channel_id=1, source_target_pairs={{1,0},{2,1},{3,2},{5,4},{6,5},{7,6},{9,8},{10,9},{11,10},{13,12},{... | collective-permute-start | bytes 1327112 | tf_op jit(solution)/shard_map/ppermute | solution.py:1775
  15.6 46.8 %collective-permute-start.3 = (bf16[3,96,768]{2,1,0:T(8,128)(2,1)}, bf16[3,96,768]{2,1,0:T(8,128)(2,1)S(1)}, u32[]{:S(2)}, u32[]{:S(2)}) collective-permute-start(bf16[3,96,768]{2,1,0:T(8,128)(2,1)} %bitcast.34), channel_id=1, source_target_pairs={{0,1},{1,2},{2,3},{4,5},{5,6},{6,7},{8,9},{9,10},{10,11},{12,13},{... | collective-permute-start | bytes 1327112 | tf_op jit(solution)/shard_map/ppermute | solution.py:1775
  50.3 13.8 %collective-permute-start.2 = (bf16[4,48,768]{2,1,0:T(8,128)(2,1)}, bf16[4,48,768]{2,1,0:T(8,128)(2,1)S(1)}, u32[]{:S(2)}, u32[]{:S(2)}) collective-permute-start(bf16[4,48,768]{2,1,0:T(8,128)(2,1)} %get-tuple-element.66.o0), channel_id=1, source_target_pairs={{0,24},{4,28},{8,16},{12,20},{16,8},{20,12},{24,0},{28,4},{1,25},{... | collective-permute-start | bytes 884744 | tf_op jit(solution)/shard_map/ppermute | solution.py:1779
  52.6 32.3 %collective-permute-start.7 = (bf16[3,96,768]{2,1,0:T(8,128)(2,1)}, bf16[3,96,768]{2,1,0:T(8,128)(2,1)S(1)}, u32[]{:S(2)}, u32[]{:S(2)}) collective-permute-start(bf16[3,96,768]{2,1,0:T(8,128)(2,1)} %bitcast.35), channel_id=1, source_target_pairs={{0,3},{3,0},{4,7},{7,4},{8,11},{11,8},{12,15},{15,12},{16,19},{19,... | collective-permute-start | bytes 1327112 | tf_op jit(solution)/shard_map/ppermute | solution.py:1775
  53.3 31.5 %copy-start.2 = (bf16[3,96,768]{2,1,0:T(8,128)(2,1)}, bf16[3,96,768]{2,1,0:T(8,128)(2,1)S(1)}, u32[]{:S(2)}) copy-start(bf16[3,96,768]{2,1,0:T(8,128)(2,1)S(1)} %collective-permute-done.5.f3) | copy-start | bytes 1327108
  53.3 31.6 %collective-permute-start.6 = (bf16[3,96,768]{2,1,0:T(8,128)(2,1)S(1)}, bf16[3,96,768]{2,1,0:T(8,128)(2,1)S(1)}, u32[]{:S(2)}, u32[]{:S(2)}) collective-permute-start(bf16[3,96,768]{2,1,0:T(8,128)(2,1)S(1)} %collective-permute-done.5.f3), channel_id=1, source_target_pairs={{1,0},{2,1},{5,4},{6,5},{9,8},{10,9},{13,12},{14,13},{17,16},{18,1... | collective-permute-start | bytes 1327112 | tf_op jit(solution)/shard_map/ppermute | solution.py:1775
  62.4 22.4 %copy-start.3 = (bf16[3,96,768]{2,1,0:T(8,128)(2,1)}, bf16[3,96,768]{2,1,0:T(8,128)(2,1)S(1)}, u32[]{:S(2)}) copy-start(bf16[3,96,768]{2,1,0:T(8,128)(2,1)S(1)} %collective-permute-done.3.f1) | copy-start | bytes 1327108
  62.4 22.4 %collective-permute-start.4 = (bf16[3,96,768]{2,1,0:T(8,128)(2,1)S(1)}, bf16[3,96,768]{2,1,0:T(8,128)(2,1)S(1)}, u32[]{:S(2)}, u32[]{:S(2)}) collective-permute-start(bf16[3,96,768]{2,1,0:T(8,128)(2,1)S(1)} %collective-permute-done.3.f1), channel_id=1, source_target_pairs={{1,2},{2,3},{5,6},{6,7},{9,10},{10,11},{13,14},{14,15},{17,18},{18... | collective-permute-start | bytes 1327112 | tf_op jit(solution)/shard_map/ppermute | solution.py:1775
  63.7 21.0 %collective-permute-start.1 = (bf16[4,48,768]{2,1,0:T(8,128)(2,1)}, bf16[4,48,768]{2,1,0:T(8,128)(2,1)S(1)}, u32[]{:S(2)}, u32[]{:S(2)}) collective-permute-start(bf16[4,48,768]{2,1,0:T(8,128)(2,1)} %get-tuple-element.66.o0), channel_id=1, source_target_pairs={{0,16},{4,20},{8,24},{12,28},{16,0},{20,4},{24,8},{28,12},{1,17},{... | collective-permute-start | bytes 884744 | tf_op jit(solution)/shard_map/ppermute | solution.py:1779
  64.0 20.7 %copy-start.7 = (bf16[4,48,768]{2,1,0:T(8,128)(2,1)}, bf16[4,48,768]{2,1,0:T(8,128)(2,1)S(1)}, u32[]{:S(2)}) copy-start(bf16[4,48,768]{2,1,0:T(8,128)(2,1)S(1)} %collective-permute-done.2.o3) | copy-start | bytes 884740
  64.0 20.8 %collective-permute-start = (bf16[4,48,768]{2,1,0:T(8,128)(2,1)}, bf16[4,48,768]{2,1,0:T(8,128)(2,1)S(1)}, u32[]{:S(2)}, u32[]{:S(2)}) collective-permute-start(bf16[4,48,768]{2,1,0:T(8,128)(2,1)} %get-tuple-element.66.o0), channel_id=1, source_target_pairs={{0,8},{4,12},{8,0},{12,4},{16,24},{20,28},{24,16},{28,20},{1,9},{5... | collective-permute-start | bytes 884744 | tf_op jit(solution)/shard_map/ppermute | solution.py:1779
  84.8 0.7 copy-start.8
  84.8 0.8 copy-start.9
  84.8 1.0 copy-start.4
  84.9 1.1 copy-start.5
  84.9 1.2 copy-start.6
  175.7 1.0 copy-start.15
  175.7 1.0 copy-start.14
  175.7 1.2 copy-start.13
  176.6 21.5 %collective-permute-start.8 = (bf16[192,768]{1,0:T(8,128)(2,1)S(1)}, bf16[192,768]{1,0:T(8,128)(2,1)S(1)}, u32[]{:S(2)}, u32[]{:S(2)}) collective-permute-start(bf16[192,768]{1,0:T(8,128)(2,1)S(1)} %copy-done.15), channel_id=1, source_target_pairs={{0,8},{4,12},{8,0},{12,4},{16,24},{20,28},{24,16},{28,20},{1,9},{5... | collective-permute-start | bytes 884744 | tf_op jit(solution)/shard_map/ppermute | solution.py:1779
  176.7 21.4 %collective-permute-start.9 = (bf16[192,768]{1,0:T(8,128)(2,1)S(1)}, bf16[192,768]{1,0:T(8,128)(2,1)S(1)}, u32[]{:S(2)}, u32[]{:S(2)}) collective-permute-start(bf16[192,768]{1,0:T(8,128)(2,1)S(1)} %copy-done.14), channel_id=1, source_target_pairs={{0,16},{4,20},{8,24},{12,28},{16,0},{20,4},{24,8},{28,12},{1,17},{... | collective-permute-start | bytes 884744 | tf_op jit(solution)/shard_map/ppermute | solution.py:1779
  176.9 21.2 %collective-permute-start.10 = (bf16[192,768]{1,0:T(8,128)(2,1)S(1)}, bf16[192,768]{1,0:T(8,128)(2,1)S(1)}, u32[]{:S(2)}, u32[]{:S(2)}) collective-permute-start(bf16[192,768]{1,0:T(8,128)(2,1)S(1)} %copy-done.13), channel_id=1, source_target_pairs={{0,24},{4,28},{8,16},{12,20},{16,8},{20,12},{24,0},{28,4},{1,25},{... | collective-permute-start | bytes 884744 | tf_op jit(solution)/shard_map/ppermute | solution.py:1779
  198.1 0.7 copy-start.10
  198.1 0.8 copy-start.11
  198.1 0.9 copy-start.12
  272.2 7.5 %copy-start = (bf16[256,2,768]{2,1,0:T(2,128)(2,1)S(1)}, bf16[256,2,768]{2,1,0:T(2,128)(2,1)}, u32[]{:S(2)}) copy-start(bf16[256,2,768]{2,1,0:T(2,128)(2,1)} %get-tuple-element.69) | copy-start | bytes 2359300
  279.8 1.4 copy-start.1
Sparse Core Ops, SparseCore 0:
  175.8 38.8 reduce-scatter.1

commit v4 on v3

--- a/solution.py
+++ b/solution.py
@@ -425,11 +425,14 @@
     return depth, chip, core, chip_x, chip_y, 3 - chip
 
 
-def signal_and_wait(devices):
+def signal_all(devices):
     barrier = pltpu.get_barrier_semaphore()
     for device in devices:
         pl.semaphore_signal(barrier, inc=1, device_id=device, device_id_type=MESH)
-    pl.semaphore_wait(barrier, len(devices))
+
+
+def wait_all(devices):
+    pl.semaphore_wait(pltpu.get_barrier_semaphore(), len(devices))
 
 
 def remote(src, dst, send, recv, index, device):
@@ -470,7 +473,9 @@
 
 
 NT = (((1,), (1,)), ((), ()))
+TN = (((0,), (0,)), ((), ()))
 TILE = 256
+ROWS = 32
 LOCAL_HEADS = HEADS // CHIPS
 CHIP_COLS = LOCAL_HEADS * HD
 
@@ -480,296 +485,10 @@
     return (lane >= head * HD) & (lane < (head + 1) * HD)
 
 
-def spread_rows(pieces, target):
-    depths, cores, rows, _ = pieces.shape
-    half = rows // target.shape[0]
-    for i in range(target.shape[0]):
-        for z in range(depths):
-            for c in range(cores):
-                at = (z * cores + c) * half
-                target[i, at : at + half, :] = pieces[z, c, i * half : (i + 1) * half, :]
-
-
 def aligned(index, size):
     return pl.ds(pl.multiple_of(index * size, size), size)
 
 
-def pair_blocks(slots_ref, pair, per_device):
-    core = lax.axis_index("ctx") % 2
-    pairs = per_device // 2
-    slot = (pair // pairs) * (2 * per_device) + core * per_device + 2 * (pair % pairs)
-    one, two = slots_ref[slot], slots_ref[slot + 1]
-    second = (one >= PROMPT // BLK).astype(jnp.int32)
-    return slot, second, jnp.minimum(one, two), jnp.maximum(one, two)
-
-
-def tile_tables(kind, step, slots_ref, lengths_ref, per_device):
-    lane = lax.broadcasted_iota(jnp.int32, (1, TILE), 1)
-    high = jnp.zeros((1, TILE), jnp.int32)
-    local = []
-    per_tile = TILE // BLK
-    for i in range(per_tile):
-        pair = step * per_tile + i
-        _, second, prompt, cont = pair_blocks(slots_ref, pair, per_device)
-        block = prompt if kind == 0 else cont
-        local.append(2 * pair + (second if kind == 0 else 1 - second))
-        high = jnp.where(lane >= i * BLK, (block - i) * BLK + lane, high)
-    low = jnp.zeros((1, TILE), jnp.int32)
-    if kind == 1:
-        start = PROMPT
-        for i in range(lengths_ref.shape[0]):
-            low = jnp.where(high >= start, start, low)
-            start = start + lengths_ref[i]
-    return local, low, high
-
-
-def attention_forward(all_rows, weights, slots, lengths):
-    tokens, width = all_rows.shape
-    queries = tokens // 2
-    tiles = queries // TILE
-    blocks = tokens // BLK
-    per_device = blocks // (2 * CHIPS)
-
-    def kernel(
-        slots_ref, lengths_ref, x_ref, w_ref,
-        att_ref, oT_ref, q_ref, k_ref, v_ref, lse_ref, slot_of, w_all, xs, xq, vT, s_ref, p_ref,
-    ):
-        def place_slot(s, _):
-            slot_of[slots_ref[s]] = s
-            return 0
-
-        lax.fori_loop(0, blocks, place_slot, 0)
-        spread_rows(w_ref, w_all)
-        def gather_block(b, _):
-            xs[aligned(b, BLK), :] = x_ref[aligned(slot_of[b], BLK), :]
-            return 0
-
-        lax.fori_loop(0, blocks, gather_block, 0)
-
-        def gather_query(pair, _):
-            slot, second, _, _ = pair_blocks(slots_ref, pair, per_device)
-            xq[aligned(pair, BLK), :] = x_ref[aligned(slot + second, BLK), :]
-            xq[aligned(pair + queries // (2 * BLK), BLK), :] = x_ref[
-                aligned(slot + 1 - second, BLK), :
-            ]
-            return 0
-
-        lax.fori_loop(0, queries // (2 * BLK), gather_query, 0)
-
-        def project_keys(i, _):
-            rows = aligned(i, TILE)
-            x = xs[rows, :]
-            k_ref[rows, :] = jnp.dot(x, w_all[1], preferred_element_type=F32).astype(BF16)
-            v = jnp.dot(x, w_all[2], preferred_element_type=F32).astype(BF16)
-            v_ref[rows, :] = v
-            vT[:, rows] = v.T
-            return 0
-
-        lax.fori_loop(0, tokens // TILE, project_keys, 0)
-
-        def project_queries(i, _):
-            rows = aligned(i, TILE)
-            q_ref[rows, :] = jnp.dot(xq[rows, :], w_all[0], preferred_element_type=F32).astype(BF16)
-            return 0
-
-        lax.fori_loop(0, tiles, project_queries, 0)
-
-        for kind in range(2):
-            key_tiles = (PROMPT if kind == 0 else tokens) // TILE
-            first_masked = 0 if kind == 0 else PROMPT // TILE
-
-            def one_tile(step, _):
-                tile = kind * (tiles // 2) + step
-                q = q_ref[aligned(tile, TILE), :]
-                local, q_low, q_high = tile_tables(kind, step, slots_ref, lengths_ref, per_device)
-                for head in range(LOCAL_HEADS):
-                    q_head = jnp.where(head_mask(TILE, head), q, jnp.zeros_like(q))
-                    top = jnp.full((1, TILE), NEGATIVE, F32)
-                    for k_tile in range(key_tiles):
-                        rows = pl.ds(k_tile * TILE, TILE)
-                        s = lax.dot_general(k_ref[rows, :], q_head, NT, preferred_element_type=F32)
-                        if k_tile >= first_masked:
-                            place = lax.broadcasted_iota(jnp.int32, (TILE, TILE), 0) + k_tile * TILE
-                            seen = (place >= q_low) & (place <= q_high)
-                            s = jnp.where(seen, s, NEGATIVE)
-                        s_ref[rows, :] = s
-                        top = jnp.maximum(top, jnp.max(s, axis=0, keepdims=True))
-                    total = jnp.zeros((1, TILE), F32)
-                    for k_tile in range(key_tiles):
-                        rows = pl.ds(k_tile * TILE, TILE)
-                        p = jnp.exp(s_ref[rows, :] - top)
-                        total = total + jnp.sum(p, axis=0, keepdims=True)
-                        p_ref[rows, :] = p.astype(BF16)
-                    keys = key_tiles * TILE
-                    out = jnp.dot(
-                        vT[head * HD : (head + 1) * HD, :keys],
-                        p_ref[:keys, :],
-                        preferred_element_type=F32,
-                    )
-                    oT_ref[tile, head * HD : (head + 1) * HD, :] = out / total
-                    lse_ref[tile, head] = top + jnp.log(total)
-                att = oT_ref[tile].T.astype(BF16)
-                for b in range(TILE // BLK):
-                    att_ref[aligned(local[b], BLK), :] = att[b * BLK : (b + 1) * BLK]
-                return 0
-
-            lax.fori_loop(0, tiles // 2, one_tile, 0)
-
-    return pl.pallas_call(
-        kernel,
-        out_shape=[
-            jax.ShapeDtypeStruct((queries, CHIP_COLS), BF16),
-            jax.ShapeDtypeStruct((tiles, CHIP_COLS, TILE), F32),
-            jax.ShapeDtypeStruct((queries, CHIP_COLS), BF16),
-            jax.ShapeDtypeStruct((tokens, CHIP_COLS), BF16),
-            jax.ShapeDtypeStruct((tokens, CHIP_COLS), BF16),
-            jax.ShapeDtypeStruct((tiles, LOCAL_HEADS, 1, TILE), F32),
-        ],
-        in_specs=[SM, SM, VM, VM],
-        out_specs=[VM] * 6,
-        scratch_shapes=[
-            pltpu.SMEM((blocks,), jnp.int32),
-            pltpu.VMEM((3, width, CHIP_COLS), BF16),
-            pltpu.VMEM((tokens, width), BF16),
-            pltpu.VMEM((queries, width), BF16),
-            pltpu.VMEM((CHIP_COLS, tokens), BF16),
-            pltpu.VMEM((tokens, TILE), F32),
-            pltpu.VMEM((tokens, TILE), BF16),
-        ],
-        compiler_params=pltpu.CompilerParams(vmem_limit_bytes=VMEM_LIMIT),
-        cost_estimate=pl.CostEstimate(
-            flops=8 * queries * tokens * CHIP_COLS, bytes_accessed=12 * tokens * width, transcendentals=queries * tokens
-        ),
-        name="attention_forward",
-    )(slots, lengths, all_rows, weights)
-
-
-def attention_backward(att_grad, saved, slots, lengths):
-    oT, q, k, v, lse = saved
-    queries = att_grad.shape[0]
-    tokens = k.shape[0]
-    tiles = queries // TILE
-    blocks = tokens // BLK
-    per_device = blocks // (2 * CHIPS)
-    wide = LOCAL_HEADS * TILE
-
-    def kernel(
-        slots_ref, lengths_ref, g_ref, oT_ref, q_ref, k_ref, v_ref, lse_ref,
-        dq_ref, dk_ref, dv_ref, hq, kT, doT, dqT, q_stack, do_stack, p_buf, ds_buf, dk_acc, dv_acc,
-    ):
-        def gather_query(pair, _):
-            _, second, _, _ = pair_blocks(slots_ref, pair, per_device)
-            hq[aligned(pair, BLK), :] = g_ref[aligned(2 * pair + second, BLK), :]
-            hq[aligned(pair + queries // (2 * BLK), BLK), :] = g_ref[
-                aligned(2 * pair + 1 - second, BLK), :
-            ]
-            return 0
-
-        lax.fori_loop(0, queries // (2 * BLK), gather_query, 0)
-
-        def transpose_keys(i, _):
-            rows = aligned(i, TILE)
-            kT[:, rows] = k_ref[rows, :].T
-            return 0
-
-        lax.fori_loop(0, tokens // TILE, transpose_keys, 0)
-
-        for kind in (1, 0):
-            key_tiles = (PROMPT if kind == 0 else tokens) // TILE
-            first_masked = 0 if kind == 0 else PROMPT // TILE
-
-            def one_tile(step, _):
-                tile = kind * (tiles // 2) + step
-                q_tile = q_ref[aligned(tile, TILE), :]
-                local, q_low, q_high = tile_tables(kind, step, slots_ref, lengths_ref, per_device)
-                do_tile = hq[aligned(tile, TILE), :]
-                doT[...] = do_tile.astype(F32).T * oT_ref[tile]
-                for head in range(LOCAL_HEADS):
-                    lanes = pl.ds(head * TILE, TILE)
-                    heads = pl.ds(head * HD, HD)
-                    mask = head_mask(TILE, head)
-                    q_head = jnp.where(mask, q_tile, jnp.zeros_like(q_tile))
-                    do_head = jnp.where(mask, do_tile, jnp.zeros_like(do_tile))
-                    q_stack[lanes, :] = q_head
-                    do_stack[lanes, :] = do_head
-                    delta = jnp.sum(doT[heads, :], axis=0, keepdims=True)
-                    norm = lse_ref[tile, head]
-                    for k_tile in range(key_tiles):
-                        rows = pl.ds(k_tile * TILE, TILE)
-                        s = lax.dot_general(k_ref[rows, :], q_head, NT, preferred_element_type=F32)
-                        dp = lax.dot_general(v_ref[rows, :], do_head, NT, preferred_element_type=F32)
-                        p = jnp.exp(s - norm)
-                        if k_tile >= first_masked:
-                            place = lax.broadcasted_iota(jnp.int32, (TILE, TILE), 0) + k_tile * TILE
-                            seen = (place >= q_low) & (place <= q_high)
-                            p = jnp.where(seen, p, 0.0)
-                        p_buf[rows, lanes] = p.astype(BF16)
-                        ds_buf[rows, lanes] = (p * (dp - delta)).astype(BF16)
-                    keys = key_tiles * TILE
-                    dqT[heads, :] = jnp.dot(
-                        kT[heads, :keys], ds_buf[:keys, lanes], preferred_element_type=F32
-                    )
-                for k_tile in range(key_tiles):
-                    rows = pl.ds(k_tile * TILE, TILE)
-                    dv = jnp.dot(p_buf[rows, :], do_stack[...], preferred_element_type=F32)
-                    dk = jnp.dot(ds_buf[rows, :], q_stack[...], preferred_element_type=F32)
-                    if kind == 1:
-                        fresh = step == 0
-                        dv = dv + jnp.where(fresh, 0.0, dv_acc[rows, :])
-                        dk = dk + jnp.where(fresh, 0.0, dk_acc[rows, :])
-                    else:
-                        dv = dv + dv_acc[rows, :]
-                        dk = dk + dk_acc[rows, :]
-                    dv_acc[rows, :] = dv
-                    dk_acc[rows, :] = dk
-                dq = dqT[...].T.astype(BF16)
-                for b in range(TILE // BLK):
-                    dq_ref[aligned(local[b], BLK), :] = dq[b * BLK : (b + 1) * BLK]
-                return 0
-
-            lax.fori_loop(0, tiles // 2, one_tile, 0)
-
-        def give_block(slot, _):
-            block = aligned(slots_ref[slot], BLK)
-            dk_ref[aligned(slot, BLK), :] = dk_acc[block, :].astype(BF16)
-            dv_ref[aligned(slot, BLK), :] = dv_acc[block, :].astype(BF16)
-            return 0
-
-        lax.fori_loop(0, blocks, give_block, 0)
-
-    return pl.pallas_call(
-        kernel,
-        out_shape=[
-            jax.ShapeDtypeStruct((queries, CHIP_COLS), BF16),
-            jax.ShapeDtypeStruct((tokens, CHIP_COLS), BF16),
-            jax.ShapeDtypeStruct((tokens, CHIP_COLS), BF16),
-        ],
-        in_specs=[SM, SM] + [VM] * 6,
-        out_specs=[VM] * 3,
-        scratch_shapes=[
-            pltpu.VMEM((queries, CHIP_COLS), BF16),
-            pltpu.VMEM((CHIP_COLS, tokens), BF16),
-            pltpu.VMEM((CHIP_COLS, TILE), F32),
-            pltpu.VMEM((CHIP_COLS, TILE), F32),
-            pltpu.VMEM((wide, CHIP_COLS), BF16),
-            pltpu.VMEM((wide, CHIP_COLS), BF16),
-            pltpu.VMEM((tokens, wide), BF16),
-            pltpu.VMEM((tokens, wide), BF16),
-            pltpu.VMEM((tokens, CHIP_COLS), F32),
-            pltpu.VMEM((tokens, CHIP_COLS), F32),
-        ],
-        compiler_params=pltpu.CompilerParams(vmem_limit_bytes=VMEM_LIMIT),
-        cost_estimate=pl.CostEstimate(
-            flops=20 * queries * tokens * CHIP_COLS, bytes_accessed=20 * tokens * CHIP_COLS, transcendentals=queries * tokens
-        ),
-        name="attention_backward",
-    )(slots, lengths, att_grad, oT, q, k, v, lse)
-
-
-TN = (((0,), (0,)), ((), ()))
-ROWS = 32
-
-
 def norm_factor(rows):
     return lax.rsqrt(jnp.mean(rows * rows, axis=1, keepdims=True) + EPSILON)
 
@@ -780,91 +499,6 @@
 
 def mix(states_ref, at, p_ref, i):
     return p_ref[i, 0] * states_ref[at, 0, :].astype(F32) + p_ref[i, 1] * states_ref[at, 1, :].astype(F32)
-
-
-def prepare(states, predict, valid, gain_one, gain_two, w_query, w_key, w_value, w_gate, w_up, w_down):
-    rows, _, width = states.shape
-    shard = w_query.shape[0]
-    half = shard // 2
-    hidden_cols = w_gate.shape[1]
-    columns = hidden_cols // CHIPS
-    depths = width // shard
-    split = columns // depths
-
-    def kernel(
-        s_ref, p_ref, v_ref, g1_ref, g2_ref, q_ref, k_ref, vw_ref, gate_ref, up_ref, down_ref,
-        pre_ref, qkv_ref, ff_ref, count_ref, buf, wide, sems,
-    ):
-        _, chip, core, _, _, _ = place_on_mesh()
-        mine = pl.ds(core * half, half)
-        loads = [
-            pltpu.make_async_copy(w.at[mine], buf.at[i], sems.at[i])
-            for i, w in enumerate((q_ref, k_ref, vw_ref))
-        ] + [
-            pltpu.make_async_copy(gate_ref.at[mine], wide.at[0], sems.at[3]),
-            pltpu.make_async_copy(up_ref.at[mine], wide.at[1], sems.at[4]),
-            pltpu.make_async_copy(
-                down_ref.at[pl.ds(chip * split + core * (split // 2), half)],
-                ff_ref.at[pl.ds(2 * half, half)],
-                sems.at[5],
-            ),
-        ]
-        for copy in loads:
-            copy.start()
-        count_ref[...] = jnp.broadcast_to(
-            jnp.sum(v_ref[...].astype(F32), axis=1, keepdims=True), count_ref.shape
-        )
-
-        def norm(i, _):
-            at = aligned(i, ROWS)
-            active = mix(s_ref, at, p_ref, 0)
-            pre_ref[at, :] = (active * norm_factor(active)).astype(BF16)
-            return 0
-
-        lax.fori_loop(0, rows // ROWS, norm, 0)
-
-        def gain_column(ref):
-            both = jnp.broadcast_to(ref[...].astype(F32), (8, shard)).T
-            return jnp.where(core == 0, both[:half, 0:1], both[half:, 0:1])
-
-        one, two = gain_column(g1_ref), gain_column(g2_ref)
-        for copy in loads:
-            copy.wait()
-        for p in range(CHIPS):
-
-            @pl.when(chip == p)
-            def _(p=p):
-                for i in range(3):
-                    cols = buf[i, :, p * CHIP_COLS : (p + 1) * CHIP_COLS]
-                    qkv_ref[i * half : (i + 1) * half, :] = (cols.astype(F32) * one).astype(BF16)
-                for i in range(2):
-                    cols = jnp.concatenate(
-                        [
-                            wide[i, :, (z * CHIPS + p) * split : (z * CHIPS + p + 1) * split].astype(F32)
-                            for z in range(depths)
-                        ],
-                        axis=1,
-                    )
-                    ff_ref[i * half : (i + 1) * half, :] = (cols * two).astype(BF16)
-
-    return pl.pallas_call(
-        kernel,
-        out_shape=[
-            jax.ShapeDtypeStruct((rows, width), BF16),
-            jax.ShapeDtypeStruct((3 * half, CHIP_COLS), BF16),
-            jax.ShapeDtypeStruct((3 * half, columns), BF16),
-            jax.ShapeDtypeStruct((8, 128), F32),
-        ],
-        in_specs=[VM, SM] + [VM] * 3 + [ANY] * 6,
-        out_specs=[VM] * 4,
-        scratch_shapes=[
-            pltpu.VMEM((3, half, width), BF16),
-            pltpu.VMEM((2, half, hidden_cols), BF16),
-            DMA((6,)),
-        ],
-        compiler_params=pltpu.CompilerParams(vmem_limit_bytes=VMEM_LIMIT),
-        name="prepare",
-    )(states, predict, valid, gain_one, gain_two, w_query, w_key, w_value, w_gate, w_up, w_down)
 
 
 def plane_peers(chip, core, depth, chip_x, chip_y, chip_d):
@@ -915,114 +549,6 @@
     ]
 
 
-def gather_inputs(pre, qkv, w_out, count, collective_id):
-    depths = lax.axis_size("wsh")
-    out_rows = w_out.shape[0] // CHIPS
-
-    def kernel(
-        x_ref, w_ref, o_ref, c_ref, out_ref, wall_ref, oall_ref, total_ref,
-        send, recv, wsend, wrecv, osend, orecv, ssend, srecv, local, *total_refs,
-    ):
-        depth, chip, core, chip_x, chip_y, chip_d = place_on_mesh()
-        other = (2 * chip + 1 - core, depth)
-        across = [
-            (2 * chip + core, lax.rem(depth + step, depths)) for step in range(1, depths)
-        ]
-        peers = plane_peers(chip, core, depth, chip_x, chip_y, chip_d)
-        signal_and_wait(peers + across)
-
-        def slot(chip_index):
-            return 2 * chip_index + core
-
-        start, turn, end = total_over_mesh(c_ref, *total_refs[:3], across, peers, *total_refs[3:])
-        start()
-        copies = ring_sends(
-            x_ref, out_ref, slot, chip, core, depth, chip_x, chip_y, send, recv
-        )
-        for copy in copies[:4]:
-            copy.start()
-        w_copies = [
-            remote(w_ref, wall_ref.at[depth, core], wsend, wrecv, i, device)
-            for i, device in enumerate(across)
-        ]
-        out_mine = o_ref.at[pl.ds(chip * out_rows, out_rows)]
-        o_copies = [
-            remote(out_mine, oall_ref.at[depth], osend, orecv, i, device)
-            for i, device in enumerate(across)
-        ]
-        for copy in w_copies + o_copies:
-            copy.start()
-
-        def shared(index, ref, source=None):
-            return remote(ref if source is None else source, ref, ssend, srecv, index, other)
-
-        to_other = [
-            shared(0, out_ref.at[slot(chip)], x_ref),
-            shared(1, out_ref.at[slot(chip_x)]),
-            shared(2, out_ref.at[slot(chip_y)]),
-            shared(3, out_ref.at[slot(chip_d)]),
-            shared(4, wall_ref.at[depth, core], w_ref),
-        ] + [
-            shared(5 + i, wall_ref.at[lax.rem(depth + depths - 1 - i, depths), core])
-            for i in range(depths - 1)
-        ]
-        to_other[0].start()
-        to_other[4].start()
-        mine = pltpu.make_async_copy(x_ref, out_ref.at[slot(chip)], local)
-        mine.start()
-        wall_ref[depth, core] = w_ref[...]
-        oall_ref[depth] = o_ref[aligned(chip, out_rows), :]
-        turn()
-        copies[0].wait_recv()
-        copies[4].start()
-        copies[1].wait_recv()
-        copies[5].start()
-        for i in range(depths - 1):
-            w_copies[i].wait_recv()
-            to_other[5 + i].start()
-        copies[2].wait_recv()
-        to_other[1].start()
-        copies[3].wait_recv()
-        to_other[2].start()
-        copies[4].wait_recv()
-        copies[5].wait_recv()
-        to_other[3].start()
-        for copy in o_copies:
-            copy.wait_recv()
-        total_ref[...] = end()
-        for copy in to_other:
-            copy.wait()
-        for copy in copies + w_copies + o_copies:
-            copy.wait_send()
-        mine.wait()
-
-    return pl.pallas_call(
-        kernel,
-        out_shape=[
-            jax.ShapeDtypeStruct((2 * CHIPS,) + pre.shape, BF16),
-            jax.ShapeDtypeStruct((depths, 2) + qkv.shape, BF16),
-            jax.ShapeDtypeStruct((depths, out_rows, w_out.shape[1]), BF16),
-            jax.ShapeDtypeStruct(count.shape, F32),
-        ],
-        in_specs=[VM] * 4,
-        out_specs=[ANY, VM, VM, VM],
-        scratch_shapes=[
-            DMA((6,)),
-            DMA((6,)),
-            DMA((depths - 1,)),
-            DMA((depths - 1,)),
-            DMA((depths - 1,)),
-            DMA((depths - 1,)),
-            DMA((depths + 4,)),
-            DMA((depths + 4,)),
-            DMA,
-        ]
-        + total_scratch(count.shape, depths),
-        compiler_params=comm_params(collective_id),
-        name="gather_inputs",
-    )(pre, qkv, w_out, count)
-
-
 def gelu_parts(v):
     scale = math.sqrt(2 / math.pi)
     square = v * v
@@ -1031,106 +557,454 @@
     return v * rise, rise + 0.5 * v * (1.0 - t * t) * scale * (1.0 + 0.134145 * square)
 
 
-def middle(attended, out_pieces, ff_pieces, states, out_grad, teacher, valid, count, predict, correct, collective_id):
+def pair_places(slots_ref, pair):
+    one, two = slots_ref[2 * pair], slots_ref[2 * pair + 1]
+    second = (one >= PROMPT // BLK).astype(jnp.int32)
+    return second, jnp.minimum(one, two), jnp.maximum(one, two)
+
+
+def own_pair(pair, per_device):
+    core = lax.axis_index("ctx") % 2
+    pairs = per_device // 2
+    return (pair // pairs) * per_device + core * pairs + pair % pairs
+
+
+PER_TILE = TILE // BLK
+
+
+def fill_bias(bias, kind, tile_step, slots_ref, lengths_ref, per_device, group_pairs):
+    lane = lax.broadcasted_iota(jnp.int32, (1, TILE), 1)
+    high = jnp.zeros((1, TILE), jnp.int32)
+    for i in range(PER_TILE):
+        _, prompt, cont = pair_places(slots_ref, own_pair(tile_step * PER_TILE + i, per_device))
+        block = prompt if kind == 0 else cont
+        high = jnp.where(lane >= i * BLK, (block - i) * BLK + lane, high)
+    low = jnp.zeros((1, TILE), jnp.int32)
+    if kind == 1:
+        start = PROMPT
+        for i in range(lengths_ref.shape[0]):
+            low = jnp.where(high >= start, start, low)
+            start = start + lengths_ref[i]
+    offset = lax.broadcasted_iota(jnp.int32, (BLK, TILE), 0)
+
+    def one_block(pair, _):
+        _, prompt, cont = pair_places(slots_ref, pair)
+        base = (prompt if kind == 0 else cont) * BLK
+        seen = offset <= high - base
+        if kind == 1:
+            seen = seen & (offset >= low - base)
+        bias[pair // PER_TILE, aligned(pair % PER_TILE, BLK), 0:TILE] = jnp.where(seen, 0.0, NEGATIVE)
+        return 0
+
+    lax.fori_loop(0, group_pairs, one_block, 0)
+
+
+def either(second, one, two):
+    swap = second == 1
+    return jnp.where(swap, two, one), jnp.where(swap, one, two)
+
+
+def to_pair_order(source, target, slots_ref, group_pairs):
+    def one_pair(pair, _):
+        second, _, _ = pair_places(slots_ref, pair)
+        first, last = either(second, source[aligned(2 * pair, BLK), :], source[aligned(2 * pair + 1, BLK), :])
+        target[aligned(pair, BLK), :] = first
+        target[aligned(group_pairs + pair, BLK), :] = last
+        return 0
+
+    lax.fori_loop(0, group_pairs, one_pair, 0)
+
+
+def own_to_pair_order(source, target, slots_ref, pairs, per_device):
+    def one_pair(pair, _):
+        second, _, _ = pair_places(slots_ref, own_pair(pair, per_device))
+        first, last = either(second, source[aligned(2 * pair, BLK), :], source[aligned(2 * pair + 1, BLK), :])
+        target[aligned(pair, BLK), :] = first
+        target[aligned(pairs + pair, BLK), :] = last
+        return 0
+
+    lax.fori_loop(0, pairs, one_pair, 0)
+
+
+def own_to_slot_order(source, target, slots_ref, pairs, per_device):
+    def one_pair(pair, _):
+        second, _, _ = pair_places(slots_ref, own_pair(pair, per_device))
+        first, last = either(second, source[aligned(pair, BLK), :], source[aligned(pairs + pair, BLK), :])
+        target[aligned(2 * pair, BLK), :] = first
+        target[aligned(2 * pair + 1, BLK), :] = last
+        return 0
+
+    lax.fori_loop(0, pairs, one_pair, 0)
+
+
+def forward(
+    slots, lengths, predict, correct, states, out_grad, teacher, valid, gain_one, gain_two,
+    w_query, w_key, w_value, w_out, w_gate, w_up, w_down, collective_id,
+):
     rows, _, width = states.shape
-    _, half, columns = ff_pieces[0].shape
-    depths, out_rows, _ = out_pieces[0].shape
-    shard = 2 * half
+    shard = w_query.shape[0]
+    half = shard // 2
+    depths = width // shard
+    hidden_cols = w_gate.shape[1]
+    columns = hidden_cols // CHIPS
+    split = columns // depths
+    out_rows = shard // CHIPS
     blocks = rows // ROWS
     col_tiles = columns // TILE
-    tokens = 2 * CHIPS * rows * depths
+    tokens = 2 * CHIPS * rows
+    queries = CHIPS * rows
+    tiles = queries // TILE
+    per_device = rows // BLK
+    group_pairs = tokens // (2 * BLK)
+    pairs = queries // (2 * BLK)
+    mesh_tokens = tokens * depths
+    piece_lanes = 3 * CHIP_COLS
 
     def kernel(
-        att_ref, o0, o1, o2, o3, f0, f1, f2, f3, f4, f5, s_ref, g_ref, t_ref, v_ref, n_ref, p_ref, c_ref,
+        slots_ref, lengths_ref, p_ref, c_ref, s_ref, g_ref, t_ref, v_ref, g1_ref, g2_ref,
+        wq_ref, wk_ref, wv_ref, wo_ref, wg_ref, wu_ref, wd_ref,
         new_ref, up0_ref, up1_ref, hg_ref, da_ref, dw0_ref, dw1_ref, dw2_ref, dw3_ref, ff_ref, sums_ref,
-        w_all, w_out, att_all, hidden, own, x_rows, r_rows, xT, innerT, inner, gate, up, gate_low, up_low,
-        part0, part1, part2, got1, got2, dw, dw_other,
-        wsend, wrecv, wlocal, olocal, send0, recv0, send1, recv1, send2, recv2, send3, recv3,
-        ag1s, ag1r, ag2s, ag2r, dsend, drecv,
+        all_rows, w_all, q_pairs, k_pairs, v_pairs, oT_ref, lse_ref,
+        w_ff, w_wo, qkv, att_all, hidden, own, x_rows, r_rows, xT, innerT, inner, gate, up, gate_low, up_low,
+        own_weight, part1, part2, got1, got2, dw, dw_other, buf, wide, count, q_slot, k_slot, v_slot, vT,
+        lsend, fsend, frecv, fosend, forecv, qsend, qrecv, qosend, qorecv,
+        osend, orecv, oosend, oorecv, opsend, oprecv,
+        rsend, rrecv, rosend, rorecv, send0, recv0, send1, recv1, send2, recv2, send3, recv3,
+        ag1s, ag1r, ag2s, ag2r, dsend, drecv, *total_refs,
     ):
         depth, chip, core, chip_x, chip_y, chip_d = place_on_mesh()
         near = [(c, (2 * c + core, depth)) for c in (chip_x, chip_y, chip_d)]
         other = (2 * chip + 1 - core, depth)
-        signal_and_wait([device for _, device in near] + [other])
-
-        def exchange(source_of, target, send, recv):
-            return [
-                remote(source_of(c), target, send, recv, i, device)
-                for i, (c, device) in enumerate(near)
-            ]
+        across = [
+            (2 * chip + core, lax.rem(depth + step, depths)) for step in range(1, depths)
+        ]
+        peers = plane_peers(chip, core, depth, chip_x, chip_y, chip_d)
+        signal_all(peers + across)
+
+        mine = pl.ds(core * half, half)
+        loads = [
+            pltpu.make_async_copy(w.at[mine], buf.at[i], lsend.at[i])
+            for i, w in enumerate((wq_ref, wk_ref, wv_ref))
+        ] + [
+            pltpu.make_async_copy(wg_ref.at[mine], wide.at[0], lsend.at[3]),
+            pltpu.make_async_copy(wu_ref.at[mine], wide.at[1], lsend.at[4]),
+            pltpu.make_async_copy(
+                wd_ref.at[pl.ds(chip * split + core * half, half)], w_ff.at[2, depth, core], lsend.at[5]
+            ),
+            pltpu.make_async_copy(
+                wo_ref.at[pl.ds(chip * out_rows, out_rows)], w_wo.at[depth, chip], lsend.at[6]
+            ),
+        ]
+        for copy in loads:
+            copy.start()
+        count[...] = jnp.broadcast_to(
+            jnp.sum(v_ref[...].astype(F32), axis=1, keepdims=True), count.shape
+        )
+
+        def input_norm(i, _):
+            at = aligned(i, ROWS)
+            active = mix(s_ref, at, p_ref, 0)
+            own[0, at, :] = (active * norm_factor(active)).astype(BF16)
+            return 0
+
+        lax.fori_loop(0, blocks, input_norm, 0)
+
+        def gain_column(ref):
+            both = jnp.broadcast_to(ref[...].astype(F32), (8, shard)).T
+            return jnp.where(core == 0, both[:half, 0:1], both[half:, 0:1])
+
+        one, two = gain_column(g1_ref), gain_column(g2_ref)
+        wait_all(peers + across)
+
+        def slot(chip_index):
+            return 2 * chip_index + core
+
+        start_count, turn_count, end_count = total_over_mesh(
+            count, *total_refs[:3], across, peers, *total_refs[3:]
+        )
+        start_count()
+        ring0 = ring_sends(
+            own.at[0], all_rows, slot, chip, core, depth, chip_x, chip_y, rsend, rrecv
+        )
+        for copy in ring0[:4]:
+            copy.start()
+
+        def rows_to_other(index, chip_index):
+            ref = all_rows.at[slot(chip_index)]
+            return remote(own.at[0] if index == 0 else ref, ref, rosend, rorecv, index, other)
+
+        shared0 = [rows_to_other(i, c) for i, c in enumerate((chip, chip_x, chip_y, chip_d))]
+        shared0[0].start()
+        all_rows[slot(chip)] = own[0]
+
+        for copy in loads[:3]:
+            copy.wait()
+        for p in range(CHIPS):
+
+            @pl.when(chip == p)
+            def _(p=p):
+                cols = jnp.concatenate(
+                    [buf[i, :, p * CHIP_COLS : (p + 1) * CHIP_COLS].astype(F32) for i in range(3)], axis=1
+                )
+                qkv[depth, core] = (cols * one).astype(BF16)
+
+        qkv_mine = qkv.at[depth, core]
+        q_copies = [
+            remote(qkv_mine, qkv_mine, qsend, qrecv, i, device) for i, device in enumerate(across)
+        ]
+        q_shared = [remote(qkv_mine, qkv_mine, qosend, qorecv, 0, other)]
+        for copy in q_copies + q_shared:
+            copy.start()
+
+        loads[6].wait()
+        o_copies = [
+            remote(w_wo.at[depth, chip], w_wo.at[depth, chip], osend, orecv, i, device)
+            for i, device in enumerate(across)
+        ]
+        o_shared = []
+        for i in range(depths - 1):
+            came = w_wo.at[lax.rem(depth + depths - 1 - i, depths), chip]
+            o_shared.append(remote(came, came, oosend, oorecv, i, other))
+
+        def carried(i, act):
+            pl.when(core == (i + 1) % 2)(act)
+
+        def not_carried(i, act):
+            pl.when(core != (i + 1) % 2)(act)
+
+        for i in range(depths - 1):
+            carried(i, o_copies[i].start)
+
+        for copy in loads[3:6]:
+            copy.wait()
+        for p in range(CHIPS):
+
+            @pl.when(chip == p)
+            def _(p=p):
+                for i in range(2):
+                    cols = jnp.concatenate(
+                        [
+                            wide[i, :, (z * CHIPS + p) * split : (z * CHIPS + p + 1) * split].astype(F32)
+                            for z in range(depths)
+                        ],
+                        axis=1,
+                    )
+                    w_ff[i, depth, core] = (cols * two).astype(BF16)
+
+        line_up = (2 * chip + core, lax.rem(depth + 1, depths))
+        line_down = (2 * chip + core, lax.rem(depth + depths - 1, depths))
+        hops = []
+        for stage in range(1, depths):
+            for direction, device, index in ((1, line_up, stage - 1), (-1, line_down, depths + stage - 2)):
+                goes = jnp.clip(depth - direction * (stage - 1), 0, depths - 1)
+                comes = jnp.clip(depth - direction * stage, 0, depths - 1)
+                piece, came = w_ff.at[:, goes, core], w_ff.at[:, comes, core]
+                if direction == 1:
+                    sends, receives = (depth >= stage - 1) & (depth < depths - 1), depth >= stage
+                else:
+                    sends, receives = (depth <= depths - stage) & (depth > 0), depth < depths - stage
+                hops.append(
+                    (
+                        stage,
+                        sends,
+                        receives,
+                        remote(piece, piece, fsend, frecv, index, device),
+                        remote(came, came, fosend, forecv, index, other),
+                    )
+                )
+        ff_mine = remote(w_ff.at[:, depth, core], w_ff.at[:, depth, core], fosend, forecv, 2 * depths - 2, other)
+        ff_mine.start()
+
+        def send_hop(stage):
+            for at, sends, _, hop, _ in hops:
+                if at == stage:
+                    pl.when(sends)(hop.start)
+
+        def take_hop(stage):
+            for at, _, receives, hop, share in hops:
+                if at == stage:
+
+                    @pl.when(receives)
+                    def _(hop=hop, share=share):
+                        hop.wait_recv()
+                        share.start()
+
+        send_hop(1)
+        turn_count()
+        ring0[0].wait_recv()
+        ring0[4].start()
+        ring0[1].wait_recv()
+        ring0[5].start()
+        for i in range(depths - 1):
+            q_copies[i].wait_recv()
+            came = qkv.at[lax.rem(depth + depths - 1 - i, depths), core]
+            share = remote(came, came, qosend, qorecv, 1 + i, other)
+            share.start()
+            q_shared.append(share)
+        ring0[2].wait_recv()
+        shared0[1].start()
+        ring0[3].wait_recv()
+        shared0[2].start()
+        for copy in q_shared:
+            copy.wait_recv()
+        for i in range(3):
+            for z in range(depths):
+                for c in range(2):
+                    at = (z * 2 + c) * half
+                    w_all[i, at : at + half, :] = qkv[z, c, :, i * CHIP_COLS : (i + 1) * CHIP_COLS]
+
+        def project(device_slot, with_queries):
+            x = all_rows[device_slot]
+            at = aligned(device_slot, rows)
+            k_slot[at, :] = jnp.dot(x, w_all[1], preferred_element_type=F32).astype(BF16)
+            v_slot[at, :] = jnp.dot(x, w_all[2], preferred_element_type=F32).astype(BF16)
+            if with_queries:
+                q_slot[aligned(device_slot // 2, rows), :] = jnp.dot(
+                    x, w_all[0], preferred_element_type=F32
+                ).astype(BF16)
+
+        for c in (chip, chip_x, chip_y):
+            project(slot(c), True)
+        for i, c in enumerate((chip, chip_x, chip_y)):
+            shared0[i].wait_recv()
+            project(2 * c + 1 - core, False)
+        ring0[4].wait_recv()
+        ring0[5].wait_recv()
+        shared0[3].start()
+        project(slot(chip_d), True)
+        for i in range(depths - 1):
+
+            def came_here(i=i):
+                o_copies[i].wait_recv()
+                o_shared[i].start()
+
+            carried(i, came_here)
+        for i in range(depths - 1):
+            not_carried(i, o_shared[i].wait_recv)
+        o_plane = [
+            remote(w_wo.at[:, chip], w_wo.at[:, chip], opsend, oprecv, i, device)
+            for i, (_, device) in enumerate(near)
+        ]
+        for copy in o_plane:
+            copy.start()
+        shared0[3].wait_recv()
+        project(2 * chip_d + 1 - core, False)
+
+        to_pair_order(k_slot, k_pairs, slots_ref, group_pairs)
+        to_pair_order(v_slot, v_pairs, slots_ref, group_pairs)
+        own_to_pair_order(q_slot, q_pairs, slots_ref, pairs, per_device)
+
+        def turn_values(i, _):
+            vT[:, aligned(i, TILE)] = v_pairs[aligned(i, TILE), :].T
+            return 0
+
+        lax.fori_loop(0, tokens // TILE, turn_values, 0)
+        half_keys = group_pairs * BLK
+        half_tiles = half_keys // TILE
+        scores, bias = gate, up
+
+        def cell(k_tile):
+            lanes = (k_tile // CHIPS) * TILE
+            return k_tile % CHIPS, slice(lanes, lanes + TILE)
+
+        def attend(kind, step):
+            tile = kind * (tiles // 2) + step
+            key_tiles = half_tiles * (kind + 1)
+            q = q_pairs[aligned(tile, TILE), :]
+            fill_bias(bias, kind, step, slots_ref, lengths_ref, per_device, group_pairs)
+            for head in range(LOCAL_HEADS):
+                heads = slice(head * HD, (head + 1) * HD)
+                q_head = jnp.where(head_mask(TILE, head), q, jnp.zeros_like(q))
+                top = jnp.full((1, TILE), NEGATIVE, F32)
+                for k_tile in range(key_tiles):
+                    s = lax.dot_general(
+                        k_pairs[k_tile * TILE : (k_tile + 1) * TILE, :], q_head, NT, preferred_element_type=F32
+                    )
+                    if k_tile >= key_tiles - half_tiles:
+                        s = s + bias[k_tile - (key_tiles - half_tiles), :, 0:TILE]
+                    index, lanes = cell(k_tile)
+                    scores[index, :, lanes] = s
+                    top = jnp.maximum(top, jnp.max(s, axis=0, keepdims=True))
+                total = jnp.zeros((1, TILE), F32)
+                out = jnp.zeros((HD, TILE), F32)
+                for k_tile in range(key_tiles):
+                    index, lanes = cell(k_tile)
+                    e = jnp.exp(scores[index, :, lanes] - top)
+                    total = total + jnp.sum(e, axis=0, keepdims=True)
+                    out = out + jnp.dot(
+                        vT[heads, k_tile * TILE : (k_tile + 1) * TILE], e.astype(BF16), preferred_element_type=F32
+                    )
+                oT_ref[tile, heads, :] = out / total
+                lse_ref[tile, head] = top + jnp.log(total)
+            q_slot[aligned(tile, TILE), :] = oT_ref[tile].T.astype(BF16)
+
+        def both_steps(kind):
+            def body(step, _):
+                attend(kind, step)
+                return 0
+
+            lax.fori_loop(0, tiles // 2, body, 0)
+
+        both_steps(1)
+        take_hop(1)
+        send_hop(2)
+        both_steps(0)
+
+        own_to_slot_order(q_slot, k_slot, slots_ref, pairs, per_device)
+        for c in range(CHIPS):
+            att_all[CHIPS + c] = k_slot[c * rows : (c + 1) * rows, :]
+        sends0 = [
+            remote(att_all.at[CHIPS + c], att_all.at[chip], send0, recv0, i, device)
+            for i, (c, device) in enumerate(near)
+        ]
+        for copy in sends0:
+            copy.start()
+        att_all[chip] = att_all[CHIPS + chip]
+        take_hop(2)
+        send_hop(3)
+        for copy in o_plane:
+            copy.wait_recv()
+        for copy in sends0:
+            copy.wait()
+
+        def w_out_rows(p):
+            return w_wo[p].reshape(CHIP_COLS, width)
+
+        for p in range(CHIPS):
+            term = jnp.dot(att_all[p], w_out_rows(p), preferred_element_type=F32)
+            hidden[...] = term if p == 0 else hidden[...] + term
+
+        def first_norm(i, _):
+            at = aligned(i, ROWS)
+            h = hidden[at, :] + mix(s_ref, at, p_ref, 0)
+            hidden[at, :] = h
+            own[1, at, :] = (h * norm_factor(h)).astype(BF16)
+            return 0
+
+        lax.fori_loop(0, blocks, first_norm, 0)
 
         def ring(source, target, send, recv):
             return ring_sends(
                 source, target, lambda c: c, chip, core, depth, chip_x, chip_y, send, recv
             )
 
-        sends0 = exchange(lambda c: att_ref.at[c], att_all.at[chip], send0, recv0)
-        for copy in sends0:
-            copy.start()
-        out_loads = [
-            pltpu.make_async_copy(piece, w_out.at[:, c], olocal.at[i])
-            for i, (piece, c) in enumerate(zip((o0, o1, o2, o3), (chip, chip_x, chip_y, chip_d)))
-        ]
-        for copy in out_loads:
-            copy.start()
-        sources = (
-            (f0, 0, None),
-            (f1, -1, depth >= 1),
-            (f2, -2, depth >= 2),
-            (f3, 1, depth <= depths - 2),
-            (f4, 2, depth <= depths - 3),
-            (f5, None, (depth == 0) | (depth == depths - 1)),
-        )
-
-        def each_source(act):
-            for i, (ref, shift, present) in enumerate(sources):
-                z = depths - 1 - depth if shift is None else depth + shift
-                z = jnp.clip(z, 0, depths - 1)
-                dst = w_all.at[:, z, core]
-                copies = (
-                    remote(ref, dst, wsend, wrecv, i, other),
-                    pltpu.make_async_copy(ref, dst, wlocal.at[i]),
-                )
-                if present is None:
-                    act(copies)
-                else:
-
-                    @pl.when(present)
-                    def _(copies=copies):
-                        act(copies)
-
-        each_source(lambda copies: [copy.start() for copy in copies])
-        att_all[chip] = att_ref[chip]
-        for copy in out_loads:
-            copy.wait()
-        for copy in sends0:
-            copy.wait_recv()
-
-        def w_out_rows(p):
-            return w_out[p].reshape(CHIP_COLS, width)
-
-        for p in range(CHIPS):
-            term = jnp.dot(att_all[p], w_out_rows(p), preferred_element_type=F32)
-            hidden[...] = term if p == 0 else hidden[...] + term
-
-        def first_norm(i, _):
-            at = aligned(i, ROWS)
-            h = hidden[at, :] + mix(s_ref, at, p_ref, 0)
-            hidden[at, :] = h
-            own[0, at, :] = (h * norm_factor(h)).astype(BF16)
-            return 0
-
-        lax.fori_loop(0, blocks, first_norm, 0)
-        ring1 = ring(own.at[0], x_rows, ag1s, ag1r)
+        ring1 = ring(own.at[1], x_rows, ag1s, ag1r)
         for copy in ring1[:4]:
             copy.start()
-        x_rows[chip] = own[0]
-        each_source(lambda copies: [copy.wait() for copy in copies])
+        x_rows[chip] = own[1]
+        ring1[0].wait_recv()
+        ring1[4].start()
+        ring1[1].wait_recv()
+        ring1[5].start()
+        take_hop(3)
+        ff_mine.wait_recv()
+        for _, _, receives, _, share in hops:
+            pl.when(receives)(share.wait_recv)
 
         def w_rows(i):
-            return w_all[i].reshape(width, columns)
-
-        def forward(c):
+            return w_ff[i].reshape(width, columns)
+
+        def ff_forward(c):
             x = x_rows[c]
             for n in range(col_tiles):
                 cols = slice(n * TILE, (n + 1) * TILE)
@@ -1144,18 +1018,14 @@
         sends1 = [
             remote(part1.at[c], got1.at[i], send1, recv1, i, device) for i, (c, device) in enumerate(near)
         ]
-        up0_ref[...] = forward(chip)
-        ring1[0].wait_recv()
-        ring1[4].start()
-        ring1[1].wait_recv()
-        ring1[5].start()
+        up0_ref[...] = ff_forward(chip)
         for i, (c, _) in enumerate(near):
             if i < 2:
                 ring1[2 + i].wait_recv()
             else:
                 ring1[4].wait_recv()
                 ring1[5].wait_recv()
-            part1[c] = forward(c).astype(BF16)
+            part1[c] = ff_forward(c).astype(BF16)
             sends1[i].start()
 
         def turn(i, _):
@@ -1164,8 +1034,8 @@
             return 0
 
         lax.fori_loop(0, CHIPS, turn, 0)
-        weight = as_column(v_ref[...].astype(F32)) * (tokens / n_ref[0:1, 0:1])
-        own_weight = part0
+        valid_count = end_count()
+        weight = as_column(v_ref[...].astype(F32)) * (mesh_tokens / valid_count[0:1, 0:1])
         own_weight[...] = jnp.broadcast_to(weight, own_weight.shape)
         for copy in sends1:
             copy.wait_recv()
@@ -1187,7 +1057,7 @@
             up1 = g_ref[at, 1, :].astype(F32) + row_weight * (out1 - t_ref[at, 1, :].astype(F32))
             up0_ref[at, :] = up0
             up1_ref[at, :] = up1
-            own[1, at, :] = (c0 * up0 + c1 * up1).astype(BF16)
+            own[2, at, :] = (c0 * up0 + c1 * up1).astype(BF16)
             return (
                 sums[0] + jnp.sum(up0 * difference, axis=0, keepdims=True),
                 sums[1] + jnp.sum(up1 * difference, axis=0, keepdims=True),
@@ -1199,12 +1069,12 @@
         sums_ref[2:3, :] = correct_sums[0]
         sums_ref[3:4, :] = correct_sums[1]
 
-        ring2 = ring(own.at[1], r_rows, ag2s, ag2r)
+        ring2 = ring(own.at[2], r_rows, ag2s, ag2r)
         for copy in ring2[:4]:
             copy.start()
-        r_rows[chip] = own[1]
-
-        def backward(c):
+        r_rows[chip] = own[2]
+
+        def ff_backward(c):
             r = r_rows[c]
             for n in range(col_tiles):
                 cols = slice(n * TILE, (n + 1) * TILE)
@@ -1219,7 +1089,7 @@
         sends2 = [
             remote(part2.at[c], got2.at[i], send2, recv2, i, device) for i, (c, device) in enumerate(near)
         ]
-        hg_ref[...] = backward(chip)
+        hg_ref[...] = ff_backward(chip)
         ring2[0].wait_recv()
         ring2[4].start()
         ring2[1].wait_recv()
@@ -1230,17 +1100,17 @@
             else:
                 ring2[4].wait_recv()
                 ring2[5].wait_recv()
-            part2[c] = backward(c).astype(BF16)
+            part2[c] = ff_backward(c).astype(BF16)
             sends2[i].start()
 
         def weight_grads(z, _):
             at = aligned(z, shard)
             for i, (left, right) in enumerate(((xT, gate_low), (xT, up_low), (innerT, r_rows))):
-                wide = jnp.dot(
-                    left[at, :], right[...].reshape(CHIPS * rows, -1), preferred_element_type=F32
+                grad = jnp.dot(
+                    left[at, :], right[...].reshape(queries, -1), preferred_element_type=F32
                 ).astype(BF16)
-                dw[z, 0, i * half : (i + 1) * half, :] = wide[:half]
-                dw[z, 1, i * half : (i + 1) * half, :] = wide[half:]
+                dw[z, 0, i * half : (i + 1) * half, :] = grad[:half]
+                dw[z, 1, i * half : (i + 1) * half, :] = grad[half:]
             return 0
 
         lax.fori_loop(0, depths, weight_grads, 0)
@@ -1260,22 +1130,25 @@
             result_grad = c_ref[0] * up0_ref[at, :] + c_ref[1] * up1_ref[at, :]
             hidden_grad = result_grad + (factor * weighted - h * (factor * factor * factor * mean))
             hg_ref[at, :] = hidden_grad
-            own[2, at, :] = hidden_grad.astype(BF16)
+            own[3, at, :] = hidden_grad.astype(BF16)
             return gain_sum + jnp.sum(weighted * h * factor, axis=0, keepdims=True)
 
         sums_ref[1:2, :] = lax.fori_loop(0, blocks, second_norm, zero)
 
-        sends3 = exchange(lambda c: att_all.at[CHIPS + c], da_ref.at[chip], send3, recv3)
+        sends3 = [
+            remote(att_all.at[CHIPS + c], da_ref.at[chip], send3, recv3, i, device)
+            for i, (c, device) in enumerate(near)
+        ]
 
         def att_grad(c):
-            return lax.dot_general(own[2], w_out_rows(c), NT, preferred_element_type=F32).astype(BF16)
+            return lax.dot_general(own[3], w_out_rows(c), NT, preferred_element_type=F32).astype(BF16)
 
         for i in (2, 0, 1):
             att_all[CHIPS + near[i][0]] = att_grad(near[i][0])
             sends3[i].start()
         da_ref[chip] = att_grad(chip)
         for c, ref in zip((chip, chip_x, chip_y, chip_d), (dw0_ref, dw1_ref, dw2_ref, dw3_ref)):
-            ref[...] = jnp.dot(att_all[c].T, own[2], preferred_element_type=F32).astype(BF16)
+            ref[...] = jnp.dot(att_all[c].T, own[3], preferred_element_type=F32).astype(BF16)
         swap.wait_recv()
 
         def add_cores(z, _):
@@ -1285,78 +1158,129 @@
         lax.fori_loop(0, depths, add_cores, 0)
         for copy in sends3:
             copy.wait_recv()
-        for copy in sends0 + sends1 + sends2 + sends3 + ring1 + ring2 + [swap]:
+        sent = ring0 + shared0 + q_copies + q_shared + o_plane + sends1 + sends2 + sends3
+        for copy in sent + ring1 + ring2 + [swap, ff_mine]:
             copy.wait_send()
+        for i in range(depths - 1):
+            carried(i, o_copies[i].wait_send)
+            carried(i, o_shared[i].wait_send)
+        for _, sends, receives, hop, share in hops:
+            pl.when(sends)(hop.wait_send)
+            pl.when(receives)(share.wait_send)
 
     block = (rows, width)
     pair = (rows, 2, width)
     wide_rows = (CHIPS, rows, width)
     hid_rows = (CHIPS, rows, columns)
+
+    def out(shape, dtype):
+        return jax.ShapeDtypeStruct(shape, dtype)
+
+    vmem = pltpu.VMEM
+    outs = [
+        out(pair, BF16),
+        out(block, F32),
+        out(block, F32),
+        out(block, F32),
+        out((CHIPS, rows, CHIP_COLS), BF16),
+        out((CHIP_COLS, width), BF16),
+        out((CHIP_COLS, width), BF16),
+        out((CHIP_COLS, width), BF16),
+        out((CHIP_COLS, width), BF16),
+        out((depths, 3 * half, columns), BF16),
+        out((8, width), F32),
+        out((2 * CHIPS, rows, width), BF16),
+        out((3, width, CHIP_COLS), BF16),
+        out((queries, CHIP_COLS), BF16),
+        out((tokens, CHIP_COLS), BF16),
+        out((tokens, CHIP_COLS), BF16),
+        out((tiles, CHIP_COLS, TILE), F32),
+        out((tiles, LOCAL_HEADS, 1, TILE), F32),
+    ]
     return pl.pallas_call(
         kernel,
-        out_shape=[
-            jax.ShapeDtypeStruct(pair, BF16),
-            jax.ShapeDtypeStruct(block, F32),
-            jax.ShapeDtypeStruct(block, F32),
-            jax.ShapeDtypeStruct(block, F32),
-            jax.ShapeDtypeStruct((CHIPS, rows, CHIP_COLS), BF16),
-            jax.ShapeDtypeStruct((CHIP_COLS, width), BF16),
-            jax.ShapeDtypeStruct((CHIP_COLS, width), BF16),
-            jax.ShapeDtypeStruct((CHIP_COLS, width), BF16),
-            jax.ShapeDtypeStruct((CHIP_COLS, width), BF16),
-            jax.ShapeDtypeStruct((depths, 3 * half, columns), BF16),
-            jax.ShapeDtypeStruct((8, width), F32),
-        ],
-        in_specs=[VM] + [ANY] * 10 + [VM] * 5 + [SM] * 2,
-        out_specs=[VM] * 11,
+        out_shape=outs,
+        in_specs=[SM] * 4 + [VM] * 6 + [ANY] * 7,
+        out_specs=[VM] * len(outs),
         scratch_shapes=[
-            pltpu.VMEM((3, depths, 2, half, columns), BF16),
-            pltpu.VMEM((depths, CHIPS, out_rows, width), BF16),
-            pltpu.VMEM((2 * CHIPS, rows, CHIP_COLS), BF16),
-            pltpu.VMEM(block, F32),
-            pltpu.VMEM((3,) + block, BF16),
-            pltpu.VMEM(wide_rows, BF16),
-            pltpu.VMEM(wide_rows, BF16),
-            pltpu.VMEM((width, CHIPS * rows), BF16),
-            pltpu.VMEM((columns, CHIPS * rows), BF16),
-            pltpu.VMEM(hid_rows, BF16),
-            pltpu.VMEM(hid_rows, F32),
-            pltpu.VMEM(hid_rows, F32),
-            pltpu.VMEM(hid_rows, BF16),
-            pltpu.VMEM(hid_rows, BF16),
-            pltpu.VMEM((rows, 128), F32),
-            pltpu.VMEM(wide_rows, BF16),
-            pltpu.VMEM(wide_rows, BF16),
-            pltpu.VMEM((3,) + block, BF16),
-            pltpu.VMEM((3,) + block, BF16),
-            pltpu.VMEM((depths, 2, 3 * half, columns), BF16),
-            pltpu.VMEM((depths, 3 * half, columns), BF16),
+            vmem((3, depths, 2, half, columns), BF16),
+            vmem((depths, CHIPS, out_rows, width), BF16),
+            vmem((depths, 2, half, piece_lanes), BF16),
+            vmem((2 * CHIPS, rows, CHIP_COLS), BF16),
+            vmem(block, F32),
+            vmem((4,) + block, BF16),
+            vmem(wide_rows, BF16),
+            vmem(wide_rows, BF16),
+            vmem((width, queries), BF16),
+            vmem((columns, queries), BF16),
+            vmem(hid_rows, BF16),
+            vmem(hid_rows, F32),
+            vmem(hid_rows, F32),
+            vmem(hid_rows, BF16),
+            vmem(hid_rows, BF16),
+            vmem((rows, 128), F32),
+            vmem(wide_rows, BF16),
+            vmem(wide_rows, BF16),
+            vmem((3,) + block, BF16),
+            vmem((3,) + block, BF16),
+            vmem((depths, 2, 3 * half, columns), BF16),
+            vmem((depths, 3 * half, columns), BF16),
+            vmem((3, half, width), BF16),
+            vmem((2, half, hidden_cols), BF16),
+            vmem((8, 128), F32),
+            vmem((queries, CHIP_COLS), BF16),
+            vmem((tokens, CHIP_COLS), BF16),
+            vmem((tokens, CHIP_COLS), BF16),
+            vmem((CHIP_COLS, tokens), BF16),
         ]
-        + [DMA((6,))] * 3
-        + [DMA((CHIPS,))]
+        + [DMA((7,))]
+        + [DMA((2 * depths - 2,))] * 2
+        + [DMA((2 * depths - 1,))] * 2
+        + [DMA((depths - 1,))] * 2
+        + [DMA((depths,))] * 2
+        + [DMA((depths - 1,))] * 4
+        + [DMA((3,))] * 2
+        + [DMA((6,))] * 2
+        + [DMA((4,))] * 2
         + [DMA((3,))] * 8
         + [DMA((6,))] * 4
-        + [DMA((1,))] * 2,
+        + [DMA((1,))] * 2
+        + total_scratch((8, 128), depths),
         compiler_params=comm_params(collective_id),
-        name="middle",
-    )(attended, *out_pieces, *ff_pieces, states, out_grad, teacher, valid, count, predict, correct)
-
-
-def input_gradients(
-    dq, dk, dv, qkv, all_rows, out_grads, states, up0, up1, hidden_grad, sums, predict, correct, collective_id
+        name="forward",
+    )(
+        slots, lengths, predict, correct, states, out_grad, teacher, valid, gain_one, gain_two,
+        w_query, w_key, w_value, w_out, w_gate, w_up, w_down,
+    )
+
+
+def backward(
+    slots, lengths, predict, correct, att_grad, q_pairs, k_pairs, v_pairs, oT, lse, weights, states, up0, up1,
+    hidden_grad, sums, out_grads, all_rows, collective_id,
 ):
     rows, _, width = states.shape
-    depths, _, part_rows, columns = qkv.shape
-    half = part_rows // 3
+    depths = lax.axis_size("wsh")
+    columns = CHIP_COLS
+    half = width // (2 * depths)
+    part_rows = 3 * half
     blocks = rows // ROWS
+    tokens = k_pairs.shape[0]
+    queries = q_pairs.shape[0]
+    tiles = queries // TILE
+    per_device = rows // BLK
+    group_pairs = tokens // (2 * BLK)
+    pairs = queries // (2 * BLK)
+    half_tiles = group_pairs * BLK // TILE
+    wide_lanes = LOCAL_HEADS * TILE
 
     def kernel(
-        dq_ref, dk_ref, dv_ref, qkv_ref, rows_ref, o0, o1, o2, o3, s_ref, up0_ref, up1_ref, hg_ref, sums_ref,
-        p_ref, c_ref,
+        slots_ref, lengths_ref, p_ref, c_ref, g_ref, q_ref, k_ref, v_ref, oT_ref, lse_ref, w_all, s_ref,
+        up0_ref, up1_ref, hg_ref, sums_ref, o0, o1, o2, o3, rows_ref,
         grad_ref, qsum_ref, osum_ref, all_sums,
-        w_all, x_own, xT, dk_other, dv_other, dkv, part, got, mine, q_grad, q_other, q_mine, q_far,
-        o_grad, o_other, o_mine, o_far,
-        xload, ksend, krecv, send, recv, ssend, srecv, zsend, zrecv, osend, orecv,
+        g_pairs, kT, doT, dqT, q_stack, do_stack, p_buf, ds_buf, dk_acc, dv_acc, bias, dq_pairs, dq_rows,
+        give, kept, came, x_own, xT, part, got, mine, q_grad, q_other, q_mine, q_far,
+        o_near, o_grad, o_other, o_mine, o_far,
+        xload, nsend, nrecv, ksend, krecv, send, recv, ssend, srecv, zsend, zrecv, osend, orecv,
     ):
         depth, chip, core, chip_x, chip_y, chip_d = place_on_mesh()
         near = [(c, (2 * c + core, depth)) for c in (chip_x, chip_y, chip_d)]
@@ -1364,31 +1288,110 @@
         across = [
             (2 * chip + core, lax.rem(depth + step, depths)) for step in range(1, depths)
         ]
-        signal_and_wait([device for _, device in near] + [other] + across)
-        swaps = [
-            remote(dk_ref.at[:, 1 - core], dk_other, ksend, krecv, 0, other),
-            remote(dv_ref.at[:, 1 - core], dv_other, ksend, krecv, 1, other),
-        ]
-        for copy in swaps:
-            copy.start()
+        everyone = [device for _, device in near] + [other] + across
+        signal_all(everyone)
         load = pltpu.make_async_copy(rows_ref.at[:, core], x_own, xload)
         load.start()
-        spread_rows(qkv_ref, w_all)
-        for copy in swaps:
-            copy.wait_recv()
+        own_to_pair_order(g_ref, g_pairs, slots_ref, pairs, per_device)
+
+        def turn_keys(i, _):
+            at = aligned(i, TILE)
+            kT[:, at] = k_ref[at, :].T
+            return 0
+
+        lax.fori_loop(0, tokens // TILE, turn_keys, 0)
+        wait_all(everyone)
+        near_grads = [
+            remote(ref, o_near.at[i], nsend, nrecv, i, near[i][1]) for i, ref in enumerate((o1, o2, o3))
+        ]
+        for copy in near_grads:
+            copy.start()
+
+        def attend(kind, step):
+            tile = kind * (tiles // 2) + step
+            key_tiles = half_tiles * (kind + 1)
+            q_tile = q_ref[aligned(tile, TILE), :]
+            fill_bias(bias, kind, step, slots_ref, lengths_ref, per_device, group_pairs)
+            do_tile = g_pairs[aligned(tile, TILE), :]
+            doT[...] = do_tile.astype(F32).T * oT_ref[tile]
+            for head in range(LOCAL_HEADS):
+                lanes = slice(head * TILE, (head + 1) * TILE)
+                heads = slice(head * HD, (head + 1) * HD)
+                mask = head_mask(TILE, head)
+                q_head = jnp.where(mask, q_tile, jnp.zeros_like(q_tile))
+                do_head = jnp.where(mask, do_tile, jnp.zeros_like(do_tile))
+                q_stack[lanes, :] = q_head
+                do_stack[lanes, :] = do_head
+                delta = jnp.sum(doT[heads, :], axis=0, keepdims=True)
+                norm = lse_ref[tile, head]
+                total = jnp.zeros((HD, TILE), F32)
+                for k_tile in range(key_tiles):
+                    at = slice(k_tile * TILE, (k_tile + 1) * TILE)
+                    s = lax.dot_general(k_ref[at, :], q_head, NT, preferred_element_type=F32)
+                    if k_tile >= key_tiles - half_tiles:
+                        s = s + bias[k_tile - (key_tiles - half_tiles), :, 0:TILE]
+                    dp = lax.dot_general(v_ref[at, :], do_head, NT, preferred_element_type=F32)
+                    e = jnp.exp(s - norm)
+                    p_buf[at, lanes] = e.astype(BF16)
+                    ds = (e * (dp - delta)).astype(BF16)
+                    ds_buf[at, lanes] = ds
+                    total = total + jnp.dot(kT[heads, at], ds, preferred_element_type=F32)
+                dqT[heads, :] = total
+            for k_tile in range(key_tiles):
+                at = slice(k_tile * TILE, (k_tile + 1) * TILE)
+                dv = jnp.dot(p_buf[at, :], do_stack[...], preferred_element_type=F32)
+                dk = jnp.dot(ds_buf[at, :], q_stack[...], preferred_element_type=F32)
+                if kind == 1:
+                    fresh = step == 0
+                    dv_acc[at, :] = dv + jnp.where(fresh, 0.0, dv_acc[at, :])
+                    dk_acc[at, :] = dk + jnp.where(fresh, 0.0, dk_acc[at, :])
+                else:
+                    dv_acc[at, :] = dv + dv_acc[at, :]
+                    dk_acc[at, :] = dk + dk_acc[at, :]
+            dq_pairs[aligned(tile, TILE), :] = dqT[...].T.astype(BF16)
+
+        for kind in (1, 0):
+
+            def body(step, _, kind=kind):
+                attend(kind, step)
+                return 0
+
+            lax.fori_loop(0, tiles // 2, body, 0)
+
+        def slot_rows(target, side, chip_index, pair_index):
+            pair = chip_index * per_device + side * (per_device // 2) + pair_index
+            second, _, _ = pair_places(slots_ref, pair)
+            at = 2 * pair_index * BLK
+            for i, acc in enumerate((dk_acc, dv_acc)):
+                both = either(second, acc[aligned(pair, BLK), :], acc[aligned(group_pairs + pair, BLK), :])
+                for j in range(2):
+                    target[i, chip_index, at + j * BLK : at + (j + 1) * BLK, :] = both[j].astype(BF16)
+
+        for c in range(CHIPS):
+            for i in range(per_device // 2):
+                slot_rows(give, 1 - core, c, i)
+        swap = remote(give, came, ksend, krecv, 0, other)
+        swap.start()
+        for c in range(CHIPS):
+            for i in range(per_device // 2):
+                slot_rows(kept, core, c, i)
+        own_to_slot_order(dq_pairs, dq_rows, slots_ref, pairs, per_device)
+        swap.wait_recv()
 
         def add_cores(c, _):
-            dkv[0, c] = (dk_ref[c, core].astype(F32) + dk_other[c].astype(F32)).astype(BF16)
-            dkv[1, c] = (dv_ref[c, core].astype(F32) + dv_other[c].astype(F32)).astype(BF16)
+            for i in range(2):
+                kept[i, c] = (kept[i, c].astype(F32) + came[i, c].astype(F32)).astype(BF16)
             return 0
 
         lax.fori_loop(0, CHIPS, add_cores, 0)
 
         def rows_grad(c):
             return (
-                lax.dot_general(dq_ref[c], w_all[0], NT, preferred_element_type=F32)
-                + lax.dot_general(dkv[0, c], w_all[1], NT, preferred_element_type=F32)
-                + lax.dot_general(dkv[1, c], w_all[2], NT, preferred_element_type=F32)
+                lax.dot_general(
+                    dq_rows[aligned(c, rows), :], w_all[0], NT, preferred_element_type=F32
+                )
+                + lax.dot_general(kept[0, c], w_all[1], NT, preferred_element_type=F32)
+                + lax.dot_general(kept[1, c], w_all[2], NT, preferred_element_type=F32)
             )
 
         sends = [
@@ -1409,20 +1412,21 @@
         def weight_grads(z, _):
             at = aligned(z, 2 * half)
             for i in range(3):
-                right = dq_ref[...] if i == 0 else dkv[i - 1]
-                wide = jnp.dot(
-                    xT[at, :], right.reshape(CHIPS * rows, columns), preferred_element_type=F32
-                ).astype(BF16)
-                q_grad[z, 0, i * half : (i + 1) * half, :] = wide[:half]
-                q_grad[z, 1, i * half : (i + 1) * half, :] = wide[half:]
+                right = dq_rows[...] if i == 0 else kept[i - 1].reshape(queries, columns)
+                grad = jnp.dot(xT[at, :], right, preferred_element_type=F32).astype(BF16)
+                q_grad[z, 0, i * half : (i + 1) * half, :] = grad[:half]
+                q_grad[z, 1, i * half : (i + 1) * half, :] = grad[half:]
             return 0
 
         lax.fori_loop(0, depths, weight_grads, 0)
-        wide = (
-            o0[...].astype(F32) + o1[...].astype(F32) + o2[...].astype(F32) + o3[...].astype(F32)
-        ).astype(BF16)
-        o_grad[0] = wide[:half]
-        o_grad[1] = wide[half:]
+        for copy in near_grads:
+            copy.wait_recv()
+        whole = o0[...].astype(F32)
+        for i in range(3):
+            whole = whole + o_near[i].astype(F32)
+        whole = whole.astype(BF16)
+        o_grad[0] = whole[:half]
+        o_grad[1] = whole[half:]
         core_swaps = [
             remote(q_grad.at[:, 1 - core], q_other, ssend, srecv, 0, other),
             remote(o_grad.at[1 - core], o_other, ssend, srecv, 1, other),
@@ -1445,11 +1449,7 @@
             remote(o_mine, o_far.at[i], osend, orecv, i, device) for i, device in enumerate(across)
         ]
         for i in range(depths - 1):
-
-            @pl.when(distance == i + 1)
-            def _(i=i):
-                o_copies[i].start()
-
+            pl.when(distance == i + 1)(o_copies[i].start)
         for copy in sends:
             copy.wait_recv()
 
@@ -1495,16 +1495,16 @@
                 total = total + o_far[i].astype(F32)
             osum_ref[...] = total.astype(BF16)
 
-        for copy in swaps + sends + core_swaps + q_copies:
+        for copy in near_grads + [swap] + sends + core_swaps + q_copies:
             copy.wait_send()
         for i in range(depths - 1):
-
-            @pl.when(distance == i + 1)
-            def _(i=i):
-                o_copies[i].wait_send()
-
+            pl.when(distance == i + 1)(o_copies[i].wait_send)
+
+    vmem = pltpu.VMEM
     block = (rows, width)
+    wide_rows = (CHIPS, rows, width)
     q_block, o_block = (part_rows, columns), (half, width)
+    kv_half = (2, CHIPS, rows, columns)
     return pl.pallas_call(
         kernel,
         out_shape=[
@@ -1513,29 +1513,44 @@
             jax.ShapeDtypeStruct(o_block, BF16),
             jax.ShapeDtypeStruct((8, width), F32),
         ],
-        in_specs=[VM] * 4 + [ANY] + [VM] * 9 + [SM] * 2,
+        in_specs=[SM] * 4 + [VM] * 16 + [ANY],
         out_specs=[VM] * 4,
         scratch_shapes=[
-            pltpu.VMEM((3, width, columns), BF16),
-            pltpu.VMEM((CHIPS,) + block, BF16),
-            pltpu.VMEM((width, CHIPS * rows), BF16),
-            pltpu.VMEM((CHIPS, rows, columns), BF16),
-            pltpu.VMEM((CHIPS, rows, columns), BF16),
-            pltpu.VMEM((2, CHIPS, rows, columns), BF16),
-            pltpu.VMEM((CHIPS,) + block, BF16),
-            pltpu.VMEM((3,) + block, BF16),
-            pltpu.VMEM(block, F32),
-            pltpu.VMEM((depths, 2) + q_block, BF16),
-            pltpu.VMEM((depths,) + q_block, BF16),
-            pltpu.VMEM((depths,) + q_block, BF16),
-            pltpu.VMEM((depths - 1,) + q_block, BF16),
-            pltpu.VMEM((2,) + o_block, BF16),
-            pltpu.VMEM(o_block, BF16),
-            pltpu.VMEM(o_block, BF16),
-            pltpu.VMEM((depths - 1,) + o_block, BF16),
+            vmem((queries, columns), BF16),
+            vmem((columns, tokens), BF16),
+            vmem((columns, TILE), F32),
+            vmem((columns, TILE), F32),
+            vmem((wide_lanes, columns), BF16),
+            vmem((wide_lanes, columns), BF16),
+            vmem((tokens, wide_lanes), BF16),
+            vmem((tokens, wide_lanes), BF16),
+            vmem((tokens, columns), F32),
+            vmem((tokens, columns), F32),
+            vmem((half_tiles, TILE, TILE), F32),
+            vmem((queries, columns), BF16),
+            vmem((queries, columns), BF16),
+            vmem(kv_half, BF16),
+            vmem(kv_half, BF16),
+            vmem(kv_half, BF16),
+            vmem(wide_rows, BF16),
+            vmem((width, queries), BF16),
+            vmem(wide_rows, BF16),
+            vmem((3,) + block, BF16),
+            vmem(block, F32),
+            vmem((depths, 2) + q_block, BF16),
+            vmem((depths,) + q_block, BF16),
+            vmem((depths,) + q_block, BF16),
+            vmem((depths - 1,) + q_block, BF16),
+            vmem((3, columns, width), BF16),
+            vmem((2,) + o_block, BF16),
+            vmem(o_block, BF16),
+            vmem(o_block, BF16),
+            vmem((depths - 1,) + o_block, BF16),
             DMA,
-            DMA((2,)),
-            DMA((2,)),
+            DMA((3,)),
+            DMA((3,)),
+            DMA((1,)),
+            DMA((1,)),
             DMA((3,)),
             DMA((3,)),
             DMA((2,)),
@@ -1546,8 +1561,11 @@
             DMA((depths - 1,)),
         ],
         compiler_params=comm_params(collective_id),
-        name="input_gradients",
-    )(dq, dk, dv, qkv, all_rows, *out_grads, states, up0, up1, hidden_grad, sums, predict, correct)
+        name="backward",
+    )(
+        slots, lengths, predict, correct, att_grad, q_pairs, k_pairs, v_pairs, oT, lse, weights, states, up0, up1,
+        hidden_grad, sums, *out_grads, all_rows,
+    )
 
 
 def gather_gradients(ff, qkv, out, sums, collective_id):
@@ -1565,7 +1583,8 @@
             (2 * chip + core, lax.rem(depth + step, depths)) for step in range(1, depths)
         ]
         peers = plane_peers(chip, core, depth, chip_x, chip_y, chip_d)
-        signal_and_wait(peers + across)
+        signal_all(peers + across)
+        wait_all(peers + across)
 
         def slot(chip_index):
             return 2 * chip_index + core
@@ -1768,53 +1787,21 @@
     half = w_query.shape[0] // 2
     hidden_cols = w_gate.shape[1] // CHIPS
     slots, lengths = block_slot[0], cont_lengths[0]
-    states, out_grad, teacher = states[0], out_grad[0], teacher[0]
     gain_one, gain_two = norm_attn[None], norm_ffn[None]
-
-    def along_depth(value, pairs):
-        return lax.ppermute(value, "wsh", pairs)
-
-    def over_plane(value, step):
-        pairs = [(2 * c + k, 2 * (c ^ step) + k) for c in range(CHIPS) for k in range(2)]
-        return lax.ppermute(value, "ctx", pairs)
-
-    pre, qkv_piece, ff_piece, count = prepare(
-        states, predict, valid_mask, gain_one, gain_two, w_query, w_key, w_value, w_gate, w_up, w_down
-    )
-    ff_piece = ff_piece.reshape(3, half, hidden_cols)
-    above = [(z, z + 1) for z in range(depths - 1)]
-    below = [(z + 1, z) for z in range(depths - 1)]
-    from_below = along_depth(ff_piece, above)
-    from_above = along_depth(ff_piece, below)
-    all_rows, qkv, out_piece, count = gather_inputs(pre, qkv_piece, w_out, count, 1)
-    ff_pieces = [
-        ff_piece,
-        from_below,
-        along_depth(from_below, above[1:]),
-        from_above,
-        along_depth(from_above, below[:-1]),
-        along_depth(ff_piece, [(0, depths - 1), (depths - 1, 0)]),
-    ]
-    out_pieces = [out_piece] + [over_plane(out_piece, step) for step in (1, 2, 3)]
-    attended, *saved = attention_forward(all_rows.reshape(-1, width), qkv, slots, lengths)
-    new_states, up0, up1, hidden_grad, att_grad, *rest = middle(
-        attended.reshape(CHIPS, rows, CHIP_COLS), out_pieces, ff_pieces, states, out_grad, teacher,
-        valid_mask, count, predict, correct, 2,
-    )
-    out_grads, (ff_sum, sums) = rest[:4], rest[4:]
+    states = states[0]
+    new_states, up0, up1, hidden_grad, att_grad, *rest = forward(
+        slots, lengths, predict, correct, states, out_grad[0], teacher[0], valid_mask, gain_one, gain_two,
+        w_query, w_key, w_value, w_out, w_gate, w_up, w_down, 1,
+    )
+    out_grads, (ff_sum, sums, all_rows, weights, q_pairs, k_pairs, v_pairs, oT, lse) = rest[:4], rest[4:]
     ff_sum = lax.psum_scatter(
         ff_sum.reshape(depths * 3 * half, hidden_cols), "wsh", scatter_dimension=0, tiled=True
     )
-    out_grads = [out_grads[0]] + [over_plane(g, step) for step, g in zip((1, 2, 3), out_grads[1:])]
-    dq, dk, dv = attention_backward(att_grad.reshape(-1, CHIP_COLS), saved, slots, lengths)
-    states_grad, qkv_sum, out_sum, sums = input_gradients(
-        dq.reshape(CHIPS, rows, CHIP_COLS),
-        dk.reshape(CHIPS, 2, rows, CHIP_COLS),
-        dv.reshape(CHIPS, 2, rows, CHIP_COLS),
-        qkv, all_rows.reshape(CHIPS, 2, rows, width), out_grads,
-        states, up0, up1, hidden_grad, sums, predict, correct, 3,
-    )
-    gathered = gather_gradients(ff_sum, qkv_sum, out_sum, sums, 4)
+    states_grad, qkv_sum, out_sum, sums = backward(
+        slots, lengths, predict, correct, att_grad.reshape(-1, CHIP_COLS), q_pairs, k_pairs, v_pairs, oT, lse,
+        weights, states, up0, up1, hidden_grad, sums, out_grads, all_rows.reshape(CHIPS, 2, rows, width), 2,
+    )
+    gathered = gather_gradients(ff_sum, qkv_sum, out_sum, sums, 3)
     dq, dk, dv, do, dg, du, dd, g_one, g_two, predict_grad, correct_grad = lay_out(
         *gathered, gain_one, gain_two
     )

time: 289 us -> 244 us (0.84)
  starting transfers between devices: 21.8 us -> 0.04 us
  Pallas kernels: 245 us -> 225 us
  local copies, waits for them, and re-layouts: 7.81 us -> 4.73 us
    ppermute x11 -> x0, starting transfers between devices: 21.7 us -> none  [the longest x5 16.4 us: along_depth(): return lax.ppermute(value, 'wsh', pairs)]
    pallas_call x6 -> x2, Pallas kernels: 201 us -> 181 us  [the longest x1 123 us: forward(): pl.pallas_call(kernel, out_shape=outs, in_specs=[SM] * 4 + [VM] * 6 + [AN...]
    unnamed x34 -> x6, local copies, waits for them, and re-layouts: 5.34 us -> 2.29 us
  transfers between devices with their start and end apart: 12 -> 1, of which waited for: 0 -> 0; matrix products, arithmetic and copies ran while one was open for 0% -> 0% of each run, Pallas kernels for 37% -> 24%
where the time goes in v4:
time: 244 us
  Pallas kernels  225 us (92%)
  between operations  14.1 us (6%)
  local copies, waits for them, and re-layouts  4.73 us (2%)
    pallas_call x1, Pallas kernels, forward(): pl.pallas_call(kernel, out_shape=outs, in_specs=[SM] * 4 + [VM] * 6 + [AN...  123 us
    pallas_call x1, Pallas kernels, backward(): pl.pallas_call(kernel, out_shape=[jax.ShapeDtypeStruct((rows, 2, width),...  57.5 us
    pallas_call x1, Pallas kernels, gather_gradients(): pl.pallas_call(kernel, out_shape=[jax.ShapeDtypeStruct((2 * CHIPS,) + ff....  36.5 us
    pallas_call x1, Pallas kernels, lay_out(): pl.pallas_call(kernel, out_shape=[square, square, square, square, tall, t...  7.52 us
  transfers between devices with their start and end apart: 1, of which 0 were waited for; matrix products, arithmetic and copies ran while one was open for 0% of the time, Pallas kernels for 24%

profile of v4, /device:TPU:9, one launch (start us, length us, event | category | flops | bytes accessed | tf_op | source)
XLA Modules:
  0.0 244.0 jit_solution(12587221707006012475)
XLA Ops:
  7.2 0.0 reduce-scatter.2.cloned.1.call-start
  7.2 1.2 broadcast_in_dim.12.g1_ref
  8.4 1.2 broadcast_in_dim.13.g2_ref
  9.7 123.5 %forward.1 = (bf16[256,2,768]{2,1,0:T(2,128)(2,1)}, f32[256,768]{1,0:T(8,128)}, f32[256,768]{1,0:T(8,128)}, f32[256,768]{1,0:T(8,128)}, bf16[4,256,192]{2,1,0:T(...) custom-call(s32[32]{0:T(128)} %bitcast.22, ...), custom_call_target="tpu_custom_call" | custom-call | tf_op jit(solution)/shard_map/forward/pallas_call | solution.py:1200
  133.2 0.0 reduce-scatter.2.cloned.1.call-update
  133.2 57.5 %backward.1 = (bf16[256,2,768]{2,1,0:T(2,128)(2,1)}, bf16[288,192]{1,0:T(8,128)(2,1)}, bf16[96,768]{1,0:T(8,128)(2,1)}, f32[8,768]{1,0:T(8,128)}) custom-call(s32[32]{0:T(128)} %bitcast.23, s32[4]{0:T(128)} %bitcast.25, f32[2,2]{1,0:T(2,128)} %p_ref.3, f32[2]{0:T(128)} %c_ref.3, bf16[1024,192]{1,0:T(8,128)(2,1)} %bitcast.21, ...), custom_call_target="tpu_custom_call" | custom-call | tf_op jit(solution)/shard_map/backward/pallas_call | solution.py:1508
  190.7 0.0 reduce-scatter.2.cloned.1.call-done.f_ref
  190.7 36.5 %gather_gradients.1 = (bf16[8,288,768]{2,1,0:T(8,128)(2,1)}, bf16[8,288,192]{2,1,0:T(8,128)(2,1)}, bf16[2,96,768]{2,1,0:T(8,128)(2,1)}, f32[8,768]{1,0:T(8,128)}) custom-call(bf16[288,768]{1,0:T(8,128)(2,1)} %reduce-scatter.2.cloned.1.call-done.f_ref, bf16[288,192]{1,0:T(8,128)(2,1)} %get-tuple-element.69.q_ref, bf16[96,768]{1,0:T(8,128)(2,1)} %get-tuple-element.70.o_ref, ...), custom_call_target="tpu_custom_call" | custom-call | tf_op jit(solution)/shard_map/gather_gradients/pallas_call | solution.py:1688
  227.3 0.0 copy-start
  227.3 7.5 %lay_out.1 = (f32[192,768]{1,0:T(8,128)}, f32[192,768]{1,0:T(8,128)}, f32[192,768]{1,0:T(8,128)}, f32[192,768]{1,0:T(8,128)}, f32[192,3072]{1,0:T(8,128)}, /*ind...) custom-call(bf16[8,288,768]{2,1,0:T(8,128)(2,1)} %get-tuple-element., ...), custom_call_target="tpu_custom_call" | custom-call | tf_op jit(solution)/shard_map/lay_out/pallas_call | solution.py:1759
  234.8 0.0 copy-start.1
  234.8 0.0 copy-done
  234.8 0.9 copy.32
  235.7 0.5 copy-done.1
  236.3 0.9 copy.33
Async XLA Ops:
  7.2 183.6 %reduce-scatter.2.cloned.1.call-start = ((), (), s32[]{:S(2)}) async-start(), calls=%async_computation.1 | async-start | bytes 2211840 | tf_op jit(solution)/shard_map/reduce_scatter | solution.py:1797
  227.3 7.5 %copy-start = (bf16[256,2,768]{2,1,0:T(2,128)(2,1)S(1)}, bf16[256,2,768]{2,1,0:T(2,128)(2,1)}, u32[]{:S(2)}) copy-start(bf16[256,2,768]{2,1,0:T(2,128)(2,1)} %get-tuple-element.50) | copy-start | bytes 2359300
  234.8 1.4 copy-start.1
Sparse Core Ops, SparseCore 0:
  133.3 40.8 reduce-scatter.1

commit v5 on v4

--- a/solution.py
+++ b/solution.py
@@ -635,6 +635,90 @@
         return 0
 
     lax.fori_loop(0, pairs, one_pair, 0)
+
+
+def line_reduce(pieces, acc, up_in, down_in, up_out, down_out, sems):
+    depth, chip, core, _, _, _ = place_on_mesh()
+    depths = pieces.shape[0]
+    last = depths - 1
+    up_send, up_recv, down_send, down_recv = sems
+    above = (2 * chip + core, lax.rem(depth + 1, depths))
+    below = (2 * chip + core, lax.rem(depth + last, depths))
+
+    def up(source, k):
+        return remote(source, up_in.at[k], up_send, up_recv, k, above)
+
+    def down(source, k):
+        return remote(source, down_in.at[k], down_send, down_recv, k, below)
+
+    def start():
+        @pl.when(depth == 0)
+        def _():
+            for k in range(last):
+                up(pieces.at[last - k], k).start()
+
+        @pl.when(depth == last)
+        def _():
+            for k in range(last):
+                down(pieces.at[k], k).start()
+
+    def hop(k):
+        @pl.when((depth >= 1) & (depth <= k))
+        def _():
+            up(up_in.at[k - 1], k - 1).wait_recv()
+            mine = pieces[jnp.clip(depth + last - k, 0, last)]
+            up_out[k - 1] = (mine.astype(F32) + up_in[k - 1].astype(F32)).astype(BF16)
+            up(up_out.at[k - 1], k).start()
+
+        @pl.when((depth <= last - 1) & (depth >= last - k))
+        def _():
+            down(down_in.at[k - 1], k - 1).wait_recv()
+            mine = pieces[jnp.clip(depth + k - last, 0, last)]
+            down_out[k - 1] = (mine.astype(F32) + down_in[k - 1].astype(F32)).astype(BF16)
+            down(down_out.at[k - 1], k).start()
+
+    def result():
+        acc[...] = pieces[depth].astype(F32)
+
+        @pl.when(depth >= 1)
+        def _():
+            up(up_in.at[last - 1], last - 1).wait_recv()
+            acc[...] += up_in[last - 1].astype(F32)
+
+        @pl.when(depth <= last - 1)
+        def _():
+            down(down_in.at[last - 1], last - 1).wait_recv()
+            acc[...] += down_in[last - 1].astype(F32)
+
+    def finish():
+        @pl.when(depth == 0)
+        def _():
+            for k in range(last):
+                up(pieces.at[last - k], k).wait_send()
+
+        @pl.when(depth == last)
+        def _():
+            for k in range(last):
+                down(pieces.at[k], k).wait_send()
+
+        for k in range(1, last):
+
+            @pl.when((depth >= 1) & (depth <= k))
+            def _(k=k):
+                up(up_out.at[k - 1], k).wait_send()
+
+            @pl.when((depth <= last - 1) & (depth >= last - k))
+            def _(k=k):
+                down(down_out.at[k - 1], k).wait_send()
+
+    return start, hop, result, finish
+
+
+def line_reduce_scratch(shape, depths):
+    buffers = [(depths - 1,), (depths - 1,), (depths - 2,), (depths - 2,)]
+    return [pltpu.VMEM(shape, F32)] + [pltpu.VMEM(lead + shape, BF16) for lead in buffers], [
+        DMA((depths - 1,))
+    ] * 4
 
 
 def forward(
@@ -1256,7 +1340,7 @@
 
 def backward(
     slots, lengths, predict, correct, att_grad, q_pairs, k_pairs, v_pairs, oT, lse, weights, states, up0, up1,
-    hidden_grad, sums, out_grads, all_rows, collective_id,
+    hidden_grad, sums, ff_grads, out_grads, all_rows, collective_id,
 ):
     rows, _, width = states.shape
     depths = lax.axis_size("wsh")
@@ -1275,20 +1359,25 @@
 
     def kernel(
         slots_ref, lengths_ref, p_ref, c_ref, g_ref, q_ref, k_ref, v_ref, oT_ref, lse_ref, w_all, s_ref,
-        up0_ref, up1_ref, hg_ref, sums_ref, o0, o1, o2, o3, rows_ref,
-        grad_ref, qsum_ref, osum_ref, all_sums,
+        up0_ref, up1_ref, hg_ref, sums_ref, ff_ref, o0, o1, o2, o3, rows_ref,
+        grad_ref, f_all, q_all, o_all, total_ref,
         g_pairs, kT, doT, dqT, q_stack, do_stack, p_buf, ds_buf, dk_acc, dv_acc, bias, dq_pairs, dq_rows,
         give, kept, came, x_own, xT, part, got, mine, q_grad, q_other, q_mine, q_far,
-        o_near, o_grad, o_other, o_mine, o_far,
-        xload, nsend, nrecv, ksend, krecv, send, recv, ssend, srecv, zsend, zrecv, osend, orecv,
+        o_near, o_grad, o_other, o_mine, o_far, f_mine, q_sum, o_sum, all_sums, *rest,
     ):
+        (
+            f_acc, f_up_in, f_down_in, f_up_out, f_down_out, f_us, f_ur, f_ds, f_dr,
+            xload, nsend, nrecv, ksend, krecv, send, recv, ssend, srecv, zsend, zrecv, osend, orecv,
+            fsend, frecv, gsend, grecv, bsend, brecv, psend, precv, *total_refs,
+        ) = rest
         depth, chip, core, chip_x, chip_y, chip_d = place_on_mesh()
         near = [(c, (2 * c + core, depth)) for c in (chip_x, chip_y, chip_d)]
         other = (2 * chip + 1 - core, depth)
         across = [
             (2 * chip + core, lax.rem(depth + step, depths)) for step in range(1, depths)
         ]
-        everyone = [device for _, device in near] + [other] + across
+        peers = plane_peers(chip, core, depth, chip_x, chip_y, chip_d)
+        everyone = peers + across
         signal_all(everyone)
         load = pltpu.make_async_copy(rows_ref.at[:, core], x_own, xload)
         load.start()
@@ -1306,6 +1395,10 @@
         ]
         for copy in near_grads:
             copy.start()
+        ff_start, ff_hop, ff_result, ff_finish = line_reduce(
+            ff_ref, f_acc, f_up_in, f_down_in, f_up_out, f_down_out, (f_us, f_ur, f_ds, f_dr)
+        )
+        ff_start()
 
         def attend(kind, step):
             tile = kind * (tiles // 2) + step
@@ -1357,6 +1450,7 @@
                 return 0
 
             lax.fori_loop(0, tiles // 2, body, 0)
+            ff_hop(2 - kind)
 
         def slot_rows(target, side, chip_index, pair_index):
             pair = chip_index * per_device + side * (per_device // 2) + pair_index
@@ -1450,6 +1544,26 @@
         ]
         for i in range(depths - 1):
             pl.when(distance == i + 1)(o_copies[i].start)
+        ff_result()
+        f_mine[...] = f_acc[...].astype(BF16)
+
+        def slot(chip_index):
+            return 2 * chip_index + core
+
+        f_copies = ring_sends(
+            f_mine, f_all, slot, chip, core, depth, chip_x, chip_y, fsend, frecv
+        )
+        for copy in f_copies[:4]:
+            copy.start()
+        f_all[slot(chip)] = f_mine[...]
+
+        def shared(index, ref):
+            return remote(ref, ref, psend, precv, index, other)
+
+        f_shared = [shared(i, f_all.at[slot(c)]) for i, c in enumerate((chip, chip_x, chip_y, chip_d))]
+        q_shared = [shared(4 + i, q_all.at[slot(c)]) for i, c in enumerate((chip, chip_x, chip_y, chip_d))]
+        o_shared = shared(8, o_all.at[core])
+        f_shared[0].start()
         for copy in sends:
             copy.wait_recv()
 
@@ -1478,43 +1592,121 @@
         all_sums[0:1, :] = totals[0]
         for i in range(4):
             all_sums[4 + i : 5 + i, :] = totals[1 + i]
+        start, turn_sums, end = total_over_mesh(
+            all_sums, *total_refs[:3], across, peers, *total_refs[3:]
+        )
+        start()
+        f_copies[0].wait_recv()
+        f_copies[4].start()
+        f_copies[1].wait_recv()
+        f_copies[5].start()
         for copy in q_copies:
             copy.wait_recv()
         total = q_mine[depth].astype(F32)
         for i in range(depths - 1):
             total = total + q_far[i].astype(F32)
-        qsum_ref[...] = total.astype(BF16)
-        osum_ref[...] = jnp.zeros_like(osum_ref)
-
-        @pl.when(distance == 0)
+        q_sum[...] = total.astype(BF16)
+        r_copies = ring_sends(
+            q_sum, q_all, slot, chip, core, depth, chip_x, chip_y, gsend, grecv
+        )
+        for copy in r_copies[:4]:
+            copy.start()
+        q_all[slot(chip)] = q_sum[...]
+        q_shared[0].start()
+        quarter = half // 2
+        o_top, o_low = o_all.at[core, pl.ds(0, quarter)], o_all.at[core, pl.ds(quarter, quarter)]
+        o_source_top, o_source_low = o_sum.at[pl.ds(0, quarter)], o_sum.at[pl.ds(quarter, quarter)]
+        dev_x, dev_y = near[0][1], near[1][1]
+        b_copies = [
+            remote(o_source_top, o_top, bsend, brecv, 0, dev_x),
+            remote(o_source_low, o_low, bsend, brecv, 1, dev_y),
+            remote(o_source_low, o_low, bsend, brecv, 2, dev_x),
+            remote(o_source_top, o_top, bsend, brecv, 3, dev_y),
+            remote(o_top, o_top, bsend, brecv, 4, dev_y),
+            remote(o_low, o_low, bsend, brecv, 5, dev_x),
+        ]
+        source, from_x, from_y = chip == depth, chip_x == depth, chip_y == depth
+
+        @pl.when(source)
         def _():
             for copy in o_copies:
                 copy.wait_recv()
             total = o_mine[...].astype(F32)
             for i in range(depths - 1):
                 total = total + o_far[i].astype(F32)
-            osum_ref[...] = total.astype(BF16)
-
-        for copy in near_grads + [swap] + sends + core_swaps + q_copies:
+            o_sum[...] = total.astype(BF16)
+            for copy in b_copies[:4]:
+                copy.start()
+            o_all[core] = o_sum[...]
+
+        turn_sums()
+        r_copies[0].wait_recv()
+        r_copies[4].start()
+        r_copies[1].wait_recv()
+        r_copies[5].start()
+
+        @pl.when(from_x)
+        def _():
+            b_copies[0].wait_recv()
+            b_copies[4].start()
+            b_copies[2].wait_recv()
+
+        @pl.when(from_y)
+        def _():
+            b_copies[1].wait_recv()
+            b_copies[5].start()
+            b_copies[3].wait_recv()
+
+        for copies, passed in ((f_copies, f_shared), (r_copies, q_shared)):
+            copies[2].wait_recv()
+            passed[1].start()
+            copies[3].wait_recv()
+            passed[2].start()
+            copies[4].wait_recv()
+            copies[5].wait_recv()
+            passed[3].start()
+
+        @pl.when(chip_d == depth)
+        def _():
+            b_copies[4].wait_recv()
+            b_copies[5].wait_recv()
+
+        o_shared.start()
+        total_ref[...] = end()
+        for copy in f_shared + q_shared + [o_shared]:
+            copy.wait()
+        for copy in near_grads + [swap] + sends + core_swaps + q_copies + f_copies + r_copies:
             copy.wait_send()
         for i in range(depths - 1):
             pl.when(distance == i + 1)(o_copies[i].wait_send)
+        ff_finish()
+
+        @pl.when(source)
+        def _():
+            for copy in b_copies[:4]:
+                copy.wait_send()
+
+        pl.when(from_x)(b_copies[4].wait_send)
+        pl.when(from_y)(b_copies[5].wait_send)
 
     vmem = pltpu.VMEM
     block = (rows, width)
     wide_rows = (CHIPS, rows, width)
     q_block, o_block = (part_rows, columns), (half, width)
     kv_half = (2, CHIPS, rows, columns)
+    f_block = ff_grads.shape[1:]
+    line_buffers, line_sems = line_reduce_scratch(f_block, depths)
     return pl.pallas_call(
         kernel,
         out_shape=[
             jax.ShapeDtypeStruct((rows, 2, width), BF16),
-            jax.ShapeDtypeStruct(q_block, BF16),
-            jax.ShapeDtypeStruct(o_block, BF16),
+            jax.ShapeDtypeStruct((2 * CHIPS,) + f_block, BF16),
+            jax.ShapeDtypeStruct((2 * CHIPS,) + q_block, BF16),
+            jax.ShapeDtypeStruct((2,) + o_block, BF16),
             jax.ShapeDtypeStruct((8, width), F32),
         ],
-        in_specs=[SM] * 4 + [VM] * 16 + [ANY],
-        out_specs=[VM] * 4,
+        in_specs=[SM] * 4 + [VM] * 17 + [ANY],
+        out_specs=[VM] * 5,
         scratch_shapes=[
             vmem((queries, columns), BF16),
             vmem((columns, tokens), BF16),
@@ -1546,6 +1738,12 @@
             vmem(o_block, BF16),
             vmem(o_block, BF16),
             vmem((depths - 1,) + o_block, BF16),
+            vmem(f_block, BF16),
+            vmem(q_block, BF16),
+            vmem(o_block, BF16),
+            vmem((8, width), F32),
+            *line_buffers,
+            *line_sems,
             DMA,
             DMA((3,)),
             DMA((3,)),
@@ -1559,146 +1757,16 @@
             DMA((depths - 1,)),
             DMA((depths - 1,)),
             DMA((depths - 1,)),
+            *[DMA((6,))] * 6,
+            *[DMA((9,))] * 2,
+            *total_scratch((8, width), depths),
         ],
         compiler_params=comm_params(collective_id),
         name="backward",
     )(
         slots, lengths, predict, correct, att_grad, q_pairs, k_pairs, v_pairs, oT, lse, weights, states, up0, up1,
-        hidden_grad, sums, *out_grads, all_rows,
-    )
-
-
-def gather_gradients(ff, qkv, out, sums, collective_id):
-    depths = lax.axis_size("wsh")
-    half, width = out.shape
-
-    def kernel(
-        f_ref, q_ref, o_ref, s_ref, f_all, q_all, o_all, total_ref,
-        fsend, frecv, qsend, qrecv, osend, orecv, ssend, srecv, *total_refs,
-    ):
-        depth, chip, core, chip_x, chip_y, chip_d = place_on_mesh()
-        dev_x, dev_y = (2 * chip_x + core, depth), (2 * chip_y + core, depth)
-        other = (2 * chip + 1 - core, depth)
-        across = [
-            (2 * chip + core, lax.rem(depth + step, depths)) for step in range(1, depths)
-        ]
-        peers = plane_peers(chip, core, depth, chip_x, chip_y, chip_d)
-        signal_all(peers + across)
-        wait_all(peers + across)
-
-        def slot(chip_index):
-            return 2 * chip_index + core
-
-        start, turn, end = total_over_mesh(s_ref, *total_refs[:3], across, peers, *total_refs[3:])
-        start()
-        f_copies = ring_sends(
-            f_ref, f_all, slot, chip, core, depth, chip_x, chip_y, fsend, frecv
-        )
-        q_copies = ring_sends(
-            q_ref, q_all, slot, chip, core, depth, chip_x, chip_y, qsend, qrecv
-        )
-        for copy in f_copies[:2] + q_copies[:2]:
-            copy.start()
-        quarter = half // 2
-        o_top, o_low = o_all.at[core, pl.ds(0, quarter)], o_all.at[core, pl.ds(quarter, quarter)]
-        o_source_top, o_source_low = o_ref.at[pl.ds(0, quarter)], o_ref.at[pl.ds(quarter, quarter)]
-        o_copies = [
-            remote(o_source_top, o_top, osend, orecv, 0, dev_x),
-            remote(o_source_low, o_low, osend, orecv, 1, dev_y),
-            remote(o_source_low, o_low, osend, orecv, 2, dev_x),
-            remote(o_source_top, o_top, osend, orecv, 3, dev_y),
-            remote(o_top, o_top, osend, orecv, 4, dev_y),
-            remote(o_low, o_low, osend, orecv, 5, dev_x),
-        ]
-        source, from_x, from_y = chip == depth, chip_x == depth, chip_y == depth
-
-        @pl.when(source)
-        def _():
-            for copy in o_copies[:4]:
-                copy.start()
-            o_all[core] = o_ref[...]
-
-        for copy in f_copies[2:4] + q_copies[2:4]:
-            copy.start()
-        f_all[slot(chip)] = f_ref[...]
-        q_all[slot(chip)] = q_ref[...]
-
-        def shared(index, ref):
-            return remote(ref, ref, ssend, srecv, index, other)
-
-        f_shared = [shared(i, f_all.at[slot(c)]) for i, c in enumerate((chip, chip_x, chip_y, chip_d))]
-        q_shared = [shared(4 + i, q_all.at[slot(c)]) for i, c in enumerate((chip, chip_x, chip_y, chip_d))]
-        o_shared = shared(8, o_all.at[core])
-        f_shared[0].start()
-        q_shared[0].start()
-        turn()
-        for copies in (f_copies, q_copies):
-            copies[0].wait_recv()
-            copies[4].start()
-            copies[1].wait_recv()
-            copies[5].start()
-
-        @pl.when(from_x)
-        def _():
-            o_copies[0].wait_recv()
-            o_copies[4].start()
-            o_copies[2].wait_recv()
-
-        @pl.when(from_y)
-        def _():
-            o_copies[1].wait_recv()
-            o_copies[5].start()
-            o_copies[3].wait_recv()
-
-        for copies, passed in ((f_copies, f_shared), (q_copies, q_shared)):
-            copies[2].wait_recv()
-            passed[1].start()
-            copies[3].wait_recv()
-            passed[2].start()
-        for copies, passed in ((f_copies, f_shared), (q_copies, q_shared)):
-            copies[4].wait_recv()
-            copies[5].wait_recv()
-            passed[3].start()
-
-        @pl.when(chip_d == depth)
-        def _():
-            o_copies[4].wait_recv()
-            o_copies[5].wait_recv()
-
-        o_shared.start()
-        total_ref[...] = end()
-        for copy in f_shared + q_shared + [o_shared]:
-            copy.wait()
-        for copy in f_copies + q_copies:
-            copy.wait_send()
-
-        @pl.when(source)
-        def _():
-            for copy in o_copies[:4]:
-                copy.wait_send()
-
-        @pl.when(from_x)
-        def _():
-            o_copies[4].wait_send()
-
-        @pl.when(from_y)
-        def _():
-            o_copies[5].wait_send()
-
-    return pl.pallas_call(
-        kernel,
-        out_shape=[
-            jax.ShapeDtypeStruct((2 * CHIPS,) + ff.shape, BF16),
-            jax.ShapeDtypeStruct((2 * CHIPS,) + qkv.shape, BF16),
-            jax.ShapeDtypeStruct((2,) + out.shape, BF16),
-            jax.ShapeDtypeStruct(sums.shape, F32),
-        ],
-        in_specs=[VM] * 4,
-        out_specs=[VM] * 4,
-        scratch_shapes=[DMA((6,))] * 6 + [DMA((9,))] * 2 + total_scratch(sums.shape, depths),
-        compiler_params=comm_params(collective_id),
-        name="gather_gradients",
-    )(ff, qkv, out, sums)
+        hidden_grad, sums, ff_grads, *out_grads, all_rows,
+    )
 
 
 def lay_out(ff, qkv, out, sums, gain_one, gain_two):
@@ -1782,10 +1850,7 @@
     states, block_slot, cont_lengths, valid_mask, teacher, out_grad, predict, correct,
     norm_attn, w_query, w_key, w_value, w_out, norm_ffn, w_gate, w_up, w_down,
 ):
-    depths = lax.axis_size("wsh")
     _, rows, _, width = states.shape
-    half = w_query.shape[0] // 2
-    hidden_cols = w_gate.shape[1] // CHIPS
     slots, lengths = block_slot[0], cont_lengths[0]
     gain_one, gain_two = norm_attn[None], norm_ffn[None]
     states = states[0]
@@ -1794,14 +1859,10 @@
         w_query, w_key, w_value, w_out, w_gate, w_up, w_down, 1,
     )
     out_grads, (ff_sum, sums, all_rows, weights, q_pairs, k_pairs, v_pairs, oT, lse) = rest[:4], rest[4:]
-    ff_sum = lax.psum_scatter(
-        ff_sum.reshape(depths * 3 * half, hidden_cols), "wsh", scatter_dimension=0, tiled=True
-    )
-    states_grad, qkv_sum, out_sum, sums = backward(
+    states_grad, *gathered = backward(
         slots, lengths, predict, correct, att_grad.reshape(-1, CHIP_COLS), q_pairs, k_pairs, v_pairs, oT, lse,
-        weights, states, up0, up1, hidden_grad, sums, out_grads, all_rows.reshape(CHIPS, 2, rows, width), 2,
-    )
-    gathered = gather_gradients(ff_sum, qkv_sum, out_sum, sums, 3)
+        weights, states, up0, up1, hidden_grad, sums, ff_sum, out_grads, all_rows.reshape(CHIPS, 2, rows, width), 2,
+    )
     dq, dk, dv, do, dg, du, dd, g_one, g_two, predict_grad, correct_grad = lay_out(
         *gathered, gain_one, gain_two
     )

time: 244 us -> 222 us (0.910)
  between operations: 14.1 us -> 0.68 us
  Pallas kernels: 225 us -> 216 us
    pallas_call x1 -> x0, Pallas kernels: 36.5 us -> none  [gather_gradients(): pl.pallas_call(kernel, out_shape=[jax.ShapeDtypeStruct((2 * CHIPS,) + ff....]
    pallas_call x1, Pallas kernels: 57.5 us -> 84.7 us  [backward(): pl.pallas_call(kernel, out_shape=[jax.ShapeDtypeStruct((rows, 2, width),...]
  transfers between devices with their start and end apart: 1 -> 0, of which waited for: 0 -> 0; matrix products, arithmetic and copies ran while one was open for 0% -> 0% of each run, Pallas kernels for 24% -> 0%
where the time goes in v5:
time: 222 us; the launch traced here: 221 us
  Pallas kernels  216 us (97%)
  local copies, waits for them, and re-layouts  4.73 us (2%)
    pallas_call x1, Pallas kernels, forward(): pl.pallas_call(kernel, out_shape=outs, in_specs=[SM] * 4 + [VM] * 6 + [AN...  124 us
    pallas_call x1, Pallas kernels, backward(): pl.pallas_call(kernel, out_shape=[jax.ShapeDtypeStruct((rows, 2, width),...  84.7 us
    pallas_call x1, Pallas kernels, lay_out(): pl.pallas_call(kernel, out_shape=[square, square, square, square, tall, t...  7.52 us

profile of v5, /device:TPU:9, one launch (start us, length us, event | category | flops | bytes accessed | tf_op | source)
XLA Modules:
  0.0 221.1 jit_solution(227618403453536598)
XLA Ops:
  0.6 1.2 broadcast_in_dim.12.g1_ref
  1.9 1.2 broadcast_in_dim.13.g2_ref
  3.1 123.6 %forward.1 = (bf16[256,2,768]{2,1,0:T(2,128)(2,1)}, f32[256,768]{1,0:T(8,128)}, f32[256,768]{1,0:T(8,128)}, f32[256,768]{1,0:T(8,128)}, bf16[4,256,192]{2,1,0:T(...) custom-call(s32[32]{0:T(128)} %bitcast.20, ...), custom_call_target="tpu_custom_call" | custom-call | tf_op jit(solution)/shard_map/forward/pallas_call | solution.py:1284
  126.6 84.7 %backward.1 = (bf16[256,2,768]{2,1,0:T(2,128)(2,1)}, bf16[8,288,768]{2,1,0:T(8,128)(2,1)}, bf16[8,288,192]{2,1,0:T(8,128)(2,1)}, bf16[2,96,768]{2,1,0:T(8,128)(2,1)}, f32[8,768]{1,0:T(8,128)}) custom-call(s32[32]{0:T(128)} %bitcast.21, s32[4]{0:T(128)} %bitcast.23, f32[2,2]{1,0:T(2,128)} %p_ref.3, f32[2]{0:T(128)} %c_ref.3, bf16[1024,192]{1,0:T(8,128)(2,1)} %bitcast.19, ...), custom_call_target="tpu_custom_call" | custom-call | tf_op jit(solution)/shard_map/backward/pallas_call | solution.py:1699
  211.3 0.0 copy-start
  211.3 7.5 %lay_out.1 = (f32[192,768]{1,0:T(8,128)}, f32[192,768]{1,0:T(8,128)}, f32[192,768]{1,0:T(8,128)}, f32[192,768]{1,0:T(8,128)}, f32[192,3072]{1,0:T(8,128)}, /*ind...) custom-call(bf16[8,288,768]{2,1,0:T(8,128)(2,1)} %get-tuple-element., ...), custom_call_target="tpu_custom_call" | custom-call | tf_op jit(solution)/shard_map/lay_out/pallas_call | solution.py:1827
  218.8 0.0 copy-start.1
  218.9 0.0 copy-done
  218.9 0.9 copy.32
  219.7 0.5 copy-done.1
  220.3 0.9 copy.33
Async XLA Ops:
  211.3 7.5 %copy-start = (bf16[256,2,768]{2,1,0:T(2,128)(2,1)S(1)}, bf16[256,2,768]{2,1,0:T(2,128)(2,1)}, u32[]{:S(2)}) copy-start(bf16[256,2,768]{2,1,0:T(2,128)(2,1)} %get-tuple-element.47) | copy-start | bytes 2359300
  218.8 1.4 copy-start.1

commit v6 on v5

--- a/solution.py
+++ b/solution.py
@@ -501,6 +501,36 @@
     return p_ref[i, 0] * states_ref[at, 0, :].astype(F32) + p_ref[i, 1] * states_ref[at, 1, :].astype(F32)
 
 
+def plane_sum(parts, near_in, far_in, chip, core, depth, chip_x, chip_y, chip_d, send, recv):
+    half = parts.shape[1] // 2
+    top, low = pl.ds(0, half), pl.ds(half, half)
+    dev_x, dev_y = (2 * chip_x + core, depth), (2 * chip_y + core, depth)
+    copies = [
+        remote(parts.at[chip_d, top], far_in.at[0], send, recv, 0, dev_x),
+        remote(parts.at[chip_d, low], far_in.at[1], send, recv, 1, dev_y),
+        remote(parts.at[chip_x, top], near_in.at[0, top], send, recv, 2, dev_x),
+        remote(parts.at[chip_y, low], near_in.at[1, low], send, recv, 3, dev_y),
+        remote(parts.at[chip_y, top], near_in.at[1, top], send, recv, 4, dev_y),
+        remote(parts.at[chip_x, low], near_in.at[0, low], send, recv, 5, dev_x),
+    ]
+
+    def give(i):
+        for copy in (copies[:2] if i == 2 else copies[2 + i : 3 + i]):
+            copy.start()
+
+    def relay():
+        for i, (c, rows) in enumerate(((chip_y, slice(0, half)), (chip_x, slice(half, 2 * half)))):
+            copies[i].wait_recv()
+            parts[c, rows] = (parts[c, rows].astype(F32) + far_in[i].astype(F32)).astype(BF16)
+            copies[4 + i].start()
+
+    def receive():
+        for copy in copies[2:]:
+            copy.wait_recv()
+
+    return give, relay, receive, copies
+
+
 def plane_peers(chip, core, depth, chip_x, chip_y, chip_d):
     same = [(2 * c + core, depth) for c in (chip_x, chip_y, chip_d)]
     return same + [(2 * c + 1 - core, depth) for c in (chip, chip_x, chip_y, chip_d)]
@@ -712,13 +742,6 @@
                 down(down_out.at[k - 1], k).wait_send()
 
     return start, hop, result, finish
-
-
-def line_reduce_scratch(shape, depths):
-    buffers = [(depths - 1,), (depths - 1,), (depths - 2,), (depths - 2,)]
-    return [pltpu.VMEM(shape, F32)] + [pltpu.VMEM(lead + shape, BF16) for lead in buffers], [
-        DMA((depths - 1,))
-    ] * 4
 
 
 def forward(
@@ -747,15 +770,24 @@
     def kernel(
         slots_ref, lengths_ref, p_ref, c_ref, s_ref, g_ref, t_ref, v_ref, g1_ref, g2_ref,
         wq_ref, wk_ref, wv_ref, wo_ref, wg_ref, wu_ref, wd_ref,
-        new_ref, up0_ref, up1_ref, hg_ref, da_ref, dw0_ref, dw1_ref, dw2_ref, dw3_ref, ff_ref, sums_ref,
-        all_rows, w_all, q_pairs, k_pairs, v_pairs, oT_ref, lse_ref,
+        new_out, up0_out, up1_out, hg_out, da_ref, dwo_ref, ffa_ref, ffb_ref, sums_ref,
+        x_out, w_out_ref, q_out, k_out, v_out, oT_out, lse_ref,
+        new_ref, up0_ref, up1_ref, hg_ref, all_rows, w_all, q_pairs, k_pairs, v_pairs, oT_ref, dwo, dwo_other,
         w_ff, w_wo, qkv, att_all, hidden, own, x_rows, r_rows, xT, innerT, inner, gate, up, gate_low, up_low,
-        own_weight, part1, part2, got1, got2, dw, dw_other, buf, wide, count, q_slot, k_slot, v_slot, vT,
+        own_weight, part1, part2, got1, got2, far1, far2, dw, dw_other, a_up, a_down, buf, wide, count, q_slot, k_slot, v_slot, vT,
         lsend, fsend, frecv, fosend, forecv, qsend, qrecv, qosend, qorecv,
         osend, orecv, oosend, oorecv, opsend, oprecv,
         rsend, rrecv, rosend, rorecv, send0, recv0, send1, recv1, send2, recv2, send3, recv3,
-        ag1s, ag1r, ag2s, ag2r, dsend, drecv, *total_refs,
+        ag1s, ag1r, ag2s, ag2r, dsend, drecv, osems, xsems, *rest,
     ):
+        a_sems, total_refs = rest[:4], rest[4:]
+        stores = []
+
+        def store(index, source, target):
+            copy = pltpu.make_async_copy(source, target, osems.at[index])
+            copy.start()
+            stores.append(copy)
+
         depth, chip, core, chip_x, chip_y, chip_d = place_on_mesh()
         near = [(c, (2 * c + core, depth)) for c in (chip_x, chip_y, chip_d)]
         other = (2 * chip + 1 - core, depth)
@@ -965,18 +997,33 @@
             carried(i, came_here)
         for i in range(depths - 1):
             not_carried(i, o_shared[i].wait_recv)
+        carry = pl.ds(core * (depths // 2), depths // 2)
         o_plane = [
-            remote(w_wo.at[:, chip], w_wo.at[:, chip], opsend, oprecv, i, device)
+            remote(w_wo.at[carry, chip], w_wo.at[carry, chip], opsend, oprecv, i, device)
             for i, (_, device) in enumerate(near)
         ]
         for copy in o_plane:
             copy.start()
+        o_across = [
+            remote(w_wo.at[carry, c], w_wo.at[carry, c], opsend, oprecv, 3 + i, other)
+            for i, (c, _) in enumerate(near)
+        ]
         shared0[3].wait_recv()
         project(2 * chip_d + 1 - core, False)
+
+        for i in range(CHIPS):
+            x_copy = pltpu.make_async_copy(all_rows.at[2 * i + core], x_out.at[i], xsems.at[i])
+            x_copy.start()
+            stores.append(x_copy)
+        store(0, w_all, w_out_ref)
 
         to_pair_order(k_slot, k_pairs, slots_ref, group_pairs)
         to_pair_order(v_slot, v_pairs, slots_ref, group_pairs)
         own_to_pair_order(q_slot, q_pairs, slots_ref, pairs, per_device)
+
+        store(1, q_pairs, q_out)
+        store(2, k_pairs, k_out)
+        store(3, v_pairs, v_out)
 
         def turn_values(i, _):
             vT[:, aligned(i, TILE)] = v_pairs[aligned(i, TILE), :].T
@@ -1032,8 +1079,12 @@
         both_steps(1)
         take_hop(1)
         send_hop(2)
+        for copy, passed in zip(o_plane, o_across):
+            copy.wait_recv()
+            passed.start()
         both_steps(0)
 
+        store(4, oT_ref, oT_out)
         own_to_slot_order(q_slot, k_slot, slots_ref, pairs, per_device)
         for c in range(CHIPS):
             att_all[CHIPS + c] = k_slot[c * rows : (c + 1) * rows, :]
@@ -1046,7 +1097,7 @@
         att_all[chip] = att_all[CHIPS + chip]
         take_hop(2)
         send_hop(3)
-        for copy in o_plane:
+        for copy in o_across:
             copy.wait_recv()
         for copy in sends0:
             copy.wait()
@@ -1099,9 +1150,9 @@
                 inner[c, :, cols] = (gelu_parts(g)[0] * u).astype(BF16)
             return jnp.dot(inner[c], w_rows(2), preferred_element_type=F32)
 
-        sends1 = [
-            remote(part1.at[c], got1.at[i], send1, recv1, i, device) for i, (c, device) in enumerate(near)
-        ]
+        give1, relay1, receive1, sends1 = plane_sum(
+            part1, got1, far1, chip, core, depth, chip_x, chip_y, chip_d, send1, recv1
+        )
         up0_ref[...] = ff_forward(chip)
         for i, (c, _) in enumerate(near):
             if i < 2:
@@ -1110,7 +1161,8 @@
                 ring1[4].wait_recv()
                 ring1[5].wait_recv()
             part1[c] = ff_forward(c).astype(BF16)
-            sends1[i].start()
+            give1(i)
+        relay1()
 
         def turn(i, _):
             xT[:, aligned(i, rows)] = x_rows[i].T
@@ -1121,14 +1173,13 @@
         valid_count = end_count()
         weight = as_column(v_ref[...].astype(F32)) * (mesh_tokens / valid_count[0:1, 0:1])
         own_weight[...] = jnp.broadcast_to(weight, own_weight.shape)
-        for copy in sends1:
-            copy.wait_recv()
+        receive1()
 
         def outputs(i, sums):
             at = aligned(i, ROWS)
             a = mix(s_ref, at, p_ref, 0)
             result = hidden[at, :] + up0_ref[at, :]
-            for j in range(3):
+            for j in range(2):
                 result = result + got1[j, at, :].astype(F32)
             difference = result - a
             row_weight = own_weight[at, 0:1]
@@ -1152,6 +1203,9 @@
         sums_ref[...] = jnp.zeros_like(sums_ref)
         sums_ref[2:3, :] = correct_sums[0]
         sums_ref[3:4, :] = correct_sums[1]
+        store(5, new_ref, new_out)
+        store(6, up0_ref, up0_out)
+        store(7, up1_ref, up1_out)
 
         ring2 = ring(own.at[2], r_rows, ag2s, ag2r)
         for copy in ring2[:4]:
@@ -1170,9 +1224,9 @@
                 gate_low[c], w_rows(0), NT, preferred_element_type=F32
             ) + lax.dot_general(up_low[c], w_rows(1), NT, preferred_element_type=F32)
 
-        sends2 = [
-            remote(part2.at[c], got2.at[i], send2, recv2, i, device) for i, (c, device) in enumerate(near)
-        ]
+        give2, relay2, receive2, sends2 = plane_sum(
+            part2, got2, far2, chip, core, depth, chip_x, chip_y, chip_d, send2, recv2
+        )
         hg_ref[...] = ff_backward(chip)
         ring2[0].wait_recv()
         ring2[4].start()
@@ -1185,29 +1239,58 @@
                 ring2[4].wait_recv()
                 ring2[5].wait_recv()
             part2[c] = ff_backward(c).astype(BF16)
-            sends2[i].start()
-
-        def weight_grads(z, _):
-            at = aligned(z, shard)
-            for i, (left, right) in enumerate(((xT, gate_low), (xT, up_low), (innerT, r_rows))):
-                grad = jnp.dot(
-                    left[at, :], right[...].reshape(queries, -1), preferred_element_type=F32
+            give2(i)
+
+        def weight_grads(terms):
+            def body(z, _):
+                at = aligned(z, shard)
+                for i, left, right in terms:
+                    grad = jnp.dot(
+                        left[at, :], right[...].reshape(queries, -1), preferred_element_type=F32
+                    ).astype(BF16)
+                    dw[z, 0, i * half : (i + 1) * half, :] = grad[:half]
+                    dw[z, 1, i * half : (i + 1) * half, :] = grad[half:]
+                return 0
+
+            lax.fori_loop(0, depths, body, 0)
+
+        early, late = pl.ds(0, half), pl.ds(half, 2 * half)
+
+        def swap_rows(index, part):
+            return remote(dw.at[:, 1 - core, part], dw_other.at[:, part], dsend, drecv, index, other)
+
+        def add_cores(part):
+            def body(z, _):
+                dw_other[z, part, :] = (
+                    dw[z, core, part, :].astype(F32) + dw_other[z, part, :].astype(F32)
                 ).astype(BF16)
-                dw[z, 0, i * half : (i + 1) * half, :] = grad[:half]
-                dw[z, 1, i * half : (i + 1) * half, :] = grad[half:]
-            return 0
-
-        lax.fori_loop(0, depths, weight_grads, 0)
-        swap = remote(dw.at[:, 1 - core], dw_other, dsend, drecv, 0, other)
-        swap.start()
-        for copy in sends2:
-            copy.wait_recv()
+                return 0
+
+            lax.fori_loop(0, depths, body, 0)
+
+        swaps = [swap_rows(0, early), swap_rows(1, late)]
+        weight_grads(((0, innerT, r_rows),))
+        swaps[0].start()
+        for copy in sends1:
+            copy.wait_send()
+        a_start, a_hop, a_result, a_finish = line_reduce(
+            dw_other.at[:, early], gate.at[0, pl.ds(0, half)], a_up, a_down,
+            part1.at[pl.ds(0, 2), pl.ds(0, half)], part1.at[pl.ds(2, 2), pl.ds(0, half)], a_sems,
+        )
+        swaps[0].wait_recv()
+        add_cores(early)
+        a_start()
+        relay2()
+        weight_grads(((1, xT, gate_low), (2, xT, up_low)))
+        swaps[1].start()
+        a_hop(1)
+        receive2()
 
         def second_norm(i, gain_sum):
             at = aligned(i, ROWS)
             h = hidden[at, :]
             weighted = hg_ref[at, :]
-            for j in range(3):
+            for j in range(2):
                 weighted = weighted + got2[j, at, :].astype(F32)
             factor = norm_factor(h)
             mean = jnp.mean(weighted * h, axis=1, keepdims=True)
@@ -1218,6 +1301,7 @@
             return gain_sum + jnp.sum(weighted * h * factor, axis=0, keepdims=True)
 
         sums_ref[1:2, :] = lax.fori_loop(0, blocks, second_norm, zero)
+        store(10, hg_ref, hg_out)
 
         sends3 = [
             remote(att_all.at[CHIPS + c], da_ref.at[chip], send3, recv3, i, device)
@@ -1231,26 +1315,36 @@
             att_all[CHIPS + near[i][0]] = att_grad(near[i][0])
             sends3[i].start()
         da_ref[chip] = att_grad(chip)
-        for c, ref in zip((chip, chip_x, chip_y, chip_d), (dw0_ref, dw1_ref, dw2_ref, dw3_ref)):
-            ref[...] = jnp.dot(att_all[c].T, own[3], preferred_element_type=F32).astype(BF16)
-        swap.wait_recv()
-
-        def add_cores(z, _):
-            ff_ref[z] = (dw[z, core].astype(F32) + dw_other[z].astype(F32)).astype(BF16)
-            return 0
-
-        lax.fori_loop(0, depths, add_cores, 0)
+        for i, c in enumerate((chip, chip_x, chip_y, chip_d)):
+            grad = jnp.dot(att_all[c].T, own[3], preferred_element_type=F32).astype(BF16)
+            dwo[i, 0] = grad[:half]
+            dwo[i, 1] = grad[half:]
+        out_swap = remote(dwo.at[:, 1 - core], dwo_other, dsend, drecv, 2, other)
+        out_swap.start()
+        swaps[1].wait_recv()
+        add_cores(late)
+        store(8, dw_other.at[:, late], ffb_ref)
+        a_hop(2)
+        out_swap.wait_recv()
+        for i in range(CHIPS):
+            dwo_other[i] = (dwo[i, core].astype(F32) + dwo_other[i].astype(F32)).astype(BF16)
+        store(9, dwo_other, dwo_ref)
+        a_result()
+        ffa_ref[...] = gate[0, 0:half, :].astype(BF16)
         for copy in sends3:
             copy.wait_recv()
-        sent = ring0 + shared0 + q_copies + q_shared + o_plane + sends1 + sends2 + sends3
-        for copy in sent + ring1 + ring2 + [swap, ff_mine]:
+        sent = ring0 + shared0 + q_copies + q_shared + o_plane + o_across + sends2 + sends3
+        for copy in sent + ring1 + ring2 + swaps + [out_swap, ff_mine]:
             copy.wait_send()
+        a_finish()
         for i in range(depths - 1):
             carried(i, o_copies[i].wait_send)
             carried(i, o_shared[i].wait_send)
         for _, sends, receives, hop, share in hops:
             pl.when(sends)(hop.wait_send)
             pl.when(receives)(share.wait_send)
+        for copy in stores:
+            copy.wait()
 
     block = (rows, width)
     pair = (rows, 2, width)
@@ -1267,13 +1361,11 @@
         out(block, F32),
         out(block, F32),
         out((CHIPS, rows, CHIP_COLS), BF16),
-        out((CHIP_COLS, width), BF16),
-        out((CHIP_COLS, width), BF16),
-        out((CHIP_COLS, width), BF16),
-        out((CHIP_COLS, width), BF16),
-        out((depths, 3 * half, columns), BF16),
+        out((CHIPS, half, width), BF16),
+        out((half, columns), BF16),
+        out((depths, 2 * half, columns), BF16),
         out((8, width), F32),
-        out((2 * CHIPS, rows, width), BF16),
+        out(wide_rows, BF16),
         out((3, width, CHIP_COLS), BF16),
         out((queries, CHIP_COLS), BF16),
         out((tokens, CHIP_COLS), BF16),
@@ -1285,8 +1377,20 @@
         kernel,
         out_shape=outs,
         in_specs=[SM] * 4 + [VM] * 6 + [ANY] * 7,
-        out_specs=[VM] * len(outs),
+        out_specs=[ANY] * 4 + [VM, ANY, VM, ANY, VM] + [ANY] * 6 + [VM],
         scratch_shapes=[
+            vmem(pair, BF16),
+            vmem(block, F32),
+            vmem(block, F32),
+            vmem(block, F32),
+            vmem((2 * CHIPS, rows, width), BF16),
+            vmem((3, width, CHIP_COLS), BF16),
+            vmem((queries, CHIP_COLS), BF16),
+            vmem((tokens, CHIP_COLS), BF16),
+            vmem((tokens, CHIP_COLS), BF16),
+            vmem((tiles, CHIP_COLS, TILE), F32),
+            vmem((CHIPS, 2, half, width), BF16),
+            vmem((CHIPS, half, width), BF16),
             vmem((3, depths, 2, half, columns), BF16),
             vmem((depths, CHIPS, out_rows, width), BF16),
             vmem((depths, 2, half, piece_lanes), BF16),
@@ -1305,10 +1409,14 @@
             vmem((rows, 128), F32),
             vmem(wide_rows, BF16),
             vmem(wide_rows, BF16),
-            vmem((3,) + block, BF16),
-            vmem((3,) + block, BF16),
+            vmem((2,) + block, BF16),
+            vmem((2,) + block, BF16),
+            vmem((2, rows // 2, width), BF16),
+            vmem((2, rows // 2, width), BF16),
             vmem((depths, 2, 3 * half, columns), BF16),
             vmem((depths, 3 * half, columns), BF16),
+            vmem((depths - 1, half, columns), BF16),
+            vmem((depths - 1, half, columns), BF16),
             vmem((3, half, width), BF16),
             vmem((2, half, hidden_cols), BF16),
             vmem((8, 128), F32),
@@ -1323,12 +1431,16 @@
         + [DMA((depths - 1,))] * 2
         + [DMA((depths,))] * 2
         + [DMA((depths - 1,))] * 4
-        + [DMA((3,))] * 2
+        + [DMA((6,))] * 2
         + [DMA((6,))] * 2
         + [DMA((4,))] * 2
-        + [DMA((3,))] * 8
+        + [DMA((3,))] * 2
         + [DMA((6,))] * 4
-        + [DMA((1,))] * 2
+        + [DMA((3,))] * 2
+        + [DMA((6,))] * 4
+        + [DMA((3,))] * 2
+        + [DMA((11,)), DMA((CHIPS,))]
+        + [DMA((depths - 1,))] * 4
         + total_scratch((8, 128), depths),
         compiler_params=comm_params(collective_id),
         name="forward",
@@ -1339,14 +1451,14 @@
 
 
 def backward(
-    slots, lengths, predict, correct, att_grad, q_pairs, k_pairs, v_pairs, oT, lse, weights, states, up0, up1,
-    hidden_grad, sums, ff_grads, out_grads, all_rows, collective_id,
+    slots, lengths, predict, correct, att_grad, q_pairs, k_pairs, v_pairs, oT, lse, sums, up_grads,
+    out_grads, ff_early, weights, states, up0, up1, hidden_grad, own_rows, collective_id,
 ):
     rows, _, width = states.shape
-    depths = lax.axis_size("wsh")
+    depths, late_rows, ff_columns = up_grads.shape
+    half = late_rows // 2
     columns = CHIP_COLS
-    half = width // (2 * depths)
-    part_rows = 3 * half
+    lanes_all = 3 * columns
     blocks = rows // ROWS
     tokens = k_pairs.shape[0]
     queries = q_pairs.shape[0]
@@ -1358,18 +1470,16 @@
     wide_lanes = LOCAL_HEADS * TILE
 
     def kernel(
-        slots_ref, lengths_ref, p_ref, c_ref, g_ref, q_ref, k_ref, v_ref, oT_ref, lse_ref, w_all, s_ref,
-        up0_ref, up1_ref, hg_ref, sums_ref, ff_ref, o0, o1, o2, o3, rows_ref,
-        grad_ref, f_all, q_all, o_all, total_ref,
+        slots_ref, lengths_ref, p_ref, c_ref, g_ref, q_ref, k_ref, v_ref, oT_ref, lse_ref, sums_ref, u_ref,
+        og_ref, fa_ref, w_in, s_in, up0_in, up1_in, hg_in, x_in,
+        grad_ref, fa_all, fb_all, q_all, o_all, total_ref,
+        w_all, s_ref, up0_ref, up1_ref, hg_ref, x_own, fa_own,
         g_pairs, kT, doT, dqT, q_stack, do_stack, p_buf, ds_buf, dk_acc, dv_acc, bias, dq_pairs, dq_rows,
-        give, kept, came, x_own, xT, part, got, mine, q_grad, q_other, q_mine, q_far,
-        o_near, o_grad, o_other, o_mine, o_far, f_mine, q_sum, o_sum, all_sums, *rest,
+        give, kept, came, xT, part, got, far, mine, q_grad, q_other, q_mine, q_far, q_sum,
+        o_near, o_mine, o_far, o_sum, u_far, u_sum, all_sums,
+        loads, nsend, nrecv, ksend, krecv, send, recv, ssend, srecv, zsend, zrecv, osend, orecv, usend, urecv,
+        asend, arecv, fsend, frecv, gsend, grecv, bsend, brecv, psend, precv, *total_refs,
     ):
-        (
-            f_acc, f_up_in, f_down_in, f_up_out, f_down_out, f_us, f_ur, f_ds, f_dr,
-            xload, nsend, nrecv, ksend, krecv, send, recv, ssend, srecv, zsend, zrecv, osend, orecv,
-            fsend, frecv, gsend, grecv, bsend, brecv, psend, precv, *total_refs,
-        ) = rest
         depth, chip, core, chip_x, chip_y, chip_d = place_on_mesh()
         near = [(c, (2 * c + core, depth)) for c in (chip_x, chip_y, chip_d)]
         other = (2 * chip + 1 - core, depth)
@@ -1379,9 +1489,55 @@
         peers = plane_peers(chip, core, depth, chip_x, chip_y, chip_d)
         everyone = peers + across
         signal_all(everyone)
-        load = pltpu.make_async_copy(rows_ref.at[:, core], x_own, xload)
-        load.start()
+
+        def slot(chip_index):
+            return 2 * chip_index + core
+
+        def load(index, source, target):
+            copy = pltpu.make_async_copy(source, target, loads.at[index])
+            copy.start()
+            return copy
+
+        early_load = load(0, fa_ref, fa_own)
+        other_loads = [
+            load(1 + i, source, target)
+            for i, (source, target) in enumerate(
+                (
+                    (w_in, w_all), (x_in, x_own), (s_in, s_ref), (up0_in, up0_ref), (up1_in, up1_ref), (hg_in, hg_ref)
+                )
+            )
+        ]
+
+        def depth_sum(source_of, inbox, sends, receives):
+            return [
+                remote(source_of(lax.rem(depth + i + 1, depths)), inbox.at[i], sends, receives, i, device)
+                for i, device in enumerate(across)
+            ]
+
         own_to_pair_order(g_ref, g_pairs, slots_ref, pairs, per_device)
+        early_load.wait()
+        wait_all(everyone)
+        u_copies = depth_sum(lambda z: u_ref.at[z], u_far, usend, urecv)
+        near_grads = [
+            remote(og_ref.at[1 + i], o_near.at[i], nsend, nrecv, i, device)
+            for i, (_, device) in enumerate(near)
+        ]
+        a_ring = ring_sends(
+            fa_own, fa_all, slot, chip, core, depth, chip_x, chip_y, asend, arecv
+        )
+        for copy in u_copies + near_grads + a_ring[:4]:
+            copy.start()
+
+        def shared(index, ref):
+            return remote(ref, ref, psend, precv, index, other)
+
+        in_plane = (chip, chip_x, chip_y, chip_d)
+        a_shared = [shared(i, fa_all.at[slot(c)]) for i, c in enumerate(in_plane)]
+        b_shared = [shared(4 + i, fb_all.at[slot(c)]) for i, c in enumerate(in_plane)]
+        q_shared = [shared(8 + i, q_all.at[slot(c)]) for i, c in enumerate(in_plane)]
+        o_shared = shared(12, o_all.at[core])
+        fa_all[slot(chip)] = fa_own[...]
+        a_shared[0].start()
 
         def turn_keys(i, _):
             at = aligned(i, TILE)
@@ -1389,16 +1545,6 @@
             return 0
 
         lax.fori_loop(0, tokens // TILE, turn_keys, 0)
-        wait_all(everyone)
-        near_grads = [
-            remote(ref, o_near.at[i], nsend, nrecv, i, near[i][1]) for i, ref in enumerate((o1, o2, o3))
-        ]
-        for copy in near_grads:
-            copy.start()
-        ff_start, ff_hop, ff_result, ff_finish = line_reduce(
-            ff_ref, f_acc, f_up_in, f_down_in, f_up_out, f_down_out, (f_us, f_ur, f_ds, f_dr)
-        )
-        ff_start()
 
         def attend(kind, step):
             tile = kind * (tiles // 2) + step
@@ -1450,7 +1596,11 @@
                 return 0
 
             lax.fori_loop(0, tiles // 2, body, 0)
-            ff_hop(2 - kind)
+            if kind == 1:
+                a_ring[0].wait_recv()
+                a_ring[4].start()
+                a_ring[1].wait_recv()
+                a_ring[5].start()
 
         def slot_rows(target, side, chip_index, pair_index):
             pair = chip_index * per_device + side * (per_device // 2) + pair_index
@@ -1470,6 +1620,19 @@
             for i in range(per_device // 2):
                 slot_rows(kept, core, c, i)
         own_to_slot_order(dq_pairs, dq_rows, slots_ref, pairs, per_device)
+
+        for copy in near_grads:
+            copy.wait_recv()
+        whole = og_ref[0].astype(F32)
+        for i in range(3):
+            whole = whole + o_near[i].astype(F32)
+        o_mine[...] = whole.astype(BF16)
+        distance = lax.rem(chip + depths - depth, depths)
+        o_copies = [
+            remote(o_mine, o_far.at[i], osend, orecv, i, device) for i, device in enumerate(across)
+        ]
+        for i in range(depths - 1):
+            pl.when(distance == i + 1)(o_copies[i].start)
         swap.wait_recv()
 
         def add_cores(c, _):
@@ -1478,6 +1641,8 @@
             return 0
 
         lax.fori_loop(0, CHIPS, add_cores, 0)
+        for copy in other_loads:
+            copy.wait()
 
         def rows_grad(c):
             return (
@@ -1488,14 +1653,13 @@
                 + lax.dot_general(kept[1, c], w_all[2], NT, preferred_element_type=F32)
             )
 
-        sends = [
-            remote(part.at[c], got.at[i], send, recv, i, device) for i, (c, device) in enumerate(near)
-        ]
+        give_rows, relay_rows, receive_rows, sends = plane_sum(
+            part, got, far, chip, core, depth, chip_x, chip_y, chip_d, send, recv
+        )
         for i in (2, 0, 1):
             part[near[i][0]] = rows_grad(near[i][0]).astype(BF16)
-            sends[i].start()
+            give_rows(i)
         mine[...] = rows_grad(chip)
-        load.wait()
 
         def turn(c, _):
             xT[:, aligned(c, rows)] = x_own[c].T
@@ -1505,74 +1669,58 @@
 
         def weight_grads(z, _):
             at = aligned(z, 2 * half)
+            grads = []
             for i in range(3):
                 right = dq_rows[...] if i == 0 else kept[i - 1].reshape(queries, columns)
-                grad = jnp.dot(xT[at, :], right, preferred_element_type=F32).astype(BF16)
-                q_grad[z, 0, i * half : (i + 1) * half, :] = grad[:half]
-                q_grad[z, 1, i * half : (i + 1) * half, :] = grad[half:]
+                grads.append(jnp.dot(xT[at, :], right, preferred_element_type=F32))
+            grad = jnp.concatenate(grads, axis=1).astype(BF16)
+            q_grad[z, 0] = grad[:half]
+            q_grad[z, 1] = grad[half:]
             return 0
 
+        for copy in u_copies:
+            copy.wait_recv()
+        whole = u_ref[depth].astype(F32)
+        for i in range(depths - 1):
+            whole = whole + u_far[i].astype(F32)
+        u_sum[...] = whole.astype(BF16)
+        b_ring = ring_sends(
+            u_sum, fb_all, slot, chip, core, depth, chip_x, chip_y, fsend, frecv
+        )
+        for copy in b_ring[:4]:
+            copy.start()
+        fb_all[slot(chip)] = u_sum[...]
+        b_shared[0].start()
+
         lax.fori_loop(0, depths, weight_grads, 0)
-        for copy in near_grads:
-            copy.wait_recv()
-        whole = o0[...].astype(F32)
-        for i in range(3):
-            whole = whole + o_near[i].astype(F32)
-        whole = whole.astype(BF16)
-        o_grad[0] = whole[:half]
-        o_grad[1] = whole[half:]
-        core_swaps = [
-            remote(q_grad.at[:, 1 - core], q_other, ssend, srecv, 0, other),
-            remote(o_grad.at[1 - core], o_other, ssend, srecv, 1, other),
-        ]
-        for copy in core_swaps:
-            copy.start()
-        for copy in core_swaps:
-            copy.wait_recv()
+        core_swap = remote(q_grad.at[:, 1 - core], q_other, ssend, srecv, 0, other)
+        core_swap.start()
+        relay_rows()
+        core_swap.wait_recv()
         for i in range(depths):
             q_mine[i] = (q_grad[i, core].astype(F32) + q_other[i].astype(F32)).astype(BF16)
-        q_copies = [
-            remote(q_mine.at[lax.rem(depth + i + 1, depths)], q_far.at[i], zsend, zrecv, i, device)
-            for i, device in enumerate(across)
-        ]
+        q_copies = depth_sum(lambda z: q_mine.at[z], q_far, zsend, zrecv)
         for copy in q_copies:
             copy.start()
-        o_mine[...] = (o_grad[core].astype(F32) + o_other[...].astype(F32)).astype(BF16)
-        distance = lax.rem(chip + depths - depth, depths)
-        o_copies = [
-            remote(o_mine, o_far.at[i], osend, orecv, i, device) for i, device in enumerate(across)
-        ]
-        for i in range(depths - 1):
-            pl.when(distance == i + 1)(o_copies[i].start)
-        ff_result()
-        f_mine[...] = f_acc[...].astype(BF16)
-
-        def slot(chip_index):
-            return 2 * chip_index + core
-
-        f_copies = ring_sends(
-            f_mine, f_all, slot, chip, core, depth, chip_x, chip_y, fsend, frecv
-        )
-        for copy in f_copies[:4]:
-            copy.start()
-        f_all[slot(chip)] = f_mine[...]
-
-        def shared(index, ref):
-            return remote(ref, ref, psend, precv, index, other)
-
-        f_shared = [shared(i, f_all.at[slot(c)]) for i, c in enumerate((chip, chip_x, chip_y, chip_d))]
-        q_shared = [shared(4 + i, q_all.at[slot(c)]) for i, c in enumerate((chip, chip_x, chip_y, chip_d))]
-        o_shared = shared(8, o_all.at[core])
-        f_shared[0].start()
-        for copy in sends:
-            copy.wait_recv()
+        b_ring[0].wait_recv()
+        b_ring[4].start()
+        b_ring[1].wait_recv()
+        b_ring[5].start()
+        a_ring[2].wait_recv()
+        a_shared[1].start()
+        a_ring[3].wait_recv()
+        a_shared[2].start()
+        a_ring[4].wait_recv()
+        a_ring[5].wait_recv()
+        a_shared[3].start()
+        receive_rows()
 
         def state_grads(i, totals):
             at = aligned(i, ROWS)
             s0, s1 = s_ref[at, 0, :].astype(F32), s_ref[at, 1, :].astype(F32)
             a = p_ref[0, 0] * s0 + p_ref[0, 1] * s1
             weighted = mine[at, :]
-            for j in range(3):
+            for j in range(2):
                 weighted = weighted + got[j, at, :].astype(F32)
             factor = norm_factor(a)
             mean = jnp.mean(weighted * a, axis=1, keepdims=True)
@@ -1596,20 +1744,16 @@
             all_sums, *total_refs[:3], across, peers, *total_refs[3:]
         )
         start()
-        f_copies[0].wait_recv()
-        f_copies[4].start()
-        f_copies[1].wait_recv()
-        f_copies[5].start()
         for copy in q_copies:
             copy.wait_recv()
-        total = q_mine[depth].astype(F32)
+        whole = q_mine[depth].astype(F32)
         for i in range(depths - 1):
-            total = total + q_far[i].astype(F32)
-        q_sum[...] = total.astype(BF16)
-        r_copies = ring_sends(
+            whole = whole + q_far[i].astype(F32)
+        q_sum[...] = whole.astype(BF16)
+        q_ring = ring_sends(
             q_sum, q_all, slot, chip, core, depth, chip_x, chip_y, gsend, grecv
         )
-        for copy in r_copies[:4]:
+        for copy in q_ring[:4]:
             copy.start()
         q_all[slot(chip)] = q_sum[...]
         q_shared[0].start()
@@ -1617,7 +1761,7 @@
         o_top, o_low = o_all.at[core, pl.ds(0, quarter)], o_all.at[core, pl.ds(quarter, quarter)]
         o_source_top, o_source_low = o_sum.at[pl.ds(0, quarter)], o_sum.at[pl.ds(quarter, quarter)]
         dev_x, dev_y = near[0][1], near[1][1]
-        b_copies = [
+        o_ring = [
             remote(o_source_top, o_top, bsend, brecv, 0, dev_x),
             remote(o_source_low, o_low, bsend, brecv, 1, dev_y),
             remote(o_source_low, o_low, bsend, brecv, 2, dev_x),
@@ -1631,33 +1775,33 @@
         def _():
             for copy in o_copies:
                 copy.wait_recv()
-            total = o_mine[...].astype(F32)
+            whole = o_mine[...].astype(F32)
             for i in range(depths - 1):
-                total = total + o_far[i].astype(F32)
-            o_sum[...] = total.astype(BF16)
-            for copy in b_copies[:4]:
+                whole = whole + o_far[i].astype(F32)
+            o_sum[...] = whole.astype(BF16)
+            for copy in o_ring[:4]:
                 copy.start()
             o_all[core] = o_sum[...]
 
         turn_sums()
-        r_copies[0].wait_recv()
-        r_copies[4].start()
-        r_copies[1].wait_recv()
-        r_copies[5].start()
+        q_ring[0].wait_recv()
+        q_ring[4].start()
+        q_ring[1].wait_recv()
+        q_ring[5].start()
 
         @pl.when(from_x)
         def _():
-            b_copies[0].wait_recv()
-            b_copies[4].start()
-            b_copies[2].wait_recv()
+            o_ring[0].wait_recv()
+            o_ring[4].start()
+            o_ring[2].wait_recv()
 
         @pl.when(from_y)
         def _():
-            b_copies[1].wait_recv()
-            b_copies[5].start()
-            b_copies[3].wait_recv()
-
-        for copies, passed in ((f_copies, f_shared), (r_copies, q_shared)):
+            o_ring[1].wait_recv()
+            o_ring[5].start()
+            o_ring[3].wait_recv()
+
+        for copies, passed in ((b_ring, b_shared), (q_ring, q_shared)):
             copies[2].wait_recv()
             passed[1].start()
             copies[3].wait_recv()
@@ -1668,46 +1812,53 @@
 
         @pl.when(chip_d == depth)
         def _():
-            b_copies[4].wait_recv()
-            b_copies[5].wait_recv()
+            o_ring[4].wait_recv()
+            o_ring[5].wait_recv()
 
         o_shared.start()
         total_ref[...] = end()
-        for copy in f_shared + q_shared + [o_shared]:
+        for copy in a_shared + b_shared + q_shared + [o_shared]:
             copy.wait()
-        for copy in near_grads + [swap] + sends + core_swaps + q_copies + f_copies + r_copies:
+        for copy in u_copies + near_grads + [swap] + sends + [core_swap] + q_copies + a_ring + b_ring + q_ring:
             copy.wait_send()
         for i in range(depths - 1):
             pl.when(distance == i + 1)(o_copies[i].wait_send)
-        ff_finish()
 
         @pl.when(source)
         def _():
-            for copy in b_copies[:4]:
+            for copy in o_ring[:4]:
                 copy.wait_send()
 
-        pl.when(from_x)(b_copies[4].wait_send)
-        pl.when(from_y)(b_copies[5].wait_send)
+        pl.when(from_x)(o_ring[4].wait_send)
+        pl.when(from_y)(o_ring[5].wait_send)
 
     vmem = pltpu.VMEM
     block = (rows, width)
     wide_rows = (CHIPS, rows, width)
-    q_block, o_block = (part_rows, columns), (half, width)
+    q_block, o_block = (half, lanes_all), (half, width)
     kv_half = (2, CHIPS, rows, columns)
-    f_block = ff_grads.shape[1:]
-    line_buffers, line_sems = line_reduce_scratch(f_block, depths)
+    a_block, b_block = ff_early.shape, (late_rows, ff_columns)
+    ctx = 2 * CHIPS
     return pl.pallas_call(
         kernel,
         out_shape=[
             jax.ShapeDtypeStruct((rows, 2, width), BF16),
-            jax.ShapeDtypeStruct((2 * CHIPS,) + f_block, BF16),
-            jax.ShapeDtypeStruct((2 * CHIPS,) + q_block, BF16),
+            jax.ShapeDtypeStruct((ctx,) + a_block, BF16),
+            jax.ShapeDtypeStruct((ctx,) + b_block, BF16),
+            jax.ShapeDtypeStruct((ctx,) + q_block, BF16),
             jax.ShapeDtypeStruct((2,) + o_block, BF16),
             jax.ShapeDtypeStruct((8, width), F32),
         ],
-        in_specs=[SM] * 4 + [VM] * 17 + [ANY],
-        out_specs=[VM] * 5,
+        in_specs=[SM] * 4 + [VM] * 9 + [ANY] * 7,
+        out_specs=[VM] * 6,
         scratch_shapes=[
+            vmem((3, width, columns), BF16),
+            vmem((rows, 2, width), BF16),
+            vmem(block, F32),
+            vmem(block, F32),
+            vmem(block, F32),
+            vmem(wide_rows, BF16),
+            vmem(a_block, BF16),
             vmem((queries, columns), BF16),
             vmem((columns, tokens), BF16),
             vmem((columns, TILE), F32),
@@ -1724,108 +1875,114 @@
             vmem(kv_half, BF16),
             vmem(kv_half, BF16),
             vmem(kv_half, BF16),
-            vmem(wide_rows, BF16),
             vmem((width, queries), BF16),
             vmem(wide_rows, BF16),
-            vmem((3,) + block, BF16),
+            vmem((2,) + block, BF16),
+            vmem((2, rows // 2, width), BF16),
             vmem(block, F32),
             vmem((depths, 2) + q_block, BF16),
             vmem((depths,) + q_block, BF16),
             vmem((depths,) + q_block, BF16),
             vmem((depths - 1,) + q_block, BF16),
-            vmem((3, columns, width), BF16),
-            vmem((2,) + o_block, BF16),
-            vmem(o_block, BF16),
+            vmem(q_block, BF16),
+            vmem((3,) + o_block, BF16),
             vmem(o_block, BF16),
             vmem((depths - 1,) + o_block, BF16),
-            vmem(f_block, BF16),
-            vmem(q_block, BF16),
             vmem(o_block, BF16),
+            vmem((depths - 1,) + b_block, BF16),
+            vmem(b_block, BF16),
             vmem((8, width), F32),
-            *line_buffers,
-            *line_sems,
-            DMA,
-            DMA((3,)),
-            DMA((3,)),
-            DMA((1,)),
-            DMA((1,)),
-            DMA((3,)),
-            DMA((3,)),
-            DMA((2,)),
-            DMA((2,)),
-            DMA((depths - 1,)),
-            DMA((depths - 1,)),
-            DMA((depths - 1,)),
-            DMA((depths - 1,)),
-            *[DMA((6,))] * 6,
-            *[DMA((9,))] * 2,
+            DMA((7,)),
+            *[DMA((3,))] * 2,
+            *[DMA((1,))] * 2,
+            *[DMA((6,))] * 2,
+            *[DMA((1,))] * 2,
+            *[DMA((depths - 1,))] * 6,
+            *[DMA((6,))] * 8,
+            *[DMA((13,))] * 2,
             *total_scratch((8, width), depths),
         ],
         compiler_params=comm_params(collective_id),
         name="backward",
     )(
-        slots, lengths, predict, correct, att_grad, q_pairs, k_pairs, v_pairs, oT, lse, weights, states, up0, up1,
-        hidden_grad, sums, ff_grads, *out_grads, all_rows,
-    )
-
-
-def lay_out(ff, qkv, out, sums, gain_one, gain_two):
-    ctx, part_rows, columns = ff.shape
-    half, width = out.shape[1:]
+        slots, lengths, predict, correct, att_grad, q_pairs, k_pairs, v_pairs, oT, lse, sums, up_grads,
+        out_grads, ff_early, weights, states, up0, up1, hidden_grad, own_rows,
+    )
+
+
+def lay_out(early, late, qkv, out, sums, gain_one, gain_two):
+    ctx, half, columns = early.shape
+    width = out.shape[2]
     shard = 2 * half
     depths = width // shard
     split = columns // depths
+    steps = 3
+    strip = half // steps
 
     def kernel(
-        f_ref, q_ref, o_ref, s_ref, g1_ref, g2_ref,
-        dq_ref, dk_ref, dv_ref, do_ref, dg_ref, du_ref, dd_ref, g1_out, g2_out, p_out, c_out,
+        d_ref, g_ref, u_ref, q_ref, o_ref, s_ref, g1_ref, g2_ref,
+        dq_ref, dk_ref, dv_ref, do_ref, dg_ref, du_ref, dd_ref, g1_out, g2_out, p_out, c_out, columns_ref,
     ):
+        core, step = pl.program_id(0), pl.program_id(1)
         depth = lax.axis_index("wsh")
-        one, two = g1_ref[...].astype(F32), g2_ref[...].astype(F32)
-        one_column, two_column = as_column(one), as_column(two)
-        for c in range(2):
-            rows = slice(c * half, (c + 1) * half)
-            do_ref[rows, :] = o_ref[c].astype(F32)
-            for i, ref in enumerate((dq_ref, dk_ref, dv_ref)):
+
+        @pl.when((core == 0) & (step == 0))
+        def _():
+            one, two = g1_ref[...].astype(F32), g2_ref[...].astype(F32)
+            columns_ref[0] = jnp.broadcast_to(as_column(one), (shard, 128))
+            columns_ref[1] = jnp.broadcast_to(as_column(two), (shard, 128))
+            for z in range(depths):
+
+                @pl.when(depth == z)
+                def _(z=z):
+                    g1_out[...] = s_ref[0:1, z * shard : (z + 1) * shard] / one
+                    g2_out[...] = s_ref[1:2, z * shard : (z + 1) * shard] / two
+
+            scalars = jnp.sum(s_ref[...], axis=1, keepdims=True)
+            for i in range(2):
+                c_out[:, i : i + 1] = scalars[2 + i : 3 + i]
+                for j in range(2):
+                    at = 4 + 2 * i + j
+                    p_out[i : i + 1, j : j + 1] = scalars[at : at + 1]
+
+        rows = aligned(core * steps + step, strip)
+        one, two = columns_ref[0, rows, 0:1], columns_ref[1, rows, 0:1]
+        do_ref[...] = o_ref[...].astype(F32)
+        for i, ref in enumerate((dq_ref, dk_ref, dv_ref)):
+            wide = jnp.concatenate(
+                [q_ref[p, :, i * CHIP_COLS : (i + 1) * CHIP_COLS].astype(F32) for p in range(CHIPS)], axis=1
+            )
+            ref[...] = wide * one
+        for source, ref in ((g_ref, dg_ref), (u_ref, du_ref)):
+            for z in range(depths):
                 wide = jnp.concatenate(
-                    [q_ref[2 * p + c, i * half : (i + 1) * half, :].astype(F32) for p in range(CHIPS)],
-                    axis=1,
+                    [source[p, :, z * split : (z + 1) * split].astype(F32) for p in range(CHIPS)], axis=1
                 )
-                ref[rows, :] = wide * one_column[rows]
-            for i, ref in enumerate((dg_ref, du_ref)):
-                for z in range(depths):
-                    wide = jnp.concatenate(
-                        [
-                            f_ref[
-                                2 * p + c, i * half : (i + 1) * half, z * split : (z + 1) * split
-                            ].astype(F32)
-                            for p in range(CHIPS)
-                        ],
-                        axis=1,
-                    )
-                    ref[rows, z * CHIPS * split : (z + 1) * CHIPS * split] = wide * two_column[rows]
-            for p in range(CHIPS):
-                at = (2 * p + c) * half
-                dd_ref[at : at + half, :] = f_ref[2 * p + c, 2 * half :, :].astype(F32)
-        for z in range(depths):
-
-            @pl.when(depth == z)
-            def _(z=z):
-                g1_out[...] = s_ref[0:1, z * shard : (z + 1) * shard] / one
-                g2_out[...] = s_ref[1:2, z * shard : (z + 1) * shard] / two
-
-        scalars = jnp.sum(s_ref[...], axis=1, keepdims=True)
-        for i in range(2):
-            c_out[:, i : i + 1] = scalars[2 + i : 3 + i]
-            for j in range(2):
-                at = 4 + 2 * i + j
-                p_out[i : i + 1, j : j + 1] = scalars[at : at + 1]
-
+                ref[:, z * CHIPS * split : (z + 1) * CHIPS * split] = wide * two
+        dd_ref[...] = d_ref[...].astype(F32)
+
+    early = early.reshape(CHIPS, 2, half, columns)
+    late = late.reshape(CHIPS, 2, 2, half, columns)
+    qkv = qkv.reshape(CHIPS, 2, half, -1)
     square = jax.ShapeDtypeStruct((shard, width), F32)
     tall = jax.ShapeDtypeStruct((shard, columns * CHIPS), F32)
     row = jax.ShapeDtypeStruct((1, shard), F32)
-    return pl.pallas_call(
+
+    def whole(shape):
+        return pl.BlockSpec(shape, lambda c, r: (0,) * len(shape))
+
+    def piece(lanes):
+        return pl.BlockSpec((CHIPS, None, strip, lanes), lambda c, r: (0, c, r, 0))
+
+    def part(i):
+        return pl.BlockSpec((CHIPS, None, None, strip, columns), lambda c, r: (0, c, i, r, 0))
+
+    def strip_of(lanes):
+        return pl.BlockSpec((strip, lanes), lambda c, r: (c * steps + r, 0))
+
+    outs = pl.pallas_call(
         kernel,
+        grid=(2, steps),
         out_shape=[
             square,
             square,
@@ -1833,35 +1990,57 @@
             square,
             tall,
             tall,
-            jax.ShapeDtypeStruct((ctx * half, width), F32),
+            jax.ShapeDtypeStruct((CHIPS, 2, half, width), F32),
             row,
             row,
             jax.ShapeDtypeStruct((2, 2), F32),
             jax.ShapeDtypeStruct((1, 2), F32),
         ],
-        in_specs=[VM] * 6,
-        out_specs=[VM] * 11,
+        in_specs=[
+            piece(columns),
+            part(0),
+            part(1),
+            piece(3 * CHIP_COLS),
+            pl.BlockSpec((None, strip, width), lambda c, r: (c, r, 0)),
+            whole((8, width)),
+            whole((1, shard)),
+            whole((1, shard)),
+        ],
+        out_specs=[
+            strip_of(width),
+            strip_of(width),
+            strip_of(width),
+            strip_of(width),
+            strip_of(columns * CHIPS),
+            strip_of(columns * CHIPS),
+            piece(width),
+            whole((1, shard)),
+            whole((1, shard)),
+            whole((2, 2)),
+            whole((1, 2)),
+        ],
+        scratch_shapes=[pltpu.VMEM((2, shard, 128), F32)],
         compiler_params=pltpu.CompilerParams(vmem_limit_bytes=VMEM_LIMIT),
         name="lay_out",
-    )(ff, qkv, out, sums, gain_one, gain_two)
+    )(early, late, late, qkv, out, sums, gain_one, gain_two)
+    return (*outs[:6], outs[6].reshape(ctx * half, width), *outs[7:])
 
 
 def plane_shards(
     states, block_slot, cont_lengths, valid_mask, teacher, out_grad, predict, correct,
     norm_attn, w_query, w_key, w_value, w_out, norm_ffn, w_gate, w_up, w_down,
 ):
-    _, rows, _, width = states.shape
     slots, lengths = block_slot[0], cont_lengths[0]
     gain_one, gain_two = norm_attn[None], norm_ffn[None]
     states = states[0]
-    new_states, up0, up1, hidden_grad, att_grad, *rest = forward(
+    new_states, up0, up1, hidden_grad, att_grad, out_grads, ff_early, up_grads, sums, *saved = forward(
         slots, lengths, predict, correct, states, out_grad[0], teacher[0], valid_mask, gain_one, gain_two,
         w_query, w_key, w_value, w_out, w_gate, w_up, w_down, 1,
     )
-    out_grads, (ff_sum, sums, all_rows, weights, q_pairs, k_pairs, v_pairs, oT, lse) = rest[:4], rest[4:]
+    own_rows, weights, q_pairs, k_pairs, v_pairs, oT, lse = saved
     states_grad, *gathered = backward(
         slots, lengths, predict, correct, att_grad.reshape(-1, CHIP_COLS), q_pairs, k_pairs, v_pairs, oT, lse,
-        weights, states, up0, up1, hidden_grad, sums, ff_sum, out_grads, all_rows.reshape(CHIPS, 2, rows, width), 2,
+        sums, up_grads, out_grads, ff_early, weights, states, up0, up1, hidden_grad, own_rows, 2,
     )
     dq, dk, dv, do, dg, du, dd, g_one, g_two, predict_grad, correct_grad = lay_out(
         *gathered, gain_one, gain_two

time: 222 us -> 201 us (0.905)
  Pallas kernels: 216 us -> 195 us
    pallas_call x1, Pallas kernels: 84.7 us -> 70 us  [backward(): pl.pallas_call(kernel, out_shape=[jax.ShapeDtypeStruct((rows, 2, width),...]
    pallas_call x1, Pallas kernels: 124 us -> 117 us  [forward(): pl.pallas_call(kernel, out_shape=outs, in_specs=[SM] * 4 + [VM] * 6 + [AN...]
where the time goes in v6:
time: 201 us; the launch traced here: 200 us
  Pallas kernels  195 us (97%)
  local copies, waits for them, and re-layouts  4.72 us (2%)
    pallas_call x1, Pallas kernels, forward(): pl.pallas_call(kernel, out_shape=outs, in_specs=[SM] * 4 + [VM] * 6 + [AN...  117 us
    pallas_call x1, Pallas kernels, backward(): pl.pallas_call(kernel, out_shape=[jax.ShapeDtypeStruct((rows, 2, width),...  70 us
    pallas_call x1, Pallas kernels, lay_out(): pl.pallas_call(kernel, grid=(2, steps), out_shape=[square, square, square...  7.95 us

profile of v6, /device:TPU:9, one launch (start us, length us, event | category | flops | bytes accessed | tf_op | source)
XLA Modules:
  0.0 200.5 jit_solution(13710386291594426093)
XLA Ops:
  0.6 1.2 broadcast_in_dim.12.g1_ref
  1.9 1.2 broadcast_in_dim.13.g2_ref
  3.1 117.1 %forward.1 = (bf16[256,2,768]{2,1,0:T(2,128)(2,1)}, f32[256,768]{1,0:T(8,128)}, f32[256,768]{1,0:T(8,128)}, f32[256,768]{1,0:T(8,128)}, bf16[4,256,192]{2,1,0:T(...) custom-call(s32[32]{0:T(128)} %bitcast.26, ...), custom_call_target="tpu_custom_call" | custom-call | tf_op jit(solution)/shard_map/forward/pallas_call | solution.py:1376
  120.2 70.0 %backward.1 = (bf16[256,2,768]{2,1,0:T(2,128)(2,1)}, bf16[8,96,768]{2,1,0:T(8,128)(2,1)}, bf16[8,192,768]{2,1,0:T(8,128)(2,1)}, bf16[8,96,576]{2,1,0:T(8,128)(2,...) custom-call(s32[32]{0:T(128)} %bitcast.27, s32[4]{0:T(128)} %bitcast.29, f32[2,2]{1,0:T(2,128)} %p_ref.3, f32[2]{0:T(128)} %c_ref.3, ...), custom_call_target="tpu_custom_call" | custom-call | tf_op jit(solution)/shard_map/backward/pallas_call | solution.py:1842
  190.2 0.0 copy-start
  190.2 8.0 %lay_out.1 = (f32[192,768]{1,0:T(8,128)}, f32[192,768]{1,0:T(8,128)}, f32[192,768]{1,0:T(8,128)}, f32[192,768]{1,0:T(8,128)}, f32[192,3072]{1,0:T(8,128)}, /*ind...) custom-call(bf16[4,2,96,768]{3,2,1,0:T(8,128)(2,1)} %bitcast.19, ...), custom_call_target="tpu_custom_call" | custom-call | tf_op jit(solution)/shard_map/lay_out/pallas_call | solution.py:1983
  198.2 0.0 copy-start.1
  198.2 0.0 copy-done
  198.2 0.9 copy.32
  199.1 0.5 copy-done.1
  199.6 0.9 copy.33
Async XLA Ops:
  190.2 8.0 %copy-start = (bf16[256,2,768]{2,1,0:T(2,128)(2,1)S(1)}, bf16[256,2,768]{2,1,0:T(2,128)(2,1)}, u32[]{:S(2)}) copy-start(bf16[256,2,768]{2,1,0:T(2,128)(2,1)} %get-tuple-element.46) | copy-start | bytes 2359300
  198.2 1.4 copy-start.1

commit v7 on v6

--- a/solution.py
+++ b/solution.py
@@ -773,7 +773,7 @@
         new_out, up0_out, up1_out, hg_out, da_ref, dwo_ref, ffa_ref, ffb_ref, sums_ref,
         x_out, w_out_ref, q_out, k_out, v_out, oT_out, lse_ref,
         new_ref, up0_ref, up1_ref, hg_ref, all_rows, w_all, q_pairs, k_pairs, v_pairs, oT_ref, dwo, dwo_other,
-        w_ff, w_wo, qkv, att_all, hidden, own, x_rows, r_rows, xT, innerT, inner, gate, up, gate_low, up_low,
+        w_ff, w_wo, qkv, att_all, packs, packed_in, packed_grad, hidden, own, x_rows, r_rows, xT, innerT, inner, gate, up, gate_low, up_low,
         own_weight, part1, part2, got1, got2, far1, far2, dw, dw_other, a_up, a_down, buf, wide, count, q_slot, k_slot, v_slot, vT,
         lsend, fsend, frecv, fosend, forecv, qsend, qrecv, qosend, qorecv,
         osend, orecv, oosend, oorecv, opsend, oprecv,
@@ -826,7 +826,7 @@
         lax.fori_loop(0, blocks, input_norm, 0)
 
         def gain_column(ref):
-            both = jnp.broadcast_to(ref[...].astype(F32), (8, shard)).T
+            both = jnp.broadcast_to(ref[...].astype(F32).reshape(1, shard), (8, shard)).T
             return jnp.where(core == 0, both[:half, 0:1], both[half:, 0:1])
 
         one, two = gain_column(g1_ref), gain_column(g2_ref)
@@ -1086,21 +1086,32 @@
 
         store(4, oT_ref, oT_out)
         own_to_slot_order(q_slot, k_slot, slots_ref, pairs, per_device)
+        half_rows = rows // 2
+
+        def pack(value):
+            return jnp.concatenate([value[:half_rows].astype(F32), value[half_rows:].astype(F32)], axis=1).astype(BF16)
+
+        def unpack(target, packed):
+            target[0:half_rows, :] = packed[:, 0:CHIP_COLS]
+            target[half_rows:rows, :] = packed[:, CHIP_COLS : 2 * CHIP_COLS]
+
         for c in range(CHIPS):
-            att_all[CHIPS + c] = k_slot[c * rows : (c + 1) * rows, :]
+            packs[c] = pack(k_slot[c * rows : (c + 1) * rows, :])
         sends0 = [
-            remote(att_all.at[CHIPS + c], att_all.at[chip], send0, recv0, i, device)
+            remote(packs.at[c], packed_in.at[i], send0, recv0, i, device)
             for i, (c, device) in enumerate(near)
         ]
         for copy in sends0:
             copy.start()
-        att_all[chip] = att_all[CHIPS + chip]
+        unpack(att_all.at[chip], packs[chip])
         take_hop(2)
         send_hop(3)
         for copy in o_across:
             copy.wait_recv()
         for copy in sends0:
             copy.wait()
+        for i, (c, _) in enumerate(near):
+            unpack(att_all.at[c], packed_in[i])
 
         def w_out_rows(p):
             return w_wo[p].reshape(CHIP_COLS, width)
@@ -1304,17 +1315,17 @@
         store(10, hg_ref, hg_out)
 
         sends3 = [
-            remote(att_all.at[CHIPS + c], da_ref.at[chip], send3, recv3, i, device)
+            remote(packs.at[c], packed_grad.at[i], send3, recv3, i, device)
             for i, (c, device) in enumerate(near)
         ]
 
         def att_grad(c):
-            return lax.dot_general(own[3], w_out_rows(c), NT, preferred_element_type=F32).astype(BF16)
+            return lax.dot_general(own[3], w_out_rows(c), NT, preferred_element_type=F32)
 
         for i in (2, 0, 1):
-            att_all[CHIPS + near[i][0]] = att_grad(near[i][0])
+            packs[near[i][0]] = pack(att_grad(near[i][0]))
             sends3[i].start()
-        da_ref[chip] = att_grad(chip)
+        da_ref[chip] = att_grad(chip).astype(BF16)
         for i, c in enumerate((chip, chip_x, chip_y, chip_d)):
             grad = jnp.dot(att_all[c].T, own[3], preferred_element_type=F32).astype(BF16)
             dwo[i, 0] = grad[:half]
@@ -1333,6 +1344,8 @@
         ffa_ref[...] = gate[0, 0:half, :].astype(BF16)
         for copy in sends3:
             copy.wait_recv()
+        for i, (c, _) in enumerate(near):
+            unpack(da_ref.at[c], packed_grad[i])
         sent = ring0 + shared0 + q_copies + q_shared + o_plane + o_across + sends2 + sends3
         for copy in sent + ring1 + ring2 + swaps + [out_swap, ff_mine]:
             copy.wait_send()
@@ -1394,7 +1407,10 @@
             vmem((3, depths, 2, half, columns), BF16),
             vmem((depths, CHIPS, out_rows, width), BF16),
             vmem((depths, 2, half, piece_lanes), BF16),
-            vmem((2 * CHIPS, rows, CHIP_COLS), BF16),
+            vmem((CHIPS, rows, CHIP_COLS), BF16),
+            vmem((CHIPS, rows // 2, 2 * CHIP_COLS), BF16),
+            vmem((3, rows // 2, 2 * CHIP_COLS), BF16),
+            vmem((3, rows // 2, 2 * CHIP_COLS), BF16),
             vmem(block, F32),
             vmem((4,) + block, BF16),
             vmem(wide_rows, BF16),
@@ -1470,10 +1486,10 @@
     wide_lanes = LOCAL_HEADS * TILE
 
     def kernel(
-        slots_ref, lengths_ref, p_ref, c_ref, g_ref, q_ref, k_ref, v_ref, oT_ref, lse_ref, sums_ref, u_ref,
-        og_ref, fa_ref, w_in, s_in, up0_in, up1_in, hg_in, x_in,
+        slots_ref, lengths_ref, p_ref, c_ref, g_in, q_in, k_in, v_in, oT_in, lse_ref, sums_ref, u_in,
+        og_in, fa_ref, w_in, s_in, up0_in, up1_in, hg_in, x_in,
         grad_ref, fa_all, fb_all, q_all, o_all, total_ref,
-        w_all, s_ref, up0_ref, up1_ref, hg_ref, x_own, fa_own,
+        w_all, s_ref, up0_ref, up1_ref, hg_ref, x_own, fa_own, g_ref, q_ref, k_ref, v_ref, oT_ref, u_ref, og_ref,
         g_pairs, kT, doT, dqT, q_stack, do_stack, p_buf, ds_buf, dk_acc, dv_acc, bias, dq_pairs, dq_rows,
         give, kept, came, xT, part, got, far, mine, q_grad, q_other, q_mine, q_far, q_sum,
         o_near, o_mine, o_far, o_sum, u_far, u_sum, all_sums,
@@ -1498,7 +1514,14 @@
             copy.start()
             return copy
 
+        first_loads = [
+            load(7 + i, source, target)
+            for i, (source, target) in enumerate(
+                ((g_in, g_ref), (k_in, k_ref), (q_in, q_ref), (v_in, v_ref), (oT_in, oT_ref))
+            )
+        ]
         early_load = load(0, fa_ref, fa_own)
+        sum_loads = [load(12, u_in, u_ref), load(13, og_in, og_ref)]
         other_loads = [
             load(1 + i, source, target)
             for i, (source, target) in enumerate(
@@ -1514,8 +1537,9 @@
                 for i, device in enumerate(across)
             ]
 
-        own_to_pair_order(g_ref, g_pairs, slots_ref, pairs, per_device)
         early_load.wait()
+        for copy in sum_loads:
+            copy.wait()
         wait_all(everyone)
         u_copies = depth_sum(lambda z: u_ref.at[z], u_far, usend, urecv)
         near_grads = [
@@ -1538,6 +1562,10 @@
         o_shared = shared(12, o_all.at[core])
         fa_all[slot(chip)] = fa_own[...]
         a_shared[0].start()
+
+        for copy in first_loads:
+            copy.wait()
+        own_to_pair_order(g_ref, g_pairs, slots_ref, pairs, per_device)
 
         def turn_keys(i, _):
             at = aligned(i, TILE)
@@ -1678,6 +1706,17 @@
             q_grad[z, 1] = grad[half:]
             return 0
 
+        lax.fori_loop(0, depths, weight_grads, 0)
+        core_swap = remote(q_grad.at[:, 1 - core], q_other, ssend, srecv, 0, other)
+        core_swap.start()
+        relay_rows()
+        core_swap.wait_recv()
+        for i in range(depths):
+            q_mine[i] = (q_grad[i, core].astype(F32) + q_other[i].astype(F32)).astype(BF16)
+        q_copies = depth_sum(lambda z: q_mine.at[z], q_far, zsend, zrecv)
+        for copy in q_copies:
+            copy.start()
+
         for copy in u_copies:
             copy.wait_recv()
         whole = u_ref[depth].astype(F32)
@@ -1691,21 +1730,6 @@
             copy.start()
         fb_all[slot(chip)] = u_sum[...]
         b_shared[0].start()
-
-        lax.fori_loop(0, depths, weight_grads, 0)
-        core_swap = remote(q_grad.at[:, 1 - core], q_other, ssend, srecv, 0, other)
-        core_swap.start()
-        relay_rows()
-        core_swap.wait_recv()
-        for i in range(depths):
-            q_mine[i] = (q_grad[i, core].astype(F32) + q_other[i].astype(F32)).astype(BF16)
-        q_copies = depth_sum(lambda z: q_mine.at[z], q_far, zsend, zrecv)
-        for copy in q_copies:
-            copy.start()
-        b_ring[0].wait_recv()
-        b_ring[4].start()
-        b_ring[1].wait_recv()
-        b_ring[5].start()
         a_ring[2].wait_recv()
         a_shared[1].start()
         a_ring[3].wait_recv()
@@ -1736,6 +1760,10 @@
         totals = lax.fori_loop(
             0, blocks, state_grads, tuple(jnp.zeros((1, width), F32) for _ in range(5))
         )
+        b_ring[0].wait_recv()
+        b_ring[4].start()
+        b_ring[1].wait_recv()
+        b_ring[5].start()
         all_sums[...] = sums_ref[...]
         all_sums[0:1, :] = totals[0]
         for i in range(4):
@@ -1849,7 +1877,7 @@
             jax.ShapeDtypeStruct((2,) + o_block, BF16),
             jax.ShapeDtypeStruct((8, width), F32),
         ],
-        in_specs=[SM] * 4 + [VM] * 9 + [ANY] * 7,
+        in_specs=[SM] * 4 + [ANY] * 5 + [VM] * 2 + [ANY] * 9,
         out_specs=[VM] * 6,
         scratch_shapes=[
             vmem((3, width, columns), BF16),
@@ -1859,6 +1887,13 @@
             vmem(block, F32),
             vmem(wide_rows, BF16),
             vmem(a_block, BF16),
+            vmem((queries, columns), BF16),
+            vmem((queries, columns), BF16),
+            vmem((tokens, columns), BF16),
+            vmem((tokens, columns), BF16),
+            vmem(oT.shape, F32),
+            vmem(up_grads.shape, BF16),
+            vmem(out_grads.shape, BF16),
             vmem((queries, columns), BF16),
             vmem((columns, tokens), BF16),
             vmem((columns, TILE), F32),
@@ -1892,7 +1927,7 @@
             vmem((depths - 1,) + b_block, BF16),
             vmem(b_block, BF16),
             vmem((8, width), F32),
-            DMA((7,)),
+            DMA((14,)),
             *[DMA((3,))] * 2,
             *[DMA((1,))] * 2,
             *[DMA((6,))] * 2,
@@ -1916,7 +1951,7 @@
     shard = 2 * half
     depths = width // shard
     split = columns // depths
-    steps = 3
+    steps = 1
     strip = half // steps
 
     def kernel(
@@ -1928,7 +1963,8 @@
 
         @pl.when((core == 0) & (step == 0))
         def _():
-            one, two = g1_ref[...].astype(F32), g2_ref[...].astype(F32)
+            one = g1_ref[...].astype(F32).reshape(1, shard)
+            two = g2_ref[...].astype(F32).reshape(1, shard)
             columns_ref[0] = jnp.broadcast_to(as_column(one), (shard, 128))
             columns_ref[1] = jnp.broadcast_to(as_column(two), (shard, 128))
             for z in range(depths):
@@ -2003,8 +2039,8 @@
             piece(3 * CHIP_COLS),
             pl.BlockSpec((None, strip, width), lambda c, r: (c, r, 0)),
             whole((8, width)),
-            whole((1, shard)),
-            whole((1, shard)),
+            whole((shard,)),
+            whole((shard,)),
         ],
         out_specs=[
             strip_of(width),
@@ -2031,7 +2067,7 @@
     norm_attn, w_query, w_key, w_value, w_out, norm_ffn, w_gate, w_up, w_down,
 ):
     slots, lengths = block_slot[0], cont_lengths[0]
-    gain_one, gain_two = norm_attn[None], norm_ffn[None]
+    gain_one, gain_two = norm_attn, norm_ffn
     states = states[0]
     new_states, up0, up1, hidden_grad, att_grad, out_grads, ff_early, up_grads, sums, *saved = forward(
         slots, lengths, predict, correct, states, out_grad[0], teacher[0], valid_mask, gain_one, gain_two,

time: 201 us -> 193 us (0.960)
  Pallas kernels: 195 us -> 189 us
  local copies, waits for them, and re-layouts: 4.72 us -> 2.28 us
    pallas_call x1, Pallas kernels: 70 us -> 65.5 us  [backward(): pl.pallas_call(kernel, out_shape=[jax.ShapeDtypeStruct((rows, 2, width),...]
    broadcast_in_dim x2 -> x0, local copies, waits for them, and re-layouts: 2.44 us -> none  [plane_shards(): gain_one, gain_two = (norm_attn[None], norm_ffn[None])]
where the time goes in v7:
time: 193 us; the launch traced here: 192 us
  Pallas kernels  189 us (98%)
  local copies, waits for them, and re-layouts  2.28 us (1%)
    pallas_call x1, Pallas kernels, forward(): pl.pallas_call(kernel, out_shape=outs, in_specs=[SM] * 4 + [VM] * 6 + [AN...  118 us
    pallas_call x1, Pallas kernels, backward(): pl.pallas_call(kernel, out_shape=[jax.ShapeDtypeStruct((rows, 2, width),...  65.5 us
    pallas_call x1, Pallas kernels, lay_out(): pl.pallas_call(kernel, grid=(2, steps), out_shape=[square, square, square...  6.15 us

profile of v7, /device:TPU:9, one launch (start us, length us, event | category | flops | bytes accessed | tf_op | source)
XLA Modules:
  0.0 192.2 jit_solution(7755706579512448547)
XLA Ops:
  0.6 117.6 %forward.1 = (bf16[256,2,768]{2,1,0:T(2,128)(2,1)}, f32[256,768]{1,0:T(8,128)}, f32[256,768]{1,0:T(8,128)}, f32[256,768]{1,0:T(8,128)}, bf16[4,256,192]{2,1,0:T(...) custom-call(s32[32]{0:T(128)} %bitcast.26, ...), custom_call_target="tpu_custom_call" | custom-call | tf_op jit(solution)/shard_map/forward/pallas_call | solution.py:1389
  118.2 65.5 %backward.1 = (bf16[256,2,768]{2,1,0:T(2,128)(2,1)}, bf16[8,96,768]{2,1,0:T(8,128)(2,1)}, bf16[8,192,768]{2,1,0:T(8,128)(2,1)}, bf16[8,96,576]{2,1,0:T(8,128)(2,...) custom-call(s32[32]{0:T(128)} %bitcast.27, s32[4]{0:T(128)} %bitcast.29, f32[2,2]{1,0:T(2,128)} %p_ref.3, f32[2]{0:T(128)} %c_ref.3, ...), custom_call_target="tpu_custom_call" | custom-call | tf_op jit(solution)/shard_map/backward/pallas_call | solution.py:1870
  183.7 0.0 copy-start
  183.7 6.1 %lay_out.1 = (f32[192,768]{1,0:T(8,128)}, f32[192,768]{1,0:T(8,128)}, f32[192,768]{1,0:T(8,128)}, f32[192,768]{1,0:T(8,128)}, f32[192,3072]{1,0:T(8,128)}, /*ind...) custom-call(bf16[4,2,96,768]{3,2,1,0:T(8,128)(2,1)} %bitcast.19, ...), custom_call_target="tpu_custom_call" | custom-call | tf_op jit(solution)/shard_map/lay_out/pallas_call | solution.py:2019
  189.9 0.0 copy-start.1
  189.9 0.0 copy-done
  189.9 0.9 copy.32
  190.8 0.5 copy-done.1
  191.3 0.9 copy.33
Async XLA Ops:
  183.7 6.2 %copy-start = (bf16[256,2,768]{2,1,0:T(2,128)(2,1)S(1)}, bf16[256,2,768]{2,1,0:T(2,128)(2,1)}, u32[]{:S(2)}) copy-start(bf16[256,2,768]{2,1,0:T(2,128)(2,1)} %get-tuple-element.46) | copy-start | bytes 2359300
  189.9 1.4 copy-start.1

commit v8 on v7

--- a/solution.py
+++ b/solution.py
@@ -768,12 +768,12 @@
     piece_lanes = 3 * CHIP_COLS
 
     def kernel(
-        slots_ref, lengths_ref, p_ref, c_ref, s_ref, g_ref, t_ref, v_ref, g1_ref, g2_ref,
+        slots_ref, lengths_ref, p_ref, c_ref, s_ref, g_in, t_in, v_ref, g1_ref, g2_ref,
         wq_ref, wk_ref, wv_ref, wo_ref, wg_ref, wu_ref, wd_ref,
         new_out, up0_out, up1_out, hg_out, da_ref, dwo_ref, ffa_ref, ffb_ref, sums_ref,
         x_out, w_out_ref, q_out, k_out, v_out, oT_out, lse_ref,
         new_ref, up0_ref, up1_ref, hg_ref, all_rows, w_all, q_pairs, k_pairs, v_pairs, oT_ref, dwo, dwo_other,
-        w_ff, w_wo, qkv, att_all, packs, packed_in, packed_grad, hidden, own, x_rows, r_rows, xT, innerT, inner, gate, up, gate_low, up_low,
+        g_ref, t_ref, w_ff, w_wo, qkv, att_all, packs, packed_in, packed_grad, hidden, own, x_rows, r_rows, xT, innerT, inner, gate, up, gate_low, up_low,
         own_weight, part1, part2, got1, got2, far1, far2, dw, dw_other, a_up, a_down, buf, wide, count, q_slot, k_slot, v_slot, vT,
         lsend, fsend, frecv, fosend, forecv, qsend, qrecv, qosend, qorecv,
         osend, orecv, oosend, oorecv, opsend, oprecv,
@@ -810,6 +810,8 @@
             pltpu.make_async_copy(
                 wo_ref.at[pl.ds(chip * out_rows, out_rows)], w_wo.at[depth, chip], lsend.at[6]
             ),
+            pltpu.make_async_copy(g_in, g_ref, lsend.at[7]),
+            pltpu.make_async_copy(t_in, t_ref, lsend.at[8]),
         ]
         for copy in loads:
             copy.start()
@@ -1181,6 +1183,8 @@
             return 0
 
         lax.fori_loop(0, CHIPS, turn, 0)
+        for copy in loads[7:]:
+            copy.wait()
         valid_count = end_count()
         weight = as_column(v_ref[...].astype(F32)) * (mesh_tokens / valid_count[0:1, 0:1])
         own_weight[...] = jnp.broadcast_to(weight, own_weight.shape)
@@ -1389,7 +1393,7 @@
     return pl.pallas_call(
         kernel,
         out_shape=outs,
-        in_specs=[SM] * 4 + [VM] * 6 + [ANY] * 7,
+        in_specs=[SM] * 4 + [VM, ANY, ANY] + [VM] * 3 + [ANY] * 7,
         out_specs=[ANY] * 4 + [VM, ANY, VM, ANY, VM] + [ANY] * 6 + [VM],
         scratch_shapes=[
             vmem(pair, BF16),
@@ -1404,6 +1408,8 @@
             vmem((tiles, CHIP_COLS, TILE), F32),
             vmem((CHIPS, 2, half, width), BF16),
             vmem((CHIPS, half, width), BF16),
+            vmem(pair, BF16),
+            vmem(pair, BF16),
             vmem((3, depths, 2, half, columns), BF16),
             vmem((depths, CHIPS, out_rows, width), BF16),
             vmem((depths, 2, half, piece_lanes), BF16),
@@ -1441,7 +1447,7 @@
             vmem((tokens, CHIP_COLS), BF16),
             vmem((CHIP_COLS, tokens), BF16),
         ]
-        + [DMA((7,))]
+        + [DMA((9,))]
         + [DMA((2 * depths - 2,))] * 2
         + [DMA((2 * depths - 1,))] * 2
         + [DMA((depths - 1,))] * 2
@@ -1488,8 +1494,8 @@
     def kernel(
         slots_ref, lengths_ref, p_ref, c_ref, g_in, q_in, k_in, v_in, oT_in, lse_ref, sums_ref, u_in,
         og_in, fa_ref, w_in, s_in, up0_in, up1_in, hg_in, x_in,
-        grad_ref, fa_all, fb_all, q_all, o_all, total_ref,
-        w_all, s_ref, up0_ref, up1_ref, hg_ref, x_own, fa_own, g_ref, q_ref, k_ref, v_ref, oT_ref, u_ref, og_ref,
+        grad_out, fa_out, fb_out, q_all, o_all, total_ref,
+        grad_ref, fa_all, fb_all, w_all, s_ref, up0_ref, up1_ref, hg_ref, x_own, fa_own, g_ref, q_ref, k_ref, v_ref, oT_ref, u_ref, og_ref,
         g_pairs, kT, doT, dqT, q_stack, do_stack, p_buf, ds_buf, dk_acc, dv_acc, bias, dq_pairs, dq_rows,
         give, kept, came, xT, part, got, far, mine, q_grad, q_other, q_mine, q_far, q_sum,
         o_near, o_mine, o_far, o_sum, u_far, u_sum, all_sums,
@@ -1764,6 +1770,7 @@
         b_ring[4].start()
         b_ring[1].wait_recv()
         b_ring[5].start()
+        stores = [load(14, grad_ref, grad_out)]
         all_sums[...] = sums_ref[...]
         all_sums[0:1, :] = totals[0]
         for i in range(4):
@@ -1829,6 +1836,9 @@
             o_ring[5].start()
             o_ring[3].wait_recv()
 
+        for copy in a_shared:
+            copy.wait_recv()
+        stores.append(load(15, fa_all, fa_out))
         for copies, passed in ((b_ring, b_shared), (q_ring, q_shared)):
             copies[2].wait_recv()
             passed[1].start()
@@ -1837,6 +1847,9 @@
             copies[4].wait_recv()
             copies[5].wait_recv()
             passed[3].start()
+        for copy in b_shared:
+            copy.wait_recv()
+        stores.append(load(16, fb_all, fb_out))
 
         @pl.when(chip_d == depth)
         def _():
@@ -1845,7 +1858,11 @@
 
         o_shared.start()
         total_ref[...] = end()
-        for copy in a_shared + b_shared + q_shared + [o_shared]:
+        for copy in q_shared + [o_shared]:
+            copy.wait()
+        for copy in a_shared + b_shared:
+            copy.wait_send()
+        for copy in stores:
             copy.wait()
         for copy in u_copies + near_grads + [swap] + sends + [core_swap] + q_copies + a_ring + b_ring + q_ring:
             copy.wait_send()
@@ -1878,8 +1895,11 @@
             jax.ShapeDtypeStruct((8, width), F32),
         ],
         in_specs=[SM] * 4 + [ANY] * 5 + [VM] * 2 + [ANY] * 9,
-        out_specs=[VM] * 6,
+        out_specs=[ANY] * 3 + [VM] * 3,
         scratch_shapes=[
+            vmem((rows, 2, width), BF16),
+            vmem((ctx,) + a_block, BF16),
+            vmem((ctx,) + b_block, BF16),
             vmem((3, width, columns), BF16),
             vmem((rows, 2, width), BF16),
             vmem(block, F32),
@@ -1927,7 +1947,7 @@
             vmem((depths - 1,) + b_block, BF16),
             vmem(b_block, BF16),
             vmem((8, width), F32),
-            DMA((14,)),
+            DMA((17,)),
             *[DMA((3,))] * 2,
             *[DMA((1,))] * 2,
             *[DMA((6,))] * 2,
@@ -1945,7 +1965,7 @@
     )
 
 
-def lay_out(early, late, qkv, out, sums, gain_one, gain_two):
+def lay_out(new_states, states_grad, early, late, qkv, out, sums, gain_one, gain_two):
     ctx, half, columns = early.shape
     width = out.shape[2]
     shard = 2 * half
@@ -1955,8 +1975,8 @@
     strip = half // steps
 
     def kernel(
-        d_ref, g_ref, u_ref, q_ref, o_ref, s_ref, g1_ref, g2_ref,
-        dq_ref, dk_ref, dv_ref, do_ref, dg_ref, du_ref, dd_ref, g1_out, g2_out, p_out, c_out, columns_ref,
+        new_in, grad_in, d_ref, g_ref, u_ref, q_ref, o_ref, s_ref, g1_ref, g2_ref,
+        new_ref, grad_ref, dq_ref, dk_ref, dv_ref, do_ref, dg_ref, du_ref, dd_ref, g1_out, g2_out, p_out, c_out, columns_ref,
     ):
         core, step = pl.program_id(0), pl.program_id(1)
         depth = lax.axis_index("wsh")
@@ -1983,6 +2003,8 @@
 
         rows = aligned(core * steps + step, strip)
         one, two = columns_ref[0, rows, 0:1], columns_ref[1, rows, 0:1]
+        new_ref[...] = new_in[...]
+        grad_ref[...] = grad_in[...]
         do_ref[...] = o_ref[...].astype(F32)
         for i, ref in enumerate((dq_ref, dk_ref, dv_ref)):
             wide = jnp.concatenate(
@@ -2016,10 +2038,14 @@
     def strip_of(lanes):
         return pl.BlockSpec((strip, lanes), lambda c, r: (c * steps + r, 0))
 
+    rows = new_states.shape[0] // (2 * steps)
+    state_rows = pl.BlockSpec((rows,) + new_states.shape[1:], lambda c, r: (c * steps + r, 0, 0))
     outs = pl.pallas_call(
         kernel,
         grid=(2, steps),
         out_shape=[
+            jax.ShapeDtypeStruct(new_states.shape, BF16),
+            jax.ShapeDtypeStruct(states_grad.shape, BF16),
             square,
             square,
             square,
@@ -2033,6 +2059,8 @@
             jax.ShapeDtypeStruct((1, 2), F32),
         ],
         in_specs=[
+            state_rows,
+            state_rows,
             piece(columns),
             part(0),
             part(1),
@@ -2043,6 +2071,8 @@
             whole((shard,)),
         ],
         out_specs=[
+            state_rows,
+            state_rows,
             strip_of(width),
             strip_of(width),
             strip_of(width),
@@ -2058,8 +2088,8 @@
         scratch_shapes=[pltpu.VMEM((2, shard, 128), F32)],
         compiler_params=pltpu.CompilerParams(vmem_limit_bytes=VMEM_LIMIT),
         name="lay_out",
-    )(early, late, late, qkv, out, sums, gain_one, gain_two)
-    return (*outs[:6], outs[6].reshape(ctx * half, width), *outs[7:])
+    )(new_states, states_grad, early, late, late, qkv, out, sums, gain_one, gain_two)
+    return (*outs[:8], outs[8].reshape(ctx * half, width), *outs[9:])
 
 
 def plane_shards(
@@ -2078,8 +2108,8 @@
         slots, lengths, predict, correct, att_grad.reshape(-1, CHIP_COLS), q_pairs, k_pairs, v_pairs, oT, lse,
         sums, up_grads, out_grads, ff_early, weights, states, up0, up1, hidden_grad, own_rows, 2,
     )
-    dq, dk, dv, do, dg, du, dd, g_one, g_two, predict_grad, correct_grad = lay_out(
-        *gathered, gain_one, gain_two
+    new_states, states_grad, dq, dk, dv, do, dg, du, dd, g_one, g_two, predict_grad, correct_grad = lay_out(
+        new_states, states_grad, *gathered, gain_one, gain_two
     )
     return (
         new_states[None], states_grad[None], predict_grad, correct_grad[0],

time: 193 us -> 190 us (0.984)
  local copies, waits for them, and re-layouts: 2.28 us -> 0 us
    unnamed x6 -> x0, local copies, waits for them, and re-layouts: 2.28 us -> none
where the time goes in v8:
time: 190 us; the launch traced here: 189 us
  Pallas kernels  188 us (99%)
    pallas_call x1, Pallas kernels, forward(): pl.pallas_call(kernel, out_shape=outs, in_specs=[SM] * 4 + [VM, ANY, ANY]...  117 us
    pallas_call x1, Pallas kernels, backward(): pl.pallas_call(kernel, out_shape=[jax.ShapeDtypeStruct((rows, 2, width),...  64.2 us
    pallas_call x1, Pallas kernels, lay_out(): pl.pallas_call(kernel, grid=(2, steps), out_shape=[jax.ShapeDtypeStruct(n...  6.9 us

profile of v8, /device:TPU:9, one launch (start us, length us, event | category | flops | bytes accessed | tf_op | source)
XLA Modules:
  0.0 189.2 jit_solution(9174701871057205641)
XLA Ops:
  0.6 117.3 %forward.1 = (bf16[256,2,768]{2,1,0:T(2,128)(2,1)}, f32[256,768]{1,0:T(8,128)}, f32[256,768]{1,0:T(8,128)}, f32[256,768]{1,0:T(8,128)}, bf16[4,256,192]{2,1,0:T(...) custom-call(s32[32]{0:T(128)} %bitcast.24, ...), custom_call_target="tpu_custom_call" | custom-call | tf_op jit(solution)/shard_map/forward/pallas_call | solution.py:1393
  117.9 64.2 %backward.1 = (bf16[256,2,768]{2,1,0:T(2,128)(2,1)}, bf16[8,96,768]{2,1,0:T(8,128)(2,1)}, bf16[8,192,768]{2,1,0:T(8,128)(2,1)}, bf16[8,96,576]{2,1,0:T(8,128)(2,...) custom-call(s32[32]{0:T(128)} %bitcast.25, s32[4]{0:T(128)} %bitcast.27, f32[2,2]{1,0:T(2,128)} %p_ref.3, f32[2]{0:T(128)} %c_ref.3, ...), custom_call_target="tpu_custom_call" | custom-call | tf_op jit(solution)/shard_map/backward/pallas_call | solution.py:1887
  182.1 6.9 %lay_out.1 = (bf16[256,2,768]{2,1,0:T(2,128)(2,1)}, bf16[256,2,768]{2,1,0:T(2,128)(2,1)}, f32[192,768]{1,0:T(8,128)}, f32[192,768]{1,0:T(8,128)}, f32[192,768]{1...) custom-call(bf16[256,2,768]{2,1,0:T(2,128)(2,1)} %get-tuple-element., ...), custom_call_target="tpu_custom_call" | custom-call | tf_op jit(solution)/shard_map/lay_out/pallas_call | solution.py:2043

commit v9 on v8

--- a/solution.py
+++ b/solution.py
@@ -1106,8 +1106,6 @@
         for copy in sends0:
             copy.start()
         unpack(att_all.at[chip], packs[chip])
-        take_hop(2)
-        send_hop(3)
         for copy in o_across:
             copy.wait_recv()
         for copy in sends0:
@@ -1121,6 +1119,9 @@
         for p in range(CHIPS):
             term = jnp.dot(att_all[p], w_out_rows(p), preferred_element_type=F32)
             hidden[...] = term if p == 0 else hidden[...] + term
+
+        take_hop(2)
+        send_hop(3)
 
         def first_norm(i, _):
             at = aligned(i, ROWS)
@@ -1781,6 +1782,7 @@
         start()
         for copy in q_copies:
             copy.wait_recv()
+        turn_sums()
         whole = q_mine[depth].astype(F32)
         for i in range(depths - 1):
             whole = whole + q_far[i].astype(F32)
@@ -1818,7 +1820,6 @@
                 copy.start()
             o_all[core] = o_sum[...]
 
-        turn_sums()
         q_ring[0].wait_recv()
         q_ring[4].start()
         q_ring[1].wait_recv()

time: 190 us -> 191 us (level)
    pallas_call x1, Pallas kernels: 64.2 us -> 66.9 us  [backward(): pl.pallas_call(kernel, out_shape=[jax.ShapeDtypeStruct((rows, 2, width),...]
    pallas_call x1, Pallas kernels: 117 us -> 115 us  [forward(): pl.pallas_call(kernel, out_shape=outs, in_specs=[SM] * 4 + [VM, ANY, ANY]...]
where the time goes in v9:
time: 191 us; the launch traced here: 190 us
  Pallas kernels  189 us (99%)
    pallas_call x1, Pallas kernels, forward(): pl.pallas_call(kernel, out_shape=outs, in_specs=[SM] * 4 + [VM, ANY, ANY]...  115 us
    pallas_call x1, Pallas kernels, backward(): pl.pallas_call(kernel, out_shape=[jax.ShapeDtypeStruct((rows, 2, width),...  66.9 us
    pallas_call x1, Pallas kernels, lay_out(): pl.pallas_call(kernel, grid=(2, steps), out_shape=[jax.ShapeDtypeStruct(n...  6.9 us

profile of v9, /device:TPU:9, one launch (start us, length us, event | category | flops | bytes accessed | tf_op | source)
XLA Modules:
  0.0 189.9 jit_solution(2324242208726471800)
XLA Ops:
  0.6 115.3 %forward.1 = (bf16[256,2,768]{2,1,0:T(2,128)(2,1)}, f32[256,768]{1,0:T(8,128)}, f32[256,768]{1,0:T(8,128)}, f32[256,768]{1,0:T(8,128)}, bf16[4,256,192]{2,1,0:T(...) custom-call(s32[32]{0:T(128)} %bitcast.24, ...), custom_call_target="tpu_custom_call" | custom-call | tf_op jit(solution)/shard_map/forward/pallas_call | solution.py:1394
  116.0 66.9 %backward.1 = (bf16[256,2,768]{2,1,0:T(2,128)(2,1)}, bf16[8,96,768]{2,1,0:T(8,128)(2,1)}, bf16[8,192,768]{2,1,0:T(8,128)(2,1)}, bf16[8,96,576]{2,1,0:T(8,128)(2,...) custom-call(s32[32]{0:T(128)} %bitcast.25, s32[4]{0:T(128)} %bitcast.27, f32[2,2]{1,0:T(2,128)} %p_ref.3, f32[2]{0:T(128)} %c_ref.3, ...), custom_call_target="tpu_custom_call" | custom-call | tf_op jit(solution)/shard_map/backward/pallas_call | solution.py:1888
  182.8 6.9 %lay_out.1 = (bf16[256,2,768]{2,1,0:T(2,128)(2,1)}, bf16[256,2,768]{2,1,0:T(2,128)(2,1)}, f32[192,768]{1,0:T(8,128)}, f32[192,768]{1,0:T(8,128)}, f32[192,768]{1...) custom-call(bf16[256,2,768]{2,1,0:T(2,128)(2,1)} %get-tuple-element., ...), custom_call_target="tpu_custom_call" | custom-call | tf_op jit(solution)/shard_map/lay_out/pallas_call | solution.py:2044
